TPU v7x, 32 devices: a whole 2x2x4 slice. The times are simulated.
32 devices in a mesh: grp: 2 (over x), xp: 8 (over z, y), yp: 2 (over core).
Axes of the slice: x: 2, y: 2, z: 4, core: 2. Of those that a mesh axis runs over, the one named last changes fastest.
Arguments:
- features: bfloat16 [64, 30, 512], P(('grp', 'xp', 'yp')), parts along dimension 0, may hold values from -6 to 6
- cotangent: bfloat16 [64, 30, 512], P(('grp', 'xp', 'yp')), parts along dimension 0, may hold values from -6 to 6
- w_first: bfloat16 [27, 84], replicated, may hold values from -0.4375 to 0.4375
- w_second: bfloat16 [27, 84], replicated, may hold values from -0.4375 to 0.4375
- neighbours: int32 [64, 27], P(('grp', 'xp', 'yp')), parts along dimension 0, may hold values from 0 to 18
- mirror: int32 [64, 3], P(('grp', 'xp', 'yp')), parts along dimension 0, may hold values from 0 to 1, as said below
Outputs:
- denoised: bfloat16 [64, 30, 512], P(('grp', 'xp', 'yp')), parts along dimension 0
- grad_first: float32 [54, 84], P('grp'), parts along dimension 0
- grad_second: float32 [54, 84], P('grp'), parts along dimension 0
There are 2 independent parts, one for each index of `grp`. A program takes and returns all parts, laid end to end along the dimension named above; an argument that names none is the same for every part. Nothing has to cross between parts.
Inputs may be any that keep to these rules, and one draw needn't show every extreme that they name: mirror[n, r] is the slot on the image pencil of the image of brick n under half-turn r.
All inputs are finite; a program needn't handle non-finite values.
Results may differ from a plain program's by a relative error of at most 0.0056.
Values may be sent and summed in bfloat16 or wider, within the bound.
No kernel may reach another device: no remote copies, remote signals or barrier semaphores. Data moves between devices by JAX's collectives and lax.ppermute only.
A program may use at most 192 MiB of HBM per device.

v0:
```python
import jax
import jax.numpy as jnp
from jax import lax
from jax.sharding import PartitionSpec as P

flip_sets = ((3, 4), (2, 4), (2, 3))


def padded_2(value, sides, width):
    for axis, dim in sides:
        size, length = (lax.axis_size(axis), value.shape[dim])
        up = [(i, (i + 1) % size) for i in range(size - 1)]
        down = [(j, i) for i, j in up]
        last = lax.slice_in_dim(value, length - width, length, axis=dim)
        initial = lax.slice_in_dim(value, 0, width, axis=dim)
        before = lax.ppermute(last, axis, up)
        after = lax.ppermute(initial, axis, down)
        value = jnp.concatenate([before, value, after], axis=dim)
    return value


def swapped(value, axis, bit):
    mask = 2**bit
    pairs = [(source, source ^ mask) for source in range(lax.axis_size(axis))]
    return lax.ppermute(value, axis, pairs)


def rim_slice(index_value):
    return (slice(7, 8), slice(0, 8), slice(0, 1))[index_value]


def neighbourhood(field):
    count = field.shape[0]
    beside_all = padded_2(field[None, None], (("xp", 0), ("yp", 1)), 1)
    flat_bricks = beside_all.reshape(9 * count, 30, 8, 8, 8)
    return jnp.concatenate([flat_bricks, jnp.zeros((1, 30, 8, 8, 8), field.dtype)], axis=0)


def assemble(brick_table, rows):
    count = rows.shape[0]
    planes = []
    for a in range(3):
        stripes = []
        for b in range(3):
            pieces = []
            for c in range(3):
                rim = brick_table[:, :, rim_slice(a), rim_slice(b), rim_slice(c)]
                pieces.append(jnp.take(rim, rows[:, a * 9 + b * 3 + c], axis=0))
            stripes.append(jnp.concatenate(pieces, axis=4))
        planes.append(jnp.concatenate(stripes, axis=3))
    return jnp.concatenate(planes, axis=2).reshape(count, 30, 1000)


def window(padded, start):
    return lax.slice_in_dim(padded, start, start + 778, axis=2)


def interior(full):
    count = full.shape[0]
    wide = jnp.pad(full, ((0, 0), (0, 0), (0, 22)))
    wide = wide.reshape(count, 30, 8, 100)[:, :, :, :80].reshape(count, 30, 8, 8, 10)
    return wide[:, :, :, :, :8].reshape(count, 30, 512)


def embed(field):
    count = field.shape[0]
    cube = jnp.pad(field.reshape(count, 30, 8, 8, 8), ((0, 0), (0, 0), (0, 0), (0, 2), (0, 2)))
    return cube.reshape(count, 30, 800)[:, :, :778]


def split_weights(weights):
    scalar_w = weights[:, :64].reshape(27, 8, 8)
    vector_w = weights[:, 64:80].reshape(27, 4, 4)
    tensor_w = weights[:, 80:84].reshape(27, 2, 2) * 2
    vector_k = jnp.einsum("mn,oij->ominj", jnp.eye(3, dtype=weights.dtype), vector_w).reshape(
        27, 12, 12
    )
    tensor_k = jnp.einsum("mn,oij->ominj", jnp.eye(5, dtype=weights.dtype), tensor_w).reshape(
        27, 10, 10
    )
    blocks = jnp.zeros((27, 30, 30), weights.dtype)
    blocks = blocks.at[:, :8, :8].set(scalar_w)
    blocks = blocks.at[:, 8:20, 8:20].set(vector_k)
    blocks = blocks.at[:, 20:30, 20:30].set(tensor_k)
    return (scalar_w, vector_k, tensor_k, blocks)


def combine(parts, offset, source, transpose):
    scalar_w, vector_k, tensor_k, blocks = parts
    flat_form = "ji,njq->niq" if transpose else "ij,njq->niq"
    scalar_out = jnp.einsum(
        flat_form, scalar_w[offset], source[:, :8], preferred_element_type=jnp.float32
    )
    vector_out = jnp.einsum(
        flat_form, vector_k[offset], source[:, 8:20], preferred_element_type=jnp.float32
    )
    tensor_out = jnp.einsum(
        flat_form, tensor_k[offset], source[:, 20:], preferred_element_type=jnp.float32
    )
    return jnp.concatenate([scalar_out, vector_out, tensor_out], axis=1)


def convolve(padded, parts, transpose):
    total = jnp.zeros((padded.shape[0], 30, 778), jnp.float32)
    for a in range(3):
        for b in range(3):
            for c in range(3):
                if transpose:
                    start = (2 - a) * 100 + (2 - b) * 10 + (2 - c)
                else:
                    start = a * 100 + b * 10 + c
                total = total + combine(parts, a * 9 + b * 3 + c, window(padded, start), transpose)
    return interior(total)


def diagonal_blocks(full_g, start, width, repeats):
    block_sum = full_g[start : start + width, start : start + width]
    for m in range(1, repeats):
        low = start + width * m
        block_sum = block_sum + full_g[low : low + width, low : low + width]
    return block_sum


def weight_grad(grad, padded):
    placed = embed(grad)
    rows_out = []
    for a in range(3):
        for b in range(3):
            for c in range(3):
                source = window(padded, a * 100 + b * 10 + c)
                scalar_g = jnp.einsum(
                    "niq,njq->ij", placed[:, :8], source[:, :8], preferred_element_type=jnp.float32
                )
                vector_full = jnp.einsum(
                    "niq,njq->ij",
                    placed[:, 8:20],
                    source[:, 8:20],
                    preferred_element_type=jnp.float32,
                )
                tensor_full = jnp.einsum(
                    "niq,njq->ij",
                    placed[:, 20:],
                    source[:, 20:],
                    preferred_element_type=jnp.float32,
                )
                vector_g = diagonal_blocks(vector_full, 0, 4, 3)
                tensor_g = diagonal_blocks(tensor_full, 0, 2, 5) * 2.0
                rows_out.append(
                    jnp.concatenate(
                        [scalar_g.reshape(64), vector_g.reshape(16), tensor_g.reshape(4)]
                    )
                )
    return jnp.stack(rows_out)


def gate(pre):
    count = pre.shape[0]
    scalar_pre = pre[:, :8]
    sigmas = jax.nn.sigmoid(scalar_pre)
    vector_out = pre[:, 8:20].reshape(count, 3, 4, 512) * sigmas[:, None, :4]
    tensor_out = pre[:, 20:].reshape(count, 5, 2, 512) * sigmas[:, None, 4:6]
    return jnp.concatenate(
        [
            jax.nn.silu(scalar_pre),
            vector_out.reshape(count, 12, 512),
            tensor_out.reshape(count, 10, 512),
        ],
        axis=1,
    )


def gate_backward(pre, grad):
    count = pre.shape[0]
    scalar_pre = pre[:, :8]
    sigmas = jax.nn.sigmoid(scalar_pre)
    vector_pre = pre[:, 8:20].reshape(count, 3, 4, 512)
    tensor_pre = pre[:, 20:].reshape(count, 5, 2, 512)
    vector_grad = grad[:, 8:20].reshape(count, 3, 4, 512)
    tensor_grad = grad[:, 20:].reshape(count, 5, 2, 512)
    slope = sigmas * (1.0 + scalar_pre * (1.0 - sigmas))
    bend = sigmas * (1.0 - sigmas)
    vector_gate = jnp.sum(vector_grad * vector_pre, axis=1) * bend[:, :4]
    tensor_gate = jnp.sum(tensor_grad * tensor_pre, axis=1) * bend[:, 4:6]
    extra = jnp.concatenate(
        [vector_gate, tensor_gate, jnp.zeros((count, 2, 512), jnp.float32)], axis=1
    )
    scalar_grad = grad[:, :8] * slope + extra
    vector_out = vector_grad * sigmas[:, None, :4]
    tensor_out = tensor_grad * sigmas[:, None, 4:6]
    return jnp.concatenate(
        [scalar_grad, vector_out.reshape(count, 12, 512), tensor_out.reshape(count, 10, 512)],
        axis=1,
    )


def sign_table(which_turn):
    vector_signs = ((1.0, -1.0, -1.0), (-1.0, 1.0, -1.0), (-1.0, -1.0, 1.0))[which_turn]
    tensor_signs = (
        (-1.0, -1.0, 1.0, 1.0, 1.0),
        (-1.0, 1.0, -1.0, 1.0, 1.0),
        (1.0, -1.0, -1.0, 1.0, 1.0),
    )[which_turn]
    values = (
        [1.0] * 8
        + [vector_signs[m] for m in range(3) for k in range(4)]
        + [tensor_signs[m] for m in range(5) for k in range(2)]
    )
    return jnp.array(values, jnp.float32)


def rotate(stacked, slots, which_turn):
    moved = jnp.take(stacked, slots, axis=1)
    layers = moved.shape[0]
    count = moved.shape[1]
    cube = moved.reshape(layers, count, 30, 8, 8, 8)
    flip_axes = tuple((axis + 1 for axis in flip_sets[which_turn]))
    cube = jnp.flip(cube, flip_axes).reshape(layers, count, 30, 512).astype(jnp.float32)
    return cube * sign_table(which_turn)[:, None]


def flip_across_y(stacked):
    stacked = swapped(stacked, "yp", 0)
    return stacked


def flip_across_x(stacked):
    for bit in range(lax.axis_size("xp").bit_length() - 1):
        stacked = swapped(stacked, "xp", bit)
    return stacked


def symmetrize(stacked, mirror):
    layers = stacked.shape[0]
    across_y = flip_across_y(stacked)
    across = flip_across_x(jnp.concatenate([stacked, across_y], axis=0))
    total = stacked.astype(jnp.float32)
    total = total + rotate(across_y, mirror[:, 0], 0)
    total = total + rotate(across[:layers], mirror[:, 1], 1)
    total = total + rotate(across[layers:], mirror[:, 2], 2)
    return total * 0.25


def on_device(features, cotangent, w_first, w_second, neighbours, mirror):
    count = features.shape[0]
    first_parts = split_weights(w_first)
    second_parts = split_weights(w_second)
    padded_in = assemble(neighbourhood(features), neighbours)
    pre = convolve(padded_in, first_parts, False)
    hidden = gate(pre).astype(jnp.bfloat16)
    padded_hidden = assemble(neighbourhood(hidden), neighbours)
    second = convolve(padded_hidden, second_parts, False).astype(jnp.bfloat16)
    joined = symmetrize(jnp.stack([second, cotangent]), mirror)
    denoised = joined[0].astype(jnp.bfloat16)
    back = joined[1].astype(jnp.bfloat16)
    back_hidden = convolve(assemble(neighbourhood(back), neighbours), second_parts, True)
    back_pre = gate_backward(pre, back_hidden).astype(jnp.bfloat16)
    local_second = weight_grad(back, padded_hidden)
    local_first = weight_grad(back_pre, padded_in)
    sum_first, sum_second = lax.psum((local_first, local_second), ("xp", "yp"))
    total_bricks = count * lax.axis_size("xp") * lax.axis_size("yp")
    return (denoised, sum_first / total_bricks, sum_second / total_bricks)


def solution(mesh):
    in_specs = (
        P(("grp", "xp", "yp"), None, None),
        P(("grp", "xp", "yp"), None, None),
        P(),
        P(),
        P(("grp", "xp", "yp"), None),
        P(("grp", "xp", "yp"), None),
    )
    out_specs = (P(("grp", "xp", "yp"), None, None), P("grp", None), P("grp", None))
    return jax.shard_map(
        on_device, mesh=mesh, in_specs=in_specs, out_specs=out_specs, check_vma=False
    )
```

profile of v0, /device:TPU:0, one launch (start us, length us, event | category | flops | bytes accessed | tf_op | source)
XLA Modules:
  0.0 1108.8 jit_solution(581089140994526348)
XLA Ops:
  0.6 4.9 collective-permute-start
  139.9 2.7 copy.2107
  212.6 2.5 gather_fusion.13
  218.3 10.6 fusion.322
  228.9 10.6 fusion.321
  239.5 8.2 fusion.320
  247.7 4.7 fusion.325
  252.4 4.7 fusion.324
  257.1 3.3 fusion.323
  422.1 4.4 collective-permute-start.4
  458.8 2.7 copy.2241
  508.4 2.5 gather_fusion.40
  524.4 10.6 fusion.316
  535.0 10.8 fusion.315
  545.9 8.0 fusion.314
  553.9 4.7 fusion.319
  558.6 4.7 fusion.318
  563.3 3.3 fusion.317
  727.6 3.1 collective-permute-start.9
  731.3 5.9 collective-permute-done.9
  737.2 2.9 collective-permute-start.10
  812.0 2.7 collective-permute-start.11
  815.1 10.2 collective-permute-done.11
  877.9 2.7 copy.2384
  933.8 2.5 gather_fusion.70
  949.8 9.3 fusion.310
  959.1 9.5 fusion.309
  968.6 6.7 fusion.308
  975.3 3.6 fusion.313
  978.8 3.6 fusion.312
  982.5 2.6 fusion.311
  1044.8 62.6 %all-reduce.8 = (f32[27,84]{1,0:T(8,128)S(1)}, f32[27,84]{1,0:T(8,128)S(1)}) all-reduce(f32[27,84]{1,0:T(8,128)S(1)} %stack.204, f32[27,84]{1,0:T(8,128)S(1)} %copy-done.498), channel_id=1, replica_groups=mesh['grp'=2,'xp'=8,'yp'=2] {'xp','yp'}, use_global_device_ids=true, to_apply=%region_2.12 | all-reduce | flops 4536 | bytes 36288 | tf_op jit(solution)/shard_map/psum | solution.py:259
  (3138 shorter events, 866.1 us)
Async XLA Ops:
  0.6 131.2 %collective-permute-start = (bf16[1,1,2,30,512]{4,2,3,1,0:T(2,128)(2,1)}, bf16[1,1,2,30,512]{4,2,3,1,0:T(2,128)(2,1)S(1)}, u32[]{:S(2)}, u32[]{:S(2)}) collective-permute-start(bf16[1,1,2,30,512]{4,2,3,1,0:T(2,128)(2,1)} %bitcast.2289), channel_id=1, source_target_pairs={{0,2},{2,4},{4,6},{6,8},{8,10},{10,12},{12,14},{1,3},{3,5},{5,7},{... | collective-permute-start | bytes 184328 | tf_op jit(solution)/shard_map/ppermute | solution.py:16
  5.5 126.3 %collective-permute-start.1 = (bf16[1,1,2,30,512]{4,2,3,1,0:T(2,128)(2,1)}, bf16[1,1,2,30,512]{4,2,3,1,0:T(2,128)(2,1)S(1)}, u32[]{:S(2)}, u32[]{:S(2)}) collective-permute-start(bf16[1,1,2,30,512]{4,2,3,1,0:T(2,128)(2,1)} %bitcast.2290), channel_id=1, source_target_pairs={{2,0},{4,2},{6,4},{8,6},{10,8},{12,10},{14,12},{3,1},{5,3},{7,5},{... | collective-permute-start | bytes 184328 | tf_op jit(solution)/shard_map/ppermute | solution.py:17
  12.9 139.3 %copy-start.728 = (pred[2]{0:T(512)(128)(4,1)}, pred[2]{0:T(512)(128)(4,1)S(1)}, u32[]{:S(2)}) copy-start(pred[2]{0:T(512)(128)(4,1)S(1)} %get-tuple-element.584) | copy-start | bytes 10
  26.5 110.4 %copy-start.470 = (bf16[1,3,4,3,4]{4,3,2,1,0:T(4,128)(2,1)}, bf16[1,3,4,3,4]{4,3,2,1,0:T(4,128)(2,1)S(1)}, u32[]{:S(2)}) copy-start(bf16[1,3,4,3,4]{4,3,2,1,0:T(4,128)(2,1)S(1)} %get-tuple-element.478) | copy-start | bytes 868
  26.5 110.4 %copy-start.472 = (bf16[1,3,4,3,4]{4,3,2,1,0:T(4,128)(2,1)}, bf16[1,3,4,3,4]{4,3,2,1,0:T(4,128)(2,1)S(1)}, u32[]{:S(2)}) copy-start(bf16[1,3,4,3,4]{4,3,2,1,0:T(4,128)(2,1)S(1)} %get-tuple-element.496) | copy-start | bytes 868
  26.5 110.4 %copy-start.474 = (bf16[1,3,4,3,4]{4,3,2,1,0:T(4,128)(2,1)}, bf16[1,3,4,3,4]{4,3,2,1,0:T(4,128)(2,1)S(1)}, u32[]{:S(2)}) copy-start(bf16[1,3,4,3,4]{4,3,2,1,0:T(4,128)(2,1)S(1)} %get-tuple-element.495) | copy-start | bytes 868
  26.5 110.4 %copy-start.476 = (bf16[1,3,4,3,4]{4,3,2,1,0:T(4,128)(2,1)}, bf16[1,3,4,3,4]{4,3,2,1,0:T(4,128)(2,1)S(1)}, u32[]{:S(2)}) copy-start(bf16[1,3,4,3,4]{4,3,2,1,0:T(4,128)(2,1)S(1)} %get-tuple-element.494) | copy-start | bytes 868
  26.5 110.4 %copy-start.478 = (bf16[1,3,4,3,4]{4,3,2,1,0:T(4,128)(2,1)}, bf16[1,3,4,3,4]{4,3,2,1,0:T(4,128)(2,1)S(1)}, u32[]{:S(2)}) copy-start(bf16[1,3,4,3,4]{4,3,2,1,0:T(4,128)(2,1)S(1)} %get-tuple-element.493) | copy-start | bytes 868
  26.5 110.4 %copy-start.480 = (bf16[1,3,4,3,4]{4,3,2,1,0:T(4,128)(2,1)}, bf16[1,3,4,3,4]{4,3,2,1,0:T(4,128)(2,1)S(1)}, u32[]{:S(2)}) copy-start(bf16[1,3,4,3,4]{4,3,2,1,0:T(4,128)(2,1)S(1)} %get-tuple-element.492) | copy-start | bytes 868
  26.5 110.4 %copy-start.482 = (bf16[1,3,4,3,4]{4,3,2,1,0:T(4,128)(2,1)}, bf16[1,3,4,3,4]{4,3,2,1,0:T(4,128)(2,1)S(1)}, u32[]{:S(2)}) copy-start(bf16[1,3,4,3,4]{4,3,2,1,0:T(4,128)(2,1)S(1)} %get-tuple-element.491) | copy-start | bytes 868
  26.6 110.4 %copy-start.483 = (bf16[1,3,4,3,4]{4,3,2,1,0:T(4,128)(2,1)}, bf16[1,3,4,3,4]{4,3,2,1,0:T(4,128)(2,1)S(1)}, u32[]{:S(2)}) copy-start(bf16[1,3,4,3,4]{4,3,2,1,0:T(4,128)(2,1)S(1)} %get-tuple-element.490) | copy-start | bytes 868
  26.6 110.4 %copy-start.484 = (bf16[1,3,4,3,4]{4,3,2,1,0:T(4,128)(2,1)}, bf16[1,3,4,3,4]{4,3,2,1,0:T(4,128)(2,1)S(1)}, u32[]{:S(2)}) copy-start(bf16[1,3,4,3,4]{4,3,2,1,0:T(4,128)(2,1)S(1)} %get-tuple-element.489) | copy-start | bytes 868
  26.6 110.4 %copy-start.485 = (bf16[1,3,4,3,4]{4,3,2,1,0:T(4,128)(2,1)}, bf16[1,3,4,3,4]{4,3,2,1,0:T(4,128)(2,1)S(1)}, u32[]{:S(2)}) copy-start(bf16[1,3,4,3,4]{4,3,2,1,0:T(4,128)(2,1)S(1)} %get-tuple-element.488) | copy-start | bytes 868
  26.6 110.4 %copy-start.486 = (bf16[1,3,4,3,4]{4,3,2,1,0:T(4,128)(2,1)}, bf16[1,3,4,3,4]{4,3,2,1,0:T(4,128)(2,1)S(1)}, u32[]{:S(2)}) copy-start(bf16[1,3,4,3,4]{4,3,2,1,0:T(4,128)(2,1)S(1)} %get-tuple-element.487) | copy-start | bytes 868
  26.6 110.4 %copy-start.487 = (bf16[1,3,4,3,4]{4,3,2,1,0:T(4,128)(2,1)}, bf16[1,3,4,3,4]{4,3,2,1,0:T(4,128)(2,1)S(1)}, u32[]{:S(2)}) copy-start(bf16[1,3,4,3,4]{4,3,2,1,0:T(4,128)(2,1)S(1)} %get-tuple-element.486) | copy-start | bytes 868
  26.6 110.4 %copy-start.488 = (bf16[1,3,4,3,4]{4,3,2,1,0:T(4,128)(2,1)}, bf16[1,3,4,3,4]{4,3,2,1,0:T(4,128)(2,1)S(1)}, u32[]{:S(2)}) copy-start(bf16[1,3,4,3,4]{4,3,2,1,0:T(4,128)(2,1)S(1)} %get-tuple-element.485) | copy-start | bytes 868
  132.1 3.3 collective-permute-start.2
  133.6 3.3 collective-permute-start.3
  261.9 117.8 %copy-start.87 = (bf16[2,10,778]{2,1,0:T(8,128)(2,1)}, bf16[2,10,778]{2,1,0:T(8,128)(2,1)S(1)}, u32[]{:S(2)}) copy-start(bf16[2,10,778]{2,1,0:T(8,128)(2,1)S(1)} %copy.2802) | copy-start | bytes 93364
  263.3 117.2 %copy-start.83 = (bf16[2,10,778]{2,1,0:T(8,128)(2,1)}, bf16[2,10,778]{2,1,0:T(8,128)(2,1)S(1)}, u32[]{:S(2)}) copy-start(bf16[2,10,778]{2,1,0:T(8,128)(2,1)S(1)} %copy.2777) | copy-start | bytes 93364
  422.1 28.8 %collective-permute-start.4 = (bf16[1,1,2,30,512]{4,2,3,1,0:T(2,128)(2,1)S(1)}, bf16[1,1,2,30,512]{4,2,3,1,0:T(2,128)(2,1)S(1)}, u32[]{:S(2)}, u32[]{:S(2)}) collective-permute-start(bf16[1,1,2,30,512]{4,2,3,1,0:T(2,128)(2,1)S(1)} %pad_maximum_fusion.9), channel_id=1, source_target_pairs={{0,2},{2,4},{4,6},{6,8},{8,10},{10,12},{12,14},{1,3},{3,5},{5,7},{... | collective-permute-start | bytes 184328 | tf_op jit(solution)/shard_map/ppermute | solution.py:16
  426.5 24.4 %collective-permute-start.5 = (bf16[1,1,2,30,512]{4,2,3,1,0:T(2,128)(2,1)S(1)}, bf16[1,1,2,30,512]{4,2,3,1,0:T(2,128)(2,1)S(1)}, u32[]{:S(2)}, u32[]{:S(2)}) collective-permute-start(bf16[1,1,2,30,512]{4,2,3,1,0:T(2,128)(2,1)S(1)} %pad_maximum_fusion.9), channel_id=1, source_target_pairs={{2,0},{4,2},{6,4},{8,6},{10,8},{12,10},{14,12},{3,1},{5,3},{7,5},{... | collective-permute-start | bytes 184328 | tf_op jit(solution)/shard_map/ppermute | solution.py:17
  451.2 3.7 collective-permute-start.6
  453.0 3.3 collective-permute-start.7
  725.7 1.5 collective-permute-start.8
  727.6 9.6 collective-permute-start.9
  737.2 74.8 %collective-permute-start.10 = (bf16[4,2,30,512]{3,0,2,1:T(4,128)(2,1)S(1)}, bf16[4,2,30,512]{3,0,2,1:T(4,128)(2,1)S(1)}, u32[]{:S(2)}, u32[]{:S(2)}) collective-permute-start(bf16[4,2,30,512]{3,0,2,1:T(4,128)(2,1)S(1)} %collective-permute-done.9), channel_id=1, source_target_pairs={{0,4},{2,6},{4,0},{6,2},{8,12},{10,14},{12,8},{14,10},{1,5},{3,7},... | collective-permute-start | bytes 737288 | tf_op jit(solution)/shard_map/ppermute | solution.py:25
  812.0 13.3 %collective-permute-start.11 = (bf16[4,2,30,512]{3,0,2,1:T(4,128)(2,1)S(1)}, bf16[4,2,30,512]{3,0,2,1:T(4,128)(2,1)}, u32[]{:S(2)}, u32[]{:S(2)}) collective-permute-start(bf16[4,2,30,512]{3,0,2,1:T(4,128)(2,1)S(1)} %collective-permute-done.10), channel_id=1, source_target_pairs={{0,8},{2,10},{4,12},{6,14},{8,0},{10,2},{12,4},{14,6},{1,9},{3,11}... | collective-permute-start | bytes 737288 | tf_op jit(solution)/shard_map/ppermute | solution.py:25
  852.2 17.3 %collective-permute-start.12 = (bf16[1,1,2,30,512]{4,2,3,1,0:T(2,128)(2,1)S(1)}, bf16[1,1,2,30,512]{4,2,3,1,0:T(2,128)(2,1)S(1)}, u32[]{:S(2)}, u32[]{:S(2)}) collective-permute-start(bf16[1,1,2,30,512]{4,2,3,1,0:T(2,128)(2,1)S(1)} %bitcast.2278), channel_id=1, source_target_pairs={{0,2},{2,4},{4,6},{6,8},{8,10},{10,12},{12,14},{1,3},{3,5},{5,7},{... | collective-permute-start | bytes 184328 | tf_op jit(solution)/shard_map/ppermute | solution.py:16
  854.6 14.9 %collective-permute-start.13 = (bf16[1,1,2,30,512]{4,2,3,1,0:T(2,128)(2,1)S(1)}, bf16[1,1,2,30,512]{4,2,3,1,0:T(2,128)(2,1)S(1)}, u32[]{:S(2)}, u32[]{:S(2)}) collective-permute-start(bf16[1,1,2,30,512]{4,2,3,1,0:T(2,128)(2,1)S(1)} %bitcast.2279), channel_id=1, source_target_pairs={{2,0},{4,2},{6,4},{8,6},{10,8},{12,10},{14,12},{3,1},{5,3},{7,5},{... | collective-permute-start | bytes 184328 | tf_op jit(solution)/shard_map/ppermute | solution.py:17
  869.8 5.6 collective-permute-start.14
  871.5 3.9 collective-permute-start.15
  (743 other events, 9694.4 us)
where the time goes:
time: 1130 us; the launch traced here: 1110 us
  local copies, waits for them, and re-layouts  767 us (68%)
  matrix products  123 us (11%)
  other arithmetic  93.5 us (8%)
  blocking collectives  62.6 us (6%)
  starting transfers between devices  33.2 us (3%)
  waiting for transfers between devices  19.1 us (2%)
    unnamed x1701, local copies, waits for them, and re-layouts  250 us
    gather x81, local copies, waits for them, and re-layouts, assemble(): pieces.append(jnp.take(rim, rows[:, a * 9 + b * 3 + c], axis=0))  93 us
    squeeze x81, local copies, waits for them, and re-layouts, combine(): vector_k[offset]  64 us
    psum x1, blocking collectives, on_device(): sum_first, sum_second = lax.psum((local_first, local_second), ('xp', 'yp'))  62.6 us
    squeeze x81, local copies, waits for them, and re-layouts, combine(): scalar_w[offset]  59.9 us
    another operation x75, local copies, waits for them, and re-layouts, assemble(): pieces.append(jnp.take(rim, rows[:, a * 9 + b * 3 + c], axis=0))  59.5 us
    squeeze x81, local copies, waits for them, and re-layouts, combine(): tensor_k[offset]  54.4 us
    slice x6, local copies, waits for them, and re-layouts, combine(): source[:, 8:20]  43.9 us
  transfers between devices with their start and end apart: 16, of which 4 were waited for; matrix products, arithmetic and copies ran while one was open for 22% of the time, Pallas kernels for 0%

commit v1 on v0

v1 whole, which is shorter than its diff:
```python
import functools

import jax
import jax.numpy as jnp
import numpy as np
from jax import lax
from jax.experimental import pallas as pl
from jax.experimental.pallas import tpu as pltpu
from jax.sharding import PartitionSpec as P

BF = jnp.bfloat16
F32 = jnp.float32
CH = 32
LANES = 128
BOTH = ("xp", "yp")
HIGHEST = lax.Precision.HIGHEST


def component_tables():
    kind, comp, chan = np.full(CH, -1), np.full(CH, -1), np.full(CH, -1)
    for i in range(30):
        if i < 8:
            kind[i], comp[i], chan[i] = 0, 0, i
        elif i < 20:
            kind[i], comp[i], chan[i] = 1, (i - 8) // 4, (i - 8) % 4
        else:
            kind[i], comp[i], chan[i] = 2, (i - 20) // 2, (i - 20) % 2
    return kind, comp, chan


KIND, COMP, CHAN = component_tables()
WIDTH = (8, 4, 2)
START = (0, 64, 80)


def column(i, j):
    if KIND[i] < 0 or KIND[i] != KIND[j] or COMP[i] != COMP[j]:
        return None
    return START[KIND[i]] + CHAN[i] * WIDTH[KIND[i]] + CHAN[j]


def gate_of(i):
    if KIND[i] == 1:
        return CHAN[i]
    if KIND[i] == 2:
        return 4 + CHAN[i]
    return i


def expansions():
    direct = np.zeros((84, CH, CH), np.float32)
    gates = np.zeros((84, CH, CH), np.float32)
    turned = np.zeros((84, CH, CH), np.float32)
    for i in range(30):
        for j in range(30):
            c = column(i, j)
            if c is not None:
                value = 2.0 if KIND[i] == 2 else 1.0
                direct[c, i, j] = value
                turned[c, j, i] = value
            c = column(gate_of(i), j)
            if c is not None:
                gates[c, i, j] = 1.0
    return direct, gates, turned


def lane_of(y, z):
    return 10 * (y + 1) + z + 1


def spread_table():
    table = np.zeros((128, 256), np.float32)
    for p in range(2):
        for y in range(8):
            for z in range(8):
                table[p * 64 + y * 8 + z, p * 128 + lane_of(y, z)] = 1.0
    return table


def turns_table():
    table = np.zeros((4, 128, 128), np.float32)
    for p in range(2):
        for y in range(8):
            for z in range(8):
                to = p * 64 + y * 8 + z
                table[0, p * 64 + y * 8 + z, to] = 1.0
                table[1, p * 64 + (7 - y) * 8 + 7 - z, to] = 1.0
                table[2, (1 - p) * 64 + y * 8 + 7 - z, to] = 1.0
                table[3, (1 - p) * 64 + (7 - y) * 8 + z, to] = 1.0
    return table.reshape(512, 128)


def region_masks():
    masks = np.zeros((9, 128), np.float32)
    for row in range(10):
        for col in range(10):
            b = 0 if row == 0 else 2 if row == 9 else 1
            c = 0 if col == 0 else 2 if col == 9 else 1
            masks[b * 3 + c, 10 * row + col] = 1.0
    return masks


def turn_signs():
    signs = np.zeros((4, CH), np.float32)
    vector = ((1, 1, 1), (1, -1, -1), (-1, 1, -1), (-1, -1, 1))
    tensor = ((1, 1, 1, 1, 1), (-1, -1, 1, 1, 1), (-1, 1, -1, 1, 1), (1, -1, -1, 1, 1))
    for r in range(4):
        for i in range(30):
            signs[r, i] = 1.0 if KIND[i] == 0 else (vector[r] if KIND[i] == 1 else tensor[r])[COMP[i]]
    return signs


def gradient_tables():
    blocks = np.zeros((CH, CH), np.float32)
    place = np.zeros((CH, LANES), np.float32)
    keep = np.zeros((CH, LANES), np.float32)
    for i in range(30):
        for j in range(30):
            c = column(i, j)
            if c is not None:
                blocks[j, i] = 1.0
                place[i, c] = 2.0 if KIND[i] == 2 else 1.0
                keep[j, c] = 1.0
    return (
        np.tile(blocks, (9, 3)),
        np.kron(np.eye(3, dtype=np.float32), place),
        np.tile(keep, (9, 3)),
    )


def gather_rows():
    table = np.zeros((8, CH), np.float32)
    for i in range(30):
        table[gate_of(i), i] = 1.0
    return table


def dot(a, b, **kw):
    return jnp.dot(a, b, preferred_element_type=F32, **kw)


def stage_table(mid, low, high, own, part, near_low, far_low, near_high, far_high):
    zero = jnp.zeros((CH, LANES), BF)
    for s in range(2):
        for x in range(8):
            mid[s, x] = own(s, x)
            mid[2 + s, x] = part(s, x)
        low[s] = own(s, 7)
        low[2 + s] = part(s, 7)
        low[4 + s] = near_low(s)
        low[6 + s] = far_low(s)
        high[s] = own(s, 0)
        high[2 + s] = part(s, 0)
        high[4 + s] = near_high(s)
        high[6 + s] = far_high(s)
    for x in range(8):
        mid[4, x] = zero
    low[8] = zero
    high[8] = zero


def padded_brick(codes, n, mid, low, high, masks):
    def row(o, last):
        e = codes[n, o]
        d = lax.shift_right_logical(e, 1)
        s = lax.bitwise_and(e, 1)
        dx = lax.div(d, 3)
        other_y = jnp.where(d - 3 * dx == 1, 0, 2)
        other_x = jnp.where(dx == 1, 0, 4)
        return jnp.where(e >= 18, last, jnp.minimum(other_x + other_y + s, last))

    total = None
    for b in range(3):
        for c in range(3):
            o = 3 * b + c
            planes = jnp.concatenate(
                [low[row(o, 8)], mid[row(9 + o, 4)].reshape(8 * CH, LANES), high[row(18 + o, 8)]], axis=0
            )
            shift = ((b - 1) * 80 + (c - 1) * 8) % LANES
            if shift:
                planes = pltpu.roll(planes, shift, 1)
            planes = planes * masks[o : o + 1, :]
            total = planes if total is None else total + planes
    return total


def unfold(planes, columns, n):
    for o in range(9):
        shift = (11 - 10 * (o // 3) - o % 3) % LANES
        moved = pltpu.roll(planes, shift, 1) if shift else planes
        for p in range(10):
            columns[o * CH : (o + 1) * CH, (n * 10 + p) * LANES : (n * 10 + p + 1) * LANES] = moved[
                p * CH : (p + 1) * CH
            ]


def fold(stacked, row):
    return (
        stacked[row : row + CH, 0:1024]
        + stacked[row + CH : row + 2 * CH, LANES : LANES + 1024]
        + stacked[row + 2 * CH : row + 3 * CH, 2 * LANES : 2 * LANES + 1024]
    )


def columns_of(columns, n):
    return columns[:, n * 1280 : (n + 1) * 1280]


def symmetrized(sources, signs, slots, table, k, staged):
    parts = [staged[r, :, 128 * (k if r < 2 else 3 - k) : 128 * (k if r < 2 else 3 - k) + 128] for r in range(4)]
    return dot(jnp.concatenate(parts, axis=1), table[...]) * 0.25


def stage_turns(staged, sources, signs, mirror):
    own, across_y, across_x, across = sources
    for n in range(2):
        staged[0, n * CH : (n + 1) * CH, :] = own[n]
        for r, ref in ((1, across_y), (2, across_x), (3, across)):
            staged[r, n * CH : (n + 1) * CH, :] = ref[mirror[n, r - 1]] * signs[:, r : r + 1]


def spread_kernel(features, spread, fp, face_low, face_high, staged):
    staged[...] = jnp.zeros_like(staged)
    for n in range(2):
        staged[n * CH : n * CH + 30, :] = features[n]
    for k in range(4):
        planes = dot(staged[:, k * 128 : (k + 1) * 128], spread[...]).astype(BF)
        for p in range(2):
            for n in range(2):
                plane = planes[n * CH : (n + 1) * CH, p * 128 : (p + 1) * 128]
                fp[n, 2 * k + p] = plane
                if k == 0 and p == 0:
                    face_low[n] = plane
                if k == 3 and p == 1:
                    face_high[n] = plane


def first_kernel(
    codes, mirror, own, part, near_low, far_low, near_high, far_high, cot, cot_y, cot_x, cot_xy,
    w_first, spread, turns, masks, signs, pre, gate_in, columns, both, face_low, face_high,
    mid, low, high, staged,
):
    stage_table(
        mid, low, high,
        lambda s, x: own[s, x], lambda s, x: part[s, x],
        lambda s: near_low[s], lambda s: far_low[s], lambda s: near_high[s], lambda s: far_high[s],
    )
    inside = masks[4:5, :].astype(F32)
    inside8 = jnp.concatenate([inside] * 8, axis=1)
    for n in range(2):
        unfold(padded_brick(codes, n, mid, low, high, masks), columns, n)
    for n in range(2):
        stacked = dot(w_first[...], columns_of(columns, n))
        a = fold(stacked, 0)
        g = fold(stacked, 96)
        pre[n] = a
        gate_in[n] = g
        hidden = (a * jax.nn.sigmoid(g) * inside8).astype(BF)
        for x in range(8):
            plane = hidden[:, x * 128 : (x + 1) * 128]
            both[0, n, x] = plane
            if x == 0:
                face_low[0, n] = plane
            if x == 7:
                face_high[0, n] = plane
    zero2 = jnp.zeros((2, 512), BF)
    own_c, y_c, x_c, xy_c = cot, cot_y, cot_x, cot_xy
    for n in range(2):
        for r, ref in ((0, own_c), (1, y_c), (2, x_c), (3, xy_c)):
            value = ref[n] if r == 0 else ref[mirror[n, r - 1]]
            staged[r, n * CH : n * CH + 30, :] = value * signs[0:30, r : r + 1]
            staged[r, n * CH + 30 : (n + 1) * CH, :] = zero2
    for k in range(4):
        back = symmetrized(None, None, None, turns, k, staged).astype(BF)
        planes = dot(back, spread[...]).astype(BF)
        for p in range(2):
            for n in range(2):
                plane = planes[n * CH : (n + 1) * CH, p * 128 : (p + 1) * 128]
                both[1, n, 2 * k + p] = plane
                if k == 0 and p == 0:
                    face_low[1, n] = plane
                if k == 3 and p == 1:
                    face_high[1, n] = plane


def second_kernel(
    scale, codes, own, part, near_low, far_low, near_high, far_high, pre, gate_in, columns_in,
    w_second, w_turned, compact, masks, rows8, blocks, place, keep, second, grads,
    mid, low, high, columns_h, columns_b, placed_f, placed_s,
):
    inside = masks[4:5, :].astype(F32)
    inside8 = jnp.concatenate([inside] * 8, axis=1)
    for f, columns in ((0, columns_h), (1, columns_b)):
        stage_table(
            mid.at[f], low.at[f], high.at[f],
            lambda s, x: own[f, s, x], lambda s, x: part[f, s, x],
            lambda s: near_low[f, s], lambda s: far_low[f, s], lambda s: near_high[f, s], lambda s: far_high[f, s],
        )
        for n in range(2):
            unfold(padded_brick(codes, n, mid.at[f], low.at[f], high.at[f], masks), columns, n)
    zero = jnp.zeros((CH, LANES), BF)

    def place_planes(placed, n, planes):
        for a in range(3):
            for p in range(10):
                value = planes(p - a) if 0 <= p - a < 8 else zero
                placed[a * CH : (a + 1) * CH, (n * 10 + p) * LANES : (n * 10 + p + 1) * LANES] = value

    for n in range(2):
        result = fold(dot(w_second[...], columns_of(columns_h, n)), 0).astype(BF)
        for k in range(4):
            second[n * CH : (n + 1) * CH, k * 128 : (k + 1) * 128] = dot(
                result[:, k * 256 : (k + 1) * 256], compact[...]
            ).astype(BF)
        place_planes(placed_s, n, lambda x: own[1, n, x])
        grad = fold(dot(w_turned[...], columns_of(columns_b, n)), 0)
        a = pre[n]
        sig = jax.nn.sigmoid(gate_in[n])
        through = grad * sig
        extra = dot(rows8[...], grad * a, precision=HIGHEST)
        sig8 = sig[0:8]
        top = through[0:8] + sig8 * (1.0 - sig8) * extra
        back_pre = (jnp.concatenate([top, through[8:]], axis=0) * inside8).astype(BF)
        place_planes(placed_f, n, lambda x: back_pre[:, x * 128 : (x + 1) * 128])
    for base, columns, placed in ((0, columns_in, placed_f), (27, columns_h, placed_s)):
        raw = lax.dot_general(
            columns[...], placed[...], (((1,), (1,)), ((), ())), preferred_element_type=F32
        )
        spread_out = dot(raw * blocks[...], place[...], precision=HIGHEST) * keep[...]
        sums = jnp.sum(spread_out.reshape(9, CH, 384), axis=1) * scale[0]
        for a in range(3):
            grads[base + 9 * a : base + 9 * a + 9, :] = sums[:, a * LANES : (a + 1) * LANES]
    grads[54:56, :] = jnp.zeros((2, LANES), F32)


def turn_kernel(mirror, own, across_y, across_x, across, turns, signs, out, staged):
    for n in range(2):
        staged[0, n * CH : (n + 1) * CH, :] = own[n * CH : (n + 1) * CH, :]
        for r, ref in ((1, across_y), (2, across_x), (3, across)):
            at = pl.multiple_of(mirror[n, r - 1] * CH, CH)
            staged[r, n * CH : (n + 1) * CH, :] = ref[pl.ds(at, CH), :] * signs[:, r : r + 1]
    for k in range(4):
        result = symmetrized(None, None, None, turns, k, staged).astype(BF)
        for n in range(2):
            out[n, :, k * 128 : (k + 1) * 128] = result[n * CH : n * CH + 30]


SMEM = pl.BlockSpec(memory_space=pltpu.SMEM)
VMEM = pl.BlockSpec(memory_space=pltpu.VMEM)


def call(kernel, n_smem, n_vmem, outs, scratch):
    return pl.pallas_call(
        kernel,
        out_shape=tuple(jax.ShapeDtypeStruct(s, t) for s, t in outs),
        in_specs=[SMEM] * n_smem + [VMEM] * n_vmem,
        out_specs=tuple([VMEM] * len(outs)),
        scratch_shapes=scratch,
        compiler_params=pltpu.CompilerParams(vmem_limit_bytes=40 * 1024 * 1024),
    )


def swap_y(x):
    n = lax.axis_size("yp")
    return lax.ppermute(x, "yp", [(i, n - 1 - i) for i in range(n)])


def mirror_x(x):
    n = lax.axis_size("xp")
    return lax.ppermute(x, "xp", [(i, n - 1 - i) for i in range(n)])


def from_below(x):
    n = lax.axis_size("xp")
    return lax.ppermute(x, "xp", [(i, i + 1) for i in range(n - 1)])


def from_above(x):
    n = lax.axis_size("xp")
    return lax.ppermute(x, "xp", [(i + 1, i) for i in range(n - 1)])


def halo(planes, face_low, face_high):
    near_low = from_below(face_high)
    near_high = from_above(face_low)
    part = swap_y(planes)
    far_low = swap_y(near_low)
    far_high = swap_y(near_high)
    return part, near_low, far_low, near_high, far_high


def total_over_map(x):
    x = x + swap_y(x)
    n = lax.axis_size("xp")
    bit = 1
    while bit < n:
        x = x + lax.ppermute(x, "xp", [(i, i ^ bit) for i in range(n)])
        bit *= 2
    return x


def expanded(weights, table):
    m = table.shape[1]
    full = dot(weights, jnp.asarray(table.reshape(84, -1), BF)).astype(BF)
    full = full.reshape(3, 9, m, CH, CH)
    return full.transpose(2, 0, 3, 1, 4).reshape(m * 96, 288)


def on_device(features, cotangent, w_first, w_second, codes, mirror):
    direct, gates, turned = expansions()
    spread = jnp.asarray(spread_table(), BF)
    compact = jnp.asarray(spread_table().T, BF)
    turns = jnp.asarray(turns_table(), BF)
    masks = jnp.asarray(region_masks(), BF)
    signs = jnp.asarray(turn_signs().T, BF)
    blocks, place, keep = (jnp.asarray(t, F32) for t in gradient_tables())
    rows8 = jnp.asarray(gather_rows(), F32)

    cot_x = mirror_x(cotangent)
    cot_y = swap_y(cotangent)
    cot_xy = swap_y(cot_x)
    fp, face_low, face_high = call(
        spread_kernel, 0, 2,
        [((2, 8, CH, LANES), BF), ((2, CH, LANES), BF), ((2, CH, LANES), BF)],
        [pltpu.VMEM((64, 512), BF)],
    )(features, spread)
    w1 = expanded(w_first, np.stack([direct, gates], axis=1))
    w2 = expanded(w_second, direct[:, None])
    w2t = expanded(w_second[::-1], turned[:, None])
    tables = [pltpu.VMEM(s + (CH, LANES), BF) for s in ((5, 8), (9,), (9,))]
    tables2 = [pltpu.VMEM((2,) + s + (CH, LANES), BF) for s in ((5, 8), (9,), (9,))]
    part, near_low, far_low, near_high, far_high = halo(fp, face_low, face_high)
    pre, gate_in, columns, both, both_low, both_high = call(
        first_kernel, 2, 15,
        [
            ((2, CH, 1024), F32), ((2, CH, 1024), F32), ((288, 2560), BF), ((2, 2, 8, CH, LANES), BF),
            ((2, 2, CH, LANES), BF), ((2, 2, CH, LANES), BF),
        ],
        [*tables, pltpu.VMEM((4, 64, 512), BF)],
    )(
        codes, mirror, fp, part, near_low, far_low, near_high, far_high, cotangent, cot_y, cot_x, cot_xy,
        w1, spread, turns, masks, signs,
    )
    part, near_low, far_low, near_high, far_high = halo(both, both_low, both_high)
    n_bricks = features.shape[0] * lax.axis_size("xp") * lax.axis_size("yp")
    scale = jnp.full((1,), 1.0 / n_bricks, F32)
    second, grads = call(
        second_kernel, 2, 17,
        [((64, 512), BF), ((56, LANES), F32)],
        [*tables2, pltpu.VMEM((288, 2560), BF), pltpu.VMEM((288, 2560), BF), pltpu.VMEM((96, 2560), BF), pltpu.VMEM((96, 2560), BF)],
    )(
        scale, codes, both, part, near_low, far_low, near_high, far_high, pre, gate_in, columns,
        w2, w2t, compact, masks, rows8, blocks, place, keep,
    )
    total = total_over_map(grads)
    second_y = swap_y(second)
    second_x = mirror_x(second)
    second_xy = swap_y(second_x)
    (denoised,) = call(turn_kernel, 1, 6, [((2, 30, 512), BF)], [pltpu.VMEM((4, 64, 512), BF)])(
        mirror, second, second_y, second_x, second_xy, turns, signs
    )
    return denoised, total[0:27, 0:84], total[27:54, 0:84]


def solution(mesh):
    brick = P(("grp", "xp", "yp"))
    return jax.shard_map(
        on_device,
        mesh=mesh,
        in_specs=(brick, brick, P(), P(), brick, brick),
        out_specs=(brick, P("grp"), P("grp")),
        check_vma=False,
    )
```

time: 1130 us -> 72.8 us (0.06); the launches traced: 1110 us -> 72 us
  local copies, waits for them, and re-layouts: 767 us -> 18.5 us
  matrix products: 123 us -> 3.01 us
  other arithmetic: 93.5 us -> 0.02 us
  blocking collectives: 62.6 us -> 0 us
  starting transfers between devices: 33.2 us -> 19.1 us
    unnamed x1701 -> x39, local copies, waits for them, and re-layouts: 250 us -> 6.18 us
    squeeze x243 -> x0, local copies, waits for them, and re-layouts: 178 us -> none  [the longest x81 64 us: combine(): vector_k[offset]]
    slice x58 -> x1, local copies, waits for them, and re-layouts: 137 us -> 0.62 us  [on_device(): return (denoised, total[0:27, 0:84], total[27:54, 0:84])]
    dot_general x405 -> x3, matrix products: 123 us -> 3.01 us  [dot(): return jnp.dot(a, b, preferred_element_type=F32, **kw)]
    gather x84 -> x0, local copies, waits for them, and re-layouts: 95.4 us -> none  [the longest x81 93 us: assemble(): pieces.append(jnp.take(rim, rows[:, a * 9 + b * 3 + c], axis=0))]
    psum x1 -> x0, blocking collectives: 62.6 us -> none  [on_device(): sum_first, sum_second = lax.psum((local_first, local_second), ('xp', 'yp'))]
    another operation x78 -> x0, local copies, waits for them, and re-layouts: 62.2 us -> none  [the longest x75 59.5 us: assemble(): pieces.append(jnp.take(rim, rows[:, a * 9 + b * 3 + c], axis=0))]
    select_n x100 -> x0, other arithmetic: 39 us -> none  [the longest x95 37.3 us: assemble(): pieces.append(jnp.take(rim, rows[:, a * 9 + b * 3 + c], axis=0))]
  transfers between devices with their start and end apart: 16 -> 20, of which waited for: 4 -> 6; matrix products, arithmetic and copies ran while one was open for 22% -> 22% of each run, Pallas kernels for 0% -> 0%
where the time goes in v1:
time: 72.8 us; the launch traced here: 72 us
  waiting for transfers between devices  19.3 us (27%)
  starting transfers between devices  19.1 us (26%)
  local copies, waits for them, and re-layouts  18.5 us (25%)
  Pallas kernels  11 us (15%)
  matrix products  3.01 us (4%)
  between operations  1.05 us (1%)
    ppermute x3, waiting for transfers between devices, total_over_map(): x = x + lax.ppermute(x, 'xp', [(i, i ^ bit) for i in range(n)])  10.9 us
    ppermute x2, waiting for transfers between devices, from_above(): return lax.ppermute(x, 'xp', [(i + 1, i) for i in range(n - 1)])  7.52 us
    reshape x6, local copies, waits for them, and re-layouts, expanded(): full = full.reshape(3, 9, m, CH, CH)  7.13 us
    pallas_call x1, Pallas kernels, on_device(): call(second_kernel, 2, 17, [((64, 512), BF), ((56, LANES), F32)], [*table...  6.57 us
    ppermute x2, starting transfers between devices, mirror_x(): return lax.ppermute(x, 'xp', [(i, n - 1 - i) for i in range(n)])  6.45 us
    ppermute x2, starting transfers between devices, from_below(): return lax.ppermute(x, 'xp', [(i, i + 1) for i in range(n - 1)])  6.31 us
    unnamed x39, local copies, waits for them, and re-layouts  6.18 us
    reshape x6, local copies, waits for them, and re-layouts, expanded(): return full.transpose(2, 0, 3, 1, 4).reshape(m * 96, 288)  4.53 us
  transfers between devices with their start and end apart: 20, of which 6 were waited for; matrix products, arithmetic and copies ran while one was open for 22% of the time, Pallas kernels for 0%

profile of v1, /device:TPU:0, one launch (start us, length us, event | category | flops | bytes accessed | tf_op | source)
XLA Modules:
  0.0 72.0 jit_solution(7299765812511824882)
XLA Ops:
  0.6 0.8 %copy.33.cot = bf16[2,30,512]{2,1,0:T(8,128)(2,1)S(1)} copy(bf16[2,30,512]{2,0,1:T(2,128)(2,1)} %param.19) | data formatting | bytes 122880 | tf_op args[1]
  1.5 6.1 %collective-permute-start.6 = (bf16[2,30,512]{2,1,0:T(8,128)(2,1)S(1)}, bf16[2,30,512]{2,1,0:T(8,128)(2,1)S(1)}, u32[]{:S(2)}, u32[]{:S(2)}) collective-permute-start(bf16[2,30,512]{2,1,0:T(8,128)(2,1)S(1)} %copy.33.cot), channel_id=1, source_target_pairs={{0,14},{2,12},{4,10},{6,8},{8,6},{10,4},{12,2},{14,0},{1,15},{3,13... | collective-permute-start | bytes 184328 | tf_op jit(solution)/shard_map/ppermute | solution.py:370
  7.6 0.8 %copy.29.features = bf16[2,30,512]{2,1,0:T(8,128)(2,1)S(1)} copy(bf16[2,30,512]{2,0,1:T(2,128)(2,1)} %param.18) | data formatting | bytes 122880 | tf_op args[0]
  8.4 0.8 %copy-done.3 = bf16[128,256]{1,0:T(8,128)(2,1)S(1)} copy-done((bf16[128,256]{1,0:T(8,128)(2,1)S(1)}, bf16[128,256]{1,0:T(8,128)(2,1)}, u32[]{:S(2)}) %copy-start.3) | copy-done | bytes 65560
  9.4 2.4 %collective-permute-start.1 = (bf16[2,32,128]{2,1,0:T(8,128)(2,1)S(1)}, bf16[2,32,128]{2,1,0:T(8,128)(2,1)S(1)}, u32[]{:S(2)}, u32[]{:S(2)}) collective-permute-start(bf16[2,32,128]{2,1,0:T(8,128)(2,1)S(1)} %get-tuple-element.15), channel_id=1, source_target_pairs={{0,2},{2,4},{4,6},{6,8},{8,10},{10,12},{12,14},{1,3},{3,5},{5,7},{... | collective-permute-start | bytes 49160 | tf_op jit(solution)/shard_map/ppermute | solution.py:375
  11.8 1.3 %collective-permute-start.3 = (bf16[2,32,128]{2,1,0:T(8,128)(2,1)S(1)}, bf16[2,32,128]{2,1,0:T(8,128)(2,1)S(1)}, u32[]{:S(2)}, u32[]{:S(2)}) collective-permute-start(bf16[2,32,128]{2,1,0:T(8,128)(2,1)S(1)} %get-tuple-element.16), channel_id=1, source_target_pairs={{2,0},{4,2},{6,4},{8,6},{10,8},{12,10},{14,12},{3,1},{5,3},{7,5},{... | collective-permute-start | bytes 49160 | tf_op jit(solution)/shard_map/ppermute | solution.py:380
  13.9 3.6 %collective-permute-done.3.near_high = bf16[2,32,128]{2,1,0:T(8,128)(2,1)S(1)} collective-permute-done((bf16[2,32,128]{2,1,0:T(8,128)(2,1)S(1)}, bf16[2,32,128]{2,1,0:T(8,128)(2,1)S(1)}, u32[]{:S(2)}, u32[]{:S(2)}) %collective-permute-start.3) | collective-permute-done | bytes 16416 | tf_op jit(solution)/shard_map/ppermute | solution.py:380
  18.0 1.2 %fusion = bf16[27,2048]{1,0:T(8,128)(2,1)S(1)} fusion(bf16[84,2048]{1,0:T(8,128)(2,1)} %constant.35.clone, bf16[27,84]{1,0:T(8,128)(2,1)S(1)} %copy-done), kind=kOutput, calls=%fused_computation.1 | convolution fusion | flops 9345024 | bytes 459192 | tf_op jit(solution)/shard_map/dot_general | solution.py:139
  20.7 3.4 %shard_map.194 = (f32[2,32,1024]{2,1,0:T(8,128)S(1)}, f32[2,32,1024]{2,1,0:T(8,128)S(1)}, bf16[288,2560]{1,0:T(8,128)(2,1)S(1)}, bf16[2,2,8,32,128]{4,3,2,1,0:T(...) custom-call(s32[2,27]{1,0:T(2,128)S(1)} %copy-done.11, s32[2,3]{1,0:T(2,128)S(1)} %copy-done.13, ...), custom_call_target="tpu_custom_call" | custom-call | tf_op jit(solution)/shard_map/pallas_call | solution.py:433
  24.1 3.9 %collective-permute-start.9 = (bf16[2,2,32,128]{3,2,1,0:T(8,128)(2,1)}, bf16[2,2,32,128]{3,2,1,0:T(8,128)(2,1)}, u32[]{:S(2)}, u32[]{:S(2)}) collective-permute-start(bf16[2,2,32,128]{3,2,1,0:T(8,128)(2,1)} %get-tuple-element.18), channel_id=1, source_target_pairs={{0,2},{2,4},{4,6},{6,8},{8,10},{10,12},{12,14},{1,3},{3,5},{5,7},{... | collective-permute-start | bytes 98312 | tf_op jit(solution)/shard_map/ppermute | solution.py:375
  28.0 1.3 %collective-permute-start.11 = (bf16[2,2,32,128]{3,2,1,0:T(8,128)(2,1)}, bf16[2,2,32,128]{3,2,1,0:T(8,128)(2,1)}, u32[]{:S(2)}, u32[]{:S(2)}) collective-permute-start(bf16[2,2,32,128]{3,2,1,0:T(8,128)(2,1)} %get-tuple-element.19), channel_id=1, source_target_pairs={{2,0},{4,2},{6,4},{8,6},{10,8},{12,10},{14,12},{3,1},{5,3},{7,5},{... | collective-permute-start | bytes 98312 | tf_op jit(solution)/shard_map/ppermute | solution.py:380
  30.2 4.0 %collective-permute-done.11.near_high = bf16[2,2,32,128]{3,2,1,0:T(8,128)(2,1)} collective-permute-done((bf16[2,2,32,128]{3,2,1,0:T(8,128)(2,1)}, bf16[2,2,32,128]{3,2,1,0:T(8,128)(2,1)}, u32[]{:S(2)}, u32[]{:S(2)}) %collective-permute-start.11) | collective-permute-done | bytes 32800 | tf_op jit(solution)/shard_map/ppermute | solution.py:380
  34.1 1.7 %fusion.2 = bf16[27,1024]{1,0:T(8,128)(2,1)} fusion(bf16[84,1024]{1,0:T(8,128)(2,1)} %constant.37.clone, bf16[27,84]{1,0:T(8,128)(2,1)S(1)} %rev.3), kind=kOutput, calls=%fused_computation.5 | convolution fusion | flops 4672512 | bytes 231864 | tf_op jit(solution)/shard_map/dot_general | solution.py:139
  35.8 0.9 %reshape.26 = bf16[3,9,1,32,32]{4,3,1,0,2:T(8,128)(2,1)} reshape(bf16[27,1024]{1,0:T(8,128)(2,1)S(1)} %fusion.1) | data formatting | bytes 110592 | tf_op jit(solution)/shard_map/reshape | solution.py:405
  36.7 1.8 %copy.35 = bf16[3,9,1,32,32]{3,0,4,1,2:T(4,128)(2,1)} copy(bf16[3,9,1,32,32]{4,3,1,0,2:T(8,128)(2,1)} %reshape.26) | data formatting | bytes 110592 | tf_op jit(solution)/shard_map/reshape | solution.py:405
  38.5 1.1 %reshape.27 = bf16[96,288]{0,1:T(8,128)(2,1)S(1)} reshape(bf16[1,3,32,9,32]{2,1,4,3,0:T(4,128)(2,1)} %bitcast.22) | data formatting | bytes 110592 | tf_op jit(solution)/shard_map/reshape | solution.py:406
  39.8 1.8 %reshape.28 = bf16[3,9,1,32,32]{4,3,1,0,2:T(8,128)(2,1)} reshape(bf16[27,1024]{1,0:T(8,128)(2,1)} %fusion.2) | data formatting | bytes 110592 | tf_op jit(solution)/shard_map/reshape | solution.py:405
  41.5 1.8 %copy.36 = bf16[3,9,1,32,32]{3,0,4,1,2:T(4,128)(2,1)} copy(bf16[3,9,1,32,32]{4,3,1,0,2:T(8,128)(2,1)} %reshape.28) | data formatting | bytes 110592 | tf_op jit(solution)/shard_map/reshape | solution.py:405
  43.4 1.8 %reshape.29 = bf16[96,288]{0,1:T(8,128)(2,1)} reshape(bf16[1,3,32,9,32]{2,1,4,3,0:T(4,128)(2,1)} %bitcast.23) | data formatting | bytes 110592 | tf_op jit(solution)/shard_map/reshape | solution.py:406
  45.1 1.0 %copy.38.w_turned = bf16[96,288]{1,0:T(8,128)(2,1)S(1)} copy(bf16[96,288]{0,1:T(8,128)(2,1)} %reshape.29) | data formatting | bytes 110592 | tf_op jit(solution)/shard_map/reshape | solution.py:406
  46.2 0.8 %copy-done.7 = bf16[256,128]{1,0:T(8,128)(2,1)S(1)} copy-done((bf16[256,128]{1,0:T(8,128)(2,1)S(1)}, bf16[256,128]{1,0:T(8,128)(2,1)}, u32[]{:S(2)}) %copy-start.7) | copy-done | bytes 65560
  47.0 0.7 copy-done.10
  47.7 0.7 copy-done.12
  48.4 0.7 copy-done.15
  49.1 6.6 %shard_map.195 = (bf16[64,512]{1,0:T(8,128)(2,1)S(1)}, f32[56,128]{1,0:T(8,128)S(1)}) custom-call(f32[1]{0:T(128)} %constant.12.clone.1.scale, s32[2,27]{1,0:T(2,128)S(1)} %copy-done.12, bf16[2,2,8,32,128]{4,3,2,1,0:T(8,128)(2,1)S(1)} %get-tuple-element.17.own, bf16[2,2,8,32,128]{4,3,2,1,0:T(8,128)(2,1)S(1)} %collective-permute-done.8.part, ...), custom_call_target="tpu_custom_call" | custom-call | tf_op jit(solution)/shard_map/pallas_call | solution.py:447
  56.2 0.9 %collective-permute-done.16 = f32[56,128]{1,0:T(8,128)S(1)} collective-permute-done((f32[56,128]{1,0:T(8,128)S(1)}, f32[56,128]{1,0:T(8,128)S(1)}, u32[]{:S(2)}, u32[]{:S(2)}) %collective-permute-start.16) | collective-permute-done | bytes 28704 | tf_op jit(solution)/shard_map/ppermute | solution.py:365
  57.8 3.2 %collective-permute-done.17 = f32[56,128]{1,0:T(8,128)S(1)} collective-permute-done((f32[56,128]{1,0:T(8,128)S(1)}, f32[56,128]{1,0:T(8,128)S(1)}, u32[]{:S(2)}, u32[]{:S(2)}) %collective-permute-start.17) | collective-permute-done | bytes 28704 | tf_op jit(solution)/shard_map/ppermute | solution.py:397
  61.0 4.1 %collective-permute-done.18 = f32[56,128]{1,0:T(8,128)S(1)} collective-permute-done((f32[56,128]{1,0:T(8,128)S(1)}, f32[56,128]{1,0:T(8,128)S(1)}, u32[]{:S(2)}, u32[]{:S(2)}) %collective-permute-start.18) | collective-permute-done | bytes 28704 | tf_op jit(solution)/shard_map/ppermute | solution.py:397
  66.1 3.7 %collective-permute-done.19 = f32[56,128]{1,0:T(8,128)S(1)} collective-permute-done((f32[56,128]{1,0:T(8,128)S(1)}, f32[56,128]{1,0:T(8,128)S(1)}, u32[]{:S(2)}, u32[]{:S(2)}) %collective-permute-start.19) | collective-permute-done | bytes 28704 | tf_op jit(solution)/shard_map/ppermute | solution.py:397
  69.8 0.6 fusion.3
  70.4 0.8 %shard_map.196 = bf16[2,30,512]{2,1,0:T(8,128)(2,1)S(1)} custom-call(s32[2,3]{1,0:T(2,128)S(1)} %copy-done.14, bf16[64,512]{1,0:T(8,128)(2,1)S(1)} %get-tuple-element.23.own, bf16[64,512]{1,0:T(8,128)(2,1)S(1)} %collective-permute-done.13.across_y, bf16[64,512]{1,0:T(8,128)(2,1)S(1)} %collective-permute-done.14.across_x, ...), custom_call_target="tpu_custom_call" | custom-call | tf_op jit(solution)/shard_map/pallas_call | solution.py:459
  71.3 0.7 copy.39
  (72 shorter events, 6.2 us)
Async XLA Ops:
  0.6 17.4 %copy-start = (bf16[27,84]{1,0:T(8,128)(2,1)S(1)}, bf16[27,84]{1,0:T(8,128)(2,1)}, u32[]{:S(2)}) copy-start(bf16[27,84]{1,0:T(8,128)(2,1)} %param.20) | copy-start | bytes 13612
  1.5 16.0 %collective-permute-start.6 = (bf16[2,30,512]{2,1,0:T(8,128)(2,1)S(1)}, bf16[2,30,512]{2,1,0:T(8,128)(2,1)S(1)}, u32[]{:S(2)}, u32[]{:S(2)}) collective-permute-start(bf16[2,30,512]{2,1,0:T(8,128)(2,1)S(1)} %copy.33.cot), channel_id=1, source_target_pairs={{0,14},{2,12},{4,10},{6,8},{8,6},{10,4},{12,2},{14,0},{1,15},{3,13... | collective-permute-start | bytes 184328 | tf_op jit(solution)/shard_map/ppermute | solution.py:370
  9.4 4.4 %collective-permute-start.1 = (bf16[2,32,128]{2,1,0:T(8,128)(2,1)S(1)}, bf16[2,32,128]{2,1,0:T(8,128)(2,1)S(1)}, u32[]{:S(2)}, u32[]{:S(2)}) collective-permute-start(bf16[2,32,128]{2,1,0:T(8,128)(2,1)S(1)} %get-tuple-element.15), channel_id=1, source_target_pairs={{0,2},{2,4},{4,6},{6,8},{8,10},{10,12},{12,14},{1,3},{3,5},{5,7},{... | collective-permute-start | bytes 49160 | tf_op jit(solution)/shard_map/ppermute | solution.py:375
  11.8 5.6 %collective-permute-start.3 = (bf16[2,32,128]{2,1,0:T(8,128)(2,1)S(1)}, bf16[2,32,128]{2,1,0:T(8,128)(2,1)S(1)}, u32[]{:S(2)}, u32[]{:S(2)}) collective-permute-start(bf16[2,32,128]{2,1,0:T(8,128)(2,1)S(1)} %get-tuple-element.16), channel_id=1, source_target_pairs={{2,0},{4,2},{6,4},{8,6},{10,8},{12,10},{14,12},{3,1},{5,3},{7,5},{... | collective-permute-start | bytes 49160 | tf_op jit(solution)/shard_map/ppermute | solution.py:380
  13.1 7.5 %collective-permute-start.5 = (bf16[2,30,512]{2,1,0:T(8,128)(2,1)S(1)}, bf16[2,30,512]{2,1,0:T(8,128)(2,1)S(1)}, u32[]{:S(2)}, u32[]{:S(2)}) collective-permute-start(bf16[2,30,512]{2,1,0:T(8,128)(2,1)S(1)} %copy.33.cot), channel_id=1, source_target_pairs={{0,1},{1,0},{2,3},{3,2},{4,5},{5,4},{6,7},{7,6},{8,9},{9,8},{10,11... | collective-permute-start | bytes 184328 | tf_op jit(solution)/shard_map/ppermute | solution.py:365
  13.2 7.4 %copy-start.1 = (bf16[512,128]{1,0:T(8,128)(2,1)S(1)}, bf16[512,128]{1,0:T(8,128)(2,1)}, u32[]{:S(2)}) copy-start(bf16[512,128]{1,0:T(8,128)(2,1)} %constant.28.clone.turns) | copy-start | bytes 393220
  13.2 7.4 %copy-start.4 = (bf16[128,256]{1,0:T(8,128)(2,1)S(1)}, bf16[128,256]{1,0:T(8,128)(2,1)}, u32[]{:S(2)}) copy-start(bf16[128,256]{1,0:T(8,128)(2,1)} %constant.26.clone.spread) | copy-start | bytes 196612
  13.3 7.4 %copy-start.8 = (bf16[32,4]{1,0:T(8,128)(2,1)S(1)}, bf16[32,4]{1,0:T(8,128)(2,1)}, u32[]{:S(2)}) copy-start(bf16[32,4]{1,0:T(8,128)(2,1)} %constant.30.clone.signs) | copy-start | bytes 772
  13.3 7.4 %copy-start.9 = (bf16[9,128]{1,0:T(8,128)(2,1)S(1)}, bf16[9,128]{1,0:T(8,128)(2,1)}, u32[]{:S(2)}) copy-start(bf16[9,128]{1,0:T(8,128)(2,1)} %constant.29.clone.masks) | copy-start | bytes 6916
  13.3 7.4 %copy-start.11 = (s32[2,27]{1,0:T(2,128)S(1)}, s32[2,27]{1,0:T(2,128)}, u32[]{:S(2)}) copy-start(s32[2,27]{1,0:T(2,128)} %codes.3) | copy-start | bytes 652
  13.3 7.3 %collective-permute-start = (bf16[2,8,32,128]{3,2,1,0:T(8,128)(2,1)S(1)}, bf16[2,8,32,128]{3,2,1,0:T(8,128)(2,1)S(1)}, u32[]{:S(2)}, u32[]{:S(2)}) collective-permute-start(bf16[2,8,32,128]{3,2,1,0:T(8,128)(2,1)S(1)} %get-tuple-element.14.own), channel_id=1, source_target_pairs={{0,1},{1,0},{2,3},{3,2},{4,5},{5,4},{6,7},{7,6},{8,9},{9,8},{10,11... | collective-permute-start | bytes 393224 | tf_op jit(solution)/shard_map/ppermute | solution.py:365
  13.8 6.8 %collective-permute-start.2 = (bf16[2,32,128]{2,1,0:T(8,128)(2,1)S(1)}, bf16[2,32,128]{2,1,0:T(8,128)(2,1)S(1)}, u32[]{:S(2)}, u32[]{:S(2)}) collective-permute-start(bf16[2,32,128]{2,1,0:T(8,128)(2,1)S(1)} %collective-permute-done.1.near_low), channel_id=1, source_target_pairs={{0,1},{1,0},{2,3},{3,2},{4,5},{5,4},{6,7},{7,6},{8,9},{9,8},{10,11... | collective-permute-start | bytes 49160 | tf_op jit(solution)/shard_map/ppermute | solution.py:365
  17.5 3.1 %collective-permute-start.4 = (bf16[2,32,128]{2,1,0:T(8,128)(2,1)S(1)}, bf16[2,32,128]{2,1,0:T(8,128)(2,1)S(1)}, u32[]{:S(2)}, u32[]{:S(2)}) collective-permute-start(bf16[2,32,128]{2,1,0:T(8,128)(2,1)S(1)} %collective-permute-done.3.near_high), channel_id=1, source_target_pairs={{0,1},{1,0},{2,3},{3,2},{4,5},{5,4},{6,7},{7,6},{8,9},{9,8},{10,11... | collective-permute-start | bytes 49160 | tf_op jit(solution)/shard_map/ppermute | solution.py:365
  17.5 3.2 %collective-permute-start.7 = (bf16[2,30,512]{2,1,0:T(8,128)(2,1)S(1)}, bf16[2,30,512]{2,1,0:T(8,128)(2,1)S(1)}, u32[]{:S(2)}, u32[]{:S(2)}) collective-permute-start(bf16[2,30,512]{2,1,0:T(8,128)(2,1)S(1)} %collective-permute-done.6.cot_x), channel_id=1, source_target_pairs={{0,1},{1,0},{2,3},{3,2},{4,5},{5,4},{6,7},{7,6},{8,9},{9,8},{10,11... | collective-permute-start | bytes 184328 | tf_op jit(solution)/shard_map/ppermute | solution.py:365
  19.5 9.9 %copy-start.16 = (bf16[84,1024]{1,0:T(8,128)(2,1)S(1)}, bf16[84,1024]{1,0:T(8,128)(2,1)}, u32[]{:S(2)}) copy-start(bf16[84,1024]{1,0:T(8,128)(2,1)} %constant.36.clone) | copy-start | bytes 516100
  19.5 9.9 %copy-start.17 = (bf16[27,84]{1,0:T(8,128)(2,1)S(1)}, bf16[27,84]{1,0:T(8,128)(2,1)}, u32[]{:S(2)}) copy-start(bf16[27,84]{1,0:T(8,128)(2,1)} %param.21) | copy-start | bytes 13612
  24.1 5.5 %collective-permute-start.9 = (bf16[2,2,32,128]{3,2,1,0:T(8,128)(2,1)}, bf16[2,2,32,128]{3,2,1,0:T(8,128)(2,1)}, u32[]{:S(2)}, u32[]{:S(2)}) collective-permute-start(bf16[2,2,32,128]{3,2,1,0:T(8,128)(2,1)} %get-tuple-element.18), channel_id=1, source_target_pairs={{0,2},{2,4},{4,6},{6,8},{8,10},{10,12},{12,14},{1,3},{3,5},{5,7},{... | collective-permute-start | bytes 98312 | tf_op jit(solution)/shard_map/ppermute | solution.py:375
  28.0 6.1 %collective-permute-start.11 = (bf16[2,2,32,128]{3,2,1,0:T(8,128)(2,1)}, bf16[2,2,32,128]{3,2,1,0:T(8,128)(2,1)}, u32[]{:S(2)}, u32[]{:S(2)}) collective-permute-start(bf16[2,2,32,128]{3,2,1,0:T(8,128)(2,1)} %get-tuple-element.19), channel_id=1, source_target_pairs={{2,0},{4,2},{6,4},{8,6},{10,8},{12,10},{14,12},{3,1},{5,3},{7,5},{... | collective-permute-start | bytes 98312 | tf_op jit(solution)/shard_map/ppermute | solution.py:380
  29.3 16.8 %collective-permute-start.8 = (bf16[2,2,8,32,128]{4,3,2,1,0:T(8,128)(2,1)S(1)}, bf16[2,2,8,32,128]{4,3,2,1,0:T(8,128)(2,1)S(1)}, u32[]{:S(2)}, u32[]{:S(2)}) collective-permute-start(bf16[2,2,8,32,128]{4,3,2,1,0:T(8,128)(2,1)S(1)} %get-tuple-element.17.own), channel_id=1, source_target_pairs={{0,1},{1,0},{2,3},{3,2},{4,5},{5,4},{6,7},{7,6},{8,9},{9,8},{10,11... | collective-permute-start | bytes 786440 | tf_op jit(solution)/shard_map/ppermute | solution.py:365
  29.6 16.6 %copy-start.2 = (f32[288,384]{1,0:T(8,128)S(1)}, f32[288,384]{1,0:T(8,128)}, u32[]{:S(2)}) copy-start(f32[288,384]{1,0:T(8,128)} %constant.33.clone.keep) | copy-start | bytes 1327108
  29.6 16.6 %copy-start.5 = (f32[96,384]{1,0:T(8,128)S(1)}, f32[96,384]{1,0:T(8,128)}, u32[]{:S(2)}) copy-start(f32[96,384]{1,0:T(8,128)} %constant.32.clone.place) | copy-start | bytes 442372
  29.6 16.6 %copy-start.6 = (f32[288,96]{1,0:T(8,128)S(1)}, f32[288,96]{1,0:T(8,128)}, u32[]{:S(2)}) copy-start(f32[288,96]{1,0:T(8,128)} %constant.31.clone.blocks) | copy-start | bytes 331780
  29.6 16.5 %collective-permute-start.10 = (bf16[2,2,32,128]{3,2,1,0:T(8,128)(2,1)}, bf16[2,2,32,128]{3,2,1,0:T(8,128)(2,1)}, u32[]{:S(2)}, u32[]{:S(2)}) collective-permute-start(bf16[2,2,32,128]{3,2,1,0:T(8,128)(2,1)} %collective-permute-done.9.near_low), channel_id=1, source_target_pairs={{0,1},{1,0},{2,3},{3,2},{4,5},{5,4},{6,7},{7,6},{8,9},{9,8},{10,11... | collective-permute-start | bytes 98312 | tf_op jit(solution)/shard_map/ppermute | solution.py:365
  34.1 12.0 %collective-permute-start.12 = (bf16[2,2,32,128]{3,2,1,0:T(8,128)(2,1)}, bf16[2,2,32,128]{3,2,1,0:T(8,128)(2,1)}, u32[]{:S(2)}, u32[]{:S(2)}) collective-permute-start(bf16[2,2,32,128]{3,2,1,0:T(8,128)(2,1)} %collective-permute-done.11.near_high), channel_id=1, source_target_pairs={{0,1},{1,0},{2,3},{3,2},{4,5},{5,4},{6,7},{7,6},{8,9},{9,8},{10,11... | collective-permute-start | bytes 98312 | tf_op jit(solution)/shard_map/ppermute | solution.py:365
  49.1 21.4 %copy-start.14 = (s32[2,3]{1,0:T(2,128)S(1)}, s32[2,3]{1,0:T(2,128)}, u32[]{:S(2)}) copy-start(s32[2,3]{1,0:T(2,128)} %mirror.3) | copy-start | bytes 76
  55.7 1.4 %collective-permute-start.16 = (f32[56,128]{1,0:T(8,128)S(1)}, f32[56,128]{1,0:T(8,128)S(1)}, u32[]{:S(2)}, u32[]{:S(2)}) collective-permute-start(f32[56,128]{1,0:T(8,128)S(1)} %get-tuple-element.24), channel_id=1, source_target_pairs={{0,1},{1,0},{2,3},{3,2},{4,5},{5,4},{6,7},{7,6},{8,9},{9,8},{10,11... | collective-permute-start | bytes 86024 | tf_op jit(solution)/shard_map/ppermute | solution.py:365
  57.1 3.9 %collective-permute-start.17 = (f32[56,128]{1,0:T(8,128)S(1)}, f32[56,128]{1,0:T(8,128)S(1)}, u32[]{:S(2)}, u32[]{:S(2)}) collective-permute-start(f32[56,128]{1,0:T(8,128)S(1)} %add.12), channel_id=1, source_target_pairs={{0,2},{2,0},{4,6},{6,4},{8,10},{10,8},{12,14},{14,12},{1,3},{3,1},... | collective-permute-start | bytes 86024 | tf_op jit(solution)/shard_map/ppermute | solution.py:397
  57.4 8.2 %collective-permute-start.14 = (bf16[64,512]{1,0:T(8,128)(2,1)S(1)}, bf16[64,512]{1,0:T(8,128)(2,1)S(1)}, u32[]{:S(2)}, u32[]{:S(2)}) collective-permute-start(bf16[64,512]{1,0:T(8,128)(2,1)S(1)} %get-tuple-element.23.own), channel_id=1, source_target_pairs={{0,14},{2,12},{4,10},{6,8},{8,6},{10,4},{12,2},{14,0},{1,15},{3,13... | collective-permute-start | bytes 196616 | tf_op jit(solution)/shard_map/ppermute | solution.py:370
  61.0 4.1 %collective-permute-start.18 = (f32[56,128]{1,0:T(8,128)S(1)}, f32[56,128]{1,0:T(8,128)S(1)}, u32[]{:S(2)}, u32[]{:S(2)}) collective-permute-start(f32[56,128]{1,0:T(8,128)S(1)} %add.13), channel_id=1, source_target_pairs={{0,4},{2,6},{4,0},{6,2},{8,12},{10,14},{12,8},{14,10},{1,5},{3,7},... | collective-permute-start | bytes 86024 | tf_op jit(solution)/shard_map/ppermute | solution.py:397
  65.0 4.8 %collective-permute-start.19 = (f32[56,128]{1,0:T(8,128)S(1)}, f32[56,128]{1,0:T(8,128)S(1)}, u32[]{:S(2)}, u32[]{:S(2)}) collective-permute-start(f32[56,128]{1,0:T(8,128)S(1)} %add.14), channel_id=1, source_target_pairs={{0,8},{2,10},{4,12},{6,14},{8,0},{10,2},{12,4},{14,6},{1,9},{3,11}... | collective-permute-start | bytes 86024 | tf_op jit(solution)/shard_map/ppermute | solution.py:397
  65.6 4.8 %collective-permute-start.13 = (bf16[64,512]{1,0:T(8,128)(2,1)S(1)}, bf16[64,512]{1,0:T(8,128)(2,1)S(1)}, u32[]{:S(2)}, u32[]{:S(2)}) collective-permute-start(bf16[64,512]{1,0:T(8,128)(2,1)S(1)} %get-tuple-element.23.own), channel_id=1, source_target_pairs={{0,1},{1,0},{2,3},{3,2},{4,5},{5,4},{6,7},{7,6},{8,9},{9,8},{10,11... | collective-permute-start | bytes 196616 | tf_op jit(solution)/shard_map/ppermute | solution.py:365
  65.6 4.8 %collective-permute-start.15 = (bf16[64,512]{1,0:T(8,128)(2,1)S(1)}, bf16[64,512]{1,0:T(8,128)(2,1)S(1)}, u32[]{:S(2)}, u32[]{:S(2)}) collective-permute-start(bf16[64,512]{1,0:T(8,128)(2,1)S(1)} %collective-permute-done.14.across_x), channel_id=1, source_target_pairs={{0,1},{1,0},{2,3},{3,2},{4,5},{5,4},{6,7},{7,6},{8,9},{9,8},{10,11... | collective-permute-start | bytes 196616 | tf_op jit(solution)/shard_map/ppermute | solution.py:365
  (6 other events, 11.2 us)

commit v2 on v0

v2 whole, which is shorter than its diff:
```python
import functools

import jax
import jax.numpy as jnp
from jax import lax
from jax.experimental import pallas as pl
from jax.experimental.pallas import tpu as pltpu
from jax.sharding import PartitionSpec as P

BF = jnp.bfloat16
F32 = jnp.float32
CH = 32
LANES = 128
MID = 8 * LANES
HIGHEST = lax.Precision.HIGHEST
TURNS = (0, 63, 7 + 64, 56 + 64)


def iota(shape, dim):
    return lax.broadcasted_iota(jnp.int32, shape, dim)


def component_class(i):
    tensor = jnp.where(i < 30, 12 + ((i - 20) & 1), -1)
    return jnp.where(i < 8, i, jnp.where(i < 20, 8 + ((i - 8) & 3), tensor))


def component_index(i):
    return jnp.where(i < 8, 0, jnp.where(i < 20, (i - 8) >> 2, jnp.where(i < 30, (i - 20) >> 1, -1)))


def gate_class(i):
    tensor = jnp.where(i < 30, 4 + ((i - 20) & 1), -1)
    return jnp.where(i < 8, i, jnp.where(i < 20, (i - 8) & 3, tensor))


def out_class(c):
    tensor = jnp.where(c < 84, 12 + ((c - 80) >> 1), -2)
    return jnp.where(c < 64, c >> 3, jnp.where(c < 80, 8 + ((c - 64) >> 2), tensor))


def in_class(c):
    tensor = jnp.where(c < 84, 12 + ((c - 80) & 1), -2)
    return jnp.where(c < 64, c & 7, jnp.where(c < 80, 8 + ((c - 64) & 3), tensor))


def one(condition, kind=BF):
    return jnp.where(condition, 1.0, 0.0).astype(kind)


def plane_source(q):
    lane = q & 127
    row = (lane * 205) >> 11
    y, z = row - 1, lane - 10 * row - 1
    inside = (y >= 0) & (y < 8) & (z >= 0) & (z < 8)
    return jnp.where(inside, 64 * (q >> 7) + 8 * y + z, -1)


def spread_table():
    return one(plane_source(iota((128, 256), 1)) == iota((128, 256), 0))


def compact_table():
    return one(plane_source(iota((256, 128), 0)) == iota((256, 128), 1))


def turn_table(r):
    return one((iota((128, 128), 1) ^ TURNS[r]) == iota((128, 128), 0))


def turn_signs(r, shape):
    i = iota(shape, 0) & (CH - 1)
    m = component_index(i)
    vector = (i >= 8) & (i < 20) & (m != r - 1)
    tensor = (i >= 20) & (m < 3) & (m != 3 - r)
    return jnp.where(vector | tensor, -1.0, 1.0).astype(BF)


def region_masks():
    lane = iota((1, LANES), 1)
    row = (lane * 205) >> 11
    col = lane - 10 * row

    def part(v):
        return jnp.where(v == 0, 0, jnp.where(v == 9, 2, 1))

    region = jnp.where(row < 10, 3 * part(row) + part(col), -1)
    return [one(region == o) for o in range(9)]


def dot(a, b, **kw):
    return jnp.dot(a, b, preferred_element_type=F32, **kw)


def dot_t(a, b):
    return lax.dot_general(a, b, (((1,), (1,)), ((), ())), preferred_element_type=F32)


def is_odd():
    return (lax.axis_index("xp") & 1) == 1


def table_row(codes, n, o, last):
    e = codes[n, o]
    d = e >> 1
    dx = lax.div(d, 3)
    other = jnp.where(d - 3 * dx == 1, 0, 2) + jnp.where(dx == 1, 0, 4)
    return jnp.where(e >= 18, last, jnp.minimum(other + (e & 1), last))


def gathered(pieces_of, masks):
    total = None
    for b in range(3):
        for c in range(3):
            o = 3 * b + c
            planes = jnp.concatenate(pieces_of(o), axis=0)
            shift = ((b - 1) * 80 + (c - 1) * 8) % LANES
            if shift:
                planes = pltpu.roll(planes, shift, 1)
            planes = planes * masks[o]
            total = planes if total is None else total + planes
    return total


def unfold(planes, count, columns, start):
    for o in range(9):
        shift = (11 - 10 * (o // 3) - o % 3) % LANES
        moved = pltpu.roll(planes, shift, 1) if shift else planes
        for p in range(count):
            at = start + p * LANES
            columns[o * CH : (o + 1) * CH, at : at + LANES] = moved[p * CH : (p + 1) * CH]


def stage_mid(table, own, part):
    zero = jnp.zeros((CH, LANES), BF)
    for x in range(8):
        for s in range(2):
            table[s, x] = own(s, x)
            table[2 + s, x] = part(s, x)
        table[4, x] = zero


def mid_columns(codes, masks, table, columns):
    for n in range(2):
        planes = gathered(lambda o: [table[table_row(codes, n, 9 + o, 4)].reshape(8 * CH, LANES)], masks)
        unfold(planes, 8, columns, n * MID)


def stage_edge(low, high, own, part, received, far):
    odd = is_odd()
    zero = jnp.zeros((CH, LANES), BF)
    for s in range(2):
        low[s], high[s] = own(s, 7), own(s, 0)
        low[2 + s], high[2 + s] = part(s, 7), part(s, 0)
        for base, faces in ((4, received), (6, far)):
            first, second = faces(0, s), faces(1, s)
            low[base + s] = jnp.where(odd, first, second)
            high[base + s] = jnp.where(odd, second, first)
    low[8] = zero
    high[8] = zero


def edge_columns(codes, masks, low, high, columns):
    def pieces(o):
        found = []
        for n in range(2):
            found += [low[table_row(codes, n, o, 8)], high[table_row(codes, n, 18 + o, 8)]]
        return found

    unfold(gathered(pieces, masks), 4, columns, 0)


def fold_mid(stacked, row):
    zero = jnp.zeros((CH, LANES), F32)
    before = jnp.concatenate([zero, stacked[row : row + CH, : MID - LANES]], axis=1)
    after = jnp.concatenate([stacked[row + 2 * CH : row + 3 * CH, LANES:], zero], axis=1)
    return before + stacked[row + CH : row + 2 * CH] + after


def edge_term(stacked, row, n, side):
    at = (2 * n + side) * LANES
    first = row + 2 * CH * side
    return stacked[first : first + CH, at : at + LANES]


def write_faces(face_a, face_b, index, plane_low, plane_high):
    odd = is_odd()
    face_a[index] = jnp.where(odd, plane_low, plane_high)
    face_b[index] = jnp.where(odd, plane_high, plane_low)


def spread_kernel(features, *refs):
    small, (fp, face_a, face_b), copies, staged = refs[:4], refs[4:7], refs[7:11], refs[11]
    for source, copy in zip(small, copies):
        copy[...] = source[...]
    staged[...] = jnp.zeros_like(staged)
    for n in range(2):
        staged[n * CH : n * CH + 30, :] = features[n]
    spread = spread_table()
    outer = []
    for k in range(4):
        planes = dot(staged[:, k * 128 : (k + 1) * 128], spread).astype(BF)
        for p in range(2):
            for n in range(2):
                plane = planes[n * CH : (n + 1) * CH, p * 128 : (p + 1) * 128]
                fp[n, 2 * k + p] = plane
                if 2 * k + p in (0, 7):
                    outer.append(plane)
    for n in range(2):
        write_faces(face_a, face_b, n, outer[n], outer[2 + n])


def weights_kernel(w_first, w_second, one_out, two_out, turned_out, padded, left):
    shape = (CH, LANES)
    i, c = iota(shape, 0), iota(shape, 1)
    double = jnp.where(i >= 20, 2.0, 1.0)
    j = iota((LANES, LANES), 1) & (CH - 1)
    col = iota((LANES, LANES), 0)
    by_in = one(in_class(col) == component_class(j))
    by_out = one(out_class(col) == component_class(j))
    rows_out = jnp.where(component_class(i) == out_class(c), double, 0.0)
    rows_gate = one(gate_class(i) == out_class(c), F32)
    rows_in = jnp.where(component_class(i) == in_class(c), double, 0.0)
    same = component_index(i) == component_index(c & (CH - 1))
    quarter = c >> 5
    padded[...] = jnp.zeros_like(padded)
    padded[0, 0:27, 0:84] = w_first[...].astype(F32)
    padded[1, 0:27, 0:84] = w_second[...].astype(F32)
    for which, rows, columns, blocks, out, base, flip in (
        (0, rows_out, by_in, True, one_out, 0, False),
        (0, rows_gate, by_in, False, one_out, 96, False),
        (1, rows_out, by_in, True, two_out, 0, False),
        (1, rows_in, by_out, True, turned_out, 0, True),
    ):
        for a in range(3):
            for bc in range(9):
                o = 9 * a + bc
                o = 26 - o if flip else o
                left[bc * CH : (bc + 1) * CH, :] = (rows * padded[which, o : o + 1, :]).astype(BF)
            found = dot(left[...], columns)
            for g in range(3):
                tile = jnp.zeros(shape, F32)
                for q in range(min(4, 9 - 4 * g)):
                    bc = 4 * g + q
                    keep = (quarter == q) & same if blocks else quarter == q
                    tile = tile + jnp.where(keep, found[bc * CH : (bc + 1) * CH], 0.0)
                width = min(128, 288 - 128 * g)
                out[base + a * CH : base + (a + 1) * CH, g * 128 : g * 128 + width] = tile[:, :width].astype(BF)


def first_mid_kernel(codes, own, part, w_first, columns, pre, gate_in, hidden_mid, table):
    masks = region_masks()
    inside = masks[4].astype(F32)
    stage_mid(table, lambda s, x: own[s, x], lambda s, x: part[s, x])
    mid_columns(codes, masks, table, columns)
    for n in range(2):
        stacked = dot(w_first[...], columns[:, n * MID : (n + 1) * MID])
        a, g = fold_mid(stacked, 0), fold_mid(stacked, 96)
        pre[n] = a
        gate_in[n] = g
        for x in range(1, 7):
            at = slice(x * LANES, (x + 1) * LANES)
            hidden_mid[n, x - 1] = (a[:, at] * jax.nn.sigmoid(g[:, at]) * inside).astype(BF)


def turned_sum(staged, k):
    total = None
    for r in range(4):
        block = k if r < 2 else 3 - k
        term = dot(staged[r, :, 128 * block : 128 * block + 128], turn_table(r))
        total = term if total is None else total + term
    return total * 0.25


def back_kernel(mirror, own, across_y, across_x, across, back, staged):
    zero2 = jnp.zeros((2, 512), BF)
    for n in range(2):
        for r, ref in enumerate((own, across_y, across_x, across)):
            value = ref[n] if r == 0 else ref[mirror[n, r - 1]] * turn_signs(r, (30, 512))
            staged[r, n * CH : n * CH + 30, :] = value
            staged[r, n * CH + 30 : (n + 1) * CH, :] = zero2
    spread = spread_table()
    for k in range(4):
        planes = dot(turned_sum(staged, k).astype(BF), spread).astype(BF)
        for p in range(2):
            for n in range(2):
                back[n, 2 * k + p] = planes[n * CH : (n + 1) * CH, p * 128 : (p + 1) * 128]


def first_edge_kernel(
    codes, own, part, got_a, got_b, far_a, far_b, pre, gate_in, hidden_mid, back, w_first,
    columns, pre_edge, gate_edge, both, face_a, face_b, low, high,
):
    masks = region_masks()
    inside = masks[4].astype(F32)
    stage_edge(
        low, high, lambda s, x: own[s, x], lambda s, x: part[s, x],
        lambda which, s: (got_a, got_b)[which][s], lambda which, s: (far_a, far_b)[which][s],
    )
    edge_columns(codes, masks, low, high, columns)
    stacked = dot(w_first[...], columns[...])
    for n in range(2):
        outer = []
        for side in range(2):
            at = slice(7 * side * LANES, (7 * side + 1) * LANES)
            a = pre[n, :, at] + edge_term(stacked, 0, n, side)
            g = gate_in[n, :, at] + edge_term(stacked, 96, n, side)
            pre_edge[n, side] = a
            gate_edge[n, side] = g
            outer.append((a * jax.nn.sigmoid(g) * inside).astype(BF))
            both[0, n, 7 * side] = outer[side]
        write_faces(face_a, face_b, (0, n), *outer)
        for x in range(1, 7):
            both[0, n, x] = hidden_mid[n, x - 1]
        for x in range(8):
            both[1, n, x] = back[n, x]
        write_faces(face_a, face_b, (1, n), back[n, 0], back[n, 7])


def gate_back(grad, a, g, rows8, inside):
    sig = jax.nn.sigmoid(g)
    through = grad * sig
    extra = dot(rows8, grad * a, precision=HIGHEST)
    sig8 = sig[0:8]
    top = through[0:8] + sig8 * (1.0 - sig8) * extra
    return (jnp.concatenate([top, through[8:]], axis=0) * inside).astype(BF)


def gate_rows():
    return one(gate_class(iota((8, CH), 1)) == iota((8, CH), 0), F32)


def second_mid_kernel(
    codes, own, part, pre, gate_in, columns_f, w_second, w_turned, second, through_edge, raw,
    table, columns_h, columns_b, placed_f, placed_s,
):
    masks = region_masks()
    inside = jnp.concatenate([masks[4].astype(F32)] * 6, axis=1)
    for f, columns in ((0, columns_h), (1, columns_b)):
        stage_mid(table.at[f], lambda s, x: own[f, s, x], lambda s, x: part[f, s, x])
        mid_columns(codes, masks, table.at[f], columns)
    zero = jnp.zeros((CH, LANES), BF)
    rows8 = gate_rows()

    def place(placed, n, planes, first, last):
        for a in range(3):
            for q in range(8):
                x = q + 1 - a
                at = (8 * n + q) * LANES
                placed[a * CH : (a + 1) * CH, at : at + LANES] = planes(x) if first <= x <= last else zero

    for n in range(2):
        here = slice(n * MID, (n + 1) * MID)
        second[n] = fold_mid(dot(w_second[...], columns_h[:, here]), 0)
        place(placed_s, n, lambda x: own[1, n, x], 0, 7)
        grad = fold_mid(dot(w_turned[...], columns_b[:, here]), 0)
        through_edge[n, 0] = grad[:, :LANES]
        through_edge[n, 1] = grad[:, 7 * LANES :]
        inner = slice(LANES, 7 * LANES)
        back_pre = gate_back(grad[:, inner], pre[n, :, inner], gate_in[n, :, inner], rows8, inside)
        place(placed_f, n, lambda x: back_pre[:, (x - 1) * LANES : x * LANES], 1, 6)
    raw[0] = dot_t(columns_f[...], placed_f[...])
    raw[1] = dot_t(columns_h[...], placed_s[...])


def second_edge_kernel(
    scale, codes, own, part, got_a, got_b, far_a, far_b, pre_edge, gate_edge, second_in, through_edge,
    columns_f, columns_fe, raw, w_second, w_turned, second, grads,
    low, high, columns_h, columns_b, placed_f, placed_s, place, lifted,
):
    masks = region_masks()
    inside = masks[4].astype(F32)
    for f, columns in ((0, columns_h), (1, columns_b)):
        stage_edge(
            low.at[f], high.at[f], lambda s, x: own[f, s, x], lambda s, x: part[f, s, x],
            lambda which, s: (got_a, got_b)[which][f, s], lambda which, s: (far_a, far_b)[which][f, s],
        )
        edge_columns(codes, masks, low.at[f], high.at[f], columns)
    more = dot(w_second[...], columns_h[...])
    more_t = dot(w_turned[...], columns_b[...])
    rows8 = gate_rows()
    compact = compact_table()
    placed_f[...] = jnp.zeros_like(placed_f)
    placed_s[...] = jnp.zeros_like(placed_s)
    for n in range(2):
        for k in range(4):
            planes = second_in[n, :, k * 256 : (k + 1) * 256]
            zero = jnp.zeros((CH, LANES), F32)
            if k == 0:
                planes = planes + jnp.concatenate([edge_term(more, 0, n, 0), zero], axis=1)
            if k == 3:
                planes = planes + jnp.concatenate([zero, edge_term(more, 0, n, 1)], axis=1)
            second[n * CH : (n + 1) * CH, k * 128 : (k + 1) * 128] = dot(planes.astype(BF), compact).astype(BF)
        for side in range(2):
            grad = through_edge[n, side] + edge_term(more_t, 0, n, side)
            back_pre = gate_back(grad, pre_edge[n, side], gate_edge[n, side], rows8, inside)
            at = (2 * n + side) * LANES
            a = 2 * side
            placed_s[a * CH : (a + 1) * CH, at : at + LANES] = own[1, n, 7 * side]
            for a in range(3):
                at = (6 * n + 3 * side + a) * LANES
                placed_f[a * CH : (a + 1) * CH, at : at + LANES] = back_pre
    pieces = []
    for n in range(2):
        mid, edge = n * MID, 2 * n * LANES
        pieces += [
            columns_fe[:, edge : edge + LANES], columns_f[:, mid : mid + 2 * LANES],
            columns_f[:, mid + 6 * LANES : mid + MID], columns_fe[:, edge + LANES : edge + 2 * LANES],
        ]
    shape = (CH, LANES)
    i, c = iota(shape, 0), iota(shape, 1)
    lift = jnp.where(component_class(i) == out_class(c), jnp.where(i >= 20, 2.0, 1.0), 0.0)
    keep = one(component_class(i) == in_class(c), F32)
    same = one(component_index(i) == component_index(iota(shape, 1) & (CH - 1)), F32)[:, 0:96]
    place[...] = jnp.zeros_like(place)
    for a in range(3):
        place[a * CH : (a + 1) * CH, a * LANES : (a + 1) * LANES] = lift
    found = (
        raw[0] + dot_t(jnp.concatenate(pieces, axis=1), placed_f[...]),
        raw[1] + dot_t(columns_h[...], placed_s[...]),
    )
    for layer in range(2):
        masked = (found[layer].reshape(9, CH, 96) * same).reshape(9 * CH, 96)
        lifted[...] = dot(masked, place[...], precision=HIGHEST)
        for a in range(3):
            block = lifted[:, a * LANES : (a + 1) * LANES].reshape(9, CH, LANES) * keep
            first = 27 * layer + 9 * a
            grads[first : first + 9, :] = jnp.sum(block, axis=1) * scale
    grads[54:56, :] = jnp.zeros((2, LANES), F32)


def turn_kernel(mirror, own, across_y, across_x, across, out, staged):
    for n in range(2):
        staged[0, n * CH : (n + 1) * CH, :] = own[n * CH : (n + 1) * CH, :]
        for r, ref in ((1, across_y), (2, across_x), (3, across)):
            at = pl.multiple_of(mirror[n, r - 1] * CH, CH)
            staged[r, n * CH : (n + 1) * CH, :] = ref[pl.ds(at, CH), :] * turn_signs(r, (CH, 512))
    for k in range(4):
        result = turned_sum(staged, k).astype(BF)
        for n in range(2):
            out[n, :, k * 128 : (k + 1) * 128] = result[n * CH : n * CH + 30]


SMEM = pl.BlockSpec(memory_space=pltpu.SMEM)
VMEM = pl.BlockSpec(memory_space=pltpu.VMEM)


def call(kernel, us, n_smem, outs, scratch, *args):
    return pl.pallas_call(
        kernel,
        out_shape=tuple(jax.ShapeDtypeStruct(s, t) for s, t in outs),
        in_specs=[SMEM] * n_smem + [VMEM] * (len(args) - n_smem),
        out_specs=tuple([VMEM] * len(outs)),
        scratch_shapes=[pltpu.VMEM(s, t) for s, t in scratch],
        compiler_params=pltpu.CompilerParams(vmem_limit_bytes=24 * 1024 * 1024),
        cost_estimate=pl.CostEstimate(flops=0, transcendentals=0, bytes_accessed=int(us * 3_000_000)),
    )(*args)


def swap_y(x):
    n = lax.axis_size("yp")
    return lax.ppermute(x, "yp", [(i, n - 1 - i) for i in range(n)])


def mirror_x(x):
    n = lax.axis_size("xp")
    return lax.ppermute(x, "xp", [(i, n - 1 - i) for i in range(n)])


def pair_swap(x, first):
    n = lax.axis_size("xp")
    pairs = []
    for i in range(first, n - 1, 2):
        pairs += [(i, i + 1), (i + 1, i)]
    return lax.ppermute(x, "xp", pairs)


def exchange(face_a, face_b):
    got_b = pair_swap(face_b, 1)
    got_a = pair_swap(face_a, 0)
    return got_a, got_b


def after(arrays, *others):
    return lax.optimization_barrier((tuple(arrays), others))[0]


def on_device(features, cotangent, w_first, w_second, codes, mirror):
    plane = (CH, LANES)
    fp, face_a, face_b, codes, mirror, w_first, w_second = call(
        spread_kernel, 0.2, 0,
        [
            ((2, 8) + plane, BF), ((2,) + plane, BF), ((2,) + plane, BF),
            *((x.shape, x.dtype) for x in (codes, mirror, w_first, w_second)),
        ],
        [((64, 512), BF)], features, codes, mirror, w_first, w_second,
    )
    cot_x = mirror_x(cotangent)
    cot_y = swap_y(cotangent)
    got = exchange(face_a, face_b)
    part = swap_y(fp)
    w1, w2, w2t = call(
        weights_kernel, 0.5, 0, [((192, 288), BF), ((96, 288), BF), ((96, 288), BF)],
        [((2, CH, LANES), F32), ((288, LANES), BF)], w_first, w_second,
    )
    columns, pre, gate_in, hidden_mid = call(
        first_mid_kernel, 2, 1,
        [((288, 2 * MID), BF), ((2, CH, MID), F32), ((2, CH, MID), F32), ((2, 6) + plane, BF)],
        [((5, 8) + plane, BF)], codes, fp, part, w1,
    )
    *got, cot_x = after((*got, cot_x), hidden_mid)
    faces = (*got, swap_y(got[0]), swap_y(got[1]))
    cot_xy = swap_y(cot_x)
    (back,) = call(
        back_kernel, 1.5, 1, [((2, 8) + plane, BF)], [((4, 64, 512), BF)], mirror, cotangent, cot_y, cot_x, cot_xy
    )
    columns_e, pre_e, gate_e, both, face_a, face_b = call(
        first_edge_kernel, 1.2, 1,
        [
            ((288, 4 * LANES), BF), ((2, 2) + plane, F32), ((2, 2) + plane, F32), ((2, 2, 8) + plane, BF),
            ((2, 2) + plane, BF), ((2, 2) + plane, BF),
        ],
        [((9,) + plane, BF)] * 2, codes, fp, part, *faces, pre, gate_in, hidden_mid, back, w1,
    )
    got = exchange(face_a, face_b)
    part = swap_y(both)
    second_part, through_e, raw = call(
        second_mid_kernel, 3.5, 1, [((2, CH, MID), F32), ((2, 2) + plane, F32), ((2, 288, 96), F32)],
        [((2, 5, 8) + plane, BF), ((288, 2 * MID), BF), ((288, 2 * MID), BF), ((96, 2 * MID), BF), ((96, 2 * MID), BF)],
        codes, both, part, pre, gate_in, columns, w2, w2t,
    )
    got = after(got, raw)
    faces = (*got, swap_y(got[0]), swap_y(got[1]))
    n_bricks = features.shape[0] * lax.axis_size("xp") * lax.axis_size("yp")
    second, grads = call(
        functools.partial(second_edge_kernel, 1.0 / n_bricks), 2.8, 1, [((64, 512), BF), ((56, LANES), F32)],
        [((2, 9) + plane, BF)] * 2 + [((288, 4 * LANES), BF)] * 2
        + [((96, 12 * LANES), BF), ((96, 4 * LANES), BF), ((96, 3 * LANES), F32), ((288, 3 * LANES), F32)],
        codes, both, part, *faces, pre_e, gate_e, second_part, through_e, columns, columns_e, raw, w2, w2t,
    )
    total = grads + swap_y(grads)
    (second,) = after((second,), total)
    second_y = swap_y(second)
    second_x = mirror_x(second)
    second_xy = swap_y(second_x)
    (denoised,) = call(
        turn_kernel, 0.9, 1, [((2, 30, 512), BF)], [((4, 64, 512), BF)], mirror, second, second_y, second_x, second_xy
    )
    n = lax.axis_size("xp")
    bit = 1
    while bit < n:
        total = total + lax.ppermute(total, "xp", [(i, i ^ bit) for i in range(n)])
        bit *= 2
    return denoised, total[0:27, 0:84], total[27:54, 0:84]


def solution(mesh):
    brick = P(("grp", "xp", "yp"))
    return jax.shard_map(
        on_device,
        mesh=mesh,
        in_specs=(brick, brick, P(), P(), brick, brick),
        out_specs=(brick, P("grp"), P("grp")),
        check_vma=False,
    )
```

time: 1130 us -> 49.8 us (0.04); the launches traced: 1110 us -> 49.5 us
  local copies, waits for them, and re-layouts: 767 us -> 5.73 us
  matrix products: 123 us -> 0 us
  other arithmetic: 93.5 us -> 0.02 us
  blocking collectives: 62.6 us -> 0 us
  waiting for transfers between devices: 19.1 us -> 5.92 us
  Pallas kernels: 0 us -> 12.2 us
    unnamed x1701 -> x11, local copies, waits for them, and re-layouts: 250 us -> 5.11 us
    squeeze x243 -> x0, local copies, waits for them, and re-layouts: 178 us -> none  [the longest x81 64 us: combine(): vector_k[offset]]
    slice x58 -> x1, local copies, waits for them, and re-layouts: 137 us -> 0.62 us  [on_device(): return (denoised, total[0:27, 0:84], total[27:54, 0:84])]
    dot_general x405 -> x0, matrix products: 123 us -> none  [the longest x81 39.5 us: combine(): jnp.einsum(flat_form, scalar_w[offset], source[:, :8], preferred_element_...]
    gather x84 -> x0, local copies, waits for them, and re-layouts: 95.4 us -> none  [the longest x81 93 us: assemble(): pieces.append(jnp.take(rim, rows[:, a * 9 + b * 3 + c], axis=0))]
    psum x1 -> x0, blocking collectives: 62.6 us -> none  [on_device(): sum_first, sum_second = lax.psum((local_first, local_second), ('xp', 'yp'))]
    another operation x78 -> x0, local copies, waits for them, and re-layouts: 62.2 us -> none  [the longest x75 59.5 us: assemble(): pieces.append(jnp.take(rim, rows[:, a * 9 + b * 3 + c], axis=0))]
    select_n x100 -> x0, other arithmetic: 39 us -> none  [the longest x95 37.3 us: assemble(): pieces.append(jnp.take(rim, rows[:, a * 9 + b * 3 + c], axis=0))]
  transfers between devices with their start and end apart: 16 -> 20, of which waited for: 4 -> 7; matrix products, arithmetic and copies ran while one was open for 22% -> 3% of each run, Pallas kernels for 0% -> 15%
where the time goes in v2:
time: 49.8 us; the launch traced here: 49.5 us
  starting transfers between devices  24.8 us (50%)
  Pallas kernels  12.2 us (24%)
  waiting for transfers between devices  5.92 us (12%)
  local copies, waits for them, and re-layouts  5.73 us (12%)
  between operations  0.8 us (2%)
    pallas_call x8, Pallas kernels, call(): pl.pallas_call(kernel, out_shape=tuple((jax.ShapeDtypeStruct(s, t) for s,...  12.2 us
    ppermute x3, starting transfers between devices, on_device(): total = total + lax.ppermute(total, 'xp', [(i, i ^ bit) for i in range(n)])  7.55 us
    ppermute x2, starting transfers between devices, mirror_x(): return lax.ppermute(x, 'xp', [(i, n - 1 - i) for i in range(n)])  7.48 us
    ppermute x4, starting transfers between devices, pair_swap(): return lax.ppermute(x, 'xp', pairs)  6.34 us
    unnamed x11, local copies, waits for them, and re-layouts  5.11 us
    ppermute x3, waiting for transfers between devices, on_device(): total = total + lax.ppermute(total, 'xp', [(i, i ^ bit) for i in range(n)])  3.63 us
    ppermute x11, starting transfers between devices, swap_y(): return lax.ppermute(x, 'yp', [(i, n - 1 - i) for i in range(n)])  3.45 us
    ppermute x11, waiting for transfers between devices, swap_y(): return lax.ppermute(x, 'yp', [(i, n - 1 - i) for i in range(n)])  2.12 us
  transfers between devices with their start and end apart: 20, of which 7 were waited for; matrix products, arithmetic and copies ran while one was open for 3% of the time, Pallas kernels for 15%

profile of v2, /device:TPU:0, one launch (start us, length us, event | category | flops | bytes accessed | tf_op | source)
XLA Modules:
  0.0 49.5 jit_solution(15652090577760637329)
XLA Ops:
  0.6 0.8 %copy.9.features = bf16[2,30,512]{2,1,0:T(8,128)(2,1)S(1)} copy(bf16[2,30,512]{2,0,1:T(2,128)(2,1)} %param.6) | data formatting | bytes 122880 | tf_op args[0]
  1.5 0.7 %copy-done = bf16[27,84]{1,0:T(8,128)(2,1)S(1)} copy-done((bf16[27,84]{1,0:T(8,128)(2,1)S(1)}, bf16[27,84]{1,0:T(8,128)(2,1)}, u32[]{:S(2)}) %copy-start) | copy-done | bytes 4560
  2.2 0.7 %copy-done.1 = bf16[27,84]{1,0:T(8,128)(2,1)S(1)} copy-done((bf16[27,84]{1,0:T(8,128)(2,1)S(1)}, bf16[27,84]{1,0:T(8,128)(2,1)}, u32[]{:S(2)}) %copy-start.1) | copy-done | bytes 4560
  2.9 0.7 %copy-done.2 = s32[2,27]{1,0:T(2,128)S(1)} copy-done((s32[2,27]{1,0:T(2,128)S(1)}, s32[2,27]{1,0:T(2,128)}, u32[]{:S(2)}) %copy-start.2) | copy-done | bytes 240
  3.6 0.7 %copy-done.3 = s32[2,3]{1,0:T(2,128)S(1)} copy-done((s32[2,3]{1,0:T(2,128)S(1)}, s32[2,3]{1,0:T(2,128)}, u32[]{:S(2)}) %copy-start.3) | copy-done | bytes 48
  4.4 0.5 %collective-permute-start = (bf16[2,8,32,128]{3,2,1,0:T(8,128)(2,1)S(1)}, bf16[2,8,32,128]{3,2,1,0:T(8,128)(2,1)S(1)}, u32[]{:S(2)}, u32[]{:S(2)}) collective-permute-start(bf16[2,8,32,128]{3,2,1,0:T(8,128)(2,1)S(1)} %get-tuple-element.36.own), channel_id=1, source_target_pairs={{0,1},{1,0},{2,3},{3,2},{4,5},{5,4},{6,7},{7,6},{8,9},{9,8},{10,11... | collective-permute-start | bytes 393224 | tf_op jit(solution)/shard_map/ppermute | solution.py:462
  4.9 0.8 %copy.10.own = bf16[2,30,512]{2,1,0:T(8,128)(2,1)S(1)} copy(bf16[2,30,512]{2,0,1:T(2,128)(2,1)} %param.7) | data formatting | bytes 122880 | tf_op args[1]
  5.8 5.6 %collective-permute-start.3 = (bf16[2,30,512]{2,1,0:T(8,128)(2,1)S(1)}, bf16[2,30,512]{2,1,0:T(8,128)(2,1)S(1)}, u32[]{:S(2)}, u32[]{:S(2)}) collective-permute-start(bf16[2,30,512]{2,1,0:T(8,128)(2,1)S(1)} %copy.10.own), channel_id=1, source_target_pairs={{0,14},{2,12},{4,10},{6,8},{8,6},{10,4},{12,2},{14,0},{1,15},{3,13... | collective-permute-start | bytes 184328 | tf_op jit(solution)/shard_map/ppermute | solution.py:467
  11.4 0.5 %collective-permute-start.1 = (bf16[2,32,128]{2,1,0:T(8,128)(2,1)S(1)}, bf16[2,32,128]{2,1,0:T(8,128)(2,1)S(1)}, u32[]{:S(2)}, u32[]{:S(2)}) collective-permute-start(bf16[2,32,128]{2,1,0:T(8,128)(2,1)S(1)} %get-tuple-element.37), channel_id=1, source_target_pairs={{0,2},{2,0},{4,6},{6,4},{8,10},{10,8},{12,14},{14,12},{1,3},{3,1},... | collective-permute-start | bytes 49160 | tf_op jit(solution)/shard_map/ppermute | solution.py:475
  11.9 0.7 %collective-permute-start.2 = (bf16[2,32,128]{2,1,0:T(8,128)(2,1)S(1)}, bf16[2,32,128]{2,1,0:T(8,128)(2,1)S(1)}, u32[]{:S(2)}, u32[]{:S(2)}) collective-permute-start(bf16[2,32,128]{2,1,0:T(8,128)(2,1)S(1)} %get-tuple-element.38), channel_id=1, source_target_pairs={{2,4},{4,2},{6,8},{8,6},{10,12},{12,10},{3,5},{5,3},{7,9},{9,7},{1... | collective-permute-start | bytes 49160 | tf_op jit(solution)/shard_map/ppermute | solution.py:475
  12.7 0.4 shard_map.86
  13.1 1.9 %shard_map.87 = (bf16[288,2048]{1,0:T(8,128)(2,1)S(1)}, f32[2,32,1024]{2,1,0:T(8,128)S(1)}, f32[2,32,1024]{2,1,0:T(8,128)S(1)}, bf16[2,6,32,128]{3,2,1,0:T(8,128)(2,1)S(1)}) custom-call(s32[2,27]{1,0:T(2,128)S(1)} %get-tuple-element.35.codes, bf16[2,8,32,128]{3,2,1,0:T(8,128)(2,1)S(1)} %get-tuple-element.36.own, ...), custom_call_target="tpu_custom_call" | custom-call | bytes 6000000 | tf_op jit(solution)/shard_map/pallas_call | solution.py:449
  15.2 0.4 collective-permute-start.7
  16.5 1.4 %shard_map.88.back = bf16[2,8,32,128]{3,2,1,0:T(8,128)(2,1)S(1)} custom-call(s32[2,3]{1,0:T(2,128)S(1)} %get-tuple-element.34.mirror, bf16[2,30,512]{2,1,0:T(8,128)(2,1)S(1)} %copy.10.own, bf16[2,30,512]{2,1,0:T(8,128)(2,1)S(1)} %collective-permute-done.6.across_y, bf16[2,30,512]{2,1,0:T(8,128)(2,1)S(1)} %collective-permute-done.3.across_x, ...), custom_call_target="tpu_custom_call" | custom-call | bytes 4500000 | tf_op jit(solution)/shard_map/pallas_call | solution.py:449
  18.0 1.2 %shard_map.89 = (bf16[288,512]{1,0:T(8,128)(2,1)S(1)}, f32[2,2,32,128]{3,2,1,0:T(8,128)S(1)}, f32[2,2,32,128]{3,2,1,0:T(8,128)S(1)}, bf16[2,2,8,32,128]{4,3,2,1,...) custom-call(s32[2,27]{1,0:T(2,128)S(1)} %get-tuple-element.35.codes, ...), custom_call_target="tpu_custom_call" | custom-call | bytes 3600000 | tf_op jit(solution)/shard_map/pallas_call | solution.py:449
  19.6 4.5 %collective-permute-start.9 = (bf16[2,2,32,128]{3,2,1,0:T(8,128)(2,1)S(1)}, bf16[2,2,32,128]{3,2,1,0:T(8,128)(2,1)S(1)}, u32[]{:S(2)}, u32[]{:S(2)}) collective-permute-start(bf16[2,2,32,128]{3,2,1,0:T(8,128)(2,1)S(1)} %get-tuple-element.49), channel_id=1, source_target_pairs={{0,2},{2,0},{4,6},{6,4},{8,10},{10,8},{12,14},{14,12},{1,3},{3,1},... | collective-permute-start | bytes 98312 | tf_op jit(solution)/shard_map/ppermute | solution.py:475
  24.1 0.7 %collective-permute-start.10 = (bf16[2,2,32,128]{3,2,1,0:T(8,128)(2,1)S(1)}, bf16[2,2,32,128]{3,2,1,0:T(8,128)(2,1)S(1)}, u32[]{:S(2)}, u32[]{:S(2)}) collective-permute-start(bf16[2,2,32,128]{3,2,1,0:T(8,128)(2,1)S(1)} %get-tuple-element.50), channel_id=1, source_target_pairs={{2,4},{4,2},{6,8},{8,6},{10,12},{12,10},{3,5},{5,3},{7,9},{9,7},{1... | collective-permute-start | bytes 98312 | tf_op jit(solution)/shard_map/ppermute | solution.py:475
  24.8 3.5 %shard_map.90 = (f32[2,32,1024]{2,1,0:T(8,128)S(1)}, f32[2,2,32,128]{3,2,1,0:T(8,128)S(1)}, f32[2,288,96]{2,1,0:T(8,128)S(1)}) custom-call(s32[2,27]{1,0:T(2,128)S(1)} %get-tuple-element.35.codes, bf16[2,2,8,32,128]{4,3,2,1,0:T(8,128)(2,1)S(1)} %get-tuple-element.48.own, bf16[2,2,8,32,128]{4,3,2,1,0:T(8,128)(2,1)S(1)} %collective-permute-done.8.part, ...), custom_call_target="tpu_custom_call" | custom-call | bytes 10500000 | tf_op jit(solution)/shard_map/pallas_call | solution.py:449
  28.4 0.4 collective-permute-start.12
  28.8 0.7 %collective-permute-done.11.far_a = bf16[2,2,32,128]{3,2,1,0:T(8,128)(2,1)S(1)} collective-permute-done((bf16[2,2,32,128]{3,2,1,0:T(8,128)(2,1)S(1)}, bf16[2,2,32,128]{3,2,1,0:T(8,128)(2,1)S(1)}, u32[]{:S(2)}, u32[]{:S(2)}) %collective-permute-start.11) | collective-permute-done | bytes 32800 | tf_op jit(solution)/shard_map/ppermute | solution.py:462
  29.7 2.7 %shard_map.91 = (bf16[64,512]{1,0:T(8,128)(2,1)S(1)}, f32[56,128]{1,0:T(8,128)S(1)}) custom-call(s32[2,27]{1,0:T(2,128)S(1)} %get-tuple-element.35.codes, bf16[2,2,8,32,128]{4,3,2,1,0:T(8,128)(2,1)S(1)} %get-tuple-element.48.own, bf16[2,2,8,32,128]{4,3,2,1,0:T(8,128)(2,1)S(1)} %collective-permute-done.8.part, ...), custom_call_target="tpu_custom_call" | custom-call | bytes 8400000 | tf_op jit(solution)/shard_map/pallas_call | solution.py:449
  32.9 0.9 %collective-permute-done.13 = f32[56,128]{1,0:T(8,128)S(1)} collective-permute-done((f32[56,128]{1,0:T(8,128)S(1)}, f32[56,128]{1,0:T(8,128)S(1)}, u32[]{:S(2)}, u32[]{:S(2)}) %collective-permute-start.13) | collective-permute-done | bytes 28704 | tf_op jit(solution)/shard_map/ppermute | solution.py:462
  33.7 2.5 %collective-permute-start.17 = (f32[56,128]{1,0:T(8,128)S(1)}, f32[56,128]{1,0:T(8,128)S(1)}, u32[]{:S(2)}, u32[]{:S(2)}) collective-permute-start(f32[56,128]{1,0:T(8,128)S(1)} %add.12), channel_id=1, source_target_pairs={{0,2},{2,0},{4,6},{6,4},{8,10},{10,8},{12,14},{14,12},{1,3},{3,1},... | collective-permute-start | bytes 86024 | tf_op jit(solution)/shard_map/ppermute | solution.py:552
  36.2 1.8 %collective-permute-start.15 = (bf16[64,512]{1,0:T(8,128)(2,1)S(1)}, bf16[64,512]{1,0:T(8,128)(2,1)S(1)}, u32[]{:S(2)}, u32[]{:S(2)}) collective-permute-start(bf16[64,512]{1,0:T(8,128)(2,1)S(1)} %get-tuple-element.64.own), channel_id=1, source_target_pairs={{0,14},{2,12},{4,10},{6,8},{8,6},{10,4},{12,2},{14,0},{1,15},{3,13... | collective-permute-start | bytes 196616 | tf_op jit(solution)/shard_map/ppermute | solution.py:467
  38.1 2.3 %collective-permute-start.18 = (f32[56,128]{1,0:T(8,128)S(1)}, f32[56,128]{1,0:T(8,128)S(1)}, u32[]{:S(2)}, u32[]{:S(2)}) collective-permute-start(f32[56,128]{1,0:T(8,128)S(1)} %add.13), channel_id=1, source_target_pairs={{0,4},{2,6},{4,0},{6,2},{8,12},{10,14},{12,8},{14,10},{1,5},{3,7},... | collective-permute-start | bytes 86024 | tf_op jit(solution)/shard_map/ppermute | solution.py:552
  40.3 2.2 %collective-permute-done.18 = f32[56,128]{1,0:T(8,128)S(1)} collective-permute-done((f32[56,128]{1,0:T(8,128)S(1)}, f32[56,128]{1,0:T(8,128)S(1)}, u32[]{:S(2)}, u32[]{:S(2)}) %collective-permute-start.18) | collective-permute-done | bytes 28704 | tf_op jit(solution)/shard_map/ppermute | solution.py:552
  42.5 2.8 %collective-permute-start.19 = (f32[56,128]{1,0:T(8,128)S(1)}, f32[56,128]{1,0:T(8,128)S(1)}, u32[]{:S(2)}, u32[]{:S(2)}) collective-permute-start(f32[56,128]{1,0:T(8,128)S(1)} %add.14), channel_id=1, source_target_pairs={{0,8},{2,10},{4,12},{6,14},{8,0},{10,2},{12,4},{14,6},{1,9},{3,11}... | collective-permute-start | bytes 86024 | tf_op jit(solution)/shard_map/ppermute | solution.py:552
  45.4 0.5 %collective-permute-start.16 = (bf16[64,512]{1,0:T(8,128)(2,1)S(1)}, bf16[64,512]{1,0:T(8,128)(2,1)S(1)}, u32[]{:S(2)}, u32[]{:S(2)}) collective-permute-start(bf16[64,512]{1,0:T(8,128)(2,1)S(1)} %collective-permute-done.15.across_x), channel_id=1, source_target_pairs={{0,1},{1,0},{2,3},{3,2},{4,5},{5,4},{6,7},{7,6},{8,9},{9,8},{10,11... | collective-permute-start | bytes 196616 | tf_op jit(solution)/shard_map/ppermute | solution.py:462
  45.9 1.4 %collective-permute-done.19 = f32[56,128]{1,0:T(8,128)S(1)} collective-permute-done((f32[56,128]{1,0:T(8,128)S(1)}, f32[56,128]{1,0:T(8,128)S(1)}, u32[]{:S(2)}, u32[]{:S(2)}) %collective-permute-start.19) | collective-permute-done | bytes 28704 | tf_op jit(solution)/shard_map/ppermute | solution.py:552
  47.3 0.6 %fusion = (f32[27,84]{1,0:T(8,128)}, f32[27,84]{1,0:T(8,128)}) fusion(f32[56,128]{1,0:T(8,128)S(1)} %add.15), kind=kLoop, calls=%fused_computation | loop fusion | bytes 36288 | tf_op jit(solution)/shard_map/slice | solution.py:554
  47.9 0.8 %shard_map.92 = bf16[2,30,512]{2,1,0:T(8,128)(2,1)S(1)} custom-call(s32[2,3]{1,0:T(2,128)S(1)} %get-tuple-element.34.mirror, bf16[64,512]{1,0:T(8,128)(2,1)S(1)} %get-tuple-element.64.own, bf16[64,512]{1,0:T(8,128)(2,1)S(1)} %collective-permute-done.14.across_y, bf16[64,512]{1,0:T(8,128)(2,1)S(1)} %collective-permute-done.15.across_x, ...), custom_call_target="tpu_custom_call" | custom-call | bytes 2700000 | tf_op jit(solution)/shard_map/pallas_call | solution.py:449
  48.8 0.7 %copy.13 = bf16[2,30,512]{2,0,1:T(2,128)(2,1)} copy(bf16[2,30,512]{2,1,0:T(8,128)(2,1)S(1)} %shard_map.92) | data formatting | bytes 122880
  (32 shorter events, 2.5 us)
Async XLA Ops:
  1.5 0.7 %copy-start = (bf16[27,84]{1,0:T(8,128)(2,1)S(1)}, bf16[27,84]{1,0:T(8,128)(2,1)}, u32[]{:S(2)}) copy-start(bf16[27,84]{1,0:T(8,128)(2,1)} %refs_2_.1) | copy-start | bytes 13612
  2.2 0.7 %copy-start.1 = (bf16[27,84]{1,0:T(8,128)(2,1)S(1)}, bf16[27,84]{1,0:T(8,128)(2,1)}, u32[]{:S(2)}) copy-start(bf16[27,84]{1,0:T(8,128)(2,1)} %refs_3_.1) | copy-start | bytes 13612
  2.9 0.7 %copy-start.2 = (s32[2,27]{1,0:T(2,128)S(1)}, s32[2,27]{1,0:T(2,128)}, u32[]{:S(2)}) copy-start(s32[2,27]{1,0:T(2,128)} %refs_0_.1) | copy-start | bytes 652
  3.5 0.7 %copy-start.3 = (s32[2,3]{1,0:T(2,128)S(1)}, s32[2,3]{1,0:T(2,128)}, u32[]{:S(2)}) copy-start(s32[2,3]{1,0:T(2,128)} %refs_1_.1) | copy-start | bytes 76
  4.4 8.7 %collective-permute-start = (bf16[2,8,32,128]{3,2,1,0:T(8,128)(2,1)S(1)}, bf16[2,8,32,128]{3,2,1,0:T(8,128)(2,1)S(1)}, u32[]{:S(2)}, u32[]{:S(2)}) collective-permute-start(bf16[2,8,32,128]{3,2,1,0:T(8,128)(2,1)S(1)} %get-tuple-element.36.own), channel_id=1, source_target_pairs={{0,1},{1,0},{2,3},{3,2},{4,5},{5,4},{6,7},{7,6},{8,9},{9,8},{10,11... | collective-permute-start | bytes 393224 | tf_op jit(solution)/shard_map/ppermute | solution.py:462
  5.8 9.4 %collective-permute-start.3 = (bf16[2,30,512]{2,1,0:T(8,128)(2,1)S(1)}, bf16[2,30,512]{2,1,0:T(8,128)(2,1)S(1)}, u32[]{:S(2)}, u32[]{:S(2)}) collective-permute-start(bf16[2,30,512]{2,1,0:T(8,128)(2,1)S(1)} %copy.10.own), channel_id=1, source_target_pairs={{0,14},{2,12},{4,10},{6,8},{8,6},{10,4},{12,2},{14,0},{1,15},{3,13... | collective-permute-start | bytes 184328 | tf_op jit(solution)/shard_map/ppermute | solution.py:467
  11.4 3.7 %collective-permute-start.1 = (bf16[2,32,128]{2,1,0:T(8,128)(2,1)S(1)}, bf16[2,32,128]{2,1,0:T(8,128)(2,1)S(1)}, u32[]{:S(2)}, u32[]{:S(2)}) collective-permute-start(bf16[2,32,128]{2,1,0:T(8,128)(2,1)S(1)} %get-tuple-element.37), channel_id=1, source_target_pairs={{0,2},{2,0},{4,6},{6,4},{8,10},{10,8},{12,14},{14,12},{1,3},{3,1},... | collective-permute-start | bytes 49160 | tf_op jit(solution)/shard_map/ppermute | solution.py:475
  11.9 3.2 %collective-permute-start.2 = (bf16[2,32,128]{2,1,0:T(8,128)(2,1)S(1)}, bf16[2,32,128]{2,1,0:T(8,128)(2,1)S(1)}, u32[]{:S(2)}, u32[]{:S(2)}) collective-permute-start(bf16[2,32,128]{2,1,0:T(8,128)(2,1)S(1)} %get-tuple-element.38), channel_id=1, source_target_pairs={{2,4},{4,2},{6,8},{8,6},{10,12},{12,10},{3,5},{5,3},{7,9},{9,7},{1... | collective-permute-start | bytes 49160 | tf_op jit(solution)/shard_map/ppermute | solution.py:475
  12.6 3.5 %collective-permute-start.6 = (bf16[2,30,512]{2,1,0:T(8,128)(2,1)S(1)}, bf16[2,30,512]{2,1,0:T(8,128)(2,1)S(1)}, u32[]{:S(2)}, u32[]{:S(2)}) collective-permute-start(bf16[2,30,512]{2,1,0:T(8,128)(2,1)S(1)} %copy.10.own), channel_id=1, source_target_pairs={{0,1},{1,0},{2,3},{3,2},{4,5},{5,4},{6,7},{7,6},{8,9},{9,8},{10,11... | collective-permute-start | bytes 184328 | tf_op jit(solution)/shard_map/ppermute | solution.py:462
  15.2 1.3 %collective-permute-start.7 = (bf16[2,30,512]{2,1,0:T(8,128)(2,1)S(1)}, bf16[2,30,512]{2,1,0:T(8,128)(2,1)S(1)}, u32[]{:S(2)}, u32[]{:S(2)}) collective-permute-start(bf16[2,30,512]{2,1,0:T(8,128)(2,1)S(1)} %collective-permute-done.3.across_x), channel_id=1, source_target_pairs={{0,1},{1,0},{2,3},{3,2},{4,5},{5,4},{6,7},{7,6},{8,9},{9,8},{10,11... | collective-permute-start | bytes 184328 | tf_op jit(solution)/shard_map/ppermute | solution.py:462
  15.6 2.3 %collective-permute-start.4 = (bf16[2,32,128]{2,1,0:T(8,128)(2,1)S(1)}, bf16[2,32,128]{2,1,0:T(8,128)(2,1)S(1)}, u32[]{:S(2)}, u32[]{:S(2)}) collective-permute-start(bf16[2,32,128]{2,1,0:T(8,128)(2,1)S(1)} %collective-permute-done.1.got_a), channel_id=1, source_target_pairs={{0,1},{1,0},{2,3},{3,2},{4,5},{5,4},{6,7},{7,6},{8,9},{9,8},{10,11... | collective-permute-start | bytes 49160 | tf_op jit(solution)/shard_map/ppermute | solution.py:462
  15.7 2.3 %collective-permute-start.5 = (bf16[2,32,128]{2,1,0:T(8,128)(2,1)S(1)}, bf16[2,32,128]{2,1,0:T(8,128)(2,1)S(1)}, u32[]{:S(2)}, u32[]{:S(2)}) collective-permute-start(bf16[2,32,128]{2,1,0:T(8,128)(2,1)S(1)} %collective-permute-done.2.got_b), channel_id=1, source_target_pairs={{0,1},{1,0},{2,3},{3,2},{4,5},{5,4},{6,7},{7,6},{8,9},{9,8},{10,11... | collective-permute-start | bytes 49160 | tf_op jit(solution)/shard_map/ppermute | solution.py:462
  19.2 5.6 %collective-permute-start.8 = (bf16[2,2,8,32,128]{4,3,2,1,0:T(8,128)(2,1)S(1)}, bf16[2,2,8,32,128]{4,3,2,1,0:T(8,128)(2,1)S(1)}, u32[]{:S(2)}, u32[]{:S(2)}) collective-permute-start(bf16[2,2,8,32,128]{4,3,2,1,0:T(8,128)(2,1)S(1)} %get-tuple-element.48.own), channel_id=1, source_target_pairs={{0,1},{1,0},{2,3},{3,2},{4,5},{5,4},{6,7},{7,6},{8,9},{9,8},{10,11... | collective-permute-start | bytes 786440 | tf_op jit(solution)/shard_map/ppermute | solution.py:462
  19.6 8.7 %collective-permute-start.9 = (bf16[2,2,32,128]{3,2,1,0:T(8,128)(2,1)S(1)}, bf16[2,2,32,128]{3,2,1,0:T(8,128)(2,1)S(1)}, u32[]{:S(2)}, u32[]{:S(2)}) collective-permute-start(bf16[2,2,32,128]{3,2,1,0:T(8,128)(2,1)S(1)} %get-tuple-element.49), channel_id=1, source_target_pairs={{0,2},{2,0},{4,6},{6,4},{8,10},{10,8},{12,14},{14,12},{1,3},{3,1},... | collective-permute-start | bytes 98312 | tf_op jit(solution)/shard_map/ppermute | solution.py:475
  24.1 4.2 %collective-permute-start.10 = (bf16[2,2,32,128]{3,2,1,0:T(8,128)(2,1)S(1)}, bf16[2,2,32,128]{3,2,1,0:T(8,128)(2,1)S(1)}, u32[]{:S(2)}, u32[]{:S(2)}) collective-permute-start(bf16[2,2,32,128]{3,2,1,0:T(8,128)(2,1)S(1)} %get-tuple-element.50), channel_id=1, source_target_pairs={{2,4},{4,2},{6,8},{8,6},{10,12},{12,10},{3,5},{5,3},{7,9},{9,7},{1... | collective-permute-start | bytes 98312 | tf_op jit(solution)/shard_map/ppermute | solution.py:475
  28.3 1.3 %collective-permute-start.11 = (bf16[2,2,32,128]{3,2,1,0:T(8,128)(2,1)S(1)}, bf16[2,2,32,128]{3,2,1,0:T(8,128)(2,1)S(1)}, u32[]{:S(2)}, u32[]{:S(2)}) collective-permute-start(bf16[2,2,32,128]{3,2,1,0:T(8,128)(2,1)S(1)} %collective-permute-done.9.got_a), channel_id=1, source_target_pairs={{0,1},{1,0},{2,3},{3,2},{4,5},{5,4},{6,7},{7,6},{8,9},{9,8},{10,11... | collective-permute-start | bytes 98312 | tf_op jit(solution)/shard_map/ppermute | solution.py:462
  28.4 1.3 %collective-permute-start.12 = (bf16[2,2,32,128]{3,2,1,0:T(8,128)(2,1)S(1)}, bf16[2,2,32,128]{3,2,1,0:T(8,128)(2,1)S(1)}, u32[]{:S(2)}, u32[]{:S(2)}) collective-permute-start(bf16[2,2,32,128]{3,2,1,0:T(8,128)(2,1)S(1)} %collective-permute-done.10.got_b), channel_id=1, source_target_pairs={{0,1},{1,0},{2,3},{3,2},{4,5},{5,4},{6,7},{7,6},{8,9},{9,8},{10,11... | collective-permute-start | bytes 98312 | tf_op jit(solution)/shard_map/ppermute | solution.py:462
  32.5 1.3 %collective-permute-start.13 = (f32[56,128]{1,0:T(8,128)S(1)}, f32[56,128]{1,0:T(8,128)S(1)}, u32[]{:S(2)}, u32[]{:S(2)}) collective-permute-start(f32[56,128]{1,0:T(8,128)S(1)} %get-tuple-element.63), channel_id=1, source_target_pairs={{0,1},{1,0},{2,3},{3,2},{4,5},{5,4},{6,7},{7,6},{8,9},{9,8},{10,11... | collective-permute-start | bytes 86024 | tf_op jit(solution)/shard_map/ppermute | solution.py:462
  33.7 4.3 %collective-permute-start.17 = (f32[56,128]{1,0:T(8,128)S(1)}, f32[56,128]{1,0:T(8,128)S(1)}, u32[]{:S(2)}, u32[]{:S(2)}) collective-permute-start(f32[56,128]{1,0:T(8,128)S(1)} %add.12), channel_id=1, source_target_pairs={{0,2},{2,0},{4,6},{6,4},{8,10},{10,8},{12,14},{14,12},{1,3},{3,1},... | collective-permute-start | bytes 86024 | tf_op jit(solution)/shard_map/ppermute | solution.py:552
  36.2 9.1 %collective-permute-start.15 = (bf16[64,512]{1,0:T(8,128)(2,1)S(1)}, bf16[64,512]{1,0:T(8,128)(2,1)S(1)}, u32[]{:S(2)}, u32[]{:S(2)}) collective-permute-start(bf16[64,512]{1,0:T(8,128)(2,1)S(1)} %get-tuple-element.64.own), channel_id=1, source_target_pairs={{0,14},{2,12},{4,10},{6,8},{8,6},{10,4},{12,2},{14,0},{1,15},{3,13... | collective-permute-start | bytes 196616 | tf_op jit(solution)/shard_map/ppermute | solution.py:467
  38.1 4.5 %collective-permute-start.18 = (f32[56,128]{1,0:T(8,128)S(1)}, f32[56,128]{1,0:T(8,128)S(1)}, u32[]{:S(2)}, u32[]{:S(2)}) collective-permute-start(f32[56,128]{1,0:T(8,128)S(1)} %add.13), channel_id=1, source_target_pairs={{0,4},{2,6},{4,0},{6,2},{8,12},{10,14},{12,8},{14,10},{1,5},{3,7},... | collective-permute-start | bytes 86024 | tf_op jit(solution)/shard_map/ppermute | solution.py:552
  42.5 4.8 %collective-permute-start.19 = (f32[56,128]{1,0:T(8,128)S(1)}, f32[56,128]{1,0:T(8,128)S(1)}, u32[]{:S(2)}, u32[]{:S(2)}) collective-permute-start(f32[56,128]{1,0:T(8,128)S(1)} %add.14), channel_id=1, source_target_pairs={{0,8},{2,10},{4,12},{6,14},{8,0},{10,2},{12,4},{14,6},{1,9},{3,11}... | collective-permute-start | bytes 86024 | tf_op jit(solution)/shard_map/ppermute | solution.py:552
  45.3 2.6 %collective-permute-start.14 = (bf16[64,512]{1,0:T(8,128)(2,1)S(1)}, bf16[64,512]{1,0:T(8,128)(2,1)S(1)}, u32[]{:S(2)}, u32[]{:S(2)}) collective-permute-start(bf16[64,512]{1,0:T(8,128)(2,1)S(1)} %get-tuple-element.64.own), channel_id=1, source_target_pairs={{0,1},{1,0},{2,3},{3,2},{4,5},{5,4},{6,7},{7,6},{8,9},{9,8},{10,11... | collective-permute-start | bytes 196616 | tf_op jit(solution)/shard_map/ppermute | solution.py:462
  45.4 2.6 %collective-permute-start.16 = (bf16[64,512]{1,0:T(8,128)(2,1)S(1)}, bf16[64,512]{1,0:T(8,128)(2,1)S(1)}, u32[]{:S(2)}, u32[]{:S(2)}) collective-permute-start(bf16[64,512]{1,0:T(8,128)(2,1)S(1)} %collective-permute-done.15.across_x), channel_id=1, source_target_pairs={{0,1},{1,0},{2,3},{3,2},{4,5},{5,4},{6,7},{7,6},{8,9},{9,8},{10,11... | collective-permute-start | bytes 196616 | tf_op jit(solution)/shard_map/ppermute | solution.py:462

commit v3 on v2

--- a/solution.py
+++ b/solution.py
@@ -66,6 +66,15 @@
 
 def turn_table(r):
     return one((iota((128, 128), 1) ^ TURNS[r]) == iota((128, 128), 0))
+
+
+def turns_table():
+    return jnp.concatenate([turn_table(r) for r in range(4)], axis=0)
+
+
+def turns_spread_table():
+    source = plane_source(iota((128, 256), 1))
+    return jnp.concatenate([one((source ^ TURNS[r]) == iota((128, 256), 0)) for r in range(4)], axis=0)
 
 
 def turn_signs(r, shape):
@@ -177,10 +186,16 @@
     return before + stacked[row + CH : row + 2 * CH] + after
 
 
-def edge_term(stacked, row, n, side):
-    at = (2 * n + side) * LANES
-    first = row + 2 * CH * side
-    return stacked[first : first + CH, at : at + LANES]
+def edge_terms(stacked, row):
+    blocks = []
+    for e in range(4):
+        first = row + 2 * CH * (e & 1)
+        blocks.append(stacked[first : first + CH, e * LANES : (e + 1) * LANES])
+    return jnp.concatenate(blocks, axis=1)
+
+
+def edge_planes(ref):
+    return jnp.concatenate([ref[e >> 1, :, 7 * (e & 1) * LANES : (7 * (e & 1) + 1) * LANES] for e in range(4)], axis=1)
 
 
 def write_faces(face_a, face_b, index, plane_low, plane_high):
@@ -189,28 +204,20 @@
     face_b[index] = jnp.where(odd, plane_high, plane_low)
 
 
-def spread_kernel(features, *refs):
-    small, (fp, face_a, face_b), copies, staged = refs[:4], refs[4:7], refs[7:11], refs[11]
-    for source, copy in zip(small, copies):
-        copy[...] = source[...]
+def spread_kernel(features, fp, faces, staged):
     staged[...] = jnp.zeros_like(staged)
     for n in range(2):
         staged[n * CH : n * CH + 30, :] = features[n]
-    spread = spread_table()
-    outer = []
-    for k in range(4):
-        planes = dot(staged[:, k * 128 : (k + 1) * 128], spread).astype(BF)
-        for p in range(2):
-            for n in range(2):
-                plane = planes[n * CH : (n + 1) * CH, p * 128 : (p + 1) * 128]
-                fp[n, 2 * k + p] = plane
-                if 2 * k + p in (0, 7):
-                    outer.append(plane)
-    for n in range(2):
-        write_faces(face_a, face_b, n, outer[n], outer[2 + n])
-
-
-def weights_kernel(w_first, w_second, one_out, two_out, turned_out, padded, left):
+    rows = jnp.concatenate([staged[:, k * 128 : (k + 1) * 128] for k in range(4)], axis=0)
+    planes = dot(rows, spread_table()).astype(BF)
+    for n in range(2):
+        for x in range(8):
+            first = (x >> 1) * 2 * CH + n * CH
+            fp[n, x] = planes[first : first + CH, (x & 1) * LANES : (x & 1) * LANES + LANES]
+        write_faces(faces.at[0], faces.at[1], n, fp[n, 0], fp[n, 7])
+
+
+def weights_kernel(packed, small, one_out, two_out, turned_out, codes_out, mirror_out, padded, left):
     shape = (CH, LANES)
     i, c = iota(shape, 0), iota(shape, 1)
     double = jnp.where(i >= 20, 2.0, 1.0)
@@ -224,8 +231,10 @@
     same = component_index(i) == component_index(c & (CH - 1))
     quarter = c >> 5
     padded[...] = jnp.zeros_like(padded)
-    padded[0, 0:27, 0:84] = w_first[...].astype(F32)
-    padded[1, 0:27, 0:84] = w_second[...].astype(F32)
+    for which in range(2):
+        padded[which, 0:27, 0:84] = packed[0:27, which * LANES : which * LANES + 84].astype(F32)
+    codes_out[...] = small[:, 0:27]
+    mirror_out[...] = small[:, LANES : LANES + 3]
     for which, rows, columns, blocks, out, base, flip in (
         (0, rows_out, by_in, True, one_out, 0, False),
         (0, rows_gate, by_in, False, one_out, 96, False),
@@ -263,52 +272,51 @@
             hidden_mid[n, x - 1] = (a[:, at] * jax.nn.sigmoid(g[:, at]) * inside).astype(BF)
 
 
-def turned_sum(staged, k):
-    total = None
-    for r in range(4):
-        block = k if r < 2 else 3 - k
-        term = dot(staged[r, :, 128 * block : 128 * block + 128], turn_table(r))
-        total = term if total is None else total + term
-    return total * 0.25
+def turned_sum(staged, table):
+    rows = []
+    for k in range(4):
+        blocks = (k, k, 3 - k, 3 - k)
+        rows.append(jnp.concatenate([staged[r, :, 128 * b : 128 * b + 128] for r, b in enumerate(blocks)], axis=1))
+    return dot(jnp.concatenate(rows, axis=0), table) * 0.25
 
 
 def back_kernel(mirror, own, across_y, across_x, across, back, staged):
     zero2 = jnp.zeros((2, 512), BF)
     for n in range(2):
-        for r, ref in enumerate((own, across_y, across_x, across)):
-            value = ref[n] if r == 0 else ref[mirror[n, r - 1]] * turn_signs(r, (30, 512))
+        for r in range(4):
+            if r == 0:
+                value = own[n]
+            else:
+                value = (across_y, across_x, across)[r - 1][mirror[n, r - 1]] * turn_signs(r, (30, 512))
             staged[r, n * CH : n * CH + 30, :] = value
             staged[r, n * CH + 30 : (n + 1) * CH, :] = zero2
-    spread = spread_table()
-    for k in range(4):
-        planes = dot(turned_sum(staged, k).astype(BF), spread).astype(BF)
-        for p in range(2):
-            for n in range(2):
-                back[n, 2 * k + p] = planes[n * CH : (n + 1) * CH, p * 128 : (p + 1) * 128]
+    planes = turned_sum(staged, turns_spread_table()).astype(BF)
+    for n in range(2):
+        for x in range(8):
+            first = (x >> 1) * 2 * CH + n * CH
+            back[n, x] = planes[first : first + CH, (x & 1) * LANES : (x & 1) * LANES + LANES]
 
 
 def first_edge_kernel(
-    codes, own, part, got_a, got_b, far_a, far_b, pre, gate_in, hidden_mid, back, w_first,
+    codes, own, part, got_a, got_b, pre, gate_in, hidden_mid, back, w_first,
     columns, pre_edge, gate_edge, both, face_a, face_b, low, high,
 ):
     masks = region_masks()
-    inside = masks[4].astype(F32)
+    inside = jnp.concatenate([masks[4].astype(F32)] * 4, axis=1)
     stage_edge(
         low, high, lambda s, x: own[s, x], lambda s, x: part[s, x],
-        lambda which, s: (got_a, got_b)[which][s], lambda which, s: (far_a, far_b)[which][s],
+        lambda which, s: (got_a, got_b)[which][s], lambda which, s: (got_a, got_b)[which][2 + s],
     )
     edge_columns(codes, masks, low, high, columns)
     stacked = dot(w_first[...], columns[...])
-    for n in range(2):
-        outer = []
-        for side in range(2):
-            at = slice(7 * side * LANES, (7 * side + 1) * LANES)
-            a = pre[n, :, at] + edge_term(stacked, 0, n, side)
-            g = gate_in[n, :, at] + edge_term(stacked, 96, n, side)
-            pre_edge[n, side] = a
-            gate_edge[n, side] = g
-            outer.append((a * jax.nn.sigmoid(g) * inside).astype(BF))
-            both[0, n, 7 * side] = outer[side]
+    a = edge_planes(pre) + edge_terms(stacked, 0)
+    g = edge_planes(gate_in) + edge_terms(stacked, 96)
+    pre_edge[...] = a
+    gate_edge[...] = g
+    hidden = (a * jax.nn.sigmoid(g) * inside).astype(BF)
+    for n in range(2):
+        outer = [hidden[:, e * LANES : (e + 1) * LANES] for e in (2 * n, 2 * n + 1)]
+        both[0, n, 0], both[0, n, 7] = outer
         write_faces(face_a, face_b, (0, n), *outer)
         for x in range(1, 7):
             both[0, n, x] = hidden_mid[n, x - 1]
@@ -341,6 +349,8 @@
         mid_columns(codes, masks, table.at[f], columns)
     zero = jnp.zeros((CH, LANES), BF)
     rows8 = gate_rows()
+    for placed in (placed_f, placed_s):
+        placed[3 * CH :, :] = jnp.zeros((CH, 2 * MID), BF)
 
     def place(placed, n, planes, first, last):
         for a in range(3):
@@ -354,8 +364,8 @@
         second[n] = fold_mid(dot(w_second[...], columns_h[:, here]), 0)
         place(placed_s, n, lambda x: own[1, n, x], 0, 7)
         grad = fold_mid(dot(w_turned[...], columns_b[:, here]), 0)
-        through_edge[n, 0] = grad[:, :LANES]
-        through_edge[n, 1] = grad[:, 7 * LANES :]
+        through_edge[:, 2 * n * LANES : (2 * n + 1) * LANES] = grad[:, :LANES]
+        through_edge[:, (2 * n + 1) * LANES : (2 * n + 2) * LANES] = grad[:, 7 * LANES :]
         inner = slice(LANES, 7 * LANES)
         back_pre = gate_back(grad[:, inner], pre[n, :, inner], gate_in[n, :, inner], rows8, inside)
         place(placed_f, n, lambda x: back_pre[:, (x - 1) * LANES : x * LANES], 1, 6)
@@ -366,40 +376,44 @@
 def second_edge_kernel(
     scale, codes, own, part, got_a, got_b, far_a, far_b, pre_edge, gate_edge, second_in, through_edge,
     columns_f, columns_fe, raw, w_second, w_turned, second, grads,
-    low, high, columns_h, columns_b, placed_f, placed_s, place, lifted,
+    low, high, columns_h, columns_b, placed_f, placed_s, place,
 ):
     masks = region_masks()
-    inside = masks[4].astype(F32)
+    inside = jnp.concatenate([masks[4].astype(F32)] * 4, axis=1)
     for f, columns in ((0, columns_h), (1, columns_b)):
         stage_edge(
             low.at[f], high.at[f], lambda s, x: own[f, s, x], lambda s, x: part[f, s, x],
             lambda which, s: (got_a, got_b)[which][f, s], lambda which, s: (far_a, far_b)[which][f, s],
         )
         edge_columns(codes, masks, low.at[f], high.at[f], columns)
-    more = dot(w_second[...], columns_h[...])
-    more_t = dot(w_turned[...], columns_b[...])
-    rows8 = gate_rows()
-    compact = compact_table()
+    more = edge_terms(dot(w_second[...], columns_h[...]), 0)
+    more_t = edge_terms(dot(w_turned[...], columns_b[...]), 0)
+    zero = jnp.zeros((CH, LANES), F32)
+    rows = []
+    for n in range(2):
+        for k in range(4):
+            planes = second_in[n, :, k * 256 : (k + 1) * 256]
+            if k == 0:
+                planes = planes + jnp.concatenate([more[:, 2 * n * LANES : (2 * n + 1) * LANES], zero], axis=1)
+            if k == 3:
+                planes = planes + jnp.concatenate([zero, more[:, (2 * n + 1) * LANES : (2 * n + 2) * LANES]], axis=1)
+            rows.append(planes.astype(BF))
+    packed = dot(jnp.concatenate(rows, axis=0), compact_table()).astype(BF)
+    for n in range(2):
+        for k in range(4):
+            first = (4 * n + k) * CH
+            second[n * CH : (n + 1) * CH, k * LANES : (k + 1) * LANES] = packed[first : first + CH]
+    back_pre = gate_back(through_edge[...] + more_t, pre_edge[...], gate_edge[...], gate_rows(), inside)
     placed_f[...] = jnp.zeros_like(placed_f)
     placed_s[...] = jnp.zeros_like(placed_s)
     for n in range(2):
-        for k in range(4):
-            planes = second_in[n, :, k * 256 : (k + 1) * 256]
-            zero = jnp.zeros((CH, LANES), F32)
-            if k == 0:
-                planes = planes + jnp.concatenate([edge_term(more, 0, n, 0), zero], axis=1)
-            if k == 3:
-                planes = planes + jnp.concatenate([zero, edge_term(more, 0, n, 1)], axis=1)
-            second[n * CH : (n + 1) * CH, k * 128 : (k + 1) * 128] = dot(planes.astype(BF), compact).astype(BF)
         for side in range(2):
-            grad = through_edge[n, side] + edge_term(more_t, 0, n, side)
-            back_pre = gate_back(grad, pre_edge[n, side], gate_edge[n, side], rows8, inside)
             at = (2 * n + side) * LANES
             a = 2 * side
             placed_s[a * CH : (a + 1) * CH, at : at + LANES] = own[1, n, 7 * side]
             for a in range(3):
-                at = (6 * n + 3 * side + a) * LANES
-                placed_f[a * CH : (a + 1) * CH, at : at + LANES] = back_pre
+                to = (6 * n + 3 * side + a) * LANES
+                placed_f[a * CH : (a + 1) * CH, to : to + LANES] = back_pre[:, at : at + LANES]
     pieces = []
     for n in range(2):
         mid, edge = n * MID, 2 * n * LANES
@@ -409,19 +423,22 @@
         ]
     shape = (CH, LANES)
     i, c = iota(shape, 0), iota(shape, 1)
-    lift = jnp.where(component_class(i) == out_class(c), jnp.where(i >= 20, 2.0, 1.0), 0.0)
+    lift = jnp.where(component_class(i) == out_class(c), jnp.where(i >= 20, 2.0, 1.0), 0.0).astype(BF)
     keep = one(component_class(i) == in_class(c), F32)
-    same = one(component_index(i) == component_index(iota(shape, 1) & (CH - 1)), F32)[:, 0:96]
+    same = one(component_index(i) == component_index(c & (CH - 1)), F32)
     place[...] = jnp.zeros_like(place)
     for a in range(3):
-        place[a * CH : (a + 1) * CH, a * LANES : (a + 1) * LANES] = lift
+        for half in (0, LANES):
+            place[half + a * CH : half + (a + 1) * CH, a * LANES : (a + 1) * LANES] = lift
     found = (
         raw[0] + dot_t(jnp.concatenate(pieces, axis=1), placed_f[...]),
         raw[1] + dot_t(columns_h[...], placed_s[...]),
     )
     for layer in range(2):
-        masked = (found[layer].reshape(9, CH, 96) * same).reshape(9 * CH, 96)
-        lifted[...] = dot(masked, place[...], precision=HIGHEST)
+        masked = (found[layer].reshape(9, CH, LANES) * same).reshape(9 * CH, LANES)
+        top = masked.astype(BF)
+        rest = (masked - top.astype(F32)).astype(BF)
+        lifted = dot(jnp.concatenate([top, rest], axis=1), place[...])
         for a in range(3):
             block = lifted[:, a * LANES : (a + 1) * LANES].reshape(9, CH, LANES) * keep
             first = 27 * layer + 9 * a
@@ -435,10 +452,11 @@
         for r, ref in ((1, across_y), (2, across_x), (3, across)):
             at = pl.multiple_of(mirror[n, r - 1] * CH, CH)
             staged[r, n * CH : (n + 1) * CH, :] = ref[pl.ds(at, CH), :] * turn_signs(r, (CH, 512))
+    result = turned_sum(staged, turns_table()).astype(BF)
     for k in range(4):
-        result = turned_sum(staged, k).astype(BF)
         for n in range(2):
-            out[n, :, k * 128 : (k + 1) * 128] = result[n * CH : n * CH + 30]
+            first = (2 * k + n) * CH
+            out[:, n, k * 128 : (k + 1) * 128] = result[first : first + 30]
 
 
 SMEM = pl.BlockSpec(memory_space=pltpu.SMEM)
@@ -485,23 +503,30 @@
     return lax.optimization_barrier((tuple(arrays), others))[0]
 
 
+def side_by_side(arrays, rows):
+    total = None
+    for k, x in enumerate(arrays):
+        x = jnp.pad(x, ((0, rows - x.shape[0]), (k * LANES, (len(arrays) - k) * LANES - LANES + LANES - x.shape[1])))
+        total = x if total is None else total + x
+    return lax.optimization_barrier(total)
+
+
 def on_device(features, cotangent, w_first, w_second, codes, mirror):
     plane = (CH, LANES)
-    fp, face_a, face_b, codes, mirror, w_first, w_second = call(
-        spread_kernel, 0.2, 0,
-        [
-            ((2, 8) + plane, BF), ((2,) + plane, BF), ((2,) + plane, BF),
-            *((x.shape, x.dtype) for x in (codes, mirror, w_first, w_second)),
-        ],
-        [((64, 512), BF)], features, codes, mirror, w_first, w_second,
-    )
     cot_x = mirror_x(cotangent)
     cot_y = swap_y(cotangent)
-    got = exchange(face_a, face_b)
+    fp, faces = call(
+        spread_kernel, 0.2, 0, [((2, 8) + plane, BF), ((2, 2) + plane, BF)], [((64, 512), BF)], features
+    )
+    faces = jnp.concatenate([faces, swap_y(faces)], axis=1)
+    got = exchange(faces[0], faces[1])
     part = swap_y(fp)
-    w1, w2, w2t = call(
-        weights_kernel, 0.5, 0, [((192, 288), BF), ((96, 288), BF), ((96, 288), BF)],
-        [((2, CH, LANES), F32), ((288, LANES), BF)], w_first, w_second,
+    w_first, w_second, codes, mirror = after((w_first, w_second, codes, mirror), part)
+    w1, w2, w2t, codes, mirror = call(
+        weights_kernel, 1, 0,
+        [((192, 288), BF), ((96, 288), BF), ((96, 288), BF), *((x.shape, x.dtype) for x in (codes, mirror))],
+        [((2, CH, LANES), F32), ((288, LANES), BF)],
+        side_by_side((w_first, w_second), CH), side_by_side((codes, mirror), 2),
     )
     columns, pre, gate_in, hidden_mid = call(
         first_mid_kernel, 2, 1,
@@ -509,24 +534,22 @@
         [((5, 8) + plane, BF)], codes, fp, part, w1,
     )
     *got, cot_x = after((*got, cot_x), hidden_mid)
-    faces = (*got, swap_y(got[0]), swap_y(got[1]))
-    cot_xy = swap_y(cot_x)
     (back,) = call(
-        back_kernel, 1.5, 1, [((2, 8) + plane, BF)], [((4, 64, 512), BF)], mirror, cotangent, cot_y, cot_x, cot_xy
+        back_kernel, 0.8, 1, [((2, 8) + plane, BF)], [((4, 64, 512), BF)], mirror, cotangent, cot_y, cot_x, swap_y(cot_x)
     )
     columns_e, pre_e, gate_e, both, face_a, face_b = call(
         first_edge_kernel, 1.2, 1,
         [
-            ((288, 4 * LANES), BF), ((2, 2) + plane, F32), ((2, 2) + plane, F32), ((2, 2, 8) + plane, BF),
+            ((288, 4 * LANES), BF), ((CH, 4 * LANES), F32), ((CH, 4 * LANES), F32), ((2, 2, 8) + plane, BF),
             ((2, 2) + plane, BF), ((2, 2) + plane, BF),
         ],
-        [((9,) + plane, BF)] * 2, codes, fp, part, *faces, pre, gate_in, hidden_mid, back, w1,
+        [((9,) + plane, BF)] * 2, codes, fp, part, *got, pre, gate_in, hidden_mid, back, w1,
     )
     got = exchange(face_a, face_b)
     part = swap_y(both)
     second_part, through_e, raw = call(
-        second_mid_kernel, 3.5, 1, [((2, CH, MID), F32), ((2, 2) + plane, F32), ((2, 288, 96), F32)],
-        [((2, 5, 8) + plane, BF), ((288, 2 * MID), BF), ((288, 2 * MID), BF), ((96, 2 * MID), BF), ((96, 2 * MID), BF)],
+        second_mid_kernel, 3.5, 1, [((2, CH, MID), F32), ((CH, 4 * LANES), F32), ((2, 288, LANES), F32)],
+        [((2, 5, 8) + plane, BF), ((288, 2 * MID), BF), ((288, 2 * MID), BF), ((128, 2 * MID), BF), ((128, 2 * MID), BF)],
         codes, both, part, pre, gate_in, columns, w2, w2t,
     )
     got = after(got, raw)
@@ -535,7 +558,7 @@
     second, grads = call(
         functools.partial(second_edge_kernel, 1.0 / n_bricks), 2.8, 1, [((64, 512), BF), ((56, LANES), F32)],
         [((2, 9) + plane, BF)] * 2 + [((288, 4 * LANES), BF)] * 2
-        + [((96, 12 * LANES), BF), ((96, 4 * LANES), BF), ((96, 3 * LANES), F32), ((288, 3 * LANES), F32)],
+        + [((128, 12 * LANES), BF), ((128, 4 * LANES), BF), ((256, 3 * LANES), BF)],
         codes, both, part, *faces, pre_e, gate_e, second_part, through_e, columns, columns_e, raw, w2, w2t,
     )
     total = grads + swap_y(grads)
@@ -544,8 +567,9 @@
     second_x = mirror_x(second)
     second_xy = swap_y(second_x)
     (denoised,) = call(
-        turn_kernel, 0.9, 1, [((2, 30, 512), BF)], [((4, 64, 512), BF)], mirror, second, second_y, second_x, second_xy
-    )
+        turn_kernel, 0.9, 1, [((30, 2, 512), BF)], [((4, 64, 512), BF)], mirror, second, second_y, second_x, second_xy
+    )
+    denoised = denoised.transpose(1, 0, 2)
     n = lax.axis_size("xp")
     bit = 1
     while bit < n:

time: 49.8 us -> 48.4 us (0.972)
  waiting for transfers between devices: 5.92 us -> 10.3 us
  local copies, waits for them, and re-layouts: 5.73 us -> 2.31 us
  starting transfers between devices: 24.8 us -> 21.6 us
  other arithmetic: 0.02 us -> 1.44 us
  Pallas kernels: 12.2 us -> 11.7 us
    unnamed x11 -> x3, local copies, waits for them, and re-layouts: 5.11 us -> 1.68 us
    ppermute x3, waiting for transfers between devices: 3.63 us -> 6.3 us  [on_device(): total = total + lax.ppermute(total, 'xp', [(i, i ^ bit) for i in range(n)])]
    ppermute x4, starting transfers between devices: 6.34 us -> 4.06 us  [pair_swap(): return lax.ppermute(x, 'xp', pairs)]
    ppermute x11 -> x10, waiting for transfers between devices: 2.12 us -> 3.95 us  [swap_y(): return lax.ppermute(x, 'yp', [(i, n - 1 - i) for i in range(n)])]
    add x0 -> x2, other arithmetic: none -> 1.42 us  [side_by_side(): total = x if total is None else total + x]
    ppermute x2, starting transfers between devices: 7.48 us -> 6.8 us  [mirror_x(): return lax.ppermute(x, 'xp', [(i, n - 1 - i) for i in range(n)])]
    ppermute x11 -> x10, starting transfers between devices: 3.45 us -> 2.88 us  [swap_y(): return lax.ppermute(x, 'yp', [(i, n - 1 - i) for i in range(n)])]
    pallas_call x8, Pallas kernels: 12.2 us -> 11.7 us  [call(): pl.pallas_call(kernel, out_shape=tuple((jax.ShapeDtypeStruct(s, t) for s,...]
  transfers between devices with their start and end apart: 20 -> 19, of which waited for: 7 -> 9; matrix products, arithmetic and copies ran while one was open for 3% -> 6% of each run, Pallas kernels for 15% -> 12%
where the time goes in v3:
time: 48.4 us; the launch traced here: 48.1 us
  starting transfers between devices  21.6 us (45%)
  Pallas kernels  11.7 us (24%)
  waiting for transfers between devices  10.3 us (21%)
  local copies, waits for them, and re-layouts  2.31 us (5%)
  other arithmetic  1.44 us (3%)
  between operations  0.78 us (2%)
    pallas_call x8, Pallas kernels, call(): pl.pallas_call(kernel, out_shape=tuple((jax.ShapeDtypeStruct(s, t) for s,...  11.7 us
    ppermute x3, starting transfers between devices, on_device(): total = total + lax.ppermute(total, 'xp', [(i, i ^ bit) for i in range(n)])  7.89 us
    ppermute x2, starting transfers between devices, mirror_x(): return lax.ppermute(x, 'xp', [(i, n - 1 - i) for i in range(n)])  6.8 us
    ppermute x3, waiting for transfers between devices, on_device(): total = total + lax.ppermute(total, 'xp', [(i, i ^ bit) for i in range(n)])  6.3 us
    ppermute x4, starting transfers between devices, pair_swap(): return lax.ppermute(x, 'xp', pairs)  4.06 us
    ppermute x10, waiting for transfers between devices, swap_y(): return lax.ppermute(x, 'yp', [(i, n - 1 - i) for i in range(n)])  3.95 us
    ppermute x10, starting transfers between devices, swap_y(): return lax.ppermute(x, 'yp', [(i, n - 1 - i) for i in range(n)])  2.88 us
    unnamed x3, local copies, waits for them, and re-layouts  1.68 us
  transfers between devices with their start and end apart: 19, of which 9 were waited for; matrix products, arithmetic and copies ran while one was open for 6% of the time, Pallas kernels for 12%

profile of v3, /device:TPU:0, one launch (start us, length us, event | category | flops | bytes accessed | tf_op | source)
XLA Modules:
  0.0 48.1 jit_solution(7516992821196179777)
XLA Ops:
  0.6 0.8 %copy.10.own = bf16[2,30,512]{2,1,0:T(8,128)(2,1)S(1)} copy(bf16[2,30,512]{2,0,1:T(2,128)(2,1)} %param.7) | data formatting | bytes 122880 | tf_op args[1]
  1.5 0.5 %collective-permute-start.5 = (bf16[2,30,512]{2,1,0:T(8,128)(2,1)S(1)}, bf16[2,30,512]{2,1,0:T(8,128)(2,1)S(1)}, u32[]{:S(2)}, u32[]{:S(2)}) collective-permute-start(bf16[2,30,512]{2,1,0:T(8,128)(2,1)S(1)} %copy.10.own), channel_id=1, source_target_pairs={{0,1},{1,0},{2,3},{3,2},{4,5},{5,4},{6,7},{7,6},{8,9},{9,8},{10,11... | collective-permute-start | bytes 184328 | tf_op jit(solution)/shard_map/ppermute | solution.py:480
  2.0 5.6 %collective-permute-start.4 = (bf16[2,30,512]{2,1,0:T(8,128)(2,1)S(1)}, bf16[2,30,512]{2,1,0:T(8,128)(2,1)S(1)}, u32[]{:S(2)}, u32[]{:S(2)}) collective-permute-start(bf16[2,30,512]{2,1,0:T(8,128)(2,1)S(1)} %copy.10.own), channel_id=1, source_target_pairs={{0,14},{2,12},{4,10},{6,8},{8,6},{10,4},{12,2},{14,0},{1,15},{3,13... | collective-permute-start | bytes 184328 | tf_op jit(solution)/shard_map/ppermute | solution.py:485
  7.6 0.8 %copy.9.features = bf16[2,30,512]{2,1,0:T(8,128)(2,1)S(1)} copy(bf16[2,30,512]{2,0,1:T(2,128)(2,1)} %param.6) | data formatting | bytes 122880 | tf_op args[0]
  9.2 0.7 %collective-permute-done.1 = bf16[2,2,32,128]{3,2,1,0:T(8,128)(2,1)S(1)} collective-permute-done((bf16[2,2,32,128]{3,2,1,0:T(8,128)(2,1)S(1)}, bf16[2,2,32,128]{3,2,1,0:T(8,128)(2,1)S(1)}, u32[]{:S(2)}, u32[]{:S(2)}) %collective-permute-start.1) | collective-permute-done | bytes 32800 | tf_op jit(solution)/shard_map/ppermute | solution.py:480
  10.0 0.7 %collective-permute-start.3 = (bf16[4,32,128]{2,1,0:T(8,128)(2,1)S(1)}, bf16[4,32,128]{2,1,0:T(8,128)(2,1)S(1)}, u32[]{:S(2)}, u32[]{:S(2)}) collective-permute-start(bf16[4,32,128]{2,1,0:T(8,128)(2,1)S(1)} %get-tuple-element.67), channel_id=1, source_target_pairs={{2,4},{4,2},{6,8},{8,6},{10,12},{12,10},{3,5},{5,3},{7,9},{9,7},{1... | collective-permute-start | bytes 98312 | tf_op jit(solution)/shard_map/ppermute | solution.py:493
  10.6 2.3 %collective-permute-start.2 = (bf16[4,32,128]{2,1,0:T(8,128)(2,1)S(1)}, bf16[4,32,128]{2,1,0:T(8,128)(2,1)S(1)}, u32[]{:S(2)}, u32[]{:S(2)}) collective-permute-start(bf16[4,32,128]{2,1,0:T(8,128)(2,1)S(1)} %get-tuple-element.68), channel_id=1, source_target_pairs={{0,2},{2,0},{4,6},{6,4},{8,10},{10,8},{12,14},{14,12},{1,3},{3,1},... | collective-permute-start | bytes 98312 | tf_op jit(solution)/shard_map/ppermute | solution.py:493
  12.9 0.7 %pad_add_fusion.packed = bf16[32,256]{1,0:T(8,128)(2,1)S(1)} fusion(bf16[27,84]{1,0:T(8,128)(2,1)} %param.9, bf16[27,84]{1,0:T(8,128)(2,1)} %param.8), kind=kLoop, calls=%fused_computation.2 | loop fusion | flops 32768 | bytes 25456 | tf_op jit(solution)/shard_map/add | solution.py:510
  13.7 0.7 %pad_add_fusion.1.small = s32[2,256]{1,0:T(2,128)S(1)} fusion(s32[2,3]{1,0:T(2,128)} %param.11, s32[2,27]{1,0:T(2,128)} %param.10), kind=kLoop, calls=%fused_computation.5 | loop fusion | flops 512 | bytes 2288 | tf_op jit(solution)/shard_map/add | solution.py:510
  14.4 0.4 shard_map.86
  14.8 1.9 %shard_map.87 = (bf16[288,2048]{1,0:T(8,128)(2,1)S(1)}, f32[2,32,1024]{2,1,0:T(8,128)S(1)}, f32[2,32,1024]{2,1,0:T(8,128)S(1)}, bf16[2,6,32,128]{3,2,1,0:T(8,128)(2,1)S(1)}) custom-call(s32[2,27]{1,0:T(2,128)S(1)} %get-tuple-element.41.codes, bf16[2,8,32,128]{3,2,1,0:T(8,128)(2,1)S(1)} %get-tuple-element.35.own, ...), custom_call_target="tpu_custom_call" | custom-call | bytes 6000000 | tf_op jit(solution)/shard_map/pallas_call | solution.py:467
  16.8 1.2 %collective-permute-done.6.across = bf16[2,30,512]{2,1,0:T(8,128)(2,1)S(1)} collective-permute-done((bf16[2,30,512]{2,1,0:T(8,128)(2,1)S(1)}, bf16[2,30,512]{2,1,0:T(8,128)(2,1)S(1)}, u32[]{:S(2)}, u32[]{:S(2)}) %collective-permute-start.6) | collective-permute-done | bytes 61472 | tf_op jit(solution)/shard_map/ppermute | solution.py:480
  18.0 0.8 %shard_map.88.back = bf16[2,8,32,128]{3,2,1,0:T(8,128)(2,1)S(1)} custom-call(s32[2,3]{1,0:T(2,128)S(1)} %get-tuple-element.40.mirror, bf16[2,30,512]{2,1,0:T(8,128)(2,1)S(1)} %copy.10.own, bf16[2,30,512]{2,1,0:T(8,128)(2,1)S(1)} %collective-permute-done.5.across_y, bf16[2,30,512]{2,1,0:T(8,128)(2,1)S(1)} %collective-permute-done.4.across_x, ...), custom_call_target="tpu_custom_call" | custom-call | bytes 2400000 | tf_op jit(solution)/shard_map/pallas_call | solution.py:467
  18.8 1.2 %shard_map.89 = (bf16[288,512]{1,0:T(8,128)(2,1)S(1)}, f32[32,512]{1,0:T(8,128)S(1)}, f32[32,512]{1,0:T(8,128)S(1)}, bf16[2,2,8,32,128]{4,3,2,1,0:T(8,128)(2,1)S...) custom-call(s32[2,27]{1,0:T(2,128)S(1)} %get-tuple-element.41.codes, ...), custom_call_target="tpu_custom_call" | custom-call | bytes 3600000 | tf_op jit(solution)/shard_map/pallas_call | solution.py:467
  20.3 0.4 collective-permute-start.8
  20.7 0.7 %collective-permute-start.9 = (bf16[2,2,32,128]{3,2,1,0:T(8,128)(2,1)S(1)}, bf16[2,2,32,128]{3,2,1,0:T(8,128)(2,1)S(1)}, u32[]{:S(2)}, u32[]{:S(2)}) collective-permute-start(bf16[2,2,32,128]{3,2,1,0:T(8,128)(2,1)S(1)} %get-tuple-element.52), channel_id=1, source_target_pairs={{2,4},{4,2},{6,8},{8,6},{10,12},{12,10},{3,5},{5,3},{7,9},{9,7},{1... | collective-permute-start | bytes 98312 | tf_op jit(solution)/shard_map/ppermute | solution.py:493
  21.6 3.5 %shard_map.90 = (f32[2,32,1024]{2,1,0:T(8,128)S(1)}, f32[32,512]{1,0:T(8,128)S(1)}, f32[2,288,128]{2,1,0:T(8,128)S(1)}) custom-call(s32[2,27]{1,0:T(2,128)S(1)} %get-tuple-element.41.codes, bf16[2,2,8,32,128]{4,3,2,1,0:T(8,128)(2,1)S(1)} %get-tuple-element.50.own, bf16[2,2,8,32,128]{4,3,2,1,0:T(8,128)(2,1)S(1)} %collective-permute-done.7.part, ...), custom_call_target="tpu_custom_call" | custom-call | bytes 10500000 | tf_op jit(solution)/shard_map/pallas_call | solution.py:467
  25.3 0.4 collective-permute-start.11
  25.7 0.7 %collective-permute-done.10.far_a = bf16[2,2,32,128]{3,2,1,0:T(8,128)(2,1)S(1)} collective-permute-done((bf16[2,2,32,128]{3,2,1,0:T(8,128)(2,1)S(1)}, bf16[2,2,32,128]{3,2,1,0:T(8,128)(2,1)S(1)}, u32[]{:S(2)}, u32[]{:S(2)}) %collective-permute-start.10) | collective-permute-done | bytes 32800 | tf_op jit(solution)/shard_map/ppermute | solution.py:480
  26.6 2.2 %shard_map.91 = (bf16[64,512]{1,0:T(8,128)(2,1)S(1)}, f32[56,128]{1,0:T(8,128)S(1)}) custom-call(s32[2,27]{1,0:T(2,128)S(1)} %get-tuple-element.41.codes, bf16[2,2,8,32,128]{4,3,2,1,0:T(8,128)(2,1)S(1)} %get-tuple-element.50.own, bf16[2,2,8,32,128]{4,3,2,1,0:T(8,128)(2,1)S(1)} %collective-permute-done.7.part, ...), custom_call_target="tpu_custom_call" | custom-call | bytes 8400000 | tf_op jit(solution)/shard_map/pallas_call | solution.py:467
  28.8 0.4 collective-permute-start.12
  29.2 0.9 %collective-permute-done.12 = f32[56,128]{1,0:T(8,128)S(1)} collective-permute-done((f32[56,128]{1,0:T(8,128)S(1)}, f32[56,128]{1,0:T(8,128)S(1)}, u32[]{:S(2)}, u32[]{:S(2)}) %collective-permute-start.12) | collective-permute-done | bytes 28704 | tf_op jit(solution)/shard_map/ppermute | solution.py:480
  30.1 5.0 %collective-permute-start.16 = (f32[56,128]{1,0:T(8,128)S(1)}, f32[56,128]{1,0:T(8,128)S(1)}, u32[]{:S(2)}, u32[]{:S(2)}) collective-permute-start(f32[56,128]{1,0:T(8,128)S(1)} %add.28), channel_id=1, source_target_pairs={{0,2},{2,0},{4,6},{6,4},{8,10},{10,8},{12,14},{14,12},{1,3},{3,1},... | collective-permute-start | bytes 86024 | tf_op jit(solution)/shard_map/ppermute | solution.py:576
  35.1 1.2 %collective-permute-start.14 = (bf16[64,512]{1,0:T(8,128)(2,1)S(1)}, bf16[64,512]{1,0:T(8,128)(2,1)S(1)}, u32[]{:S(2)}, u32[]{:S(2)}) collective-permute-start(bf16[64,512]{1,0:T(8,128)(2,1)S(1)} %get-tuple-element.66.own), channel_id=1, source_target_pairs={{0,14},{2,12},{4,10},{6,8},{8,6},{10,4},{12,2},{14,0},{1,15},{3,13... | collective-permute-start | bytes 196616 | tf_op jit(solution)/shard_map/ppermute | solution.py:485
  36.2 0.7 %collective-permute-done.16 = f32[56,128]{1,0:T(8,128)S(1)} collective-permute-done((f32[56,128]{1,0:T(8,128)S(1)}, f32[56,128]{1,0:T(8,128)S(1)}, u32[]{:S(2)}, u32[]{:S(2)}) %collective-permute-start.16) | collective-permute-done | bytes 28704 | tf_op jit(solution)/shard_map/ppermute | solution.py:576
  36.9 1.8 %collective-permute-start.17 = (f32[56,128]{1,0:T(8,128)S(1)}, f32[56,128]{1,0:T(8,128)S(1)}, u32[]{:S(2)}, u32[]{:S(2)}) collective-permute-start(f32[56,128]{1,0:T(8,128)S(1)} %add.29), channel_id=1, source_target_pairs={{0,4},{2,6},{4,0},{6,2},{8,12},{10,14},{12,8},{14,10},{1,5},{3,7},... | collective-permute-start | bytes 86024 | tf_op jit(solution)/shard_map/ppermute | solution.py:576
  38.7 2.5 %collective-permute-done.17 = f32[56,128]{1,0:T(8,128)S(1)} collective-permute-done((f32[56,128]{1,0:T(8,128)S(1)}, f32[56,128]{1,0:T(8,128)S(1)}, u32[]{:S(2)}, u32[]{:S(2)}) %collective-permute-start.17) | collective-permute-done | bytes 28704 | tf_op jit(solution)/shard_map/ppermute | solution.py:576
  41.2 1.1 %collective-permute-start.18 = (f32[56,128]{1,0:T(8,128)S(1)}, f32[56,128]{1,0:T(8,128)S(1)}, u32[]{:S(2)}, u32[]{:S(2)}) collective-permute-start(f32[56,128]{1,0:T(8,128)S(1)} %add.30), channel_id=1, source_target_pairs={{0,8},{2,10},{4,12},{6,14},{8,0},{10,2},{12,4},{14,6},{1,9},{3,11}... | collective-permute-start | bytes 86024 | tf_op jit(solution)/shard_map/ppermute | solution.py:576
  42.3 0.5 %collective-permute-start.15 = (bf16[64,512]{1,0:T(8,128)(2,1)S(1)}, bf16[64,512]{1,0:T(8,128)(2,1)S(1)}, u32[]{:S(2)}, u32[]{:S(2)}) collective-permute-start(bf16[64,512]{1,0:T(8,128)(2,1)S(1)} %collective-permute-done.14.across_x), channel_id=1, source_target_pairs={{0,1},{1,0},{2,3},{3,2},{4,5},{5,4},{6,7},{7,6},{8,9},{9,8},{10,11... | collective-permute-start | bytes 196616 | tf_op jit(solution)/shard_map/ppermute | solution.py:480
  42.8 3.1 %collective-permute-done.18 = f32[56,128]{1,0:T(8,128)S(1)} collective-permute-done((f32[56,128]{1,0:T(8,128)S(1)}, f32[56,128]{1,0:T(8,128)S(1)}, u32[]{:S(2)}, u32[]{:S(2)}) %collective-permute-start.18) | collective-permute-done | bytes 28704 | tf_op jit(solution)/shard_map/ppermute | solution.py:576
  46.0 0.6 %fusion = (f32[27,84]{1,0:T(8,128)}, f32[27,84]{1,0:T(8,128)}) fusion(f32[56,128]{1,0:T(8,128)S(1)} %add.31), kind=kLoop, calls=%fused_computation.6 | loop fusion | bytes 36288 | tf_op jit(solution)/shard_map/slice | solution.py:578
  46.6 1.5 %shard_map.92 = bf16[30,2,512]{2,1,0:T(2,128)(2,1)} custom-call(s32[2,3]{1,0:T(2,128)S(1)} %get-tuple-element.40.mirror, bf16[64,512]{1,0:T(8,128)(2,1)S(1)} %get-tuple-element.66.own, bf16[64,512]{1,0:T(8,128)(2,1)S(1)} %collective-permute-done.13.across_y, bf16[64,512]{1,0:T(8,128)(2,1)S(1)} %collective-permute-done.14.across_x, ...), custom_call_target="tpu_custom_call" | custom-call | bytes 2700000 | tf_op jit(solution)/shard_map/pallas_call | solution.py:467
  (26 shorter events, 1.8 us)
Async XLA Ops:
  1.5 15.3 %collective-permute-start.5 = (bf16[2,30,512]{2,1,0:T(8,128)(2,1)S(1)}, bf16[2,30,512]{2,1,0:T(8,128)(2,1)S(1)}, u32[]{:S(2)}, u32[]{:S(2)}) collective-permute-start(bf16[2,30,512]{2,1,0:T(8,128)(2,1)S(1)} %copy.10.own), channel_id=1, source_target_pairs={{0,1},{1,0},{2,3},{3,2},{4,5},{5,4},{6,7},{7,6},{8,9},{9,8},{10,11... | collective-permute-start | bytes 184328 | tf_op jit(solution)/shard_map/ppermute | solution.py:480
  2.0 14.7 %collective-permute-start.4 = (bf16[2,30,512]{2,1,0:T(8,128)(2,1)S(1)}, bf16[2,30,512]{2,1,0:T(8,128)(2,1)S(1)}, u32[]{:S(2)}, u32[]{:S(2)}) collective-permute-start(bf16[2,30,512]{2,1,0:T(8,128)(2,1)S(1)} %copy.10.own), channel_id=1, source_target_pairs={{0,14},{2,12},{4,10},{6,8},{8,6},{10,4},{12,2},{14,0},{1,15},{3,13... | collective-permute-start | bytes 184328 | tf_op jit(solution)/shard_map/ppermute | solution.py:485
  8.7 1.3 %collective-permute-start.1 = (bf16[2,2,32,128]{3,2,1,0:T(8,128)(2,1)S(1)}, bf16[2,2,32,128]{3,2,1,0:T(8,128)(2,1)S(1)}, u32[]{:S(2)}, u32[]{:S(2)}) collective-permute-start(bf16[2,2,32,128]{3,2,1,0:T(8,128)(2,1)S(1)} %get-tuple-element.42), channel_id=1, source_target_pairs={{0,1},{1,0},{2,3},{3,2},{4,5},{5,4},{6,7},{7,6},{8,9},{9,8},{10,11... | collective-permute-start | bytes 98312 | tf_op jit(solution)/shard_map/ppermute | solution.py:480
  8.9 4.1 %collective-permute-start = (bf16[2,8,32,128]{3,2,1,0:T(8,128)(2,1)S(1)}, bf16[2,8,32,128]{3,2,1,0:T(8,128)(2,1)S(1)}, u32[]{:S(2)}, u32[]{:S(2)}) collective-permute-start(bf16[2,8,32,128]{3,2,1,0:T(8,128)(2,1)S(1)} %get-tuple-element.35.own), channel_id=1, source_target_pairs={{0,1},{1,0},{2,3},{3,2},{4,5},{5,4},{6,7},{7,6},{8,9},{9,8},{10,11... | collective-permute-start | bytes 393224 | tf_op jit(solution)/shard_map/ppermute | solution.py:480
  10.0 6.8 %collective-permute-start.3 = (bf16[4,32,128]{2,1,0:T(8,128)(2,1)S(1)}, bf16[4,32,128]{2,1,0:T(8,128)(2,1)S(1)}, u32[]{:S(2)}, u32[]{:S(2)}) collective-permute-start(bf16[4,32,128]{2,1,0:T(8,128)(2,1)S(1)} %get-tuple-element.67), channel_id=1, source_target_pairs={{2,4},{4,2},{6,8},{8,6},{10,12},{12,10},{3,5},{5,3},{7,9},{9,7},{1... | collective-permute-start | bytes 98312 | tf_op jit(solution)/shard_map/ppermute | solution.py:493
  10.6 6.1 %collective-permute-start.2 = (bf16[4,32,128]{2,1,0:T(8,128)(2,1)S(1)}, bf16[4,32,128]{2,1,0:T(8,128)(2,1)S(1)}, u32[]{:S(2)}, u32[]{:S(2)}) collective-permute-start(bf16[4,32,128]{2,1,0:T(8,128)(2,1)S(1)} %get-tuple-element.68), channel_id=1, source_target_pairs={{0,2},{2,0},{4,6},{6,4},{8,10},{10,8},{12,14},{14,12},{1,3},{3,1},... | collective-permute-start | bytes 98312 | tf_op jit(solution)/shard_map/ppermute | solution.py:493
  16.7 1.3 %collective-permute-start.6 = (bf16[2,30,512]{2,1,0:T(8,128)(2,1)S(1)}, bf16[2,30,512]{2,1,0:T(8,128)(2,1)S(1)}, u32[]{:S(2)}, u32[]{:S(2)}) collective-permute-start(bf16[2,30,512]{2,1,0:T(8,128)(2,1)S(1)} %collective-permute-done.4.across_x), channel_id=1, source_target_pairs={{0,1},{1,0},{2,3},{3,2},{4,5},{5,4},{6,7},{7,6},{8,9},{9,8},{10,11... | collective-permute-start | bytes 184328 | tf_op jit(solution)/shard_map/ppermute | solution.py:480
  20.0 1.6 %collective-permute-start.7 = (bf16[2,2,8,32,128]{4,3,2,1,0:T(8,128)(2,1)S(1)}, bf16[2,2,8,32,128]{4,3,2,1,0:T(8,128)(2,1)S(1)}, u32[]{:S(2)}, u32[]{:S(2)}) collective-permute-start(bf16[2,2,8,32,128]{4,3,2,1,0:T(8,128)(2,1)S(1)} %get-tuple-element.50.own), channel_id=1, source_target_pairs={{0,1},{1,0},{2,3},{3,2},{4,5},{5,4},{6,7},{7,6},{8,9},{9,8},{10,11... | collective-permute-start | bytes 786440 | tf_op jit(solution)/shard_map/ppermute | solution.py:480
  20.3 4.8 %collective-permute-start.8 = (bf16[2,2,32,128]{3,2,1,0:T(8,128)(2,1)S(1)}, bf16[2,2,32,128]{3,2,1,0:T(8,128)(2,1)S(1)}, u32[]{:S(2)}, u32[]{:S(2)}) collective-permute-start(bf16[2,2,32,128]{3,2,1,0:T(8,128)(2,1)S(1)} %get-tuple-element.51), channel_id=1, source_target_pairs={{0,2},{2,0},{4,6},{6,4},{8,10},{10,8},{12,14},{14,12},{1,3},{3,1},... | collective-permute-start | bytes 98312 | tf_op jit(solution)/shard_map/ppermute | solution.py:493
  20.7 4.4 %collective-permute-start.9 = (bf16[2,2,32,128]{3,2,1,0:T(8,128)(2,1)S(1)}, bf16[2,2,32,128]{3,2,1,0:T(8,128)(2,1)S(1)}, u32[]{:S(2)}, u32[]{:S(2)}) collective-permute-start(bf16[2,2,32,128]{3,2,1,0:T(8,128)(2,1)S(1)} %get-tuple-element.52), channel_id=1, source_target_pairs={{2,4},{4,2},{6,8},{8,6},{10,12},{12,10},{3,5},{5,3},{7,9},{9,7},{1... | collective-permute-start | bytes 98312 | tf_op jit(solution)/shard_map/ppermute | solution.py:493
  25.1 1.3 %collective-permute-start.10 = (bf16[2,2,32,128]{3,2,1,0:T(8,128)(2,1)S(1)}, bf16[2,2,32,128]{3,2,1,0:T(8,128)(2,1)S(1)}, u32[]{:S(2)}, u32[]{:S(2)}) collective-permute-start(bf16[2,2,32,128]{3,2,1,0:T(8,128)(2,1)S(1)} %collective-permute-done.8.got_a), channel_id=1, source_target_pairs={{0,1},{1,0},{2,3},{3,2},{4,5},{5,4},{6,7},{7,6},{8,9},{9,8},{10,11... | collective-permute-start | bytes 98312 | tf_op jit(solution)/shard_map/ppermute | solution.py:480
  25.3 1.2 %collective-permute-start.11 = (bf16[2,2,32,128]{3,2,1,0:T(8,128)(2,1)S(1)}, bf16[2,2,32,128]{3,2,1,0:T(8,128)(2,1)S(1)}, u32[]{:S(2)}, u32[]{:S(2)}) collective-permute-start(bf16[2,2,32,128]{3,2,1,0:T(8,128)(2,1)S(1)} %collective-permute-done.9.got_b), channel_id=1, source_target_pairs={{0,1},{1,0},{2,3},{3,2},{4,5},{5,4},{6,7},{7,6},{8,9},{9,8},{10,11... | collective-permute-start | bytes 98312 | tf_op jit(solution)/shard_map/ppermute | solution.py:480
  28.8 1.3 %collective-permute-start.12 = (f32[56,128]{1,0:T(8,128)S(1)}, f32[56,128]{1,0:T(8,128)S(1)}, u32[]{:S(2)}, u32[]{:S(2)}) collective-permute-start(f32[56,128]{1,0:T(8,128)S(1)} %get-tuple-element.65), channel_id=1, source_target_pairs={{0,1},{1,0},{2,3},{3,2},{4,5},{5,4},{6,7},{7,6},{8,9},{9,8},{10,11... | collective-permute-start | bytes 86024 | tf_op jit(solution)/shard_map/ppermute | solution.py:480
  30.1 6.8 %collective-permute-start.16 = (f32[56,128]{1,0:T(8,128)S(1)}, f32[56,128]{1,0:T(8,128)S(1)}, u32[]{:S(2)}, u32[]{:S(2)}) collective-permute-start(f32[56,128]{1,0:T(8,128)S(1)} %add.28), channel_id=1, source_target_pairs={{0,2},{2,0},{4,6},{6,4},{8,10},{10,8},{12,14},{14,12},{1,3},{3,1},... | collective-permute-start | bytes 86024 | tf_op jit(solution)/shard_map/ppermute | solution.py:576
  35.1 7.3 %collective-permute-start.14 = (bf16[64,512]{1,0:T(8,128)(2,1)S(1)}, bf16[64,512]{1,0:T(8,128)(2,1)S(1)}, u32[]{:S(2)}, u32[]{:S(2)}) collective-permute-start(bf16[64,512]{1,0:T(8,128)(2,1)S(1)} %get-tuple-element.66.own), channel_id=1, source_target_pairs={{0,14},{2,12},{4,10},{6,8},{8,6},{10,4},{12,2},{14,0},{1,15},{3,13... | collective-permute-start | bytes 196616 | tf_op jit(solution)/shard_map/ppermute | solution.py:485
  36.9 4.3 %collective-permute-start.17 = (f32[56,128]{1,0:T(8,128)S(1)}, f32[56,128]{1,0:T(8,128)S(1)}, u32[]{:S(2)}, u32[]{:S(2)}) collective-permute-start(f32[56,128]{1,0:T(8,128)S(1)} %add.29), channel_id=1, source_target_pairs={{0,4},{2,6},{4,0},{6,2},{8,12},{10,14},{12,8},{14,10},{1,5},{3,7},... | collective-permute-start | bytes 86024 | tf_op jit(solution)/shard_map/ppermute | solution.py:576
  41.2 4.8 %collective-permute-start.18 = (f32[56,128]{1,0:T(8,128)S(1)}, f32[56,128]{1,0:T(8,128)S(1)}, u32[]{:S(2)}, u32[]{:S(2)}) collective-permute-start(f32[56,128]{1,0:T(8,128)S(1)} %add.30), channel_id=1, source_target_pairs={{0,8},{2,10},{4,12},{6,14},{8,0},{10,2},{12,4},{14,6},{1,9},{3,11}... | collective-permute-start | bytes 86024 | tf_op jit(solution)/shard_map/ppermute | solution.py:576
  42.3 4.3 %collective-permute-start.13 = (bf16[64,512]{1,0:T(8,128)(2,1)S(1)}, bf16[64,512]{1,0:T(8,128)(2,1)S(1)}, u32[]{:S(2)}, u32[]{:S(2)}) collective-permute-start(bf16[64,512]{1,0:T(8,128)(2,1)S(1)} %get-tuple-element.66.own), channel_id=1, source_target_pairs={{0,1},{1,0},{2,3},{3,2},{4,5},{5,4},{6,7},{7,6},{8,9},{9,8},{10,11... | collective-permute-start | bytes 196616 | tf_op jit(solution)/shard_map/ppermute | solution.py:480
  42.3 4.3 %collective-permute-start.15 = (bf16[64,512]{1,0:T(8,128)(2,1)S(1)}, bf16[64,512]{1,0:T(8,128)(2,1)S(1)}, u32[]{:S(2)}, u32[]{:S(2)}) collective-permute-start(bf16[64,512]{1,0:T(8,128)(2,1)S(1)} %collective-permute-done.14.across_x), channel_id=1, source_target_pairs={{0,1},{1,0},{2,3},{3,2},{4,5},{5,4},{6,7},{7,6},{8,9},{9,8},{10,11... | collective-permute-start | bytes 196616 | tf_op jit(solution)/shard_map/ppermute | solution.py:480

commit v4 on v3

--- a/solution.py
+++ b/solution.py
@@ -204,7 +204,7 @@
     face_b[index] = jnp.where(odd, plane_high, plane_low)
 
 
-def spread_kernel(features, fp, faces, staged):
+def spread_kernel(features, fp, staged):
     staged[...] = jnp.zeros_like(staged)
     for n in range(2):
         staged[n * CH : n * CH + 30, :] = features[n]
@@ -214,7 +214,6 @@
         for x in range(8):
             first = (x >> 1) * 2 * CH + n * CH
             fp[n, x] = planes[first : first + CH, (x & 1) * LANES : (x & 1) * LANES + LANES]
-        write_faces(faces.at[0], faces.at[1], n, fp[n, 0], fp[n, 7])
 
 
 def weights_kernel(packed, small, one_out, two_out, turned_out, codes_out, mirror_out, padded, left):
@@ -280,14 +279,15 @@
     return dot(jnp.concatenate(rows, axis=0), table) * 0.25
 
 
-def back_kernel(mirror, own, across_y, across_x, across, back, staged):
+def back_kernel(mirror, own, across_y, crossed, back, staged):
     zero2 = jnp.zeros((2, 512), BF)
     for n in range(2):
         for r in range(4):
             if r == 0:
                 value = own[n]
             else:
-                value = (across_y, across_x, across)[r - 1][mirror[n, r - 1]] * turn_signs(r, (30, 512))
+                slot = mirror[n, r - 1]
+                value = (across_y[slot] if r == 1 else crossed[2 * (r - 2) + slot]) * turn_signs(r, (30, 512))
             staged[r, n * CH : n * CH + 30, :] = value
             staged[r, n * CH + 30 : (n + 1) * CH, :] = zero2
     planes = turned_sum(staged, turns_spread_table()).astype(BF)
@@ -513,14 +513,13 @@
 
 def on_device(features, cotangent, w_first, w_second, codes, mirror):
     plane = (CH, LANES)
-    cot_x = mirror_x(cotangent)
     cot_y = swap_y(cotangent)
-    fp, faces = call(
-        spread_kernel, 0.2, 0, [((2, 8) + plane, BF), ((2, 2) + plane, BF)], [((64, 512), BF)], features
-    )
-    faces = jnp.concatenate([faces, swap_y(faces)], axis=1)
-    got = exchange(faces[0], faces[1])
+    crossed = mirror_x(jnp.concatenate([cotangent, cot_y], axis=0))
+    (fp,) = call(spread_kernel, 0.2, 0, [((2, 8) + plane, BF)], [((64, 512), BF)], features)
     part = swap_y(fp)
+    low, high = (jnp.concatenate([fp[:, x], part[:, x]], axis=0) for x in (0, 7))
+    odd = is_odd()
+    got = exchange(jnp.where(odd, low, high), jnp.where(odd, high, low))
     w_first, w_second, codes, mirror = after((w_first, w_second, codes, mirror), part)
     w1, w2, w2t, codes, mirror = call(
         weights_kernel, 1, 0,
@@ -533,9 +532,9 @@
         [((288, 2 * MID), BF), ((2, CH, MID), F32), ((2, CH, MID), F32), ((2, 6) + plane, BF)],
         [((5, 8) + plane, BF)], codes, fp, part, w1,
     )
-    *got, cot_x = after((*got, cot_x), hidden_mid)
+    *got, crossed = after((*got, crossed), hidden_mid)
     (back,) = call(
-        back_kernel, 0.8, 1, [((2, 8) + plane, BF)], [((4, 64, 512), BF)], mirror, cotangent, cot_y, cot_x, swap_y(cot_x)
+        back_kernel, 0.8, 1, [((2, 8) + plane, BF)], [((4, 64, 512), BF)], mirror, cotangent, cot_y, crossed
     )
     columns_e, pre_e, gate_e, both, face_a, face_b = call(
         first_edge_kernel, 1.2, 1,

time: 48.4 us -> 45.9 us (0.948)
  waiting for transfers between devices: 10.3 us -> 7.1 us
  starting transfers between devices: 21.6 us -> 23.6 us
  other arithmetic: 1.44 us -> 0.06 us
    ppermute x10 -> x8, waiting for transfers between devices: 3.95 us -> 1.73 us  [swap_y(): return lax.ppermute(x, 'yp', [(i, n - 1 - i) for i in range(n)])]
    ppermute x4, starting transfers between devices: 4.06 us -> 5.55 us  [pair_swap(): return lax.ppermute(x, 'xp', pairs)]
    add x2, other arithmetic: 1.42 us -> 0.01 us  [side_by_side(): total = x if total is None else total + x]
    ppermute x2, starting transfers between devices: 6.8 us -> 7.98 us  [mirror_x(): return lax.ppermute(x, 'xp', [(i, n - 1 - i) for i in range(n)])]
    ppermute x3, waiting for transfers between devices: 6.3 us -> 5.35 us  [on_device(): total = total + lax.ppermute(total, 'xp', [(i, i ^ bit) for i in range(n)])]
    ppermute x10 -> x8, starting transfers between devices: 2.88 us -> 2.21 us  [swap_y(): return lax.ppermute(x, 'yp', [(i, n - 1 - i) for i in range(n)])]
    unnamed x3 -> x10, local copies, waits for them, and re-layouts: 1.68 us -> 1.72 us
  transfers between devices with their start and end apart: 19 -> 17, of which waited for: 9 -> 5; matrix products, arithmetic and copies ran while one was open for 6% -> 3% of each run, Pallas kernels for 12% -> 13%
where the time goes in v4:
time: 45.9 us; the launch traced here: 45.6 us
  starting transfers between devices  23.6 us (51%)
  Pallas kernels  11.7 us (25%)
  waiting for transfers between devices  7.1 us (15%)
  local copies, waits for them, and re-layouts  2.36 us (5%)
  between operations  0.86 us (2%)
    pallas_call x8, Pallas kernels, call(): pl.pallas_call(kernel, out_shape=tuple((jax.ShapeDtypeStruct(s, t) for s,...  11.7 us
    ppermute x2, starting transfers between devices, mirror_x(): return lax.ppermute(x, 'xp', [(i, n - 1 - i) for i in range(n)])  7.98 us
    ppermute x3, starting transfers between devices, on_device(): total = total + lax.ppermute(total, 'xp', [(i, i ^ bit) for i in range(n)])  7.86 us
    ppermute x4, starting transfers between devices, pair_swap(): return lax.ppermute(x, 'xp', pairs)  5.55 us
    ppermute x3, waiting for transfers between devices, on_device(): total = total + lax.ppermute(total, 'xp', [(i, i ^ bit) for i in range(n)])  5.35 us
    ppermute x8, starting transfers between devices, swap_y(): return lax.ppermute(x, 'yp', [(i, n - 1 - i) for i in range(n)])  2.21 us
    ppermute x8, waiting for transfers between devices, swap_y(): return lax.ppermute(x, 'yp', [(i, n - 1 - i) for i in range(n)])  1.73 us
    unnamed x10, local copies, waits for them, and re-layouts  1.72 us
  transfers between devices with their start and end apart: 17, of which 5 were waited for; matrix products, arithmetic and copies ran while one was open for 3% of the time, Pallas kernels for 13%

profile of v4, /device:TPU:0, one launch (start us, length us, event | category | flops | bytes accessed | tf_op | source)
XLA Modules:
  0.0 45.6 jit_solution(11713878513126536887)
XLA Ops:
  0.7 0.9 %copy.14.own = bf16[2,30,512]{2,1,0:T(8,128)(2,1)S(1)} copy(bf16[2,30,512]{2,0,1:T(2,128)(2,1)} %param.7) | data formatting | bytes 122880 | tf_op args[1]
  1.5 0.5 %collective-permute-start.3 = (bf16[2,30,512]{2,1,0:T(8,128)(2,1)S(1)}, bf16[2,30,512]{2,1,0:T(8,128)(2,1)S(1)}, u32[]{:S(2)}, u32[]{:S(2)}) collective-permute-start(bf16[2,30,512]{2,1,0:T(8,128)(2,1)S(1)} %copy.14.own), channel_id=1, source_target_pairs={{0,1},{1,0},{2,3},{3,2},{4,5},{5,4},{6,7},{7,6},{8,9},{9,8},{10,11... | collective-permute-start | bytes 184328 | tf_op jit(solution)/shard_map/ppermute | solution.py:480
  2.1 0.8 %copy.9.features = bf16[2,30,512]{2,1,0:T(8,128)(2,1)S(1)} copy(bf16[2,30,512]{2,0,1:T(2,128)(2,1)} %param.6) | data formatting | bytes 122880 | tf_op args[0]
  2.9 0.2 shard_map.85.own
  3.1 0.1 collective-permute-start
  3.3 6.1 %collective-permute-start.4 = (bf16[4,30,512]{2,1,0:T(8,128)(2,1)S(1)}, bf16[4,30,512]{2,1,0:T(8,128)(2,1)S(1)}, u32[]{:S(2)}, u32[]{:S(2)}) collective-permute-start(bf16[4,30,512]{2,1,0:T(8,128)(2,1)S(1)} %pad_maximum_fusion), channel_id=1, source_target_pairs={{0,14},{2,12},{4,10},{6,8},{8,6},{10,4},{12,2},{14,0},{1,15},{3,13... | collective-permute-start | bytes 368648 | tf_op jit(solution)/shard_map/ppermute | solution.py:485
  9.3 0.7 %collective-permute-start.2 = (bf16[4,32,128]{2,1,0:T(8,128)(2,1)S(1)}, bf16[4,32,128]{2,1,0:T(8,128)(2,1)S(1)}, u32[]{:S(2)}, u32[]{:S(2)}) collective-permute-start(bf16[4,32,128]{2,1,0:T(8,128)(2,1)S(1)} %get-tuple-element.67), channel_id=1, source_target_pairs={{2,4},{4,2},{6,8},{8,6},{10,12},{12,10},{3,5},{5,3},{7,9},{9,7},{1... | collective-permute-start | bytes 98312 | tf_op jit(solution)/shard_map/ppermute | solution.py:493
  10.0 2.3 %collective-permute-start.1 = (bf16[4,32,128]{2,1,0:T(8,128)(2,1)S(1)}, bf16[4,32,128]{2,1,0:T(8,128)(2,1)S(1)}, u32[]{:S(2)}, u32[]{:S(2)}) collective-permute-start(bf16[4,32,128]{2,1,0:T(8,128)(2,1)S(1)} %get-tuple-element.68), channel_id=1, source_target_pairs={{0,2},{2,0},{4,6},{6,4},{8,10},{10,8},{12,14},{14,12},{1,3},{3,1},... | collective-permute-start | bytes 98312 | tf_op jit(solution)/shard_map/ppermute | solution.py:493
  12.4 0.4 shard_map.86
  12.9 1.9 %shard_map.87 = (bf16[288,2048]{1,0:T(8,128)(2,1)S(1)}, f32[2,32,1024]{2,1,0:T(8,128)S(1)}, f32[2,32,1024]{2,1,0:T(8,128)S(1)}, bf16[2,6,32,128]{3,2,1,0:T(8,128)(2,1)S(1)}) custom-call(s32[2,27]{1,0:T(2,128)S(1)} %get-tuple-element.38.codes, bf16[2,8,32,128]{3,2,1,0:T(8,128)(2,1)S(1)} %shard_map.85.own, bf16[2,8,32,128]{3,2,1,0:T(8,128)(2,1)S(1)} %copy.17.part, ...), custom_call_target="tpu_custom_call" | custom-call | bytes 6000000 | tf_op jit(solution)/shard_map/pallas_call | solution.py:467
  14.8 0.8 %shard_map.88.back = bf16[2,8,32,128]{3,2,1,0:T(8,128)(2,1)S(1)} custom-call(s32[2,3]{1,0:T(2,128)S(1)} %get-tuple-element.37.mirror, bf16[2,30,512]{2,1,0:T(8,128)(2,1)S(1)} %copy.14.own, bf16[2,30,512]{2,1,0:T(8,128)(2,1)S(1)} %collective-permute-done.3.across_y, bf16[4,30,512]{2,1,0:T(8,128)(2,1)S(1)} %collective-permute-done.4.crossed), custom_call_target="tpu_custom_call" | custom-call | bytes 2400000 | tf_op jit(solution)/shard_map/pallas_call | solution.py:467
  15.6 1.2 %shard_map.89 = (bf16[288,512]{1,0:T(8,128)(2,1)S(1)}, f32[32,512]{1,0:T(8,128)S(1)}, f32[32,512]{1,0:T(8,128)S(1)}, bf16[2,2,8,32,128]{4,3,2,1,0:T(8,128)(2,1)S...) custom-call(s32[2,27]{1,0:T(2,128)S(1)} %get-tuple-element.38.codes, ...), custom_call_target="tpu_custom_call" | custom-call | bytes 3600000 | tf_op jit(solution)/shard_map/pallas_call | solution.py:467
  16.8 0.1 collective-permute-start.5
  16.8 1.9 %collective-permute-start.6 = (bf16[2,2,32,128]{3,2,1,0:T(8,128)(2,1)S(1)}, bf16[2,2,32,128]{3,2,1,0:T(8,128)(2,1)S(1)}, u32[]{:S(2)}, u32[]{:S(2)}) collective-permute-start(bf16[2,2,32,128]{3,2,1,0:T(8,128)(2,1)S(1)} %get-tuple-element.47), channel_id=1, source_target_pairs={{0,2},{2,0},{4,6},{6,4},{8,10},{10,8},{12,14},{14,12},{1,3},{3,1},... | collective-permute-start | bytes 98312 | tf_op jit(solution)/shard_map/ppermute | solution.py:493
  18.8 0.7 %collective-permute-start.7 = (bf16[2,2,32,128]{3,2,1,0:T(8,128)(2,1)S(1)}, bf16[2,2,32,128]{3,2,1,0:T(8,128)(2,1)S(1)}, u32[]{:S(2)}, u32[]{:S(2)}) collective-permute-start(bf16[2,2,32,128]{3,2,1,0:T(8,128)(2,1)S(1)} %get-tuple-element.48), channel_id=1, source_target_pairs={{2,4},{4,2},{6,8},{8,6},{10,12},{12,10},{3,5},{5,3},{7,9},{9,7},{1... | collective-permute-start | bytes 98312 | tf_op jit(solution)/shard_map/ppermute | solution.py:493
  19.4 3.5 %shard_map.90 = (f32[2,32,1024]{2,1,0:T(8,128)S(1)}, f32[32,512]{1,0:T(8,128)S(1)}, f32[2,288,128]{2,1,0:T(8,128)S(1)}) custom-call(s32[2,27]{1,0:T(2,128)S(1)} %get-tuple-element.38.codes, bf16[2,2,8,32,128]{4,3,2,1,0:T(8,128)(2,1)S(1)} %get-tuple-element.46.own, bf16[2,2,8,32,128]{4,3,2,1,0:T(8,128)(2,1)S(1)} %collective-permute-done.5.part, ...), custom_call_target="tpu_custom_call" | custom-call | bytes 10500000 | tf_op jit(solution)/shard_map/pallas_call | solution.py:467
  22.9 0.2 collective-permute-start.8
  23.2 0.3 collective-permute-start.9
  23.5 0.7 %collective-permute-done.8.far_a = bf16[2,2,32,128]{3,2,1,0:T(8,128)(2,1)S(1)} collective-permute-done((bf16[2,2,32,128]{3,2,1,0:T(8,128)(2,1)S(1)}, bf16[2,2,32,128]{3,2,1,0:T(8,128)(2,1)S(1)}, u32[]{:S(2)}, u32[]{:S(2)}) %collective-permute-start.8) | collective-permute-done | bytes 32800 | tf_op jit(solution)/shard_map/ppermute | solution.py:480
  24.2 0.2 collective-permute-done.9.far_b
  24.4 2.2 %shard_map.91 = (bf16[64,512]{1,0:T(8,128)(2,1)S(1)}, f32[56,128]{1,0:T(8,128)S(1)}) custom-call(s32[2,27]{1,0:T(2,128)S(1)} %get-tuple-element.38.codes, bf16[2,2,8,32,128]{4,3,2,1,0:T(8,128)(2,1)S(1)} %get-tuple-element.46.own, bf16[2,2,8,32,128]{4,3,2,1,0:T(8,128)(2,1)S(1)} %collective-permute-done.5.part, ...), custom_call_target="tpu_custom_call" | custom-call | bytes 8400000 | tf_op jit(solution)/shard_map/pallas_call | solution.py:467
  26.6 0.4 collective-permute-start.10
  27.0 0.9 %collective-permute-done.10 = f32[56,128]{1,0:T(8,128)S(1)} collective-permute-done((f32[56,128]{1,0:T(8,128)S(1)}, f32[56,128]{1,0:T(8,128)S(1)}, u32[]{:S(2)}, u32[]{:S(2)}) %collective-permute-start.10) | collective-permute-done | bytes 28704 | tf_op jit(solution)/shard_map/ppermute | solution.py:480
  27.9 4.5 %collective-permute-start.14 = (f32[56,128]{1,0:T(8,128)S(1)}, f32[56,128]{1,0:T(8,128)S(1)}, u32[]{:S(2)}, u32[]{:S(2)}) collective-permute-start(f32[56,128]{1,0:T(8,128)S(1)} %add.28), channel_id=1, source_target_pairs={{0,2},{2,0},{4,6},{6,4},{8,10},{10,8},{12,14},{14,12},{1,3},{3,1},... | collective-permute-start | bytes 86024 | tf_op jit(solution)/shard_map/ppermute | solution.py:575
  32.4 1.9 %collective-permute-start.12 = (bf16[64,512]{1,0:T(8,128)(2,1)S(1)}, bf16[64,512]{1,0:T(8,128)(2,1)S(1)}, u32[]{:S(2)}, u32[]{:S(2)}) collective-permute-start(bf16[64,512]{1,0:T(8,128)(2,1)S(1)} %get-tuple-element.62.own), channel_id=1, source_target_pairs={{0,14},{2,12},{4,10},{6,8},{8,6},{10,4},{12,2},{14,0},{1,15},{3,13... | collective-permute-start | bytes 196616 | tf_op jit(solution)/shard_map/ppermute | solution.py:485
  34.3 1.7 %collective-permute-start.15 = (f32[56,128]{1,0:T(8,128)S(1)}, f32[56,128]{1,0:T(8,128)S(1)}, u32[]{:S(2)}, u32[]{:S(2)}) collective-permute-start(f32[56,128]{1,0:T(8,128)S(1)} %add.29), channel_id=1, source_target_pairs={{0,4},{2,6},{4,0},{6,2},{8,12},{10,14},{12,8},{14,10},{1,5},{3,7},... | collective-permute-start | bytes 86024 | tf_op jit(solution)/shard_map/ppermute | solution.py:575
  36.0 2.7 %collective-permute-done.15 = f32[56,128]{1,0:T(8,128)S(1)} collective-permute-done((f32[56,128]{1,0:T(8,128)S(1)}, f32[56,128]{1,0:T(8,128)S(1)}, u32[]{:S(2)}, u32[]{:S(2)}) %collective-permute-start.15) | collective-permute-done | bytes 28704 | tf_op jit(solution)/shard_map/ppermute | solution.py:575
  38.7 1.6 %collective-permute-start.16 = (f32[56,128]{1,0:T(8,128)S(1)}, f32[56,128]{1,0:T(8,128)S(1)}, u32[]{:S(2)}, u32[]{:S(2)}) collective-permute-start(f32[56,128]{1,0:T(8,128)S(1)} %add.30), channel_id=1, source_target_pairs={{0,8},{2,10},{4,12},{6,14},{8,0},{10,2},{12,4},{14,6},{1,9},{3,11}... | collective-permute-start | bytes 86024 | tf_op jit(solution)/shard_map/ppermute | solution.py:575
  40.4 0.5 %collective-permute-start.13 = (bf16[64,512]{1,0:T(8,128)(2,1)S(1)}, bf16[64,512]{1,0:T(8,128)(2,1)S(1)}, u32[]{:S(2)}, u32[]{:S(2)}) collective-permute-start(bf16[64,512]{1,0:T(8,128)(2,1)S(1)} %collective-permute-done.12.across_x), channel_id=1, source_target_pairs={{0,1},{1,0},{2,3},{3,2},{4,5},{5,4},{6,7},{7,6},{8,9},{9,8},{10,11... | collective-permute-start | bytes 196616 | tf_op jit(solution)/shard_map/ppermute | solution.py:480
  40.9 2.6 %collective-permute-done.16 = f32[56,128]{1,0:T(8,128)S(1)} collective-permute-done((f32[56,128]{1,0:T(8,128)S(1)}, f32[56,128]{1,0:T(8,128)S(1)}, u32[]{:S(2)}, u32[]{:S(2)}) %collective-permute-start.16) | collective-permute-done | bytes 28704 | tf_op jit(solution)/shard_map/ppermute | solution.py:575
  43.5 0.6 %fusion = (f32[27,84]{1,0:T(8,128)}, f32[27,84]{1,0:T(8,128)}) fusion(f32[56,128]{1,0:T(8,128)S(1)} %add.31), kind=kLoop, calls=%fused_computation.11 | loop fusion | bytes 36288 | tf_op jit(solution)/shard_map/slice | solution.py:577
  44.1 1.5 %shard_map.92 = bf16[30,2,512]{2,1,0:T(2,128)(2,1)} custom-call(s32[2,3]{1,0:T(2,128)S(1)} %get-tuple-element.37.mirror, bf16[64,512]{1,0:T(8,128)(2,1)S(1)} %get-tuple-element.62.own, bf16[64,512]{1,0:T(8,128)(2,1)S(1)} %collective-permute-done.11.across_y, bf16[64,512]{1,0:T(8,128)(2,1)S(1)} %collective-permute-done.12.across_x, ...), custom_call_target="tpu_custom_call" | custom-call | bytes 2700000 | tf_op jit(solution)/shard_map/pallas_call | solution.py:467
  (33 shorter events, 0.1 us)
Async XLA Ops:
  0.6 11.7 %copy-start.2 = (s32[2,3]{1,0:T(2,128)S(1)}, s32[2,3]{1,0:T(2,128)}, u32[]{:S(2)}) copy-start(s32[2,3]{1,0:T(2,128)} %param.11) | copy-start | bytes 76
  0.6 11.7 %copy-start.3 = (s32[2,27]{1,0:T(2,128)S(1)}, s32[2,27]{1,0:T(2,128)}, u32[]{:S(2)}) copy-start(s32[2,27]{1,0:T(2,128)} %param.10) | copy-start | bytes 652
  0.7 11.7 %copy-start = (bf16[27,84]{1,0:T(8,128)(2,1)S(1)}, bf16[27,84]{1,0:T(8,128)(2,1)}, u32[]{:S(2)}) copy-start(bf16[27,84]{1,0:T(8,128)(2,1)} %param.9) | copy-start | bytes 13612
  0.7 11.7 %copy-start.1 = (bf16[27,84]{1,0:T(8,128)(2,1)S(1)}, bf16[27,84]{1,0:T(8,128)(2,1)}, u32[]{:S(2)}) copy-start(bf16[27,84]{1,0:T(8,128)(2,1)} %param.8) | copy-start | bytes 13612
  1.5 1.7 %collective-permute-start.3 = (bf16[2,30,512]{2,1,0:T(8,128)(2,1)S(1)}, bf16[2,30,512]{2,1,0:T(8,128)(2,1)S(1)}, u32[]{:S(2)}, u32[]{:S(2)}) collective-permute-start(bf16[2,30,512]{2,1,0:T(8,128)(2,1)S(1)} %copy.14.own), channel_id=1, source_target_pairs={{0,1},{1,0},{2,3},{3,2},{4,5},{5,4},{6,7},{7,6},{8,9},{9,8},{10,11... | collective-permute-start | bytes 184328 | tf_op jit(solution)/shard_map/ppermute | solution.py:480
  3.1 6.2 %collective-permute-start = (bf16[2,8,32,128]{3,2,0,1:T(8,128)(2,1)S(1)}, bf16[2,8,32,128]{3,2,0,1:T(8,128)(2,1)S(1)}, u32[]{:S(2)}, u32[]{:S(2)}) collective-permute-start(bf16[2,8,32,128]{3,2,0,1:T(8,128)(2,1)S(1)} %copy.10), channel_id=1, source_target_pairs={{0,1},{1,0},{2,3},{3,2},{4,5},{5,4},{6,7},{7,6},{8,9},{9,8},{10,11... | collective-permute-start | bytes 393224 | tf_op jit(solution)/shard_map/ppermute | solution.py:480
  3.3 11.5 %collective-permute-start.4 = (bf16[4,30,512]{2,1,0:T(8,128)(2,1)S(1)}, bf16[4,30,512]{2,1,0:T(8,128)(2,1)S(1)}, u32[]{:S(2)}, u32[]{:S(2)}) collective-permute-start(bf16[4,30,512]{2,1,0:T(8,128)(2,1)S(1)} %pad_maximum_fusion), channel_id=1, source_target_pairs={{0,14},{2,12},{4,10},{6,8},{8,6},{10,4},{12,2},{14,0},{1,15},{3,13... | collective-permute-start | bytes 368648 | tf_op jit(solution)/shard_map/ppermute | solution.py:485
  9.3 5.4 %collective-permute-start.2 = (bf16[4,32,128]{2,1,0:T(8,128)(2,1)S(1)}, bf16[4,32,128]{2,1,0:T(8,128)(2,1)S(1)}, u32[]{:S(2)}, u32[]{:S(2)}) collective-permute-start(bf16[4,32,128]{2,1,0:T(8,128)(2,1)S(1)} %get-tuple-element.67), channel_id=1, source_target_pairs={{2,4},{4,2},{6,8},{8,6},{10,12},{12,10},{3,5},{5,3},{7,9},{9,7},{1... | collective-permute-start | bytes 98312 | tf_op jit(solution)/shard_map/ppermute | solution.py:493
  10.0 4.7 %collective-permute-start.1 = (bf16[4,32,128]{2,1,0:T(8,128)(2,1)S(1)}, bf16[4,32,128]{2,1,0:T(8,128)(2,1)S(1)}, u32[]{:S(2)}, u32[]{:S(2)}) collective-permute-start(bf16[4,32,128]{2,1,0:T(8,128)(2,1)S(1)} %get-tuple-element.68), channel_id=1, source_target_pairs={{0,2},{2,0},{4,6},{6,4},{8,10},{10,8},{12,14},{14,12},{1,3},{3,1},... | collective-permute-start | bytes 98312 | tf_op jit(solution)/shard_map/ppermute | solution.py:493
  16.8 2.7 %collective-permute-start.5 = (bf16[2,2,8,32,128]{4,3,2,1,0:T(8,128)(2,1)S(1)}, bf16[2,2,8,32,128]{4,3,2,1,0:T(8,128)(2,1)S(1)}, u32[]{:S(2)}, u32[]{:S(2)}) collective-permute-start(bf16[2,2,8,32,128]{4,3,2,1,0:T(8,128)(2,1)S(1)} %get-tuple-element.46.own), channel_id=1, source_target_pairs={{0,1},{1,0},{2,3},{3,2},{4,5},{5,4},{6,7},{7,6},{8,9},{9,8},{10,11... | collective-permute-start | bytes 786440 | tf_op jit(solution)/shard_map/ppermute | solution.py:480
  16.8 6.1 %collective-permute-start.6 = (bf16[2,2,32,128]{3,2,1,0:T(8,128)(2,1)S(1)}, bf16[2,2,32,128]{3,2,1,0:T(8,128)(2,1)S(1)}, u32[]{:S(2)}, u32[]{:S(2)}) collective-permute-start(bf16[2,2,32,128]{3,2,1,0:T(8,128)(2,1)S(1)} %get-tuple-element.47), channel_id=1, source_target_pairs={{0,2},{2,0},{4,6},{6,4},{8,10},{10,8},{12,14},{14,12},{1,3},{3,1},... | collective-permute-start | bytes 98312 | tf_op jit(solution)/shard_map/ppermute | solution.py:493
  18.8 4.2 %collective-permute-start.7 = (bf16[2,2,32,128]{3,2,1,0:T(8,128)(2,1)S(1)}, bf16[2,2,32,128]{3,2,1,0:T(8,128)(2,1)S(1)}, u32[]{:S(2)}, u32[]{:S(2)}) collective-permute-start(bf16[2,2,32,128]{3,2,1,0:T(8,128)(2,1)S(1)} %get-tuple-element.48), channel_id=1, source_target_pairs={{2,4},{4,2},{6,8},{8,6},{10,12},{12,10},{3,5},{5,3},{7,9},{9,7},{1... | collective-permute-start | bytes 98312 | tf_op jit(solution)/shard_map/ppermute | solution.py:493
  22.9 1.3 %collective-permute-start.8 = (bf16[2,2,32,128]{3,2,1,0:T(8,128)(2,1)S(1)}, bf16[2,2,32,128]{3,2,1,0:T(8,128)(2,1)S(1)}, u32[]{:S(2)}, u32[]{:S(2)}) collective-permute-start(bf16[2,2,32,128]{3,2,1,0:T(8,128)(2,1)S(1)} %collective-permute-done.6.got_a), channel_id=1, source_target_pairs={{0,1},{1,0},{2,3},{3,2},{4,5},{5,4},{6,7},{7,6},{8,9},{9,8},{10,11... | collective-permute-start | bytes 98312 | tf_op jit(solution)/shard_map/ppermute | solution.py:480
  23.2 1.2 %collective-permute-start.9 = (bf16[2,2,32,128]{3,2,1,0:T(8,128)(2,1)S(1)}, bf16[2,2,32,128]{3,2,1,0:T(8,128)(2,1)S(1)}, u32[]{:S(2)}, u32[]{:S(2)}) collective-permute-start(bf16[2,2,32,128]{3,2,1,0:T(8,128)(2,1)S(1)} %collective-permute-done.7.got_b), channel_id=1, source_target_pairs={{0,1},{1,0},{2,3},{3,2},{4,5},{5,4},{6,7},{7,6},{8,9},{9,8},{10,11... | collective-permute-start | bytes 98312 | tf_op jit(solution)/shard_map/ppermute | solution.py:480
  26.6 1.3 %collective-permute-start.10 = (f32[56,128]{1,0:T(8,128)S(1)}, f32[56,128]{1,0:T(8,128)S(1)}, u32[]{:S(2)}, u32[]{:S(2)}) collective-permute-start(f32[56,128]{1,0:T(8,128)S(1)} %get-tuple-element.61), channel_id=1, source_target_pairs={{0,1},{1,0},{2,3},{3,2},{4,5},{5,4},{6,7},{7,6},{8,9},{9,8},{10,11... | collective-permute-start | bytes 86024 | tf_op jit(solution)/shard_map/ppermute | solution.py:480
  27.9 6.4 %collective-permute-start.14 = (f32[56,128]{1,0:T(8,128)S(1)}, f32[56,128]{1,0:T(8,128)S(1)}, u32[]{:S(2)}, u32[]{:S(2)}) collective-permute-start(f32[56,128]{1,0:T(8,128)S(1)} %add.28), channel_id=1, source_target_pairs={{0,2},{2,0},{4,6},{6,4},{8,10},{10,8},{12,14},{14,12},{1,3},{3,1},... | collective-permute-start | bytes 86024 | tf_op jit(solution)/shard_map/ppermute | solution.py:575
  32.4 8.0 %collective-permute-start.12 = (bf16[64,512]{1,0:T(8,128)(2,1)S(1)}, bf16[64,512]{1,0:T(8,128)(2,1)S(1)}, u32[]{:S(2)}, u32[]{:S(2)}) collective-permute-start(bf16[64,512]{1,0:T(8,128)(2,1)S(1)} %get-tuple-element.62.own), channel_id=1, source_target_pairs={{0,14},{2,12},{4,10},{6,8},{8,6},{10,4},{12,2},{14,0},{1,15},{3,13... | collective-permute-start | bytes 196616 | tf_op jit(solution)/shard_map/ppermute | solution.py:485
  34.3 4.5 %collective-permute-start.15 = (f32[56,128]{1,0:T(8,128)S(1)}, f32[56,128]{1,0:T(8,128)S(1)}, u32[]{:S(2)}, u32[]{:S(2)}) collective-permute-start(f32[56,128]{1,0:T(8,128)S(1)} %add.29), channel_id=1, source_target_pairs={{0,4},{2,6},{4,0},{6,2},{8,12},{10,14},{12,8},{14,10},{1,5},{3,7},... | collective-permute-start | bytes 86024 | tf_op jit(solution)/shard_map/ppermute | solution.py:575
  38.7 4.8 %collective-permute-start.16 = (f32[56,128]{1,0:T(8,128)S(1)}, f32[56,128]{1,0:T(8,128)S(1)}, u32[]{:S(2)}, u32[]{:S(2)}) collective-permute-start(f32[56,128]{1,0:T(8,128)S(1)} %add.30), channel_id=1, source_target_pairs={{0,8},{2,10},{4,12},{6,14},{8,0},{10,2},{12,4},{14,6},{1,9},{3,11}... | collective-permute-start | bytes 86024 | tf_op jit(solution)/shard_map/ppermute | solution.py:575
  40.4 3.8 %collective-permute-start.11 = (bf16[64,512]{1,0:T(8,128)(2,1)S(1)}, bf16[64,512]{1,0:T(8,128)(2,1)S(1)}, u32[]{:S(2)}, u32[]{:S(2)}) collective-permute-start(bf16[64,512]{1,0:T(8,128)(2,1)S(1)} %get-tuple-element.62.own), channel_id=1, source_target_pairs={{0,1},{1,0},{2,3},{3,2},{4,5},{5,4},{6,7},{7,6},{8,9},{9,8},{10,11... | collective-permute-start | bytes 196616 | tf_op jit(solution)/shard_map/ppermute | solution.py:480
  40.4 3.8 %collective-permute-start.13 = (bf16[64,512]{1,0:T(8,128)(2,1)S(1)}, bf16[64,512]{1,0:T(8,128)(2,1)S(1)}, u32[]{:S(2)}, u32[]{:S(2)}) collective-permute-start(bf16[64,512]{1,0:T(8,128)(2,1)S(1)} %collective-permute-done.12.across_x), channel_id=1, source_target_pairs={{0,1},{1,0},{2,3},{3,2},{4,5},{5,4},{6,7},{7,6},{8,9},{9,8},{10,11... | collective-permute-start | bytes 196616 | tf_op jit(solution)/shard_map/ppermute | solution.py:480

commit v5 on v4

--- a/solution.py
+++ b/solution.py
@@ -374,8 +374,8 @@
 
 
 def second_edge_kernel(
-    scale, codes, own, part, got_a, got_b, far_a, far_b, pre_edge, gate_edge, second_in, through_edge,
-    columns_f, columns_fe, raw, w_second, w_turned, second, grads,
+    scale, codes, own, part, got_a, got_b, far_a, far_b, pre_edge, gate_edge, through_edge,
+    columns_f, columns_fe, raw, w_second, w_turned, second_edge, grads,
     low, high, columns_h, columns_b, placed_f, placed_s, place,
 ):
     masks = region_masks()
@@ -386,23 +386,8 @@
             lambda which, s: (got_a, got_b)[which][f, s], lambda which, s: (far_a, far_b)[which][f, s],
         )
         edge_columns(codes, masks, low.at[f], high.at[f], columns)
-    more = edge_terms(dot(w_second[...], columns_h[...]), 0)
+    second_edge[...] = edge_terms(dot(w_second[...], columns_h[...]), 0)
     more_t = edge_terms(dot(w_turned[...], columns_b[...]), 0)
-    zero = jnp.zeros((CH, LANES), F32)
-    rows = []
-    for n in range(2):
-        for k in range(4):
-            planes = second_in[n, :, k * 256 : (k + 1) * 256]
-            if k == 0:
-                planes = planes + jnp.concatenate([more[:, 2 * n * LANES : (2 * n + 1) * LANES], zero], axis=1)
-            if k == 3:
-                planes = planes + jnp.concatenate([zero, more[:, (2 * n + 1) * LANES : (2 * n + 2) * LANES]], axis=1)
-            rows.append(planes.astype(BF))
-    packed = dot(jnp.concatenate(rows, axis=0), compact_table()).astype(BF)
-    for n in range(2):
-        for k in range(4):
-            first = (4 * n + k) * CH
-            second[n * CH : (n + 1) * CH, k * LANES : (k + 1) * LANES] = packed[first : first + CH]
     back_pre = gate_back(through_edge[...] + more_t, pre_edge[...], gate_edge[...], gate_rows(), inside)
     placed_f[...] = jnp.zeros_like(placed_f)
     placed_s[...] = jnp.zeros_like(placed_s)
@@ -446,6 +431,24 @@
     grads[54:56, :] = jnp.zeros((2, LANES), F32)
 
 
+def compact_kernel(second_in, more, second):
+    zero = jnp.zeros((CH, LANES), F32)
+    rows = []
+    for n in range(2):
+        for k in range(4):
+            planes = second_in[n, :, k * 256 : (k + 1) * 256]
+            if k == 0:
+                planes = planes + jnp.concatenate([more[:, 2 * n * LANES : (2 * n + 1) * LANES], zero], axis=1)
+            if k == 3:
+                planes = planes + jnp.concatenate([zero, more[:, (2 * n + 1) * LANES : (2 * n + 2) * LANES]], axis=1)
+            rows.append(planes.astype(BF))
+    packed = dot(jnp.concatenate(rows, axis=0), compact_table()).astype(BF)
+    for n in range(2):
+        for k in range(4):
+            first = (4 * n + k) * CH
+            second[n * CH : (n + 1) * CH, k * LANES : (k + 1) * LANES] = packed[first : first + CH]
+
+
 def turn_kernel(mirror, own, across_y, across_x, across, out, staged):
     for n in range(2):
         staged[0, n * CH : (n + 1) * CH, :] = own[n * CH : (n + 1) * CH, :]
@@ -532,10 +535,11 @@
         [((288, 2 * MID), BF), ((2, CH, MID), F32), ((2, CH, MID), F32), ((2, 6) + plane, BF)],
         [((5, 8) + plane, BF)], codes, fp, part, w1,
     )
-    *got, crossed = after((*got, crossed), hidden_mid)
+    (crossed,) = after((crossed,), hidden_mid)
     (back,) = call(
         back_kernel, 0.8, 1, [((2, 8) + plane, BF)], [((4, 64, 512), BF)], mirror, cotangent, cot_y, crossed
     )
+    got = after(got, hidden_mid, back)
     columns_e, pre_e, gate_e, both, face_a, face_b = call(
         first_edge_kernel, 1.2, 1,
         [
@@ -554,14 +558,15 @@
     got = after(got, raw)
     faces = (*got, swap_y(got[0]), swap_y(got[1]))
     n_bricks = features.shape[0] * lax.axis_size("xp") * lax.axis_size("yp")
-    second, grads = call(
-        functools.partial(second_edge_kernel, 1.0 / n_bricks), 2.8, 1, [((64, 512), BF), ((56, LANES), F32)],
+    second_e, grads = call(
+        functools.partial(second_edge_kernel, 1.0 / n_bricks), 2, 1, [((CH, 4 * LANES), F32), ((56, LANES), F32)],
         [((2, 9) + plane, BF)] * 2 + [((288, 4 * LANES), BF)] * 2
         + [((128, 12 * LANES), BF), ((128, 4 * LANES), BF), ((256, 3 * LANES), BF)],
-        codes, both, part, *faces, pre_e, gate_e, second_part, through_e, columns, columns_e, raw, w2, w2t,
+        codes, both, part, *faces, pre_e, gate_e, through_e, columns, columns_e, raw, w2, w2t,
     )
     total = grads + swap_y(grads)
-    (second,) = after((second,), total)
+    second_part, second_e = after((second_part, second_e), total)
+    (second,) = call(compact_kernel, 0.5, 0, [((64, 512), BF)], [], second_part, second_e)
     second_y = swap_y(second)
     second_x = mirror_x(second)
     second_xy = swap_y(second_x)

time: 45.9 us -> 45.4 us (0.989)
  starting transfers between devices: 23.6 us -> 22.4 us
  waiting for transfers between devices: 7.1 us -> 7.62 us
    ppermute x4, starting transfers between devices: 5.55 us -> 4.73 us  [pair_swap(): return lax.ppermute(x, 'xp', pairs)]
    ppermute x3, starting transfers between devices: 7.86 us -> 7.14 us  [on_device(): total = total + lax.ppermute(total, 'xp', [(i, i ^ bit) for i in range(n)])]
    ppermute x3, waiting for transfers between devices: 5.35 us -> 5.87 us  [on_device(): total = total + lax.ppermute(total, 'xp', [(i, i ^ bit) for i in range(n)])]
    pallas_call x8 -> x9, Pallas kernels: 11.7 us -> 11.9 us  [call(): pl.pallas_call(kernel, out_shape=tuple((jax.ShapeDtypeStruct(s, t) for s,...]
  transfers between devices with their start and end apart: 17 -> 17, of which waited for: 5 -> 5; matrix products, arithmetic and copies ran while one was open for 3% -> 3% of each run, Pallas kernels for 13% -> 16%
where the time goes in v5:
time: 45.4 us; the launch traced here: 45.2 us
  starting transfers between devices  22.4 us (49%)
  Pallas kernels  11.9 us (26%)
  waiting for transfers between devices  7.62 us (17%)
  local copies, waits for them, and re-layouts  2.36 us (5%)
  between operations  0.87 us (2%)
    pallas_call x9, Pallas kernels, call(): pl.pallas_call(kernel, out_shape=tuple((jax.ShapeDtypeStruct(s, t) for s,...  11.9 us
    ppermute x2, starting transfers between devices, mirror_x(): return lax.ppermute(x, 'xp', [(i, n - 1 - i) for i in range(n)])  8.28 us
    ppermute x3, starting transfers between devices, on_device(): total = total + lax.ppermute(total, 'xp', [(i, i ^ bit) for i in range(n)])  7.14 us
    ppermute x3, waiting for transfers between devices, on_device(): total = total + lax.ppermute(total, 'xp', [(i, i ^ bit) for i in range(n)])  5.87 us
    ppermute x4, starting transfers between devices, pair_swap(): return lax.ppermute(x, 'xp', pairs)  4.73 us
    ppermute x8, starting transfers between devices, swap_y(): return lax.ppermute(x, 'yp', [(i, n - 1 - i) for i in range(n)])  2.2 us
    ppermute x8, waiting for transfers between devices, swap_y(): return lax.ppermute(x, 'yp', [(i, n - 1 - i) for i in range(n)])  1.73 us
    unnamed x10, local copies, waits for them, and re-layouts  1.72 us
  transfers between devices with their start and end apart: 17, of which 5 were waited for; matrix products, arithmetic and copies ran while one was open for 3% of the time, Pallas kernels for 16%

profile of v5, /device:TPU:0, one launch (start us, length us, event | category | flops | bytes accessed | tf_op | source)
XLA Modules:
  0.0 45.2 jit_solution(15675632122925651266)
XLA Ops:
  0.7 0.9 %copy.16.own = bf16[2,30,512]{2,1,0:T(8,128)(2,1)S(1)} copy(bf16[2,30,512]{2,0,1:T(2,128)(2,1)} %param.7) | data formatting | bytes 122880 | tf_op args[1]
  1.5 0.5 %collective-permute-start.3 = (bf16[2,30,512]{2,1,0:T(8,128)(2,1)S(1)}, bf16[2,30,512]{2,1,0:T(8,128)(2,1)S(1)}, u32[]{:S(2)}, u32[]{:S(2)}) collective-permute-start(bf16[2,30,512]{2,1,0:T(8,128)(2,1)S(1)} %copy.16.own), channel_id=1, source_target_pairs={{0,1},{1,0},{2,3},{3,2},{4,5},{5,4},{6,7},{7,6},{8,9},{9,8},{10,11... | collective-permute-start | bytes 184328 | tf_op jit(solution)/shard_map/ppermute | solution.py:483
  2.1 0.8 %copy.9.features = bf16[2,30,512]{2,1,0:T(8,128)(2,1)S(1)} copy(bf16[2,30,512]{2,0,1:T(2,128)(2,1)} %param.6) | data formatting | bytes 122880 | tf_op args[0]
  2.9 0.2 shard_map.85.own
  3.1 0.1 collective-permute-start
  3.3 6.1 %collective-permute-start.4 = (bf16[4,30,512]{2,1,0:T(8,128)(2,1)S(1)}, bf16[4,30,512]{2,1,0:T(8,128)(2,1)S(1)}, u32[]{:S(2)}, u32[]{:S(2)}) collective-permute-start(bf16[4,30,512]{2,1,0:T(8,128)(2,1)S(1)} %pad_maximum_fusion), channel_id=1, source_target_pairs={{0,14},{2,12},{4,10},{6,8},{8,6},{10,4},{12,2},{14,0},{1,15},{3,13... | collective-permute-start | bytes 368648 | tf_op jit(solution)/shard_map/ppermute | solution.py:488
  9.3 0.7 %collective-permute-start.2 = (bf16[4,32,128]{2,1,0:T(8,128)(2,1)S(1)}, bf16[4,32,128]{2,1,0:T(8,128)(2,1)S(1)}, u32[]{:S(2)}, u32[]{:S(2)}) collective-permute-start(bf16[4,32,128]{2,1,0:T(8,128)(2,1)S(1)} %get-tuple-element.69), channel_id=1, source_target_pairs={{2,4},{4,2},{6,8},{8,6},{10,12},{12,10},{3,5},{5,3},{7,9},{9,7},{1... | collective-permute-start | bytes 98312 | tf_op jit(solution)/shard_map/ppermute | solution.py:496
  10.0 2.3 %collective-permute-start.1 = (bf16[4,32,128]{2,1,0:T(8,128)(2,1)S(1)}, bf16[4,32,128]{2,1,0:T(8,128)(2,1)S(1)}, u32[]{:S(2)}, u32[]{:S(2)}) collective-permute-start(bf16[4,32,128]{2,1,0:T(8,128)(2,1)S(1)} %get-tuple-element.70), channel_id=1, source_target_pairs={{0,2},{2,0},{4,6},{6,4},{8,10},{10,8},{12,14},{14,12},{1,3},{3,1},... | collective-permute-start | bytes 98312 | tf_op jit(solution)/shard_map/ppermute | solution.py:496
  12.4 0.4 shard_map.86
  12.9 1.9 %shard_map.87 = (bf16[288,2048]{1,0:T(8,128)(2,1)S(1)}, f32[2,32,1024]{2,1,0:T(8,128)S(1)}, f32[2,32,1024]{2,1,0:T(8,128)S(1)}, bf16[2,6,32,128]{3,2,1,0:T(8,128)(2,1)S(1)}) custom-call(s32[2,27]{1,0:T(2,128)S(1)} %get-tuple-element.39.codes, bf16[2,8,32,128]{3,2,1,0:T(8,128)(2,1)S(1)} %shard_map.85.own, bf16[2,8,32,128]{3,2,1,0:T(8,128)(2,1)S(1)} %copy.17.part, ...), custom_call_target="tpu_custom_call" | custom-call | bytes 6000000 | tf_op jit(solution)/shard_map/pallas_call | solution.py:470
  14.8 0.8 %shard_map.88.back = bf16[2,8,32,128]{3,2,1,0:T(8,128)(2,1)S(1)} custom-call(s32[2,3]{1,0:T(2,128)S(1)} %get-tuple-element.38.mirror, bf16[2,30,512]{2,1,0:T(8,128)(2,1)S(1)} %copy.16.own, bf16[2,30,512]{2,1,0:T(8,128)(2,1)S(1)} %collective-permute-done.3.across_y, bf16[4,30,512]{2,1,0:T(8,128)(2,1)S(1)} %collective-permute-done.4.crossed), custom_call_target="tpu_custom_call" | custom-call | bytes 2400000 | tf_op jit(solution)/shard_map/pallas_call | solution.py:470
  15.6 1.2 %shard_map.89 = (bf16[288,512]{1,0:T(8,128)(2,1)S(1)}, f32[32,512]{1,0:T(8,128)S(1)}, f32[32,512]{1,0:T(8,128)S(1)}, bf16[2,2,8,32,128]{4,3,2,1,0:T(8,128)(2,1)S...) custom-call(s32[2,27]{1,0:T(2,128)S(1)} %get-tuple-element.39.codes, ...), custom_call_target="tpu_custom_call" | custom-call | bytes 3600000 | tf_op jit(solution)/shard_map/pallas_call | solution.py:470
  16.9 1.1 %collective-permute-start.6 = (bf16[2,2,32,128]{3,2,1,0:T(8,128)(2,1)S(1)}, bf16[2,2,32,128]{3,2,1,0:T(8,128)(2,1)S(1)}, u32[]{:S(2)}, u32[]{:S(2)}) collective-permute-start(bf16[2,2,32,128]{3,2,1,0:T(8,128)(2,1)S(1)} %get-tuple-element.52), channel_id=1, source_target_pairs={{0,2},{2,0},{4,6},{6,4},{8,10},{10,8},{12,14},{14,12},{1,3},{3,1},... | collective-permute-start | bytes 98312 | tf_op jit(solution)/shard_map/ppermute | solution.py:496
  17.9 0.7 %collective-permute-start.7 = (bf16[2,2,32,128]{3,2,1,0:T(8,128)(2,1)S(1)}, bf16[2,2,32,128]{3,2,1,0:T(8,128)(2,1)S(1)}, u32[]{:S(2)}, u32[]{:S(2)}) collective-permute-start(bf16[2,2,32,128]{3,2,1,0:T(8,128)(2,1)S(1)} %get-tuple-element.53), channel_id=1, source_target_pairs={{2,4},{4,2},{6,8},{8,6},{10,12},{12,10},{3,5},{5,3},{7,9},{9,7},{1... | collective-permute-start | bytes 98312 | tf_op jit(solution)/shard_map/ppermute | solution.py:496
  18.6 3.5 %shard_map.90 = (f32[2,32,1024]{2,1,0:T(8,128)S(1)}, f32[32,512]{1,0:T(8,128)S(1)}, f32[2,288,128]{2,1,0:T(8,128)S(1)}) custom-call(s32[2,27]{1,0:T(2,128)S(1)} %get-tuple-element.39.codes, bf16[2,2,8,32,128]{4,3,2,1,0:T(8,128)(2,1)S(1)} %get-tuple-element.47.own, bf16[2,2,8,32,128]{4,3,2,1,0:T(8,128)(2,1)S(1)} %collective-permute-done.5.part, ...), custom_call_target="tpu_custom_call" | custom-call | bytes 10500000 | tf_op jit(solution)/shard_map/pallas_call | solution.py:470
  22.1 0.2 collective-permute-start.8
  22.3 0.3 collective-permute-start.9
  22.7 0.7 %collective-permute-done.8.far_a = bf16[2,2,32,128]{3,2,1,0:T(8,128)(2,1)S(1)} collective-permute-done((bf16[2,2,32,128]{3,2,1,0:T(8,128)(2,1)S(1)}, bf16[2,2,32,128]{3,2,1,0:T(8,128)(2,1)S(1)}, u32[]{:S(2)}, u32[]{:S(2)}) %collective-permute-start.8) | collective-permute-done | bytes 32800 | tf_op jit(solution)/shard_map/ppermute | solution.py:483
  23.4 0.2 collective-permute-done.9.far_b
  23.6 2.2 %shard_map.91 = (f32[32,512]{1,0:T(8,128)S(1)}, f32[56,128]{1,0:T(8,128)S(1)}) custom-call(s32[2,27]{1,0:T(2,128)S(1)} %get-tuple-element.39.codes, bf16[2,2,8,32,128]{4,3,2,1,0:T(8,128)(2,1)S(1)} %get-tuple-element.47.own, bf16[2,2,8,32,128]{4,3,2,1,0:T(8,128)(2,1)S(1)} %collective-permute-done.5.part, ...), custom_call_target="tpu_custom_call" | custom-call | bytes 6000000 | tf_op jit(solution)/shard_map/pallas_call | solution.py:470
  25.8 0.4 collective-permute-start.10
  26.2 0.9 %collective-permute-done.10 = f32[56,128]{1,0:T(8,128)S(1)} collective-permute-done((f32[56,128]{1,0:T(8,128)S(1)}, f32[56,128]{1,0:T(8,128)S(1)}, u32[]{:S(2)}, u32[]{:S(2)}) %collective-permute-start.10) | collective-permute-done | bytes 28704 | tf_op jit(solution)/shard_map/ppermute | solution.py:483
  27.0 4.7 %collective-permute-start.14 = (f32[56,128]{1,0:T(8,128)S(1)}, f32[56,128]{1,0:T(8,128)S(1)}, u32[]{:S(2)}, u32[]{:S(2)}) collective-permute-start(f32[56,128]{1,0:T(8,128)S(1)} %add.28), channel_id=1, source_target_pairs={{0,2},{2,0},{4,6},{6,4},{8,10},{10,8},{12,14},{14,12},{1,3},{3,1},... | collective-permute-start | bytes 86024 | tf_op jit(solution)/shard_map/ppermute | solution.py:580
  31.7 0.3 shard_map.92.own
  32.0 2.2 %collective-permute-start.12 = (bf16[64,512]{1,0:T(8,128)(2,1)S(1)}, bf16[64,512]{1,0:T(8,128)(2,1)S(1)}, u32[]{:S(2)}, u32[]{:S(2)}) collective-permute-start(bf16[64,512]{1,0:T(8,128)(2,1)S(1)} %shard_map.92.own), channel_id=1, source_target_pairs={{0,14},{2,12},{4,10},{6,8},{8,6},{10,4},{12,2},{14,0},{1,15},{3,13... | collective-permute-start | bytes 196616 | tf_op jit(solution)/shard_map/ppermute | solution.py:488
  34.2 1.1 %collective-permute-start.15 = (f32[56,128]{1,0:T(8,128)S(1)}, f32[56,128]{1,0:T(8,128)S(1)}, u32[]{:S(2)}, u32[]{:S(2)}) collective-permute-start(f32[56,128]{1,0:T(8,128)S(1)} %add.29), channel_id=1, source_target_pairs={{0,4},{2,6},{4,0},{6,2},{8,12},{10,14},{12,8},{14,10},{1,5},{3,7},... | collective-permute-start | bytes 86024 | tf_op jit(solution)/shard_map/ppermute | solution.py:580
  35.3 2.9 %collective-permute-done.15 = f32[56,128]{1,0:T(8,128)S(1)} collective-permute-done((f32[56,128]{1,0:T(8,128)S(1)}, f32[56,128]{1,0:T(8,128)S(1)}, u32[]{:S(2)}, u32[]{:S(2)}) %collective-permute-start.15) | collective-permute-done | bytes 28704 | tf_op jit(solution)/shard_map/ppermute | solution.py:580
  38.3 1.3 %collective-permute-start.16 = (f32[56,128]{1,0:T(8,128)S(1)}, f32[56,128]{1,0:T(8,128)S(1)}, u32[]{:S(2)}, u32[]{:S(2)}) collective-permute-start(f32[56,128]{1,0:T(8,128)S(1)} %add.30), channel_id=1, source_target_pairs={{0,8},{2,10},{4,12},{6,14},{8,0},{10,2},{12,4},{14,6},{1,9},{3,11}... | collective-permute-start | bytes 86024 | tf_op jit(solution)/shard_map/ppermute | solution.py:580
  39.6 0.5 %collective-permute-start.13 = (bf16[64,512]{1,0:T(8,128)(2,1)S(1)}, bf16[64,512]{1,0:T(8,128)(2,1)S(1)}, u32[]{:S(2)}, u32[]{:S(2)}) collective-permute-start(bf16[64,512]{1,0:T(8,128)(2,1)S(1)} %collective-permute-done.12.across_x), channel_id=1, source_target_pairs={{0,1},{1,0},{2,3},{3,2},{4,5},{5,4},{6,7},{7,6},{8,9},{9,8},{10,11... | collective-permute-start | bytes 196616 | tf_op jit(solution)/shard_map/ppermute | solution.py:483
  40.1 2.9 %collective-permute-done.16 = f32[56,128]{1,0:T(8,128)S(1)} collective-permute-done((f32[56,128]{1,0:T(8,128)S(1)}, f32[56,128]{1,0:T(8,128)S(1)}, u32[]{:S(2)}, u32[]{:S(2)}) %collective-permute-start.16) | collective-permute-done | bytes 28704 | tf_op jit(solution)/shard_map/ppermute | solution.py:580
  43.0 0.6 %fusion = (f32[27,84]{1,0:T(8,128)}, f32[27,84]{1,0:T(8,128)}) fusion(f32[56,128]{1,0:T(8,128)S(1)} %add.31), kind=kLoop, calls=%fused_computation.11 | loop fusion | bytes 36288 | tf_op jit(solution)/shard_map/slice | solution.py:582
  43.7 1.5 %shard_map.93 = bf16[30,2,512]{2,1,0:T(2,128)(2,1)} custom-call(s32[2,3]{1,0:T(2,128)S(1)} %get-tuple-element.38.mirror, bf16[64,512]{1,0:T(8,128)(2,1)S(1)} %shard_map.92.own, bf16[64,512]{1,0:T(8,128)(2,1)S(1)} %collective-permute-done.11.across_y, bf16[64,512]{1,0:T(8,128)(2,1)S(1)} %collective-permute-done.12.across_x, ...), custom_call_target="tpu_custom_call" | custom-call | bytes 2700000 | tf_op jit(solution)/shard_map/pallas_call | solution.py:470
  (34 shorter events, 0.2 us)
Async XLA Ops:
  0.6 11.7 %copy-start.2 = (s32[2,3]{1,0:T(2,128)S(1)}, s32[2,3]{1,0:T(2,128)}, u32[]{:S(2)}) copy-start(s32[2,3]{1,0:T(2,128)} %param.11) | copy-start | bytes 76
  0.6 11.7 %copy-start.3 = (s32[2,27]{1,0:T(2,128)S(1)}, s32[2,27]{1,0:T(2,128)}, u32[]{:S(2)}) copy-start(s32[2,27]{1,0:T(2,128)} %param.10) | copy-start | bytes 652
  0.7 11.7 %copy-start = (bf16[27,84]{1,0:T(8,128)(2,1)S(1)}, bf16[27,84]{1,0:T(8,128)(2,1)}, u32[]{:S(2)}) copy-start(bf16[27,84]{1,0:T(8,128)(2,1)} %param.9) | copy-start | bytes 13612
  0.7 11.7 %copy-start.1 = (bf16[27,84]{1,0:T(8,128)(2,1)S(1)}, bf16[27,84]{1,0:T(8,128)(2,1)}, u32[]{:S(2)}) copy-start(bf16[27,84]{1,0:T(8,128)(2,1)} %param.8) | copy-start | bytes 13612
  1.5 1.7 %collective-permute-start.3 = (bf16[2,30,512]{2,1,0:T(8,128)(2,1)S(1)}, bf16[2,30,512]{2,1,0:T(8,128)(2,1)S(1)}, u32[]{:S(2)}, u32[]{:S(2)}) collective-permute-start(bf16[2,30,512]{2,1,0:T(8,128)(2,1)S(1)} %copy.16.own), channel_id=1, source_target_pairs={{0,1},{1,0},{2,3},{3,2},{4,5},{5,4},{6,7},{7,6},{8,9},{9,8},{10,11... | collective-permute-start | bytes 184328 | tf_op jit(solution)/shard_map/ppermute | solution.py:483
  3.1 6.2 %collective-permute-start = (bf16[2,8,32,128]{3,2,0,1:T(8,128)(2,1)S(1)}, bf16[2,8,32,128]{3,2,0,1:T(8,128)(2,1)S(1)}, u32[]{:S(2)}, u32[]{:S(2)}) collective-permute-start(bf16[2,8,32,128]{3,2,0,1:T(8,128)(2,1)S(1)} %copy.10), channel_id=1, source_target_pairs={{0,1},{1,0},{2,3},{3,2},{4,5},{5,4},{6,7},{7,6},{8,9},{9,8},{10,11... | collective-permute-start | bytes 393224 | tf_op jit(solution)/shard_map/ppermute | solution.py:483
  3.3 11.5 %collective-permute-start.4 = (bf16[4,30,512]{2,1,0:T(8,128)(2,1)S(1)}, bf16[4,30,512]{2,1,0:T(8,128)(2,1)S(1)}, u32[]{:S(2)}, u32[]{:S(2)}) collective-permute-start(bf16[4,30,512]{2,1,0:T(8,128)(2,1)S(1)} %pad_maximum_fusion), channel_id=1, source_target_pairs={{0,14},{2,12},{4,10},{6,8},{8,6},{10,4},{12,2},{14,0},{1,15},{3,13... | collective-permute-start | bytes 368648 | tf_op jit(solution)/shard_map/ppermute | solution.py:488
  9.3 6.2 %collective-permute-start.2 = (bf16[4,32,128]{2,1,0:T(8,128)(2,1)S(1)}, bf16[4,32,128]{2,1,0:T(8,128)(2,1)S(1)}, u32[]{:S(2)}, u32[]{:S(2)}) collective-permute-start(bf16[4,32,128]{2,1,0:T(8,128)(2,1)S(1)} %get-tuple-element.69), channel_id=1, source_target_pairs={{2,4},{4,2},{6,8},{8,6},{10,12},{12,10},{3,5},{5,3},{7,9},{9,7},{1... | collective-permute-start | bytes 98312 | tf_op jit(solution)/shard_map/ppermute | solution.py:496
  10.0 5.6 %collective-permute-start.1 = (bf16[4,32,128]{2,1,0:T(8,128)(2,1)S(1)}, bf16[4,32,128]{2,1,0:T(8,128)(2,1)S(1)}, u32[]{:S(2)}, u32[]{:S(2)}) collective-permute-start(bf16[4,32,128]{2,1,0:T(8,128)(2,1)S(1)} %get-tuple-element.70), channel_id=1, source_target_pairs={{0,2},{2,0},{4,6},{6,4},{8,10},{10,8},{12,14},{14,12},{1,3},{3,1},... | collective-permute-start | bytes 98312 | tf_op jit(solution)/shard_map/ppermute | solution.py:496
  16.8 1.8 %collective-permute-start.5 = (bf16[2,2,8,32,128]{4,3,2,1,0:T(8,128)(2,1)S(1)}, bf16[2,2,8,32,128]{4,3,2,1,0:T(8,128)(2,1)S(1)}, u32[]{:S(2)}, u32[]{:S(2)}) collective-permute-start(bf16[2,2,8,32,128]{4,3,2,1,0:T(8,128)(2,1)S(1)} %get-tuple-element.47.own), channel_id=1, source_target_pairs={{0,1},{1,0},{2,3},{3,2},{4,5},{5,4},{6,7},{7,6},{8,9},{9,8},{10,11... | collective-permute-start | bytes 786440 | tf_op jit(solution)/shard_map/ppermute | solution.py:483
  16.9 5.2 %collective-permute-start.6 = (bf16[2,2,32,128]{3,2,1,0:T(8,128)(2,1)S(1)}, bf16[2,2,32,128]{3,2,1,0:T(8,128)(2,1)S(1)}, u32[]{:S(2)}, u32[]{:S(2)}) collective-permute-start(bf16[2,2,32,128]{3,2,1,0:T(8,128)(2,1)S(1)} %get-tuple-element.52), channel_id=1, source_target_pairs={{0,2},{2,0},{4,6},{6,4},{8,10},{10,8},{12,14},{14,12},{1,3},{3,1},... | collective-permute-start | bytes 98312 | tf_op jit(solution)/shard_map/ppermute | solution.py:496
  17.9 4.2 %collective-permute-start.7 = (bf16[2,2,32,128]{3,2,1,0:T(8,128)(2,1)S(1)}, bf16[2,2,32,128]{3,2,1,0:T(8,128)(2,1)S(1)}, u32[]{:S(2)}, u32[]{:S(2)}) collective-permute-start(bf16[2,2,32,128]{3,2,1,0:T(8,128)(2,1)S(1)} %get-tuple-element.53), channel_id=1, source_target_pairs={{2,4},{4,2},{6,8},{8,6},{10,12},{12,10},{3,5},{5,3},{7,9},{9,7},{1... | collective-permute-start | bytes 98312 | tf_op jit(solution)/shard_map/ppermute | solution.py:496
  22.1 1.3 %collective-permute-start.8 = (bf16[2,2,32,128]{3,2,1,0:T(8,128)(2,1)S(1)}, bf16[2,2,32,128]{3,2,1,0:T(8,128)(2,1)S(1)}, u32[]{:S(2)}, u32[]{:S(2)}) collective-permute-start(bf16[2,2,32,128]{3,2,1,0:T(8,128)(2,1)S(1)} %collective-permute-done.6.got_a), channel_id=1, source_target_pairs={{0,1},{1,0},{2,3},{3,2},{4,5},{5,4},{6,7},{7,6},{8,9},{9,8},{10,11... | collective-permute-start | bytes 98312 | tf_op jit(solution)/shard_map/ppermute | solution.py:483
  22.3 1.2 %collective-permute-start.9 = (bf16[2,2,32,128]{3,2,1,0:T(8,128)(2,1)S(1)}, bf16[2,2,32,128]{3,2,1,0:T(8,128)(2,1)S(1)}, u32[]{:S(2)}, u32[]{:S(2)}) collective-permute-start(bf16[2,2,32,128]{3,2,1,0:T(8,128)(2,1)S(1)} %collective-permute-done.7.got_b), channel_id=1, source_target_pairs={{0,1},{1,0},{2,3},{3,2},{4,5},{5,4},{6,7},{7,6},{8,9},{9,8},{10,11... | collective-permute-start | bytes 98312 | tf_op jit(solution)/shard_map/ppermute | solution.py:483
  25.8 1.3 %collective-permute-start.10 = (f32[56,128]{1,0:T(8,128)S(1)}, f32[56,128]{1,0:T(8,128)S(1)}, u32[]{:S(2)}, u32[]{:S(2)}) collective-permute-start(f32[56,128]{1,0:T(8,128)S(1)} %get-tuple-element.62), channel_id=1, source_target_pairs={{0,1},{1,0},{2,3},{3,2},{4,5},{5,4},{6,7},{7,6},{8,9},{9,8},{10,11... | collective-permute-start | bytes 86024 | tf_op jit(solution)/shard_map/ppermute | solution.py:483
  27.0 7.1 %collective-permute-start.14 = (f32[56,128]{1,0:T(8,128)S(1)}, f32[56,128]{1,0:T(8,128)S(1)}, u32[]{:S(2)}, u32[]{:S(2)}) collective-permute-start(f32[56,128]{1,0:T(8,128)S(1)} %add.28), channel_id=1, source_target_pairs={{0,2},{2,0},{4,6},{6,4},{8,10},{10,8},{12,14},{14,12},{1,3},{3,1},... | collective-permute-start | bytes 86024 | tf_op jit(solution)/shard_map/ppermute | solution.py:580
  32.0 7.6 %collective-permute-start.12 = (bf16[64,512]{1,0:T(8,128)(2,1)S(1)}, bf16[64,512]{1,0:T(8,128)(2,1)S(1)}, u32[]{:S(2)}, u32[]{:S(2)}) collective-permute-start(bf16[64,512]{1,0:T(8,128)(2,1)S(1)} %shard_map.92.own), channel_id=1, source_target_pairs={{0,14},{2,12},{4,10},{6,8},{8,6},{10,4},{12,2},{14,0},{1,15},{3,13... | collective-permute-start | bytes 196616 | tf_op jit(solution)/shard_map/ppermute | solution.py:488
  34.2 4.1 %collective-permute-start.15 = (f32[56,128]{1,0:T(8,128)S(1)}, f32[56,128]{1,0:T(8,128)S(1)}, u32[]{:S(2)}, u32[]{:S(2)}) collective-permute-start(f32[56,128]{1,0:T(8,128)S(1)} %add.29), channel_id=1, source_target_pairs={{0,4},{2,6},{4,0},{6,2},{8,12},{10,14},{12,8},{14,10},{1,5},{3,7},... | collective-permute-start | bytes 86024 | tf_op jit(solution)/shard_map/ppermute | solution.py:580
  38.3 4.8 %collective-permute-start.16 = (f32[56,128]{1,0:T(8,128)S(1)}, f32[56,128]{1,0:T(8,128)S(1)}, u32[]{:S(2)}, u32[]{:S(2)}) collective-permute-start(f32[56,128]{1,0:T(8,128)S(1)} %add.30), channel_id=1, source_target_pairs={{0,8},{2,10},{4,12},{6,14},{8,0},{10,2},{12,4},{14,6},{1,9},{3,11}... | collective-permute-start | bytes 86024 | tf_op jit(solution)/shard_map/ppermute | solution.py:580
  39.6 4.1 %collective-permute-start.11 = (bf16[64,512]{1,0:T(8,128)(2,1)S(1)}, bf16[64,512]{1,0:T(8,128)(2,1)S(1)}, u32[]{:S(2)}, u32[]{:S(2)}) collective-permute-start(bf16[64,512]{1,0:T(8,128)(2,1)S(1)} %shard_map.92.own), channel_id=1, source_target_pairs={{0,1},{1,0},{2,3},{3,2},{4,5},{5,4},{6,7},{7,6},{8,9},{9,8},{10,11... | collective-permute-start | bytes 196616 | tf_op jit(solution)/shard_map/ppermute | solution.py:483
  39.6 4.1 %collective-permute-start.13 = (bf16[64,512]{1,0:T(8,128)(2,1)S(1)}, bf16[64,512]{1,0:T(8,128)(2,1)S(1)}, u32[]{:S(2)}, u32[]{:S(2)}) collective-permute-start(bf16[64,512]{1,0:T(8,128)(2,1)S(1)} %collective-permute-done.12.across_x), channel_id=1, source_target_pairs={{0,1},{1,0},{2,3},{3,2},{4,5},{5,4},{6,7},{7,6},{8,9},{9,8},{10,11... | collective-permute-start | bytes 196616 | tf_op jit(solution)/shard_map/ppermute | solution.py:483

commit v6 on v5

--- a/solution.py
+++ b/solution.py
@@ -11,6 +11,7 @@
 F32 = jnp.float32
 CH = 32
 LANES = 128
+HALF = 16
 MID = 8 * LANES
 HIGHEST = lax.Precision.HIGHEST
 TURNS = (0, 63, 7 + 64, 56 + 64)
@@ -155,28 +156,55 @@
         unfold(planes, 8, columns, n * MID)
 
 
-def stage_edge(low, high, own, part, received, far):
+def edge_planes_of(own, part, received, far):
     odd = is_odd()
-    zero = jnp.zeros((CH, LANES), BF)
-    for s in range(2):
-        low[s], high[s] = own(s, 7), own(s, 0)
-        low[2 + s], high[2 + s] = part(s, 7), part(s, 0)
-        for base, faces in ((4, received), (6, far)):
+    low = [f(s, 7) for f in (own, part) for s in range(2)]
+    high = [f(s, 0) for f in (own, part) for s in range(2)]
+    for faces in (received, far):
+        for s in range(2):
             first, second = faces(0, s), faces(1, s)
-            low[base + s] = jnp.where(odd, first, second)
-            high[base + s] = jnp.where(odd, second, first)
-    low[8] = zero
-    high[8] = zero
-
-
-def edge_columns(codes, masks, low, high, columns):
+            low.append(jnp.where(odd, first, second))
+            high.append(jnp.where(odd, second, first))
+    return [[plane.reshape(2, HALF, LANES) for plane in side] for side in (low, high)]
+
+
+def edge_columns(choose, masks, candidates, columns):
     def pieces(o):
         found = []
-        for n in range(2):
-            found += [low[table_row(codes, n, o, 8)], high[table_row(codes, n, 18 + o, 8)]]
+        for e in range(4):
+            total = None
+            for r, plane in enumerate(candidates[e & 1]):
+                term = plane * choose[8 * (9 * e + o) + r]
+                total = term if total is None else total + term
+            found.append(total.reshape(CH, LANES))
         return found
 
     unfold(gathered(pieces, masks), 4, columns, 0)
+
+
+def write_choices(codes, mirror, choose, turn_choice):
+    d = codes >> 1
+    dx = (d * 11) >> 5
+    other = jnp.where(d - 3 * dx == 1, 0, 2) + jnp.where(dx == 1, 0, 4)
+    row = jnp.where(codes >= 18, -1, other + (codes & 1))
+    shape = (HALF, LANES)
+    for e in range(4):
+        n = e >> 1
+        for o in range(9):
+            at = o + 18 * (e & 1)
+            wide = jnp.broadcast_to(row[n : n + 1, at : at + 1], shape)
+            for r in range(8):
+                choose[8 * (9 * e + o) + r] = one(wide == r)
+    for n in range(2):
+        for r in range(3):
+            wide = jnp.broadcast_to(mirror[n : n + 1, r : r + 1], shape)
+            turn_choice[3 * n + r] = wide.astype(F32).astype(BF)
+
+
+def chosen(turn_choice, n, r, first, second):
+    tile = jnp.concatenate([turn_choice[3 * n + r - 1]] * 4, axis=1)
+    slot = jnp.concatenate([tile, tile], axis=0)[: first.shape[0]]
+    return second * slot + first * (1.0 - slot).astype(BF)
 
 
 def fold_mid(stacked, row):
@@ -216,7 +244,7 @@
             fp[n, x] = planes[first : first + CH, (x & 1) * LANES : (x & 1) * LANES + LANES]
 
 
-def weights_kernel(packed, small, one_out, two_out, turned_out, codes_out, mirror_out, padded, left):
+def weights_kernel(packed, small, one_out, two_out, turned_out, codes_out, choose, turn_choice, padded, left):
     shape = (CH, LANES)
     i, c = iota(shape, 0), iota(shape, 1)
     double = jnp.where(i >= 20, 2.0, 1.0)
@@ -233,7 +261,7 @@
     for which in range(2):
         padded[which, 0:27, 0:84] = packed[0:27, which * LANES : which * LANES + 84].astype(F32)
     codes_out[...] = small[:, 0:27]
-    mirror_out[...] = small[:, LANES : LANES + 3]
+    write_choices(small[:, 0:LANES], small[:, LANES : 2 * LANES], choose, turn_choice)
     for which, rows, columns, blocks, out, base, flip in (
         (0, rows_out, by_in, True, one_out, 0, False),
         (0, rows_gate, by_in, False, one_out, 96, False),
@@ -279,15 +307,15 @@
     return dot(jnp.concatenate(rows, axis=0), table) * 0.25
 
 
-def back_kernel(mirror, own, across_y, crossed, back, staged):
+def back_kernel(turn_choice, own, across_y, crossed, back, staged):
     zero2 = jnp.zeros((2, 512), BF)
     for n in range(2):
         for r in range(4):
             if r == 0:
                 value = own[n]
             else:
-                slot = mirror[n, r - 1]
-                value = (across_y[slot] if r == 1 else crossed[2 * (r - 2) + slot]) * turn_signs(r, (30, 512))
+                first, second = (across_y[0], across_y[1]) if r == 1 else (crossed[2 * r - 4], crossed[2 * r - 3])
+                value = chosen(turn_choice, n, r, first, second) * turn_signs(r, (30, 512))
             staged[r, n * CH : n * CH + 30, :] = value
             staged[r, n * CH + 30 : (n + 1) * CH, :] = zero2
     planes = turned_sum(staged, turns_spread_table()).astype(BF)
@@ -298,16 +326,16 @@
 
 
 def first_edge_kernel(
-    codes, own, part, got_a, got_b, pre, gate_in, hidden_mid, back, w_first,
-    columns, pre_edge, gate_edge, both, face_a, face_b, low, high,
+    choose, own, part, got_a, got_b, pre, gate_in, hidden_mid, back, w_first,
+    columns, pre_edge, gate_edge, both, face_a, face_b,
 ):
     masks = region_masks()
     inside = jnp.concatenate([masks[4].astype(F32)] * 4, axis=1)
-    stage_edge(
-        low, high, lambda s, x: own[s, x], lambda s, x: part[s, x],
+    candidates = edge_planes_of(
+        lambda s, x: own[s, x], lambda s, x: part[s, x],
         lambda which, s: (got_a, got_b)[which][s], lambda which, s: (got_a, got_b)[which][2 + s],
     )
-    edge_columns(codes, masks, low, high, columns)
+    edge_columns(choose, masks, candidates, columns)
     stacked = dot(w_first[...], columns[...])
     a = edge_planes(pre) + edge_terms(stacked, 0)
     g = edge_planes(gate_in) + edge_terms(stacked, 96)
@@ -374,18 +402,18 @@
 
 
 def second_edge_kernel(
-    scale, codes, own, part, got_a, got_b, far_a, far_b, pre_edge, gate_edge, through_edge,
+    scale, choose, own, part, got_a, got_b, far_a, far_b, pre_edge, gate_edge, through_edge,
     columns_f, columns_fe, raw, w_second, w_turned, second_edge, grads,
-    low, high, columns_h, columns_b, placed_f, placed_s, place,
+    columns_h, columns_b, placed_f, placed_s, place,
 ):
     masks = region_masks()
     inside = jnp.concatenate([masks[4].astype(F32)] * 4, axis=1)
     for f, columns in ((0, columns_h), (1, columns_b)):
-        stage_edge(
-            low.at[f], high.at[f], lambda s, x: own[f, s, x], lambda s, x: part[f, s, x],
+        candidates = edge_planes_of(
+            lambda s, x: own[f, s, x], lambda s, x: part[f, s, x],
             lambda which, s: (got_a, got_b)[which][f, s], lambda which, s: (far_a, far_b)[which][f, s],
         )
-        edge_columns(codes, masks, low.at[f], high.at[f], columns)
+        edge_columns(choose, masks, candidates, columns)
     second_edge[...] = edge_terms(dot(w_second[...], columns_h[...]), 0)
     more_t = edge_terms(dot(w_turned[...], columns_b[...]), 0)
     back_pre = gate_back(through_edge[...] + more_t, pre_edge[...], gate_edge[...], gate_rows(), inside)
@@ -449,12 +477,12 @@
             second[n * CH : (n + 1) * CH, k * LANES : (k + 1) * LANES] = packed[first : first + CH]
 
 
-def turn_kernel(mirror, own, across_y, across_x, across, out, staged):
+def turn_kernel(turn_choice, own, across_y, across_x, across, out, staged):
     for n in range(2):
         staged[0, n * CH : (n + 1) * CH, :] = own[n * CH : (n + 1) * CH, :]
         for r, ref in ((1, across_y), (2, across_x), (3, across)):
-            at = pl.multiple_of(mirror[n, r - 1] * CH, CH)
-            staged[r, n * CH : (n + 1) * CH, :] = ref[pl.ds(at, CH), :] * turn_signs(r, (CH, 512))
+            value = chosen(turn_choice, n, r, ref[0:CH, :], ref[CH : 2 * CH, :])
+            staged[r, n * CH : (n + 1) * CH, :] = value * turn_signs(r, (CH, 512))
     result = turned_sum(staged, turns_table()).astype(BF)
     for k in range(4):
         for n in range(2):
@@ -524,9 +552,12 @@
     odd = is_odd()
     got = exchange(jnp.where(odd, low, high), jnp.where(odd, high, low))
     w_first, w_second, codes, mirror = after((w_first, w_second, codes, mirror), part)
-    w1, w2, w2t, codes, mirror = call(
+    w1, w2, w2t, codes, choose, turn_choice = call(
         weights_kernel, 1, 0,
-        [((192, 288), BF), ((96, 288), BF), ((96, 288), BF), *((x.shape, x.dtype) for x in (codes, mirror))],
+        [
+            ((192, 288), BF), ((96, 288), BF), ((96, 288), BF), (codes.shape, codes.dtype),
+            ((288, HALF, LANES), BF), ((6, HALF, LANES), BF),
+        ],
         [((2, CH, LANES), F32), ((288, LANES), BF)],
         side_by_side((w_first, w_second), CH), side_by_side((codes, mirror), 2),
     )
@@ -537,16 +568,16 @@
     )
     (crossed,) = after((crossed,), hidden_mid)
     (back,) = call(
-        back_kernel, 0.8, 1, [((2, 8) + plane, BF)], [((4, 64, 512), BF)], mirror, cotangent, cot_y, crossed
+        back_kernel, 0.8, 0, [((2, 8) + plane, BF)], [((4, 64, 512), BF)], turn_choice, cotangent, cot_y, crossed
     )
     got = after(got, hidden_mid, back)
     columns_e, pre_e, gate_e, both, face_a, face_b = call(
-        first_edge_kernel, 1.2, 1,
+        first_edge_kernel, 1, 0,
         [
             ((288, 4 * LANES), BF), ((CH, 4 * LANES), F32), ((CH, 4 * LANES), F32), ((2, 2, 8) + plane, BF),
             ((2, 2) + plane, BF), ((2, 2) + plane, BF),
         ],
-        [((9,) + plane, BF)] * 2, codes, fp, part, *got, pre, gate_in, hidden_mid, back, w1,
+        [], choose, fp, part, *got, pre, gate_in, hidden_mid, back, w1,
     )
     got = exchange(face_a, face_b)
     part = swap_y(both)
@@ -559,10 +590,10 @@
     faces = (*got, swap_y(got[0]), swap_y(got[1]))
     n_bricks = features.shape[0] * lax.axis_size("xp") * lax.axis_size("yp")
     second_e, grads = call(
-        functools.partial(second_edge_kernel, 1.0 / n_bricks), 2, 1, [((CH, 4 * LANES), F32), ((56, LANES), F32)],
-        [((2, 9) + plane, BF)] * 2 + [((288, 4 * LANES), BF)] * 2
+        functools.partial(second_edge_kernel, 1.0 / n_bricks), 2, 0, [((CH, 4 * LANES), F32), ((56, LANES), F32)],
+        [((288, 4 * LANES), BF)] * 2
         + [((128, 12 * LANES), BF), ((128, 4 * LANES), BF), ((256, 3 * LANES), BF)],
-        codes, both, part, *faces, pre_e, gate_e, through_e, columns, columns_e, raw, w2, w2t,
+        choose, both, part, *faces, pre_e, gate_e, through_e, columns, columns_e, raw, w2, w2t,
     )
     total = grads + swap_y(grads)
     second_part, second_e = after((second_part, second_e), total)
@@ -571,7 +602,7 @@
     second_x = mirror_x(second)
     second_xy = swap_y(second_x)
     (denoised,) = call(
-        turn_kernel, 0.9, 1, [((30, 2, 512), BF)], [((4, 64, 512), BF)], mirror, second, second_y, second_x, second_xy
+        turn_kernel, 0.9, 0, [((30, 2, 512), BF)], [((4, 64, 512), BF)], turn_choice, second, second_y, second_x, second_xy
     )
     denoised = denoised.transpose(1, 0, 2)
     n = lax.axis_size("xp")

time: 45.4 us -> 44.1 us (0.971)
  Pallas kernels: 11.9 us -> 10.4 us
    pallas_call x9, Pallas kernels: 11.9 us -> 10.4 us  [call(): pl.pallas_call(kernel, out_shape=tuple((jax.ShapeDtypeStruct(s, t) for s,...]
  transfers between devices with their start and end apart: 17 -> 17, of which waited for: 5 -> 5; matrix products, arithmetic and copies ran while one was open for 3% -> 4% of each run, Pallas kernels for 16% -> 15%
where the time goes in v6:
time: 44.1 us; the launch traced here: 43.9 us
  starting transfers between devices  22.8 us (52%)
  Pallas kernels  10.4 us (24%)
  waiting for transfers between devices  7.44 us (17%)
  local copies, waits for them, and re-layouts  2.36 us (5%)
  between operations  0.87 us (2%)
    pallas_call x9, Pallas kernels, call(): pl.pallas_call(kernel, out_shape=tuple((jax.ShapeDtypeStruct(s, t) for s,...  10.4 us
    ppermute x2, starting transfers between devices, mirror_x(): return lax.ppermute(x, 'xp', [(i, n - 1 - i) for i in range(n)])  8.05 us
    ppermute x3, starting transfers between devices, on_device(): total = total + lax.ppermute(total, 'xp', [(i, i ^ bit) for i in range(n)])  7.36 us
    ppermute x3, waiting for transfers between devices, on_device(): total = total + lax.ppermute(total, 'xp', [(i, i ^ bit) for i in range(n)])  5.69 us
    ppermute x4, starting transfers between devices, pair_swap(): return lax.ppermute(x, 'xp', pairs)  5.17 us
    ppermute x8, starting transfers between devices, swap_y(): return lax.ppermute(x, 'yp', [(i, n - 1 - i) for i in range(n)])  2.2 us
    ppermute x8, waiting for transfers between devices, swap_y(): return lax.ppermute(x, 'yp', [(i, n - 1 - i) for i in range(n)])  1.73 us
    unnamed x10, local copies, waits for them, and re-layouts  1.72 us
  transfers between devices with their start and end apart: 17, of which 5 were waited for; matrix products, arithmetic and copies ran while one was open for 4% of the time, Pallas kernels for 15%

profile of v6, /device:TPU:0, one launch (start us, length us, event | category | flops | bytes accessed | tf_op | source)
XLA Modules:
  0.0 43.9 jit_solution(7590695395985517799)
XLA Ops:
  0.7 0.9 %copy.16.own = bf16[2,30,512]{2,1,0:T(8,128)(2,1)S(1)} copy(bf16[2,30,512]{2,0,1:T(2,128)(2,1)} %param.7) | data formatting | bytes 122880 | tf_op args[1]
  1.5 0.5 %collective-permute-start.3 = (bf16[2,30,512]{2,1,0:T(8,128)(2,1)S(1)}, bf16[2,30,512]{2,1,0:T(8,128)(2,1)S(1)}, u32[]{:S(2)}, u32[]{:S(2)}) collective-permute-start(bf16[2,30,512]{2,1,0:T(8,128)(2,1)S(1)} %copy.16.own), channel_id=1, source_target_pairs={{0,1},{1,0},{2,3},{3,2},{4,5},{5,4},{6,7},{7,6},{8,9},{9,8},{10,11... | collective-permute-start | bytes 184328 | tf_op jit(solution)/shard_map/ppermute | solution.py:511
  2.1 0.8 %copy.9.features = bf16[2,30,512]{2,1,0:T(8,128)(2,1)S(1)} copy(bf16[2,30,512]{2,0,1:T(2,128)(2,1)} %param.6) | data formatting | bytes 122880 | tf_op args[0]
  2.9 0.2 shard_map.85.own
  3.1 0.1 collective-permute-start
  3.3 6.1 %collective-permute-start.4 = (bf16[4,30,512]{2,1,0:T(8,128)(2,1)S(1)}, bf16[4,30,512]{2,1,0:T(8,128)(2,1)S(1)}, u32[]{:S(2)}, u32[]{:S(2)}) collective-permute-start(bf16[4,30,512]{2,1,0:T(8,128)(2,1)S(1)} %pad_maximum_fusion), channel_id=1, source_target_pairs={{0,14},{2,12},{4,10},{6,8},{8,6},{10,4},{12,2},{14,0},{1,15},{3,13... | collective-permute-start | bytes 368648 | tf_op jit(solution)/shard_map/ppermute | solution.py:516
  9.3 0.7 %collective-permute-start.2 = (bf16[4,32,128]{2,1,0:T(8,128)(2,1)S(1)}, bf16[4,32,128]{2,1,0:T(8,128)(2,1)S(1)}, u32[]{:S(2)}, u32[]{:S(2)}) collective-permute-start(bf16[4,32,128]{2,1,0:T(8,128)(2,1)S(1)} %get-tuple-element.71), channel_id=1, source_target_pairs={{2,4},{4,2},{6,8},{8,6},{10,12},{12,10},{3,5},{5,3},{7,9},{9,7},{1... | collective-permute-start | bytes 98312 | tf_op jit(solution)/shard_map/ppermute | solution.py:524
  10.0 2.3 %collective-permute-start.1 = (bf16[4,32,128]{2,1,0:T(8,128)(2,1)S(1)}, bf16[4,32,128]{2,1,0:T(8,128)(2,1)S(1)}, u32[]{:S(2)}, u32[]{:S(2)}) collective-permute-start(bf16[4,32,128]{2,1,0:T(8,128)(2,1)S(1)} %get-tuple-element.72), channel_id=1, source_target_pairs={{0,2},{2,0},{4,6},{6,4},{8,10},{10,8},{12,14},{14,12},{1,3},{3,1},... | collective-permute-start | bytes 98312 | tf_op jit(solution)/shard_map/ppermute | solution.py:524
  12.4 0.5 %shard_map.86 = (bf16[192,288]{1,0:T(8,128)(2,1)S(1)}, bf16[96,288]{1,0:T(8,128)(2,1)S(1)}, bf16[96,288]{1,0:T(8,128)(2,1)S(1)}, s32[2,27]{1,0:T(2,128)S(1)}, bf...) custom-call(bf16[32,256]{1,0:T(8,128)(2,1)S(1)} %pad_add_fusion.packed, s32[2,256]{1,0:T(2,128)S(1)} %pad_add_fusion.1.small), custom_call_target="tpu_custom_call" | custom-call | bytes 3000000 | tf_op jit(solution)/shard_map/pallas_call | solution.py:498
  12.9 1.9 %shard_map.87 = (bf16[288,2048]{1,0:T(8,128)(2,1)S(1)}, f32[2,32,1024]{2,1,0:T(8,128)S(1)}, f32[2,32,1024]{2,1,0:T(8,128)S(1)}, bf16[2,6,32,128]{3,2,1,0:T(8,128)(2,1)S(1)}) custom-call(s32[2,27]{1,0:T(2,128)S(1)} %get-tuple-element.40.codes, bf16[2,8,32,128]{3,2,1,0:T(8,128)(2,1)S(1)} %shard_map.85.own, bf16[2,8,32,128]{3,2,1,0:T(8,128)(2,1)S(1)} %copy.17.part, ...), custom_call_target="tpu_custom_call" | custom-call | bytes 6000000 | tf_op jit(solution)/shard_map/pallas_call | solution.py:498
  14.8 0.3 shard_map.88.back
  15.1 0.8 %shard_map.89 = (bf16[288,512]{1,0:T(8,128)(2,1)S(1)}, f32[32,512]{1,0:T(8,128)S(1)}, f32[32,512]{1,0:T(8,128)S(1)}, bf16[2,2,8,32,128]{4,3,2,1,0:T(8,128)(2,1)S...) custom-call(bf16[288,16,128]{2,1,0:T(8,128)(2,1)S(1)} %get-tuple-element.41.choose, ...), custom_call_target="tpu_custom_call" | custom-call | bytes 3000000 | tf_op jit(solution)/shard_map/pallas_call | solution.py:498
  16.0 1.5 %collective-permute-start.6 = (bf16[2,2,32,128]{3,2,1,0:T(8,128)(2,1)S(1)}, bf16[2,2,32,128]{3,2,1,0:T(8,128)(2,1)S(1)}, u32[]{:S(2)}, u32[]{:S(2)}) collective-permute-start(bf16[2,2,32,128]{3,2,1,0:T(8,128)(2,1)S(1)} %get-tuple-element.54), channel_id=1, source_target_pairs={{0,2},{2,0},{4,6},{6,4},{8,10},{10,8},{12,14},{14,12},{1,3},{3,1},... | collective-permute-start | bytes 98312 | tf_op jit(solution)/shard_map/ppermute | solution.py:524
  17.6 0.7 %collective-permute-start.7 = (bf16[2,2,32,128]{3,2,1,0:T(8,128)(2,1)S(1)}, bf16[2,2,32,128]{3,2,1,0:T(8,128)(2,1)S(1)}, u32[]{:S(2)}, u32[]{:S(2)}) collective-permute-start(bf16[2,2,32,128]{3,2,1,0:T(8,128)(2,1)S(1)} %get-tuple-element.55), channel_id=1, source_target_pairs={{2,4},{4,2},{6,8},{8,6},{10,12},{12,10},{3,5},{5,3},{7,9},{9,7},{1... | collective-permute-start | bytes 98312 | tf_op jit(solution)/shard_map/ppermute | solution.py:524
  18.2 3.5 %shard_map.90 = (f32[2,32,1024]{2,1,0:T(8,128)S(1)}, f32[32,512]{1,0:T(8,128)S(1)}, f32[2,288,128]{2,1,0:T(8,128)S(1)}) custom-call(s32[2,27]{1,0:T(2,128)S(1)} %get-tuple-element.40.codes, bf16[2,2,8,32,128]{4,3,2,1,0:T(8,128)(2,1)S(1)} %get-tuple-element.49.own, bf16[2,2,8,32,128]{4,3,2,1,0:T(8,128)(2,1)S(1)} %collective-permute-done.5.part, ...), custom_call_target="tpu_custom_call" | custom-call | bytes 10500000 | tf_op jit(solution)/shard_map/pallas_call | solution.py:498
  21.7 0.2 collective-permute-start.8
  22.0 0.3 collective-permute-start.9
  22.3 0.7 %collective-permute-done.8.far_a = bf16[2,2,32,128]{3,2,1,0:T(8,128)(2,1)S(1)} collective-permute-done((bf16[2,2,32,128]{3,2,1,0:T(8,128)(2,1)S(1)}, bf16[2,2,32,128]{3,2,1,0:T(8,128)(2,1)S(1)}, u32[]{:S(2)}, u32[]{:S(2)}) %collective-permute-start.8) | collective-permute-done | bytes 32800 | tf_op jit(solution)/shard_map/ppermute | solution.py:511
  23.0 0.2 collective-permute-done.9.far_b
  23.2 2.0 %shard_map.91 = (f32[32,512]{1,0:T(8,128)S(1)}, f32[56,128]{1,0:T(8,128)S(1)}) custom-call(bf16[288,16,128]{2,1,0:T(8,128)(2,1)S(1)} %get-tuple-element.41.choose, bf16[2,2,8,32,128]{4,3,2,1,0:T(8,128)(2,1)S(1)} %get-tuple-element.49.own, bf16[2,2,8,32,128]{4,3,2,1,0:T(8,128)(2,1)S(1)} %collective-permute-done.5.part, ...), custom_call_target="tpu_custom_call" | custom-call | bytes 6000000 | tf_op jit(solution)/shard_map/pallas_call | solution.py:498
  25.2 0.4 collective-permute-start.10
  25.6 0.9 %collective-permute-done.10 = f32[56,128]{1,0:T(8,128)S(1)} collective-permute-done((f32[56,128]{1,0:T(8,128)S(1)}, f32[56,128]{1,0:T(8,128)S(1)}, u32[]{:S(2)}, u32[]{:S(2)}) %collective-permute-start.10) | collective-permute-done | bytes 28704 | tf_op jit(solution)/shard_map/ppermute | solution.py:511
  26.5 4.5 %collective-permute-start.14 = (f32[56,128]{1,0:T(8,128)S(1)}, f32[56,128]{1,0:T(8,128)S(1)}, u32[]{:S(2)}, u32[]{:S(2)}) collective-permute-start(f32[56,128]{1,0:T(8,128)S(1)} %add.28), channel_id=1, source_target_pairs={{0,2},{2,0},{4,6},{6,4},{8,10},{10,8},{12,14},{14,12},{1,3},{3,1},... | collective-permute-start | bytes 86024 | tf_op jit(solution)/shard_map/ppermute | solution.py:611
  31.0 0.2 shard_map.92.own
  31.2 2.0 %collective-permute-start.12 = (bf16[64,512]{1,0:T(8,128)(2,1)S(1)}, bf16[64,512]{1,0:T(8,128)(2,1)S(1)}, u32[]{:S(2)}, u32[]{:S(2)}) collective-permute-start(bf16[64,512]{1,0:T(8,128)(2,1)S(1)} %shard_map.92.own), channel_id=1, source_target_pairs={{0,14},{2,12},{4,10},{6,8},{8,6},{10,4},{12,2},{14,0},{1,15},{3,13... | collective-permute-start | bytes 196616 | tf_op jit(solution)/shard_map/ppermute | solution.py:516
  33.2 1.4 %collective-permute-start.15 = (f32[56,128]{1,0:T(8,128)S(1)}, f32[56,128]{1,0:T(8,128)S(1)}, u32[]{:S(2)}, u32[]{:S(2)}) collective-permute-start(f32[56,128]{1,0:T(8,128)S(1)} %add.29), channel_id=1, source_target_pairs={{0,4},{2,6},{4,0},{6,2},{8,12},{10,14},{12,8},{14,10},{1,5},{3,7},... | collective-permute-start | bytes 86024 | tf_op jit(solution)/shard_map/ppermute | solution.py:611
  34.6 2.9 %collective-permute-done.15 = f32[56,128]{1,0:T(8,128)S(1)} collective-permute-done((f32[56,128]{1,0:T(8,128)S(1)}, f32[56,128]{1,0:T(8,128)S(1)}, u32[]{:S(2)}, u32[]{:S(2)}) %collective-permute-start.15) | collective-permute-done | bytes 28704 | tf_op jit(solution)/shard_map/ppermute | solution.py:611
  37.5 1.5 %collective-permute-start.16 = (f32[56,128]{1,0:T(8,128)S(1)}, f32[56,128]{1,0:T(8,128)S(1)}, u32[]{:S(2)}, u32[]{:S(2)}) collective-permute-start(f32[56,128]{1,0:T(8,128)S(1)} %add.30), channel_id=1, source_target_pairs={{0,8},{2,10},{4,12},{6,14},{8,0},{10,2},{12,4},{14,6},{1,9},{3,11}... | collective-permute-start | bytes 86024 | tf_op jit(solution)/shard_map/ppermute | solution.py:611
  39.0 0.5 %collective-permute-start.13 = (bf16[64,512]{1,0:T(8,128)(2,1)S(1)}, bf16[64,512]{1,0:T(8,128)(2,1)S(1)}, u32[]{:S(2)}, u32[]{:S(2)}) collective-permute-start(bf16[64,512]{1,0:T(8,128)(2,1)S(1)} %collective-permute-done.12.across_x), channel_id=1, source_target_pairs={{0,1},{1,0},{2,3},{3,2},{4,5},{5,4},{6,7},{7,6},{8,9},{9,8},{10,11... | collective-permute-start | bytes 196616 | tf_op jit(solution)/shard_map/ppermute | solution.py:511
  39.5 2.8 %collective-permute-done.16 = f32[56,128]{1,0:T(8,128)S(1)} collective-permute-done((f32[56,128]{1,0:T(8,128)S(1)}, f32[56,128]{1,0:T(8,128)S(1)}, u32[]{:S(2)}, u32[]{:S(2)}) %collective-permute-start.16) | collective-permute-done | bytes 28704 | tf_op jit(solution)/shard_map/ppermute | solution.py:611
  42.3 0.6 %fusion = (f32[27,84]{1,0:T(8,128)}, f32[27,84]{1,0:T(8,128)}) fusion(f32[56,128]{1,0:T(8,128)S(1)} %add.31), kind=kLoop, calls=%fused_computation.11 | loop fusion | bytes 36288 | tf_op jit(solution)/shard_map/slice | solution.py:613
  42.9 0.9 %shard_map.93 = bf16[30,2,512]{2,1,0:T(2,128)(2,1)} custom-call(bf16[6,16,128]{2,1,0:T(8,128)(2,1)S(1)} %get-tuple-element.39.turn_choice, bf16[64,512]{1,0:T(8,128)(2,1)S(1)} %shard_map.92.own, bf16[64,512]{1,0:T(8,128)(2,1)S(1)} %collective-permute-done.11.across_y, bf16[64,512]{1,0:T(8,128)(2,1)S(1)} %collective-permute-done.12.across_x, ...), custom_call_target="tpu_custom_call" | custom-call | bytes 2700000 | tf_op jit(solution)/shard_map/pallas_call | solution.py:498
  (34 shorter events, 0.2 us)
Async XLA Ops:
  0.6 11.7 %copy-start.2 = (s32[2,3]{1,0:T(2,128)S(1)}, s32[2,3]{1,0:T(2,128)}, u32[]{:S(2)}) copy-start(s32[2,3]{1,0:T(2,128)} %param.11) | copy-start | bytes 76
  0.6 11.7 %copy-start.3 = (s32[2,27]{1,0:T(2,128)S(1)}, s32[2,27]{1,0:T(2,128)}, u32[]{:S(2)}) copy-start(s32[2,27]{1,0:T(2,128)} %param.10) | copy-start | bytes 652
  0.7 11.7 %copy-start = (bf16[27,84]{1,0:T(8,128)(2,1)S(1)}, bf16[27,84]{1,0:T(8,128)(2,1)}, u32[]{:S(2)}) copy-start(bf16[27,84]{1,0:T(8,128)(2,1)} %param.9) | copy-start | bytes 13612
  0.7 11.7 %copy-start.1 = (bf16[27,84]{1,0:T(8,128)(2,1)S(1)}, bf16[27,84]{1,0:T(8,128)(2,1)}, u32[]{:S(2)}) copy-start(bf16[27,84]{1,0:T(8,128)(2,1)} %param.8) | copy-start | bytes 13612
  1.5 1.7 %collective-permute-start.3 = (bf16[2,30,512]{2,1,0:T(8,128)(2,1)S(1)}, bf16[2,30,512]{2,1,0:T(8,128)(2,1)S(1)}, u32[]{:S(2)}, u32[]{:S(2)}) collective-permute-start(bf16[2,30,512]{2,1,0:T(8,128)(2,1)S(1)} %copy.16.own), channel_id=1, source_target_pairs={{0,1},{1,0},{2,3},{3,2},{4,5},{5,4},{6,7},{7,6},{8,9},{9,8},{10,11... | collective-permute-start | bytes 184328 | tf_op jit(solution)/shard_map/ppermute | solution.py:511
  3.1 6.2 %collective-permute-start = (bf16[2,8,32,128]{3,2,0,1:T(8,128)(2,1)S(1)}, bf16[2,8,32,128]{3,2,0,1:T(8,128)(2,1)S(1)}, u32[]{:S(2)}, u32[]{:S(2)}) collective-permute-start(bf16[2,8,32,128]{3,2,0,1:T(8,128)(2,1)S(1)} %copy.10), channel_id=1, source_target_pairs={{0,1},{1,0},{2,3},{3,2},{4,5},{5,4},{6,7},{7,6},{8,9},{9,8},{10,11... | collective-permute-start | bytes 393224 | tf_op jit(solution)/shard_map/ppermute | solution.py:511
  3.3 11.6 %collective-permute-start.4 = (bf16[4,30,512]{2,1,0:T(8,128)(2,1)S(1)}, bf16[4,30,512]{2,1,0:T(8,128)(2,1)S(1)}, u32[]{:S(2)}, u32[]{:S(2)}) collective-permute-start(bf16[4,30,512]{2,1,0:T(8,128)(2,1)S(1)} %pad_maximum_fusion), channel_id=1, source_target_pairs={{0,14},{2,12},{4,10},{6,8},{8,6},{10,4},{12,2},{14,0},{1,15},{3,13... | collective-permute-start | bytes 368648 | tf_op jit(solution)/shard_map/ppermute | solution.py:516
  9.3 5.8 %collective-permute-start.2 = (bf16[4,32,128]{2,1,0:T(8,128)(2,1)S(1)}, bf16[4,32,128]{2,1,0:T(8,128)(2,1)S(1)}, u32[]{:S(2)}, u32[]{:S(2)}) collective-permute-start(bf16[4,32,128]{2,1,0:T(8,128)(2,1)S(1)} %get-tuple-element.71), channel_id=1, source_target_pairs={{2,4},{4,2},{6,8},{8,6},{10,12},{12,10},{3,5},{5,3},{7,9},{9,7},{1... | collective-permute-start | bytes 98312 | tf_op jit(solution)/shard_map/ppermute | solution.py:524
  10.0 5.1 %collective-permute-start.1 = (bf16[4,32,128]{2,1,0:T(8,128)(2,1)S(1)}, bf16[4,32,128]{2,1,0:T(8,128)(2,1)S(1)}, u32[]{:S(2)}, u32[]{:S(2)}) collective-permute-start(bf16[4,32,128]{2,1,0:T(8,128)(2,1)S(1)} %get-tuple-element.72), channel_id=1, source_target_pairs={{0,2},{2,0},{4,6},{6,4},{8,10},{10,8},{12,14},{14,12},{1,3},{3,1},... | collective-permute-start | bytes 98312 | tf_op jit(solution)/shard_map/ppermute | solution.py:524
  16.0 2.3 %collective-permute-start.5 = (bf16[2,2,8,32,128]{4,3,2,1,0:T(8,128)(2,1)S(1)}, bf16[2,2,8,32,128]{4,3,2,1,0:T(8,128)(2,1)S(1)}, u32[]{:S(2)}, u32[]{:S(2)}) collective-permute-start(bf16[2,2,8,32,128]{4,3,2,1,0:T(8,128)(2,1)S(1)} %get-tuple-element.49.own), channel_id=1, source_target_pairs={{0,1},{1,0},{2,3},{3,2},{4,5},{5,4},{6,7},{7,6},{8,9},{9,8},{10,11... | collective-permute-start | bytes 786440 | tf_op jit(solution)/shard_map/ppermute | solution.py:511
  16.0 5.7 %collective-permute-start.6 = (bf16[2,2,32,128]{3,2,1,0:T(8,128)(2,1)S(1)}, bf16[2,2,32,128]{3,2,1,0:T(8,128)(2,1)S(1)}, u32[]{:S(2)}, u32[]{:S(2)}) collective-permute-start(bf16[2,2,32,128]{3,2,1,0:T(8,128)(2,1)S(1)} %get-tuple-element.54), channel_id=1, source_target_pairs={{0,2},{2,0},{4,6},{6,4},{8,10},{10,8},{12,14},{14,12},{1,3},{3,1},... | collective-permute-start | bytes 98312 | tf_op jit(solution)/shard_map/ppermute | solution.py:524
  17.6 4.2 %collective-permute-start.7 = (bf16[2,2,32,128]{3,2,1,0:T(8,128)(2,1)S(1)}, bf16[2,2,32,128]{3,2,1,0:T(8,128)(2,1)S(1)}, u32[]{:S(2)}, u32[]{:S(2)}) collective-permute-start(bf16[2,2,32,128]{3,2,1,0:T(8,128)(2,1)S(1)} %get-tuple-element.55), channel_id=1, source_target_pairs={{2,4},{4,2},{6,8},{8,6},{10,12},{12,10},{3,5},{5,3},{7,9},{9,7},{1... | collective-permute-start | bytes 98312 | tf_op jit(solution)/shard_map/ppermute | solution.py:524
  21.7 1.3 %collective-permute-start.8 = (bf16[2,2,32,128]{3,2,1,0:T(8,128)(2,1)S(1)}, bf16[2,2,32,128]{3,2,1,0:T(8,128)(2,1)S(1)}, u32[]{:S(2)}, u32[]{:S(2)}) collective-permute-start(bf16[2,2,32,128]{3,2,1,0:T(8,128)(2,1)S(1)} %collective-permute-done.6.got_a), channel_id=1, source_target_pairs={{0,1},{1,0},{2,3},{3,2},{4,5},{5,4},{6,7},{7,6},{8,9},{9,8},{10,11... | collective-permute-start | bytes 98312 | tf_op jit(solution)/shard_map/ppermute | solution.py:511
  22.0 1.2 %collective-permute-start.9 = (bf16[2,2,32,128]{3,2,1,0:T(8,128)(2,1)S(1)}, bf16[2,2,32,128]{3,2,1,0:T(8,128)(2,1)S(1)}, u32[]{:S(2)}, u32[]{:S(2)}) collective-permute-start(bf16[2,2,32,128]{3,2,1,0:T(8,128)(2,1)S(1)} %collective-permute-done.7.got_b), channel_id=1, source_target_pairs={{0,1},{1,0},{2,3},{3,2},{4,5},{5,4},{6,7},{7,6},{8,9},{9,8},{10,11... | collective-permute-start | bytes 98312 | tf_op jit(solution)/shard_map/ppermute | solution.py:511
  25.2 1.3 %collective-permute-start.10 = (f32[56,128]{1,0:T(8,128)S(1)}, f32[56,128]{1,0:T(8,128)S(1)}, u32[]{:S(2)}, u32[]{:S(2)}) collective-permute-start(f32[56,128]{1,0:T(8,128)S(1)} %get-tuple-element.64), channel_id=1, source_target_pairs={{0,1},{1,0},{2,3},{3,2},{4,5},{5,4},{6,7},{7,6},{8,9},{9,8},{10,11... | collective-permute-start | bytes 86024 | tf_op jit(solution)/shard_map/ppermute | solution.py:511
  26.5 6.7 %collective-permute-start.14 = (f32[56,128]{1,0:T(8,128)S(1)}, f32[56,128]{1,0:T(8,128)S(1)}, u32[]{:S(2)}, u32[]{:S(2)}) collective-permute-start(f32[56,128]{1,0:T(8,128)S(1)} %add.28), channel_id=1, source_target_pairs={{0,2},{2,0},{4,6},{6,4},{8,10},{10,8},{12,14},{14,12},{1,3},{3,1},... | collective-permute-start | bytes 86024 | tf_op jit(solution)/shard_map/ppermute | solution.py:611
  31.2 7.8 %collective-permute-start.12 = (bf16[64,512]{1,0:T(8,128)(2,1)S(1)}, bf16[64,512]{1,0:T(8,128)(2,1)S(1)}, u32[]{:S(2)}, u32[]{:S(2)}) collective-permute-start(bf16[64,512]{1,0:T(8,128)(2,1)S(1)} %shard_map.92.own), channel_id=1, source_target_pairs={{0,14},{2,12},{4,10},{6,8},{8,6},{10,4},{12,2},{14,0},{1,15},{3,13... | collective-permute-start | bytes 196616 | tf_op jit(solution)/shard_map/ppermute | solution.py:516
  33.2 4.3 %collective-permute-start.15 = (f32[56,128]{1,0:T(8,128)S(1)}, f32[56,128]{1,0:T(8,128)S(1)}, u32[]{:S(2)}, u32[]{:S(2)}) collective-permute-start(f32[56,128]{1,0:T(8,128)S(1)} %add.29), channel_id=1, source_target_pairs={{0,4},{2,6},{4,0},{6,2},{8,12},{10,14},{12,8},{14,10},{1,5},{3,7},... | collective-permute-start | bytes 86024 | tf_op jit(solution)/shard_map/ppermute | solution.py:611
  37.5 4.8 %collective-permute-start.16 = (f32[56,128]{1,0:T(8,128)S(1)}, f32[56,128]{1,0:T(8,128)S(1)}, u32[]{:S(2)}, u32[]{:S(2)}) collective-permute-start(f32[56,128]{1,0:T(8,128)S(1)} %add.30), channel_id=1, source_target_pairs={{0,8},{2,10},{4,12},{6,14},{8,0},{10,2},{12,4},{14,6},{1,9},{3,11}... | collective-permute-start | bytes 86024 | tf_op jit(solution)/shard_map/ppermute | solution.py:611
  39.0 3.9 %collective-permute-start.11 = (bf16[64,512]{1,0:T(8,128)(2,1)S(1)}, bf16[64,512]{1,0:T(8,128)(2,1)S(1)}, u32[]{:S(2)}, u32[]{:S(2)}) collective-permute-start(bf16[64,512]{1,0:T(8,128)(2,1)S(1)} %shard_map.92.own), channel_id=1, source_target_pairs={{0,1},{1,0},{2,3},{3,2},{4,5},{5,4},{6,7},{7,6},{8,9},{9,8},{10,11... | collective-permute-start | bytes 196616 | tf_op jit(solution)/shard_map/ppermute | solution.py:511
  39.0 3.9 %collective-permute-start.13 = (bf16[64,512]{1,0:T(8,128)(2,1)S(1)}, bf16[64,512]{1,0:T(8,128)(2,1)S(1)}, u32[]{:S(2)}, u32[]{:S(2)}) collective-permute-start(bf16[64,512]{1,0:T(8,128)(2,1)S(1)} %collective-permute-done.12.across_x), channel_id=1, source_target_pairs={{0,1},{1,0},{2,3},{3,2},{4,5},{5,4},{6,7},{7,6},{8,9},{9,8},{10,11... | collective-permute-start | bytes 196616 | tf_op jit(solution)/shard_map/ppermute | solution.py:511

commit v7 on v6

--- a/solution.py
+++ b/solution.py
@@ -13,7 +13,6 @@
 LANES = 128
 HALF = 16
 MID = 8 * LANES
-HIGHEST = lax.Precision.HIGHEST
 TURNS = (0, 63, 7 + 64, 56 + 64)
 
 
@@ -356,19 +355,23 @@
 def gate_back(grad, a, g, rows8, inside):
     sig = jax.nn.sigmoid(g)
     through = grad * sig
-    extra = dot(rows8, grad * a, precision=HIGHEST)
+    left, parts = grad * a, []
+    for _ in range(3):
+        parts.append(left.astype(BF))
+        left = left - parts[-1].astype(F32)
+    extra = dot(jnp.concatenate([rows8] * 3, axis=1), jnp.concatenate(parts, axis=0))
     sig8 = sig[0:8]
     top = through[0:8] + sig8 * (1.0 - sig8) * extra
     return (jnp.concatenate([top, through[8:]], axis=0) * inside).astype(BF)
 
 
 def gate_rows():
-    return one(gate_class(iota((8, CH), 1)) == iota((8, CH), 0), F32)
+    return one(gate_class(iota((8, CH), 1)) == iota((8, CH), 0))
 
 
 def second_mid_kernel(
-    codes, own, part, pre, gate_in, columns_f, w_second, w_turned, second, through_edge, raw,
-    table, columns_h, columns_b, placed_f, placed_s,
+    codes, own, part, pre, gate_in, w_second, w_turned, second, through_edge, columns_h, placed_f, placed_s,
+    table, columns_b,
 ):
     masks = region_masks()
     inside = jnp.concatenate([masks[4].astype(F32)] * 6, axis=1)
@@ -397,12 +400,15 @@
         inner = slice(LANES, 7 * LANES)
         back_pre = gate_back(grad[:, inner], pre[n, :, inner], gate_in[n, :, inner], rows8, inside)
         place(placed_f, n, lambda x: back_pre[:, (x - 1) * LANES : x * LANES], 1, 6)
+
+
+def gradient_kernel(columns_f, columns_h, placed_f, placed_s, raw):
     raw[0] = dot_t(columns_f[...], placed_f[...])
     raw[1] = dot_t(columns_h[...], placed_s[...])
 
 
 def second_edge_kernel(
-    scale, choose, own, part, got_a, got_b, far_a, far_b, pre_edge, gate_edge, through_edge,
+    scale, choose, own, part, got_a, got_b, far, pre_edge, gate_edge, through_edge,
     columns_f, columns_fe, raw, w_second, w_turned, second_edge, grads,
     columns_h, columns_b, placed_f, placed_s, place,
 ):
@@ -411,7 +417,7 @@
     for f, columns in ((0, columns_h), (1, columns_b)):
         candidates = edge_planes_of(
             lambda s, x: own[f, s, x], lambda s, x: part[f, s, x],
-            lambda which, s: (got_a, got_b)[which][f, s], lambda which, s: (far_a, far_b)[which][f, s],
+            lambda which, s: (got_a, got_b)[which][f, s], lambda which, s: far[which, f, s],
         )
         edge_columns(choose, masks, candidates, columns)
     second_edge[...] = edge_terms(dot(w_second[...], columns_h[...]), 0)
@@ -581,19 +587,22 @@
     )
     got = exchange(face_a, face_b)
     part = swap_y(both)
-    second_part, through_e, raw = call(
-        second_mid_kernel, 3.5, 1, [((2, CH, MID), F32), ((CH, 4 * LANES), F32), ((2, 288, LANES), F32)],
-        [((2, 5, 8) + plane, BF), ((288, 2 * MID), BF), ((288, 2 * MID), BF), ((128, 2 * MID), BF), ((128, 2 * MID), BF)],
-        codes, both, part, pre, gate_in, columns, w2, w2t,
-    )
-    got = after(got, raw)
-    faces = (*got, swap_y(got[0]), swap_y(got[1]))
+    second_part, through_e, columns_h, placed_f, placed_s = call(
+        second_mid_kernel, 2.5, 1,
+        [((2, CH, MID), F32), ((CH, 4 * LANES), F32), ((288, 2 * MID), BF), *[((128, 2 * MID), BF)] * 2],
+        [((2, 5, 8) + plane, BF), ((288, 2 * MID), BF)],
+        codes, both, part, pre, gate_in, w2, w2t,
+    )
+    got = after(got, second_part)
+    far = swap_y(jnp.stack(got))
+    columns_h, placed_f, placed_s = after((columns_h, placed_f, placed_s), *got)
+    (raw,) = call(gradient_kernel, 1, 0, [((2, 288, LANES), F32)], [], columns, columns_h, placed_f, placed_s)
     n_bricks = features.shape[0] * lax.axis_size("xp") * lax.axis_size("yp")
     second_e, grads = call(
         functools.partial(second_edge_kernel, 1.0 / n_bricks), 2, 0, [((CH, 4 * LANES), F32), ((56, LANES), F32)],
         [((288, 4 * LANES), BF)] * 2
         + [((128, 12 * LANES), BF), ((128, 4 * LANES), BF), ((256, 3 * LANES), BF)],
-        choose, both, part, *faces, pre_e, gate_e, through_e, columns, columns_e, raw, w2, w2t,
+        choose, both, part, *got, far, pre_e, gate_e, through_e, columns, columns_e, raw, w2, w2t,
     )
     total = grads + swap_y(grads)
     second_part, second_e = after((second_part, second_e), total)

time: 44.1 us -> 43.4 us (0.984)
  waiting for transfers between devices: 7.44 us -> 6.28 us
    ppermute x3, waiting for transfers between devices: 5.69 us -> 4.91 us  [on_device(): total = total + lax.ppermute(total, 'xp', [(i, i ^ bit) for i in range(n)])]
    ppermute x2, starting transfers between devices: 8.05 us -> 8.58 us  [mirror_x(): return lax.ppermute(x, 'xp', [(i, n - 1 - i) for i in range(n)])]
    ppermute x8 -> x7, starting transfers between devices: 2.2 us -> 1.69 us  [swap_y(): return lax.ppermute(x, 'yp', [(i, n - 1 - i) for i in range(n)])]
    ppermute x3, starting transfers between devices: 7.36 us -> 7.8 us  [on_device(): total = total + lax.ppermute(total, 'xp', [(i, i ^ bit) for i in range(n)])]
    ppermute x8 -> x7, waiting for transfers between devices: 1.73 us -> 1.36 us  [swap_y(): return lax.ppermute(x, 'yp', [(i, n - 1 - i) for i in range(n)])]
    pallas_call x9 -> x10, Pallas kernels: 10.4 us -> 10.4 us  [call(): pl.pallas_call(kernel, out_shape=tuple((jax.ShapeDtypeStruct(s, t) for s,...]
  transfers between devices with their start and end apart: 17 -> 16, of which waited for: 5 -> 4; matrix products, arithmetic and copies ran while one was open for 4% -> 4% of each run, Pallas kernels for 15% -> 15%
where the time goes in v7:
time: 43.4 us; the launch traced here: 43.2 us
  starting transfers between devices  23.2 us (53%)
  Pallas kernels  10.4 us (24%)
  waiting for transfers between devices  6.28 us (14%)
  local copies, waits for them, and re-layouts  2.36 us (5%)
  between operations  0.87 us (2%)
    pallas_call x10, Pallas kernels, call(): pl.pallas_call(kernel, out_shape=tuple((jax.ShapeDtypeStruct(s, t) for s,...  10.4 us
    ppermute x2, starting transfers between devices, mirror_x(): return lax.ppermute(x, 'xp', [(i, n - 1 - i) for i in range(n)])  8.58 us
    ppermute x3, starting transfers between devices, on_device(): total = total + lax.ppermute(total, 'xp', [(i, i ^ bit) for i in range(n)])  7.8 us
    ppermute x4, starting transfers between devices, pair_swap(): return lax.ppermute(x, 'xp', pairs)  5.17 us
    ppermute x3, waiting for transfers between devices, on_device(): total = total + lax.ppermute(total, 'xp', [(i, i ^ bit) for i in range(n)])  4.91 us
    unnamed x10, local copies, waits for them, and re-layouts  1.72 us
    ppermute x7, starting transfers between devices, swap_y(): return lax.ppermute(x, 'yp', [(i, n - 1 - i) for i in range(n)])  1.69 us
    ppermute x7, waiting for transfers between devices, swap_y(): return lax.ppermute(x, 'yp', [(i, n - 1 - i) for i in range(n)])  1.36 us
  transfers between devices with their start and end apart: 16, of which 4 were waited for; matrix products, arithmetic and copies ran while one was open for 4% of the time, Pallas kernels for 15%

profile of v7, /device:TPU:0, one launch (start us, length us, event | category | flops | bytes accessed | tf_op | source)
XLA Modules:
  0.0 43.2 jit_solution(8756815504556370947)
XLA Ops:
  0.7 0.9 %copy.16.own = bf16[2,30,512]{2,1,0:T(8,128)(2,1)S(1)} copy(bf16[2,30,512]{2,0,1:T(2,128)(2,1)} %param.7) | data formatting | bytes 122880 | tf_op args[1]
  1.5 0.5 %collective-permute-start.3 = (bf16[2,30,512]{2,1,0:T(8,128)(2,1)S(1)}, bf16[2,30,512]{2,1,0:T(8,128)(2,1)S(1)}, u32[]{:S(2)}, u32[]{:S(2)}) collective-permute-start(bf16[2,30,512]{2,1,0:T(8,128)(2,1)S(1)} %copy.16.own), channel_id=1, source_target_pairs={{0,1},{1,0},{2,3},{3,2},{4,5},{5,4},{6,7},{7,6},{8,9},{9,8},{10,11... | collective-permute-start | bytes 184328 | tf_op jit(solution)/shard_map/ppermute | solution.py:517
  2.1 0.8 %copy.9.features = bf16[2,30,512]{2,1,0:T(8,128)(2,1)S(1)} copy(bf16[2,30,512]{2,0,1:T(2,128)(2,1)} %param.6) | data formatting | bytes 122880 | tf_op args[0]
  2.9 0.2 shard_map.85.own
  3.1 0.1 collective-permute-start
  3.3 6.1 %collective-permute-start.4 = (bf16[4,30,512]{2,1,0:T(8,128)(2,1)S(1)}, bf16[4,30,512]{2,1,0:T(8,128)(2,1)S(1)}, u32[]{:S(2)}, u32[]{:S(2)}) collective-permute-start(bf16[4,30,512]{2,1,0:T(8,128)(2,1)S(1)} %pad_maximum_fusion), channel_id=1, source_target_pairs={{0,14},{2,12},{4,10},{6,8},{8,6},{10,4},{12,2},{14,0},{1,15},{3,13... | collective-permute-start | bytes 368648 | tf_op jit(solution)/shard_map/ppermute | solution.py:522
  9.3 0.7 %collective-permute-start.2 = (bf16[4,32,128]{2,1,0:T(8,128)(2,1)S(1)}, bf16[4,32,128]{2,1,0:T(8,128)(2,1)S(1)}, u32[]{:S(2)}, u32[]{:S(2)}) collective-permute-start(bf16[4,32,128]{2,1,0:T(8,128)(2,1)S(1)} %get-tuple-element.81), channel_id=1, source_target_pairs={{2,4},{4,2},{6,8},{8,6},{10,12},{12,10},{3,5},{5,3},{7,9},{9,7},{1... | collective-permute-start | bytes 98312 | tf_op jit(solution)/shard_map/ppermute | solution.py:530
  10.0 2.3 %collective-permute-start.1 = (bf16[4,32,128]{2,1,0:T(8,128)(2,1)S(1)}, bf16[4,32,128]{2,1,0:T(8,128)(2,1)S(1)}, u32[]{:S(2)}, u32[]{:S(2)}) collective-permute-start(bf16[4,32,128]{2,1,0:T(8,128)(2,1)S(1)} %get-tuple-element.82), channel_id=1, source_target_pairs={{0,2},{2,0},{4,6},{6,4},{8,10},{10,8},{12,14},{14,12},{1,3},{3,1},... | collective-permute-start | bytes 98312 | tf_op jit(solution)/shard_map/ppermute | solution.py:530
  12.4 0.5 %shard_map.86 = (bf16[192,288]{1,0:T(8,128)(2,1)S(1)}, bf16[96,288]{1,0:T(8,128)(2,1)S(1)}, bf16[96,288]{1,0:T(8,128)(2,1)S(1)}, s32[2,27]{1,0:T(2,128)S(1)}, bf...) custom-call(bf16[32,256]{1,0:T(8,128)(2,1)S(1)} %pad_add_fusion.packed, s32[2,256]{1,0:T(2,128)S(1)} %pad_add_fusion.1.small), custom_call_target="tpu_custom_call" | custom-call | bytes 3000000 | tf_op jit(solution)/shard_map/pallas_call | solution.py:504
  12.9 1.9 %shard_map.87 = (bf16[288,2048]{1,0:T(8,128)(2,1)S(1)}, f32[2,32,1024]{2,1,0:T(8,128)S(1)}, f32[2,32,1024]{2,1,0:T(8,128)S(1)}, bf16[2,6,32,128]{3,2,1,0:T(8,128)(2,1)S(1)}) custom-call(s32[2,27]{1,0:T(2,128)S(1)} %get-tuple-element.45.codes, bf16[2,8,32,128]{3,2,1,0:T(8,128)(2,1)S(1)} %shard_map.85.own, bf16[2,8,32,128]{3,2,1,0:T(8,128)(2,1)S(1)} %copy.17.part, ...), custom_call_target="tpu_custom_call" | custom-call | bytes 6000000 | tf_op jit(solution)/shard_map/pallas_call | solution.py:504
  14.8 0.3 shard_map.88.back
  15.1 0.8 %shard_map.89 = (bf16[288,512]{1,0:T(8,128)(2,1)S(1)}, f32[32,512]{1,0:T(8,128)S(1)}, f32[32,512]{1,0:T(8,128)S(1)}, bf16[2,2,8,32,128]{4,3,2,1,0:T(8,128)(2,1)S...) custom-call(bf16[288,16,128]{2,1,0:T(8,128)(2,1)S(1)} %get-tuple-element.46.choose, ...), custom_call_target="tpu_custom_call" | custom-call | bytes 3000000 | tf_op jit(solution)/shard_map/pallas_call | solution.py:504
  15.9 0.1 collective-permute-start.5
  16.0 1.5 %collective-permute-start.6 = (bf16[2,2,32,128]{3,2,1,0:T(8,128)(2,1)S(1)}, bf16[2,2,32,128]{3,2,1,0:T(8,128)(2,1)S(1)}, u32[]{:S(2)}, u32[]{:S(2)}) collective-permute-start(bf16[2,2,32,128]{3,2,1,0:T(8,128)(2,1)S(1)} %get-tuple-element.58), channel_id=1, source_target_pairs={{0,2},{2,0},{4,6},{6,4},{8,10},{10,8},{12,14},{14,12},{1,3},{3,1},... | collective-permute-start | bytes 98312 | tf_op jit(solution)/shard_map/ppermute | solution.py:530
  17.6 0.7 %collective-permute-start.7 = (bf16[2,2,32,128]{3,2,1,0:T(8,128)(2,1)S(1)}, bf16[2,2,32,128]{3,2,1,0:T(8,128)(2,1)S(1)}, u32[]{:S(2)}, u32[]{:S(2)}) collective-permute-start(bf16[2,2,32,128]{3,2,1,0:T(8,128)(2,1)S(1)} %get-tuple-element.59), channel_id=1, source_target_pairs={{2,4},{4,2},{6,8},{8,6},{10,12},{12,10},{3,5},{5,3},{7,9},{9,7},{1... | collective-permute-start | bytes 98312 | tf_op jit(solution)/shard_map/ppermute | solution.py:530
  18.2 2.7 %shard_map.90 = (f32[2,32,1024]{2,1,0:T(8,128)S(1)}, f32[32,512]{1,0:T(8,128)S(1)}, bf16[288,2048]{1,0:T(8,128)(2,1)S(1)}, bf16[128,2048]{1,0:T(8,128)(2,1)S(1)}, bf16[128,2048]{1,0:T(8,128)(2,1)S(1)}) custom-call(s32[2,27]{1,0:T(2,128)S(1)} %get-tuple-element.45.codes, bf16[2,2,8,32,128]{4,3,2,1,0:T(8,128)(2,1)S(1)} %get-tuple-element.54.own, ...), custom_call_target="tpu_custom_call" | custom-call | bytes 7500000 | tf_op jit(solution)/shard_map/pallas_call | solution.py:504
  21.0 0.2 collective-permute-start.8
  21.2 0.8 %shard_map.91.raw = f32[2,288,128]{2,1,0:T(8,128)S(1)} custom-call(bf16[288,2048]{1,0:T(8,128)(2,1)S(1)} %get-tuple-element.65.columns_f, bf16[288,2048]{1,0:T(8,128)(2,1)S(1)} %get-tuple-element.70.columns_h, bf16[128,2048]{1,0:T(8,128)(2,1)S(1)} %get-tuple-element.71.placed_f, bf16[128,2048]{1,0:T(8,128)(2,1)S(1)} %get-tuple-element.72.placed_s), custom_call_target="tpu_custom_call" | custom-call | bytes 3000000 | tf_op jit(solution)/shard_map/pallas_call | solution.py:504
  22.0 0.3 collective-permute-done.8.far
  22.3 2.0 %shard_map.92 = (f32[32,512]{1,0:T(8,128)S(1)}, f32[56,128]{1,0:T(8,128)S(1)}) custom-call(bf16[288,16,128]{2,1,0:T(8,128)(2,1)S(1)} %get-tuple-element.46.choose, bf16[2,2,8,32,128]{4,3,2,1,0:T(8,128)(2,1)S(1)} %get-tuple-element.54.own, bf16[2,2,8,32,128]{4,3,2,1,0:T(8,128)(2,1)S(1)} %collective-permute-done.5.part, ...), custom_call_target="tpu_custom_call" | custom-call | bytes 6000000 | tf_op jit(solution)/shard_map/pallas_call | solution.py:504
  24.3 0.2 collective-permute-start.9
  24.6 1.0 %collective-permute-done.9 = f32[56,128]{1,0:T(8,128)S(1)} collective-permute-done((f32[56,128]{1,0:T(8,128)S(1)}, f32[56,128]{1,0:T(8,128)S(1)}, u32[]{:S(2)}, u32[]{:S(2)}) %collective-permute-start.9) | collective-permute-done | bytes 28704 | tf_op jit(solution)/shard_map/ppermute | solution.py:517
  25.6 4.5 %collective-permute-start.13 = (f32[56,128]{1,0:T(8,128)S(1)}, f32[56,128]{1,0:T(8,128)S(1)}, u32[]{:S(2)}, u32[]{:S(2)}) collective-permute-start(f32[56,128]{1,0:T(8,128)S(1)} %add.28), channel_id=1, source_target_pairs={{0,2},{2,0},{4,6},{6,4},{8,10},{10,8},{12,14},{14,12},{1,3},{3,1},... | collective-permute-start | bytes 86024 | tf_op jit(solution)/shard_map/ppermute | solution.py:620
  30.1 0.2 shard_map.93.own
  30.4 2.5 %collective-permute-start.11 = (bf16[64,512]{1,0:T(8,128)(2,1)S(1)}, bf16[64,512]{1,0:T(8,128)(2,1)S(1)}, u32[]{:S(2)}, u32[]{:S(2)}) collective-permute-start(bf16[64,512]{1,0:T(8,128)(2,1)S(1)} %shard_map.93.own), channel_id=1, source_target_pairs={{0,14},{2,12},{4,10},{6,8},{8,6},{10,4},{12,2},{14,0},{1,15},{3,13... | collective-permute-start | bytes 196616 | tf_op jit(solution)/shard_map/ppermute | solution.py:522
  32.9 1.7 %collective-permute-start.14 = (f32[56,128]{1,0:T(8,128)S(1)}, f32[56,128]{1,0:T(8,128)S(1)}, u32[]{:S(2)}, u32[]{:S(2)}) collective-permute-start(f32[56,128]{1,0:T(8,128)S(1)} %add.29), channel_id=1, source_target_pairs={{0,4},{2,6},{4,0},{6,2},{8,12},{10,14},{12,8},{14,10},{1,5},{3,7},... | collective-permute-start | bytes 86024 | tf_op jit(solution)/shard_map/ppermute | solution.py:620
  34.6 2.3 %collective-permute-done.14 = f32[56,128]{1,0:T(8,128)S(1)} collective-permute-done((f32[56,128]{1,0:T(8,128)S(1)}, f32[56,128]{1,0:T(8,128)S(1)}, u32[]{:S(2)}, u32[]{:S(2)}) %collective-permute-start.14) | collective-permute-done | bytes 28704 | tf_op jit(solution)/shard_map/ppermute | solution.py:620
  36.8 1.6 %collective-permute-start.15 = (f32[56,128]{1,0:T(8,128)S(1)}, f32[56,128]{1,0:T(8,128)S(1)}, u32[]{:S(2)}, u32[]{:S(2)}) collective-permute-start(f32[56,128]{1,0:T(8,128)S(1)} %add.30), channel_id=1, source_target_pairs={{0,8},{2,10},{4,12},{6,14},{8,0},{10,2},{12,4},{14,6},{1,9},{3,11}... | collective-permute-start | bytes 86024 | tf_op jit(solution)/shard_map/ppermute | solution.py:620
  38.5 0.5 %collective-permute-start.12 = (bf16[64,512]{1,0:T(8,128)(2,1)S(1)}, bf16[64,512]{1,0:T(8,128)(2,1)S(1)}, u32[]{:S(2)}, u32[]{:S(2)}) collective-permute-start(bf16[64,512]{1,0:T(8,128)(2,1)S(1)} %collective-permute-done.11.across_x), channel_id=1, source_target_pairs={{0,1},{1,0},{2,3},{3,2},{4,5},{5,4},{6,7},{7,6},{8,9},{9,8},{10,11... | collective-permute-start | bytes 196616 | tf_op jit(solution)/shard_map/ppermute | solution.py:517
  39.0 2.6 %collective-permute-done.15 = f32[56,128]{1,0:T(8,128)S(1)} collective-permute-done((f32[56,128]{1,0:T(8,128)S(1)}, f32[56,128]{1,0:T(8,128)S(1)}, u32[]{:S(2)}, u32[]{:S(2)}) %collective-permute-start.15) | collective-permute-done | bytes 28704 | tf_op jit(solution)/shard_map/ppermute | solution.py:620
  41.6 0.6 %fusion = (f32[27,84]{1,0:T(8,128)}, f32[27,84]{1,0:T(8,128)}) fusion(f32[56,128]{1,0:T(8,128)S(1)} %add.31), kind=kLoop, calls=%fused_computation.12 | loop fusion | bytes 36288 | tf_op jit(solution)/shard_map/slice | solution.py:622
  42.2 0.9 %shard_map.94 = bf16[30,2,512]{2,1,0:T(2,128)(2,1)} custom-call(bf16[6,16,128]{2,1,0:T(8,128)(2,1)S(1)} %get-tuple-element.44.turn_choice, bf16[64,512]{1,0:T(8,128)(2,1)S(1)} %shard_map.93.own, bf16[64,512]{1,0:T(8,128)(2,1)S(1)} %collective-permute-done.10.across_y, bf16[64,512]{1,0:T(8,128)(2,1)S(1)} %collective-permute-done.11.across_x, ...), custom_call_target="tpu_custom_call" | custom-call | bytes 2700000 | tf_op jit(solution)/shard_map/pallas_call | solution.py:504
  (34 shorter events, 0.2 us)
Async XLA Ops:
  0.6 11.7 %copy-start.2 = (s32[2,3]{1,0:T(2,128)S(1)}, s32[2,3]{1,0:T(2,128)}, u32[]{:S(2)}) copy-start(s32[2,3]{1,0:T(2,128)} %param.11) | copy-start | bytes 76
  0.6 11.7 %copy-start.3 = (s32[2,27]{1,0:T(2,128)S(1)}, s32[2,27]{1,0:T(2,128)}, u32[]{:S(2)}) copy-start(s32[2,27]{1,0:T(2,128)} %param.10) | copy-start | bytes 652
  0.7 11.7 %copy-start = (bf16[27,84]{1,0:T(8,128)(2,1)S(1)}, bf16[27,84]{1,0:T(8,128)(2,1)}, u32[]{:S(2)}) copy-start(bf16[27,84]{1,0:T(8,128)(2,1)} %param.9) | copy-start | bytes 13612
  0.7 11.7 %copy-start.1 = (bf16[27,84]{1,0:T(8,128)(2,1)S(1)}, bf16[27,84]{1,0:T(8,128)(2,1)}, u32[]{:S(2)}) copy-start(bf16[27,84]{1,0:T(8,128)(2,1)} %param.8) | copy-start | bytes 13612
  1.5 1.7 %collective-permute-start.3 = (bf16[2,30,512]{2,1,0:T(8,128)(2,1)S(1)}, bf16[2,30,512]{2,1,0:T(8,128)(2,1)S(1)}, u32[]{:S(2)}, u32[]{:S(2)}) collective-permute-start(bf16[2,30,512]{2,1,0:T(8,128)(2,1)S(1)} %copy.16.own), channel_id=1, source_target_pairs={{0,1},{1,0},{2,3},{3,2},{4,5},{5,4},{6,7},{7,6},{8,9},{9,8},{10,11... | collective-permute-start | bytes 184328 | tf_op jit(solution)/shard_map/ppermute | solution.py:517
  3.1 6.2 %collective-permute-start = (bf16[2,8,32,128]{3,2,0,1:T(8,128)(2,1)S(1)}, bf16[2,8,32,128]{3,2,0,1:T(8,128)(2,1)S(1)}, u32[]{:S(2)}, u32[]{:S(2)}) collective-permute-start(bf16[2,8,32,128]{3,2,0,1:T(8,128)(2,1)S(1)} %copy.10), channel_id=1, source_target_pairs={{0,1},{1,0},{2,3},{3,2},{4,5},{5,4},{6,7},{7,6},{8,9},{9,8},{10,11... | collective-permute-start | bytes 393224 | tf_op jit(solution)/shard_map/ppermute | solution.py:517
  3.3 11.6 %collective-permute-start.4 = (bf16[4,30,512]{2,1,0:T(8,128)(2,1)S(1)}, bf16[4,30,512]{2,1,0:T(8,128)(2,1)S(1)}, u32[]{:S(2)}, u32[]{:S(2)}) collective-permute-start(bf16[4,30,512]{2,1,0:T(8,128)(2,1)S(1)} %pad_maximum_fusion), channel_id=1, source_target_pairs={{0,14},{2,12},{4,10},{6,8},{8,6},{10,4},{12,2},{14,0},{1,15},{3,13... | collective-permute-start | bytes 368648 | tf_op jit(solution)/shard_map/ppermute | solution.py:522
  9.3 5.8 %collective-permute-start.2 = (bf16[4,32,128]{2,1,0:T(8,128)(2,1)S(1)}, bf16[4,32,128]{2,1,0:T(8,128)(2,1)S(1)}, u32[]{:S(2)}, u32[]{:S(2)}) collective-permute-start(bf16[4,32,128]{2,1,0:T(8,128)(2,1)S(1)} %get-tuple-element.81), channel_id=1, source_target_pairs={{2,4},{4,2},{6,8},{8,6},{10,12},{12,10},{3,5},{5,3},{7,9},{9,7},{1... | collective-permute-start | bytes 98312 | tf_op jit(solution)/shard_map/ppermute | solution.py:530
  10.0 5.1 %collective-permute-start.1 = (bf16[4,32,128]{2,1,0:T(8,128)(2,1)S(1)}, bf16[4,32,128]{2,1,0:T(8,128)(2,1)S(1)}, u32[]{:S(2)}, u32[]{:S(2)}) collective-permute-start(bf16[4,32,128]{2,1,0:T(8,128)(2,1)S(1)} %get-tuple-element.82), channel_id=1, source_target_pairs={{0,2},{2,0},{4,6},{6,4},{8,10},{10,8},{12,14},{14,12},{1,3},{3,1},... | collective-permute-start | bytes 98312 | tf_op jit(solution)/shard_map/ppermute | solution.py:530
  15.9 2.3 %collective-permute-start.5 = (bf16[2,2,8,32,128]{4,3,2,1,0:T(8,128)(2,1)S(1)}, bf16[2,2,8,32,128]{4,3,2,1,0:T(8,128)(2,1)S(1)}, u32[]{:S(2)}, u32[]{:S(2)}) collective-permute-start(bf16[2,2,8,32,128]{4,3,2,1,0:T(8,128)(2,1)S(1)} %get-tuple-element.54.own), channel_id=1, source_target_pairs={{0,1},{1,0},{2,3},{3,2},{4,5},{5,4},{6,7},{7,6},{8,9},{9,8},{10,11... | collective-permute-start | bytes 786440 | tf_op jit(solution)/shard_map/ppermute | solution.py:517
  16.0 4.9 %collective-permute-start.6 = (bf16[2,2,32,128]{3,2,1,0:T(8,128)(2,1)S(1)}, bf16[2,2,32,128]{3,2,1,0:T(8,128)(2,1)S(1)}, u32[]{:S(2)}, u32[]{:S(2)}) collective-permute-start(bf16[2,2,32,128]{3,2,1,0:T(8,128)(2,1)S(1)} %get-tuple-element.58), channel_id=1, source_target_pairs={{0,2},{2,0},{4,6},{6,4},{8,10},{10,8},{12,14},{14,12},{1,3},{3,1},... | collective-permute-start | bytes 98312 | tf_op jit(solution)/shard_map/ppermute | solution.py:530
  17.6 3.4 %collective-permute-start.7 = (bf16[2,2,32,128]{3,2,1,0:T(8,128)(2,1)S(1)}, bf16[2,2,32,128]{3,2,1,0:T(8,128)(2,1)S(1)}, u32[]{:S(2)}, u32[]{:S(2)}) collective-permute-start(bf16[2,2,32,128]{3,2,1,0:T(8,128)(2,1)S(1)} %get-tuple-element.59), channel_id=1, source_target_pairs={{2,4},{4,2},{6,8},{8,6},{10,12},{12,10},{3,5},{5,3},{7,9},{9,7},{1... | collective-permute-start | bytes 98312 | tf_op jit(solution)/shard_map/ppermute | solution.py:530
  21.0 1.3 %collective-permute-start.8 = (bf16[2,2,2,32,128]{4,3,2,1,0:T(8,128)(2,1)S(1)}, bf16[2,2,2,32,128]{4,3,2,1,0:T(8,128)(2,1)S(1)}, u32[]{:S(2)}, u32[]{:S(2)}) collective-permute-start(bf16[2,2,2,32,128]{4,3,2,1,0:T(8,128)(2,1)S(1)} %pad_maximum_fusion.1), channel_id=1, source_target_pairs={{0,1},{1,0},{2,3},{3,2},{4,5},{5,4},{6,7},{7,6},{8,9},{9,8},{10,11... | collective-permute-start | bytes 196616 | tf_op jit(solution)/shard_map/ppermute | solution.py:517
  24.3 1.3 %collective-permute-start.9 = (f32[56,128]{1,0:T(8,128)S(1)}, f32[56,128]{1,0:T(8,128)S(1)}, u32[]{:S(2)}, u32[]{:S(2)}) collective-permute-start(f32[56,128]{1,0:T(8,128)S(1)} %get-tuple-element.74), channel_id=1, source_target_pairs={{0,1},{1,0},{2,3},{3,2},{4,5},{5,4},{6,7},{7,6},{8,9},{9,8},{10,11... | collective-permute-start | bytes 86024 | tf_op jit(solution)/shard_map/ppermute | solution.py:517
  25.6 7.3 %collective-permute-start.13 = (f32[56,128]{1,0:T(8,128)S(1)}, f32[56,128]{1,0:T(8,128)S(1)}, u32[]{:S(2)}, u32[]{:S(2)}) collective-permute-start(f32[56,128]{1,0:T(8,128)S(1)} %add.28), channel_id=1, source_target_pairs={{0,2},{2,0},{4,6},{6,4},{8,10},{10,8},{12,14},{14,12},{1,3},{3,1},... | collective-permute-start | bytes 86024 | tf_op jit(solution)/shard_map/ppermute | solution.py:620
  30.4 8.1 %collective-permute-start.11 = (bf16[64,512]{1,0:T(8,128)(2,1)S(1)}, bf16[64,512]{1,0:T(8,128)(2,1)S(1)}, u32[]{:S(2)}, u32[]{:S(2)}) collective-permute-start(bf16[64,512]{1,0:T(8,128)(2,1)S(1)} %shard_map.93.own), channel_id=1, source_target_pairs={{0,14},{2,12},{4,10},{6,8},{8,6},{10,4},{12,2},{14,0},{1,15},{3,13... | collective-permute-start | bytes 196616 | tf_op jit(solution)/shard_map/ppermute | solution.py:522
  32.9 3.9 %collective-permute-start.14 = (f32[56,128]{1,0:T(8,128)S(1)}, f32[56,128]{1,0:T(8,128)S(1)}, u32[]{:S(2)}, u32[]{:S(2)}) collective-permute-start(f32[56,128]{1,0:T(8,128)S(1)} %add.29), channel_id=1, source_target_pairs={{0,4},{2,6},{4,0},{6,2},{8,12},{10,14},{12,8},{14,10},{1,5},{3,7},... | collective-permute-start | bytes 86024 | tf_op jit(solution)/shard_map/ppermute | solution.py:620
  36.8 4.8 %collective-permute-start.15 = (f32[56,128]{1,0:T(8,128)S(1)}, f32[56,128]{1,0:T(8,128)S(1)}, u32[]{:S(2)}, u32[]{:S(2)}) collective-permute-start(f32[56,128]{1,0:T(8,128)S(1)} %add.30), channel_id=1, source_target_pairs={{0,8},{2,10},{4,12},{6,14},{8,0},{10,2},{12,4},{14,6},{1,9},{3,11}... | collective-permute-start | bytes 86024 | tf_op jit(solution)/shard_map/ppermute | solution.py:620
  38.5 3.8 %collective-permute-start.10 = (bf16[64,512]{1,0:T(8,128)(2,1)S(1)}, bf16[64,512]{1,0:T(8,128)(2,1)S(1)}, u32[]{:S(2)}, u32[]{:S(2)}) collective-permute-start(bf16[64,512]{1,0:T(8,128)(2,1)S(1)} %shard_map.93.own), channel_id=1, source_target_pairs={{0,1},{1,0},{2,3},{3,2},{4,5},{5,4},{6,7},{7,6},{8,9},{9,8},{10,11... | collective-permute-start | bytes 196616 | tf_op jit(solution)/shard_map/ppermute | solution.py:517
  38.5 3.8 %collective-permute-start.12 = (bf16[64,512]{1,0:T(8,128)(2,1)S(1)}, bf16[64,512]{1,0:T(8,128)(2,1)S(1)}, u32[]{:S(2)}, u32[]{:S(2)}) collective-permute-start(bf16[64,512]{1,0:T(8,128)(2,1)S(1)} %collective-permute-done.11.across_x), channel_id=1, source_target_pairs={{0,1},{1,0},{2,3},{3,2},{4,5},{5,4},{6,7},{7,6},{8,9},{9,8},{10,11... | collective-permute-start | bytes 196616 | tf_op jit(solution)/shard_map/ppermute | solution.py:517

commit v8 on v7

--- a/solution.py
+++ b/solution.py
@@ -12,6 +12,7 @@
 CH = 32
 LANES = 128
 HALF = 16
+OFFSETS = 27
 MID = 8 * LANES
 TURNS = (0, 63, 7 + 64, 56 + 64)
 
@@ -167,33 +168,59 @@
     return [[plane.reshape(2, HALF, LANES) for plane in side] for side in (low, high)]
 
 
+OTHER_X, OTHER_Y, SLOTS, N_CHOICES = 0, 8, 16, 88
+
+
 def edge_columns(choose, masks, candidates, columns):
+    def pick(row, here, there):
+        return [p * choose[row + 4] + q * choose[row] for p, q in zip(here, there)]
+
+    found = []
+    for e in range(4):
+        own, part, near, far = (candidates[e & 1][2 * k : 2 * k + 2] for k in range(4))
+        same_y = pick(OTHER_X + e, own, near)
+        other_y = pick(OTHER_X + e, part, far)
+        rows = [pick(OTHER_Y + 2 * (e >> 1) + k, same_y, other_y) for k in range(2)]
+        found.append((rows[0], same_y, rows[1]))
+
     def pieces(o):
-        found = []
+        planes = []
         for e in range(4):
-            total = None
-            for r, plane in enumerate(candidates[e & 1]):
-                term = plane * choose[8 * (9 * e + o) + r]
-                total = term if total is None else total + term
-            found.append(total.reshape(CH, LANES))
-        return found
+            first, second = found[e][o // 3]
+            at = SLOTS + 2 * (9 * e + o)
+            planes.append((first * choose[at] + second * choose[at + 1]).reshape(CH, LANES))
+        return planes
 
     unfold(gathered(pieces, masks), 4, columns, 0)
 
 
 def write_choices(codes, mirror, choose, turn_choice):
+    lane = iota(codes.shape, 1)
+    a = (lane * 57) >> 9
+    b = ((lane * 171) >> 9) - 3 * a
     d = codes >> 1
     dx = (d * 11) >> 5
-    other = jnp.where(d - 3 * dx == 1, 0, 2) + jnp.where(dx == 1, 0, 4)
-    row = jnp.where(codes >= 18, -1, other + (codes & 1))
+    dy = d - 3 * dx
+    there = (codes < 18) & (lane < OFFSETS)
+    slot = jnp.where(there, codes & 1, -1)
     shape = (HALF, LANES)
+
+    def flag(condition):
+        return jnp.max(jnp.where(there & condition, 1.0, 0.0), axis=1, keepdims=True)
+
+    for k in range(2):
+        for base, found in ((OTHER_X, flag((a == 2 * k) & (dx != 1))), (OTHER_Y, flag((b == 2 * k) & (dy != 1)))):
+            for n in range(2):
+                wide = jnp.broadcast_to(found[n : n + 1], shape)
+                choose[base + 2 * n + k] = wide.astype(BF)
+                choose[base + 4 + 2 * n + k] = (1.0 - wide).astype(BF)
     for e in range(4):
         n = e >> 1
         for o in range(9):
             at = o + 18 * (e & 1)
-            wide = jnp.broadcast_to(row[n : n + 1, at : at + 1], shape)
-            for r in range(8):
-                choose[8 * (9 * e + o) + r] = one(wide == r)
+            wide = jnp.broadcast_to(slot[n : n + 1, at : at + 1], shape)
+            for s in range(2):
+                choose[SLOTS + 2 * (9 * e + o) + s] = one(wide == s)
     for n in range(2):
         for r in range(3):
             wide = jnp.broadcast_to(mirror[n : n + 1, r : r + 1], shape)
@@ -562,7 +589,7 @@
         weights_kernel, 1, 0,
         [
             ((192, 288), BF), ((96, 288), BF), ((96, 288), BF), (codes.shape, codes.dtype),
-            ((288, HALF, LANES), BF), ((6, HALF, LANES), BF),
+            ((N_CHOICES, HALF, LANES), BF), ((6, HALF, LANES), BF),
         ],
         [((2, CH, LANES), F32), ((288, LANES), BF)],
         side_by_side((w_first, w_second), CH), side_by_side((codes, mirror), 2),

time: 43.4 us -> 42.7 us (0.984)
  Pallas kernels: 10.4 us -> 9.59 us
    pallas_call x10, Pallas kernels: 10.4 us -> 9.59 us  [call(): pl.pallas_call(kernel, out_shape=tuple((jax.ShapeDtypeStruct(s, t) for s,...]
where the time goes in v8:
time: 42.7 us; the launch traced here: 42.5 us
  starting transfers between devices  23.3 us (55%)
  Pallas kernels  9.59 us (22%)
  waiting for transfers between devices  6.3 us (15%)
  local copies, waits for them, and re-layouts  2.36 us (6%)
  between operations  0.87 us (2%)
    pallas_call x10, Pallas kernels, call(): pl.pallas_call(kernel, out_shape=tuple((jax.ShapeDtypeStruct(s, t) for s,...  9.59 us
    ppermute x2, starting transfers between devices, mirror_x(): return lax.ppermute(x, 'xp', [(i, n - 1 - i) for i in range(n)])  8.58 us
    ppermute x3, starting transfers between devices, on_device(): total = total + lax.ppermute(total, 'xp', [(i, i ^ bit) for i in range(n)])  7.78 us
    ppermute x4, starting transfers between devices, pair_swap(): return lax.ppermute(x, 'xp', pairs)  5.23 us
    ppermute x3, waiting for transfers between devices, on_device(): total = total + lax.ppermute(total, 'xp', [(i, i ^ bit) for i in range(n)])  4.92 us
    unnamed x10, local copies, waits for them, and re-layouts  1.72 us
    ppermute x7, starting transfers between devices, swap_y(): return lax.ppermute(x, 'yp', [(i, n - 1 - i) for i in range(n)])  1.68 us
    ppermute x7, waiting for transfers between devices, swap_y(): return lax.ppermute(x, 'yp', [(i, n - 1 - i) for i in range(n)])  1.36 us
  transfers between devices with their start and end apart: 16, of which 4 were waited for; matrix products, arithmetic and copies ran while one was open for 4% of the time, Pallas kernels for 15%

profile of v8, /device:TPU:0, one launch (start us, length us, event | category | flops | bytes accessed | tf_op | source)
XLA Modules:
  0.0 42.5 jit_solution(17442687040428109239)
XLA Ops:
  0.7 0.9 %copy.16.own = bf16[2,30,512]{2,1,0:T(8,128)(2,1)S(1)} copy(bf16[2,30,512]{2,0,1:T(2,128)(2,1)} %param.7) | data formatting | bytes 122880 | tf_op args[1]
  1.5 0.5 %collective-permute-start.3 = (bf16[2,30,512]{2,1,0:T(8,128)(2,1)S(1)}, bf16[2,30,512]{2,1,0:T(8,128)(2,1)S(1)}, u32[]{:S(2)}, u32[]{:S(2)}) collective-permute-start(bf16[2,30,512]{2,1,0:T(8,128)(2,1)S(1)} %copy.16.own), channel_id=1, source_target_pairs={{0,1},{1,0},{2,3},{3,2},{4,5},{5,4},{6,7},{7,6},{8,9},{9,8},{10,11... | collective-permute-start | bytes 184328 | tf_op jit(solution)/shard_map/ppermute | solution.py:544
  2.1 0.8 %copy.9.features = bf16[2,30,512]{2,1,0:T(8,128)(2,1)S(1)} copy(bf16[2,30,512]{2,0,1:T(2,128)(2,1)} %param.6) | data formatting | bytes 122880 | tf_op args[0]
  2.9 0.2 shard_map.85.own
  3.1 0.1 collective-permute-start
  3.3 6.1 %collective-permute-start.4 = (bf16[4,30,512]{2,1,0:T(8,128)(2,1)S(1)}, bf16[4,30,512]{2,1,0:T(8,128)(2,1)S(1)}, u32[]{:S(2)}, u32[]{:S(2)}) collective-permute-start(bf16[4,30,512]{2,1,0:T(8,128)(2,1)S(1)} %pad_maximum_fusion), channel_id=1, source_target_pairs={{0,14},{2,12},{4,10},{6,8},{8,6},{10,4},{12,2},{14,0},{1,15},{3,13... | collective-permute-start | bytes 368648 | tf_op jit(solution)/shard_map/ppermute | solution.py:549
  9.3 0.7 %collective-permute-start.2 = (bf16[4,32,128]{2,1,0:T(8,128)(2,1)S(1)}, bf16[4,32,128]{2,1,0:T(8,128)(2,1)S(1)}, u32[]{:S(2)}, u32[]{:S(2)}) collective-permute-start(bf16[4,32,128]{2,1,0:T(8,128)(2,1)S(1)} %get-tuple-element.81), channel_id=1, source_target_pairs={{2,4},{4,2},{6,8},{8,6},{10,12},{12,10},{3,5},{5,3},{7,9},{9,7},{1... | collective-permute-start | bytes 98312 | tf_op jit(solution)/shard_map/ppermute | solution.py:557
  10.0 2.3 %collective-permute-start.1 = (bf16[4,32,128]{2,1,0:T(8,128)(2,1)S(1)}, bf16[4,32,128]{2,1,0:T(8,128)(2,1)S(1)}, u32[]{:S(2)}, u32[]{:S(2)}) collective-permute-start(bf16[4,32,128]{2,1,0:T(8,128)(2,1)S(1)} %get-tuple-element.82), channel_id=1, source_target_pairs={{0,2},{2,0},{4,6},{6,4},{8,10},{10,8},{12,14},{14,12},{1,3},{3,1},... | collective-permute-start | bytes 98312 | tf_op jit(solution)/shard_map/ppermute | solution.py:557
  12.4 0.5 %shard_map.86 = (bf16[192,288]{1,0:T(8,128)(2,1)S(1)}, bf16[96,288]{1,0:T(8,128)(2,1)S(1)}, bf16[96,288]{1,0:T(8,128)(2,1)S(1)}, s32[2,27]{1,0:T(2,128)S(1)}, bf...) custom-call(bf16[32,256]{1,0:T(8,128)(2,1)S(1)} %pad_add_fusion.packed, s32[2,256]{1,0:T(2,128)S(1)} %pad_add_fusion.1.small), custom_call_target="tpu_custom_call" | custom-call | bytes 3000000 | tf_op jit(solution)/shard_map/pallas_call | solution.py:531
  12.9 1.9 %shard_map.87 = (bf16[288,2048]{1,0:T(8,128)(2,1)S(1)}, f32[2,32,1024]{2,1,0:T(8,128)S(1)}, f32[2,32,1024]{2,1,0:T(8,128)S(1)}, bf16[2,6,32,128]{3,2,1,0:T(8,128)(2,1)S(1)}) custom-call(s32[2,27]{1,0:T(2,128)S(1)} %get-tuple-element.45.codes, bf16[2,8,32,128]{3,2,1,0:T(8,128)(2,1)S(1)} %shard_map.85.own, bf16[2,8,32,128]{3,2,1,0:T(8,128)(2,1)S(1)} %copy.17.part, ...), custom_call_target="tpu_custom_call" | custom-call | bytes 6000000 | tf_op jit(solution)/shard_map/pallas_call | solution.py:531
  14.8 0.3 shard_map.88.back
  15.1 0.6 %shard_map.89 = (bf16[288,512]{1,0:T(8,128)(2,1)S(1)}, f32[32,512]{1,0:T(8,128)S(1)}, f32[32,512]{1,0:T(8,128)S(1)}, bf16[2,2,8,32,128]{4,3,2,1,0:T(8,128)(2,1)S...) custom-call(bf16[88,16,128]{2,1,0:T(8,128)(2,1)S(1)} %get-tuple-element.46.choose, ...), custom_call_target="tpu_custom_call" | custom-call | bytes 3000000 | tf_op jit(solution)/shard_map/pallas_call | solution.py:531
  15.6 0.1 collective-permute-start.5
  15.7 1.6 %collective-permute-start.6 = (bf16[2,2,32,128]{3,2,1,0:T(8,128)(2,1)S(1)}, bf16[2,2,32,128]{3,2,1,0:T(8,128)(2,1)S(1)}, u32[]{:S(2)}, u32[]{:S(2)}) collective-permute-start(bf16[2,2,32,128]{3,2,1,0:T(8,128)(2,1)S(1)} %get-tuple-element.58), channel_id=1, source_target_pairs={{0,2},{2,0},{4,6},{6,4},{8,10},{10,8},{12,14},{14,12},{1,3},{3,1},... | collective-permute-start | bytes 98312 | tf_op jit(solution)/shard_map/ppermute | solution.py:557
  17.3 0.7 %collective-permute-start.7 = (bf16[2,2,32,128]{3,2,1,0:T(8,128)(2,1)S(1)}, bf16[2,2,32,128]{3,2,1,0:T(8,128)(2,1)S(1)}, u32[]{:S(2)}, u32[]{:S(2)}) collective-permute-start(bf16[2,2,32,128]{3,2,1,0:T(8,128)(2,1)S(1)} %get-tuple-element.59), channel_id=1, source_target_pairs={{2,4},{4,2},{6,8},{8,6},{10,12},{12,10},{3,5},{5,3},{7,9},{9,7},{1... | collective-permute-start | bytes 98312 | tf_op jit(solution)/shard_map/ppermute | solution.py:557
  18.0 2.7 %shard_map.90 = (f32[2,32,1024]{2,1,0:T(8,128)S(1)}, f32[32,512]{1,0:T(8,128)S(1)}, bf16[288,2048]{1,0:T(8,128)(2,1)S(1)}, bf16[128,2048]{1,0:T(8,128)(2,1)S(1)}, bf16[128,2048]{1,0:T(8,128)(2,1)S(1)}) custom-call(s32[2,27]{1,0:T(2,128)S(1)} %get-tuple-element.45.codes, bf16[2,2,8,32,128]{4,3,2,1,0:T(8,128)(2,1)S(1)} %get-tuple-element.54.own, ...), custom_call_target="tpu_custom_call" | custom-call | bytes 7500000 | tf_op jit(solution)/shard_map/pallas_call | solution.py:531
  20.8 0.2 collective-permute-start.8
  21.0 0.8 %shard_map.91.raw = f32[2,288,128]{2,1,0:T(8,128)S(1)} custom-call(bf16[288,2048]{1,0:T(8,128)(2,1)S(1)} %get-tuple-element.65.columns_f, bf16[288,2048]{1,0:T(8,128)(2,1)S(1)} %get-tuple-element.70.columns_h, bf16[128,2048]{1,0:T(8,128)(2,1)S(1)} %get-tuple-element.71.placed_f, bf16[128,2048]{1,0:T(8,128)(2,1)S(1)} %get-tuple-element.72.placed_s), custom_call_target="tpu_custom_call" | custom-call | bytes 3000000 | tf_op jit(solution)/shard_map/pallas_call | solution.py:531
  21.8 0.3 collective-permute-done.8.far
  22.1 1.5 %shard_map.92 = (f32[32,512]{1,0:T(8,128)S(1)}, f32[56,128]{1,0:T(8,128)S(1)}) custom-call(bf16[88,16,128]{2,1,0:T(8,128)(2,1)S(1)} %get-tuple-element.46.choose, bf16[2,2,8,32,128]{4,3,2,1,0:T(8,128)(2,1)S(1)} %get-tuple-element.54.own, bf16[2,2,8,32,128]{4,3,2,1,0:T(8,128)(2,1)S(1)} %collective-permute-done.5.part, ...), custom_call_target="tpu_custom_call" | custom-call | bytes 6000000 | tf_op jit(solution)/shard_map/pallas_call | solution.py:531
  23.6 0.2 collective-permute-start.9
  23.8 1.0 %collective-permute-done.9 = f32[56,128]{1,0:T(8,128)S(1)} collective-permute-done((f32[56,128]{1,0:T(8,128)S(1)}, f32[56,128]{1,0:T(8,128)S(1)}, u32[]{:S(2)}, u32[]{:S(2)}) %collective-permute-start.9) | collective-permute-done | bytes 28704 | tf_op jit(solution)/shard_map/ppermute | solution.py:544
  24.9 4.5 %collective-permute-start.13 = (f32[56,128]{1,0:T(8,128)S(1)}, f32[56,128]{1,0:T(8,128)S(1)}, u32[]{:S(2)}, u32[]{:S(2)}) collective-permute-start(f32[56,128]{1,0:T(8,128)S(1)} %add.28), channel_id=1, source_target_pairs={{0,2},{2,0},{4,6},{6,4},{8,10},{10,8},{12,14},{14,12},{1,3},{3,1},... | collective-permute-start | bytes 86024 | tf_op jit(solution)/shard_map/ppermute | solution.py:647
  29.4 0.3 shard_map.93.own
  29.7 2.5 %collective-permute-start.11 = (bf16[64,512]{1,0:T(8,128)(2,1)S(1)}, bf16[64,512]{1,0:T(8,128)(2,1)S(1)}, u32[]{:S(2)}, u32[]{:S(2)}) collective-permute-start(bf16[64,512]{1,0:T(8,128)(2,1)S(1)} %shard_map.93.own), channel_id=1, source_target_pairs={{0,14},{2,12},{4,10},{6,8},{8,6},{10,4},{12,2},{14,0},{1,15},{3,13... | collective-permute-start | bytes 196616 | tf_op jit(solution)/shard_map/ppermute | solution.py:549
  32.2 1.7 %collective-permute-start.14 = (f32[56,128]{1,0:T(8,128)S(1)}, f32[56,128]{1,0:T(8,128)S(1)}, u32[]{:S(2)}, u32[]{:S(2)}) collective-permute-start(f32[56,128]{1,0:T(8,128)S(1)} %add.29), channel_id=1, source_target_pairs={{0,4},{2,6},{4,0},{6,2},{8,12},{10,14},{12,8},{14,10},{1,5},{3,7},... | collective-permute-start | bytes 86024 | tf_op jit(solution)/shard_map/ppermute | solution.py:647
  33.8 2.3 %collective-permute-done.14 = f32[56,128]{1,0:T(8,128)S(1)} collective-permute-done((f32[56,128]{1,0:T(8,128)S(1)}, f32[56,128]{1,0:T(8,128)S(1)}, u32[]{:S(2)}, u32[]{:S(2)}) %collective-permute-start.14) | collective-permute-done | bytes 28704 | tf_op jit(solution)/shard_map/ppermute | solution.py:647
  36.1 1.6 %collective-permute-start.15 = (f32[56,128]{1,0:T(8,128)S(1)}, f32[56,128]{1,0:T(8,128)S(1)}, u32[]{:S(2)}, u32[]{:S(2)}) collective-permute-start(f32[56,128]{1,0:T(8,128)S(1)} %add.30), channel_id=1, source_target_pairs={{0,8},{2,10},{4,12},{6,14},{8,0},{10,2},{12,4},{14,6},{1,9},{3,11}... | collective-permute-start | bytes 86024 | tf_op jit(solution)/shard_map/ppermute | solution.py:647
  37.7 0.5 %collective-permute-start.12 = (bf16[64,512]{1,0:T(8,128)(2,1)S(1)}, bf16[64,512]{1,0:T(8,128)(2,1)S(1)}, u32[]{:S(2)}, u32[]{:S(2)}) collective-permute-start(bf16[64,512]{1,0:T(8,128)(2,1)S(1)} %collective-permute-done.11.across_x), channel_id=1, source_target_pairs={{0,1},{1,0},{2,3},{3,2},{4,5},{5,4},{6,7},{7,6},{8,9},{9,8},{10,11... | collective-permute-start | bytes 196616 | tf_op jit(solution)/shard_map/ppermute | solution.py:544
  38.2 2.6 %collective-permute-done.15 = f32[56,128]{1,0:T(8,128)S(1)} collective-permute-done((f32[56,128]{1,0:T(8,128)S(1)}, f32[56,128]{1,0:T(8,128)S(1)}, u32[]{:S(2)}, u32[]{:S(2)}) %collective-permute-start.15) | collective-permute-done | bytes 28704 | tf_op jit(solution)/shard_map/ppermute | solution.py:647
  40.9 0.6 %fusion = (f32[27,84]{1,0:T(8,128)}, f32[27,84]{1,0:T(8,128)}) fusion(f32[56,128]{1,0:T(8,128)S(1)} %add.31), kind=kLoop, calls=%fused_computation.12 | loop fusion | bytes 36288 | tf_op jit(solution)/shard_map/slice | solution.py:649
  41.5 0.9 %shard_map.94 = bf16[30,2,512]{2,1,0:T(2,128)(2,1)} custom-call(bf16[6,16,128]{2,1,0:T(8,128)(2,1)S(1)} %get-tuple-element.44.turn_choice, bf16[64,512]{1,0:T(8,128)(2,1)S(1)} %shard_map.93.own, bf16[64,512]{1,0:T(8,128)(2,1)S(1)} %collective-permute-done.10.across_y, bf16[64,512]{1,0:T(8,128)(2,1)S(1)} %collective-permute-done.11.across_x, ...), custom_call_target="tpu_custom_call" | custom-call | bytes 2700000 | tf_op jit(solution)/shard_map/pallas_call | solution.py:531
  (34 shorter events, 0.2 us)
Async XLA Ops:
  0.6 11.7 %copy-start.2 = (s32[2,3]{1,0:T(2,128)S(1)}, s32[2,3]{1,0:T(2,128)}, u32[]{:S(2)}) copy-start(s32[2,3]{1,0:T(2,128)} %param.11) | copy-start | bytes 76
  0.6 11.7 %copy-start.3 = (s32[2,27]{1,0:T(2,128)S(1)}, s32[2,27]{1,0:T(2,128)}, u32[]{:S(2)}) copy-start(s32[2,27]{1,0:T(2,128)} %param.10) | copy-start | bytes 652
  0.7 11.7 %copy-start = (bf16[27,84]{1,0:T(8,128)(2,1)S(1)}, bf16[27,84]{1,0:T(8,128)(2,1)}, u32[]{:S(2)}) copy-start(bf16[27,84]{1,0:T(8,128)(2,1)} %param.9) | copy-start | bytes 13612
  0.7 11.7 %copy-start.1 = (bf16[27,84]{1,0:T(8,128)(2,1)S(1)}, bf16[27,84]{1,0:T(8,128)(2,1)}, u32[]{:S(2)}) copy-start(bf16[27,84]{1,0:T(8,128)(2,1)} %param.8) | copy-start | bytes 13612
  1.5 1.7 %collective-permute-start.3 = (bf16[2,30,512]{2,1,0:T(8,128)(2,1)S(1)}, bf16[2,30,512]{2,1,0:T(8,128)(2,1)S(1)}, u32[]{:S(2)}, u32[]{:S(2)}) collective-permute-start(bf16[2,30,512]{2,1,0:T(8,128)(2,1)S(1)} %copy.16.own), channel_id=1, source_target_pairs={{0,1},{1,0},{2,3},{3,2},{4,5},{5,4},{6,7},{7,6},{8,9},{9,8},{10,11... | collective-permute-start | bytes 184328 | tf_op jit(solution)/shard_map/ppermute | solution.py:544
  3.1 6.2 %collective-permute-start = (bf16[2,8,32,128]{3,2,0,1:T(8,128)(2,1)S(1)}, bf16[2,8,32,128]{3,2,0,1:T(8,128)(2,1)S(1)}, u32[]{:S(2)}, u32[]{:S(2)}) collective-permute-start(bf16[2,8,32,128]{3,2,0,1:T(8,128)(2,1)S(1)} %copy.10), channel_id=1, source_target_pairs={{0,1},{1,0},{2,3},{3,2},{4,5},{5,4},{6,7},{7,6},{8,9},{9,8},{10,11... | collective-permute-start | bytes 393224 | tf_op jit(solution)/shard_map/ppermute | solution.py:544
  3.3 11.5 %collective-permute-start.4 = (bf16[4,30,512]{2,1,0:T(8,128)(2,1)S(1)}, bf16[4,30,512]{2,1,0:T(8,128)(2,1)S(1)}, u32[]{:S(2)}, u32[]{:S(2)}) collective-permute-start(bf16[4,30,512]{2,1,0:T(8,128)(2,1)S(1)} %pad_maximum_fusion), channel_id=1, source_target_pairs={{0,14},{2,12},{4,10},{6,8},{8,6},{10,4},{12,2},{14,0},{1,15},{3,13... | collective-permute-start | bytes 368648 | tf_op jit(solution)/shard_map/ppermute | solution.py:549
  9.3 5.7 %collective-permute-start.2 = (bf16[4,32,128]{2,1,0:T(8,128)(2,1)S(1)}, bf16[4,32,128]{2,1,0:T(8,128)(2,1)S(1)}, u32[]{:S(2)}, u32[]{:S(2)}) collective-permute-start(bf16[4,32,128]{2,1,0:T(8,128)(2,1)S(1)} %get-tuple-element.81), channel_id=1, source_target_pairs={{2,4},{4,2},{6,8},{8,6},{10,12},{12,10},{3,5},{5,3},{7,9},{9,7},{1... | collective-permute-start | bytes 98312 | tf_op jit(solution)/shard_map/ppermute | solution.py:557
  10.0 5.1 %collective-permute-start.1 = (bf16[4,32,128]{2,1,0:T(8,128)(2,1)S(1)}, bf16[4,32,128]{2,1,0:T(8,128)(2,1)S(1)}, u32[]{:S(2)}, u32[]{:S(2)}) collective-permute-start(bf16[4,32,128]{2,1,0:T(8,128)(2,1)S(1)} %get-tuple-element.82), channel_id=1, source_target_pairs={{0,2},{2,0},{4,6},{6,4},{8,10},{10,8},{12,14},{14,12},{1,3},{3,1},... | collective-permute-start | bytes 98312 | tf_op jit(solution)/shard_map/ppermute | solution.py:557
  15.6 2.3 %collective-permute-start.5 = (bf16[2,2,8,32,128]{4,3,2,1,0:T(8,128)(2,1)S(1)}, bf16[2,2,8,32,128]{4,3,2,1,0:T(8,128)(2,1)S(1)}, u32[]{:S(2)}, u32[]{:S(2)}) collective-permute-start(bf16[2,2,8,32,128]{4,3,2,1,0:T(8,128)(2,1)S(1)} %get-tuple-element.54.own), channel_id=1, source_target_pairs={{0,1},{1,0},{2,3},{3,2},{4,5},{5,4},{6,7},{7,6},{8,9},{9,8},{10,11... | collective-permute-start | bytes 786440 | tf_op jit(solution)/shard_map/ppermute | solution.py:544
  15.7 5.0 %collective-permute-start.6 = (bf16[2,2,32,128]{3,2,1,0:T(8,128)(2,1)S(1)}, bf16[2,2,32,128]{3,2,1,0:T(8,128)(2,1)S(1)}, u32[]{:S(2)}, u32[]{:S(2)}) collective-permute-start(bf16[2,2,32,128]{3,2,1,0:T(8,128)(2,1)S(1)} %get-tuple-element.58), channel_id=1, source_target_pairs={{0,2},{2,0},{4,6},{6,4},{8,10},{10,8},{12,14},{14,12},{1,3},{3,1},... | collective-permute-start | bytes 98312 | tf_op jit(solution)/shard_map/ppermute | solution.py:557
  17.3 3.4 %collective-permute-start.7 = (bf16[2,2,32,128]{3,2,1,0:T(8,128)(2,1)S(1)}, bf16[2,2,32,128]{3,2,1,0:T(8,128)(2,1)S(1)}, u32[]{:S(2)}, u32[]{:S(2)}) collective-permute-start(bf16[2,2,32,128]{3,2,1,0:T(8,128)(2,1)S(1)} %get-tuple-element.59), channel_id=1, source_target_pairs={{2,4},{4,2},{6,8},{8,6},{10,12},{12,10},{3,5},{5,3},{7,9},{9,7},{1... | collective-permute-start | bytes 98312 | tf_op jit(solution)/shard_map/ppermute | solution.py:557
  20.8 1.3 %collective-permute-start.8 = (bf16[2,2,2,32,128]{4,3,2,1,0:T(8,128)(2,1)S(1)}, bf16[2,2,2,32,128]{4,3,2,1,0:T(8,128)(2,1)S(1)}, u32[]{:S(2)}, u32[]{:S(2)}) collective-permute-start(bf16[2,2,2,32,128]{4,3,2,1,0:T(8,128)(2,1)S(1)} %pad_maximum_fusion.1), channel_id=1, source_target_pairs={{0,1},{1,0},{2,3},{3,2},{4,5},{5,4},{6,7},{7,6},{8,9},{9,8},{10,11... | collective-permute-start | bytes 196616 | tf_op jit(solution)/shard_map/ppermute | solution.py:544
  23.6 1.3 %collective-permute-start.9 = (f32[56,128]{1,0:T(8,128)S(1)}, f32[56,128]{1,0:T(8,128)S(1)}, u32[]{:S(2)}, u32[]{:S(2)}) collective-permute-start(f32[56,128]{1,0:T(8,128)S(1)} %get-tuple-element.74), channel_id=1, source_target_pairs={{0,1},{1,0},{2,3},{3,2},{4,5},{5,4},{6,7},{7,6},{8,9},{9,8},{10,11... | collective-permute-start | bytes 86024 | tf_op jit(solution)/shard_map/ppermute | solution.py:544
  24.9 7.3 %collective-permute-start.13 = (f32[56,128]{1,0:T(8,128)S(1)}, f32[56,128]{1,0:T(8,128)S(1)}, u32[]{:S(2)}, u32[]{:S(2)}) collective-permute-start(f32[56,128]{1,0:T(8,128)S(1)} %add.28), channel_id=1, source_target_pairs={{0,2},{2,0},{4,6},{6,4},{8,10},{10,8},{12,14},{14,12},{1,3},{3,1},... | collective-permute-start | bytes 86024 | tf_op jit(solution)/shard_map/ppermute | solution.py:647
  29.7 8.1 %collective-permute-start.11 = (bf16[64,512]{1,0:T(8,128)(2,1)S(1)}, bf16[64,512]{1,0:T(8,128)(2,1)S(1)}, u32[]{:S(2)}, u32[]{:S(2)}) collective-permute-start(bf16[64,512]{1,0:T(8,128)(2,1)S(1)} %shard_map.93.own), channel_id=1, source_target_pairs={{0,14},{2,12},{4,10},{6,8},{8,6},{10,4},{12,2},{14,0},{1,15},{3,13... | collective-permute-start | bytes 196616 | tf_op jit(solution)/shard_map/ppermute | solution.py:549
  32.2 3.9 %collective-permute-start.14 = (f32[56,128]{1,0:T(8,128)S(1)}, f32[56,128]{1,0:T(8,128)S(1)}, u32[]{:S(2)}, u32[]{:S(2)}) collective-permute-start(f32[56,128]{1,0:T(8,128)S(1)} %add.29), channel_id=1, source_target_pairs={{0,4},{2,6},{4,0},{6,2},{8,12},{10,14},{12,8},{14,10},{1,5},{3,7},... | collective-permute-start | bytes 86024 | tf_op jit(solution)/shard_map/ppermute | solution.py:647
  36.1 4.8 %collective-permute-start.15 = (f32[56,128]{1,0:T(8,128)S(1)}, f32[56,128]{1,0:T(8,128)S(1)}, u32[]{:S(2)}, u32[]{:S(2)}) collective-permute-start(f32[56,128]{1,0:T(8,128)S(1)} %add.30), channel_id=1, source_target_pairs={{0,8},{2,10},{4,12},{6,14},{8,0},{10,2},{12,4},{14,6},{1,9},{3,11}... | collective-permute-start | bytes 86024 | tf_op jit(solution)/shard_map/ppermute | solution.py:647
  37.7 3.8 %collective-permute-start.10 = (bf16[64,512]{1,0:T(8,128)(2,1)S(1)}, bf16[64,512]{1,0:T(8,128)(2,1)S(1)}, u32[]{:S(2)}, u32[]{:S(2)}) collective-permute-start(bf16[64,512]{1,0:T(8,128)(2,1)S(1)} %shard_map.93.own), channel_id=1, source_target_pairs={{0,1},{1,0},{2,3},{3,2},{4,5},{5,4},{6,7},{7,6},{8,9},{9,8},{10,11... | collective-permute-start | bytes 196616 | tf_op jit(solution)/shard_map/ppermute | solution.py:544
  37.7 3.8 %collective-permute-start.12 = (bf16[64,512]{1,0:T(8,128)(2,1)S(1)}, bf16[64,512]{1,0:T(8,128)(2,1)S(1)}, u32[]{:S(2)}, u32[]{:S(2)}) collective-permute-start(bf16[64,512]{1,0:T(8,128)(2,1)S(1)} %collective-permute-done.11.across_x), channel_id=1, source_target_pairs={{0,1},{1,0},{2,3},{3,2},{4,5},{5,4},{6,7},{7,6},{8,9},{9,8},{10,11... | collective-permute-start | bytes 196616 | tf_op jit(solution)/shard_map/ppermute | solution.py:544

commit v9 on v8

--- a/solution.py
+++ b/solution.py
@@ -436,8 +436,8 @@
 
 def second_edge_kernel(
     scale, choose, own, part, got_a, got_b, far, pre_edge, gate_edge, through_edge,
-    columns_f, columns_fe, raw, w_second, w_turned, second_edge, grads,
-    columns_h, columns_b, placed_f, placed_s, place,
+    columns_f, columns_fe, raw, w_turned, columns_h, grads,
+    columns_b, placed_f, placed_s, place,
 ):
     masks = region_masks()
     inside = jnp.concatenate([masks[4].astype(F32)] * 4, axis=1)
@@ -447,7 +447,6 @@
             lambda which, s: (got_a, got_b)[which][f, s], lambda which, s: far[which, f, s],
         )
         edge_columns(choose, masks, candidates, columns)
-    second_edge[...] = edge_terms(dot(w_second[...], columns_h[...]), 0)
     more_t = edge_terms(dot(w_turned[...], columns_b[...]), 0)
     back_pre = gate_back(through_edge[...] + more_t, pre_edge[...], gate_edge[...], gate_rows(), inside)
     placed_f[...] = jnp.zeros_like(placed_f)
@@ -492,7 +491,8 @@
     grads[54:56, :] = jnp.zeros((2, LANES), F32)
 
 
-def compact_kernel(second_in, more, second):
+def compact_kernel(second_in, columns, w_second, second):
+    more = edge_terms(dot(w_second[...], columns[...]), 0)
     zero = jnp.zeros((CH, LANES), F32)
     rows = []
     for n in range(2):
@@ -625,15 +625,15 @@
     columns_h, placed_f, placed_s = after((columns_h, placed_f, placed_s), *got)
     (raw,) = call(gradient_kernel, 1, 0, [((2, 288, LANES), F32)], [], columns, columns_h, placed_f, placed_s)
     n_bricks = features.shape[0] * lax.axis_size("xp") * lax.axis_size("yp")
-    second_e, grads = call(
-        functools.partial(second_edge_kernel, 1.0 / n_bricks), 2, 0, [((CH, 4 * LANES), F32), ((56, LANES), F32)],
-        [((288, 4 * LANES), BF)] * 2
+    columns_he, grads = call(
+        functools.partial(second_edge_kernel, 1.0 / n_bricks), 2, 0, [((288, 4 * LANES), BF), ((56, LANES), F32)],
+        [((288, 4 * LANES), BF)]
         + [((128, 12 * LANES), BF), ((128, 4 * LANES), BF), ((256, 3 * LANES), BF)],
-        choose, both, part, *got, far, pre_e, gate_e, through_e, columns, columns_e, raw, w2, w2t,
+        choose, both, part, *got, far, pre_e, gate_e, through_e, columns, columns_e, raw, w2t,
     )
     total = grads + swap_y(grads)
-    second_part, second_e = after((second_part, second_e), total)
-    (second,) = call(compact_kernel, 0.5, 0, [((64, 512), BF)], [], second_part, second_e)
+    second_part, columns_he = after((second_part, columns_he), total)
+    (second,) = call(compact_kernel, 0.5, 0, [((64, 512), BF)], [], second_part, columns_he, w2)
     second_y = swap_y(second)
     second_x = mirror_x(second)
     second_xy = swap_y(second_x)

time: 42.7 us -> 42.6 us (level)
  transfers between devices with their start and end apart: 16 -> 16, of which waited for: 4 -> 4; matrix products, arithmetic and copies ran while one was open for 4% -> 4% of each run, Pallas kernels for 15% -> 16%
where the time goes in v9:
time: 42.6 us; the launch traced here: 42.3 us
  starting transfers between devices  23.1 us (54%)
  Pallas kernels  9.45 us (22%)
  waiting for transfers between devices  6.44 us (15%)
  local copies, waits for them, and re-layouts  2.36 us (6%)
  between operations  0.88 us (2%)
    pallas_call x10, Pallas kernels, call(): pl.pallas_call(kernel, out_shape=tuple((jax.ShapeDtypeStruct(s, t) for s,...  9.45 us
    ppermute x2, starting transfers between devices, mirror_x(): return lax.ppermute(x, 'xp', [(i, n - 1 - i) for i in range(n)])  8.58 us
    ppermute x3, starting transfers between devices, on_device(): total = total + lax.ppermute(total, 'xp', [(i, i ^ bit) for i in range(n)])  7.63 us
    ppermute x4, starting transfers between devices, pair_swap(): return lax.ppermute(x, 'xp', pairs)  5.23 us
    ppermute x3, waiting for transfers between devices, on_device(): total = total + lax.ppermute(total, 'xp', [(i, i ^ bit) for i in range(n)])  5.07 us
    unnamed x10, local copies, waits for them, and re-layouts  1.72 us
    ppermute x7, starting transfers between devices, swap_y(): return lax.ppermute(x, 'yp', [(i, n - 1 - i) for i in range(n)])  1.68 us
    ppermute x7, waiting for transfers between devices, swap_y(): return lax.ppermute(x, 'yp', [(i, n - 1 - i) for i in range(n)])  1.36 us
  transfers between devices with their start and end apart: 16, of which 4 were waited for; matrix products, arithmetic and copies ran while one was open for 4% of the time, Pallas kernels for 16%

profile of v9, /device:TPU:0, one launch (start us, length us, event | category | flops | bytes accessed | tf_op | source)
XLA Modules:
  0.0 42.3 jit_solution(3118914284922696288)
XLA Ops:
  0.7 0.9 %copy.16.own = bf16[2,30,512]{2,1,0:T(8,128)(2,1)S(1)} copy(bf16[2,30,512]{2,0,1:T(2,128)(2,1)} %param.7) | data formatting | bytes 122880 | tf_op args[1]
  1.5 0.5 %collective-permute-start.3 = (bf16[2,30,512]{2,1,0:T(8,128)(2,1)S(1)}, bf16[2,30,512]{2,1,0:T(8,128)(2,1)S(1)}, u32[]{:S(2)}, u32[]{:S(2)}) collective-permute-start(bf16[2,30,512]{2,1,0:T(8,128)(2,1)S(1)} %copy.16.own), channel_id=1, source_target_pairs={{0,1},{1,0},{2,3},{3,2},{4,5},{5,4},{6,7},{7,6},{8,9},{9,8},{10,11... | collective-permute-start | bytes 184328 | tf_op jit(solution)/shard_map/ppermute | solution.py:544
  2.1 0.8 %copy.9.features = bf16[2,30,512]{2,1,0:T(8,128)(2,1)S(1)} copy(bf16[2,30,512]{2,0,1:T(2,128)(2,1)} %param.6) | data formatting | bytes 122880 | tf_op args[0]
  2.9 0.2 shard_map.85.own
  3.1 0.1 collective-permute-start
  3.3 6.1 %collective-permute-start.4 = (bf16[4,30,512]{2,1,0:T(8,128)(2,1)S(1)}, bf16[4,30,512]{2,1,0:T(8,128)(2,1)S(1)}, u32[]{:S(2)}, u32[]{:S(2)}) collective-permute-start(bf16[4,30,512]{2,1,0:T(8,128)(2,1)S(1)} %pad_maximum_fusion), channel_id=1, source_target_pairs={{0,14},{2,12},{4,10},{6,8},{8,6},{10,4},{12,2},{14,0},{1,15},{3,13... | collective-permute-start | bytes 368648 | tf_op jit(solution)/shard_map/ppermute | solution.py:549
  9.3 0.7 %collective-permute-start.2 = (bf16[4,32,128]{2,1,0:T(8,128)(2,1)S(1)}, bf16[4,32,128]{2,1,0:T(8,128)(2,1)S(1)}, u32[]{:S(2)}, u32[]{:S(2)}) collective-permute-start(bf16[4,32,128]{2,1,0:T(8,128)(2,1)S(1)} %get-tuple-element.81), channel_id=1, source_target_pairs={{2,4},{4,2},{6,8},{8,6},{10,12},{12,10},{3,5},{5,3},{7,9},{9,7},{1... | collective-permute-start | bytes 98312 | tf_op jit(solution)/shard_map/ppermute | solution.py:557
  10.0 2.3 %collective-permute-start.1 = (bf16[4,32,128]{2,1,0:T(8,128)(2,1)S(1)}, bf16[4,32,128]{2,1,0:T(8,128)(2,1)S(1)}, u32[]{:S(2)}, u32[]{:S(2)}) collective-permute-start(bf16[4,32,128]{2,1,0:T(8,128)(2,1)S(1)} %get-tuple-element.82), channel_id=1, source_target_pairs={{0,2},{2,0},{4,6},{6,4},{8,10},{10,8},{12,14},{14,12},{1,3},{3,1},... | collective-permute-start | bytes 98312 | tf_op jit(solution)/shard_map/ppermute | solution.py:557
  12.4 0.5 %shard_map.86 = (bf16[192,288]{1,0:T(8,128)(2,1)S(1)}, bf16[96,288]{1,0:T(8,128)(2,1)S(1)}, bf16[96,288]{1,0:T(8,128)(2,1)S(1)}, s32[2,27]{1,0:T(2,128)S(1)}, bf...) custom-call(bf16[32,256]{1,0:T(8,128)(2,1)S(1)} %pad_add_fusion.packed, s32[2,256]{1,0:T(2,128)S(1)} %pad_add_fusion.1.small), custom_call_target="tpu_custom_call" | custom-call | bytes 3000000 | tf_op jit(solution)/shard_map/pallas_call | solution.py:531
  12.9 1.9 %shard_map.87 = (bf16[288,2048]{1,0:T(8,128)(2,1)S(1)}, f32[2,32,1024]{2,1,0:T(8,128)S(1)}, f32[2,32,1024]{2,1,0:T(8,128)S(1)}, bf16[2,6,32,128]{3,2,1,0:T(8,128)(2,1)S(1)}) custom-call(s32[2,27]{1,0:T(2,128)S(1)} %get-tuple-element.45.codes, bf16[2,8,32,128]{3,2,1,0:T(8,128)(2,1)S(1)} %shard_map.85.own, bf16[2,8,32,128]{3,2,1,0:T(8,128)(2,1)S(1)} %copy.17.part, ...), custom_call_target="tpu_custom_call" | custom-call | bytes 6000000 | tf_op jit(solution)/shard_map/pallas_call | solution.py:531
  14.8 0.3 shard_map.88.back
  15.1 0.6 %shard_map.89 = (bf16[288,512]{1,0:T(8,128)(2,1)S(1)}, f32[32,512]{1,0:T(8,128)S(1)}, f32[32,512]{1,0:T(8,128)S(1)}, bf16[2,2,8,32,128]{4,3,2,1,0:T(8,128)(2,1)S...) custom-call(bf16[88,16,128]{2,1,0:T(8,128)(2,1)S(1)} %get-tuple-element.46.choose, ...), custom_call_target="tpu_custom_call" | custom-call | bytes 3000000 | tf_op jit(solution)/shard_map/pallas_call | solution.py:531
  15.6 0.1 collective-permute-start.5
  15.7 1.6 %collective-permute-start.6 = (bf16[2,2,32,128]{3,2,1,0:T(8,128)(2,1)S(1)}, bf16[2,2,32,128]{3,2,1,0:T(8,128)(2,1)S(1)}, u32[]{:S(2)}, u32[]{:S(2)}) collective-permute-start(bf16[2,2,32,128]{3,2,1,0:T(8,128)(2,1)S(1)} %get-tuple-element.58), channel_id=1, source_target_pairs={{0,2},{2,0},{4,6},{6,4},{8,10},{10,8},{12,14},{14,12},{1,3},{3,1},... | collective-permute-start | bytes 98312 | tf_op jit(solution)/shard_map/ppermute | solution.py:557
  17.3 0.7 %collective-permute-start.7 = (bf16[2,2,32,128]{3,2,1,0:T(8,128)(2,1)S(1)}, bf16[2,2,32,128]{3,2,1,0:T(8,128)(2,1)S(1)}, u32[]{:S(2)}, u32[]{:S(2)}) collective-permute-start(bf16[2,2,32,128]{3,2,1,0:T(8,128)(2,1)S(1)} %get-tuple-element.59), channel_id=1, source_target_pairs={{2,4},{4,2},{6,8},{8,6},{10,12},{12,10},{3,5},{5,3},{7,9},{9,7},{1... | collective-permute-start | bytes 98312 | tf_op jit(solution)/shard_map/ppermute | solution.py:557
  18.0 2.7 %shard_map.90 = (f32[2,32,1024]{2,1,0:T(8,128)S(1)}, f32[32,512]{1,0:T(8,128)S(1)}, bf16[288,2048]{1,0:T(8,128)(2,1)S(1)}, bf16[128,2048]{1,0:T(8,128)(2,1)S(1)}, bf16[128,2048]{1,0:T(8,128)(2,1)S(1)}) custom-call(s32[2,27]{1,0:T(2,128)S(1)} %get-tuple-element.45.codes, bf16[2,2,8,32,128]{4,3,2,1,0:T(8,128)(2,1)S(1)} %get-tuple-element.54.own, ...), custom_call_target="tpu_custom_call" | custom-call | bytes 7500000 | tf_op jit(solution)/shard_map/pallas_call | solution.py:531
  20.8 0.2 collective-permute-start.8
  21.0 0.8 %shard_map.91.raw = f32[2,288,128]{2,1,0:T(8,128)S(1)} custom-call(bf16[288,2048]{1,0:T(8,128)(2,1)S(1)} %get-tuple-element.65.columns_f, bf16[288,2048]{1,0:T(8,128)(2,1)S(1)} %get-tuple-element.70.columns_h, bf16[128,2048]{1,0:T(8,128)(2,1)S(1)} %get-tuple-element.71.placed_f, bf16[128,2048]{1,0:T(8,128)(2,1)S(1)} %get-tuple-element.72.placed_s), custom_call_target="tpu_custom_call" | custom-call | bytes 3000000 | tf_op jit(solution)/shard_map/pallas_call | solution.py:531
  21.8 0.3 collective-permute-done.8.far
  22.1 1.3 %shard_map.92 = (bf16[288,512]{1,0:T(8,128)(2,1)S(1)}, f32[56,128]{1,0:T(8,128)S(1)}) custom-call(bf16[88,16,128]{2,1,0:T(8,128)(2,1)S(1)} %get-tuple-element.46.choose, bf16[2,2,8,32,128]{4,3,2,1,0:T(8,128)(2,1)S(1)} %get-tuple-element.54.own, bf16[2,2,8,32,128]{4,3,2,1,0:T(8,128)(2,1)S(1)} %collective-permute-done.5.part, ...), custom_call_target="tpu_custom_call" | custom-call | bytes 6000000 | tf_op jit(solution)/shard_map/pallas_call | solution.py:531
  23.4 0.2 collective-permute-start.9
  23.6 1.0 %collective-permute-done.9 = f32[56,128]{1,0:T(8,128)S(1)} collective-permute-done((f32[56,128]{1,0:T(8,128)S(1)}, f32[56,128]{1,0:T(8,128)S(1)}, u32[]{:S(2)}, u32[]{:S(2)}) %collective-permute-start.9) | collective-permute-done | bytes 28704 | tf_op jit(solution)/shard_map/ppermute | solution.py:544
  24.7 4.5 %collective-permute-start.13 = (f32[56,128]{1,0:T(8,128)S(1)}, f32[56,128]{1,0:T(8,128)S(1)}, u32[]{:S(2)}, u32[]{:S(2)}) collective-permute-start(f32[56,128]{1,0:T(8,128)S(1)} %add.28), channel_id=1, source_target_pairs={{0,2},{2,0},{4,6},{6,4},{8,10},{10,8},{12,14},{14,12},{1,3},{3,1},... | collective-permute-start | bytes 86024 | tf_op jit(solution)/shard_map/ppermute | solution.py:647
  29.2 0.3 shard_map.93.own
  29.5 2.5 %collective-permute-start.11 = (bf16[64,512]{1,0:T(8,128)(2,1)S(1)}, bf16[64,512]{1,0:T(8,128)(2,1)S(1)}, u32[]{:S(2)}, u32[]{:S(2)}) collective-permute-start(bf16[64,512]{1,0:T(8,128)(2,1)S(1)} %shard_map.93.own), channel_id=1, source_target_pairs={{0,14},{2,12},{4,10},{6,8},{8,6},{10,4},{12,2},{14,0},{1,15},{3,13... | collective-permute-start | bytes 196616 | tf_op jit(solution)/shard_map/ppermute | solution.py:549
  32.0 1.6 %collective-permute-start.14 = (f32[56,128]{1,0:T(8,128)S(1)}, f32[56,128]{1,0:T(8,128)S(1)}, u32[]{:S(2)}, u32[]{:S(2)}) collective-permute-start(f32[56,128]{1,0:T(8,128)S(1)} %add.29), channel_id=1, source_target_pairs={{0,4},{2,6},{4,0},{6,2},{8,12},{10,14},{12,8},{14,10},{1,5},{3,7},... | collective-permute-start | bytes 86024 | tf_op jit(solution)/shard_map/ppermute | solution.py:647
  33.6 2.4 %collective-permute-done.14 = f32[56,128]{1,0:T(8,128)S(1)} collective-permute-done((f32[56,128]{1,0:T(8,128)S(1)}, f32[56,128]{1,0:T(8,128)S(1)}, u32[]{:S(2)}, u32[]{:S(2)}) %collective-permute-start.14) | collective-permute-done | bytes 28704 | tf_op jit(solution)/shard_map/ppermute | solution.py:647
  36.0 1.5 %collective-permute-start.15 = (f32[56,128]{1,0:T(8,128)S(1)}, f32[56,128]{1,0:T(8,128)S(1)}, u32[]{:S(2)}, u32[]{:S(2)}) collective-permute-start(f32[56,128]{1,0:T(8,128)S(1)} %add.30), channel_id=1, source_target_pairs={{0,8},{2,10},{4,12},{6,14},{8,0},{10,2},{12,4},{14,6},{1,9},{3,11}... | collective-permute-start | bytes 86024 | tf_op jit(solution)/shard_map/ppermute | solution.py:647
  37.5 0.5 %collective-permute-start.12 = (bf16[64,512]{1,0:T(8,128)(2,1)S(1)}, bf16[64,512]{1,0:T(8,128)(2,1)S(1)}, u32[]{:S(2)}, u32[]{:S(2)}) collective-permute-start(bf16[64,512]{1,0:T(8,128)(2,1)S(1)} %collective-permute-done.11.across_x), channel_id=1, source_target_pairs={{0,1},{1,0},{2,3},{3,2},{4,5},{5,4},{6,7},{7,6},{8,9},{9,8},{10,11... | collective-permute-start | bytes 196616 | tf_op jit(solution)/shard_map/ppermute | solution.py:544
  38.0 2.7 %collective-permute-done.15 = f32[56,128]{1,0:T(8,128)S(1)} collective-permute-done((f32[56,128]{1,0:T(8,128)S(1)}, f32[56,128]{1,0:T(8,128)S(1)}, u32[]{:S(2)}, u32[]{:S(2)}) %collective-permute-start.15) | collective-permute-done | bytes 28704 | tf_op jit(solution)/shard_map/ppermute | solution.py:647
  40.8 0.6 %fusion = (f32[27,84]{1,0:T(8,128)}, f32[27,84]{1,0:T(8,128)}) fusion(f32[56,128]{1,0:T(8,128)S(1)} %add.31), kind=kLoop, calls=%fused_computation.12 | loop fusion | bytes 36288 | tf_op jit(solution)/shard_map/slice | solution.py:649
  41.4 0.9 %shard_map.94 = bf16[30,2,512]{2,1,0:T(2,128)(2,1)} custom-call(bf16[6,16,128]{2,1,0:T(8,128)(2,1)S(1)} %get-tuple-element.44.turn_choice, bf16[64,512]{1,0:T(8,128)(2,1)S(1)} %shard_map.93.own, bf16[64,512]{1,0:T(8,128)(2,1)S(1)} %collective-permute-done.10.across_y, bf16[64,512]{1,0:T(8,128)(2,1)S(1)} %collective-permute-done.11.across_x, ...), custom_call_target="tpu_custom_call" | custom-call | bytes 2700000 | tf_op jit(solution)/shard_map/pallas_call | solution.py:531
  (34 shorter events, 0.2 us)
Async XLA Ops:
  0.6 11.7 %copy-start.2 = (s32[2,3]{1,0:T(2,128)S(1)}, s32[2,3]{1,0:T(2,128)}, u32[]{:S(2)}) copy-start(s32[2,3]{1,0:T(2,128)} %param.11) | copy-start | bytes 76
  0.6 11.7 %copy-start.3 = (s32[2,27]{1,0:T(2,128)S(1)}, s32[2,27]{1,0:T(2,128)}, u32[]{:S(2)}) copy-start(s32[2,27]{1,0:T(2,128)} %param.10) | copy-start | bytes 652
  0.7 11.7 %copy-start = (bf16[27,84]{1,0:T(8,128)(2,1)S(1)}, bf16[27,84]{1,0:T(8,128)(2,1)}, u32[]{:S(2)}) copy-start(bf16[27,84]{1,0:T(8,128)(2,1)} %param.9) | copy-start | bytes 13612
  0.7 11.7 %copy-start.1 = (bf16[27,84]{1,0:T(8,128)(2,1)S(1)}, bf16[27,84]{1,0:T(8,128)(2,1)}, u32[]{:S(2)}) copy-start(bf16[27,84]{1,0:T(8,128)(2,1)} %param.8) | copy-start | bytes 13612
  1.5 1.7 %collective-permute-start.3 = (bf16[2,30,512]{2,1,0:T(8,128)(2,1)S(1)}, bf16[2,30,512]{2,1,0:T(8,128)(2,1)S(1)}, u32[]{:S(2)}, u32[]{:S(2)}) collective-permute-start(bf16[2,30,512]{2,1,0:T(8,128)(2,1)S(1)} %copy.16.own), channel_id=1, source_target_pairs={{0,1},{1,0},{2,3},{3,2},{4,5},{5,4},{6,7},{7,6},{8,9},{9,8},{10,11... | collective-permute-start | bytes 184328 | tf_op jit(solution)/shard_map/ppermute | solution.py:544
  3.1 6.2 %collective-permute-start = (bf16[2,8,32,128]{3,2,0,1:T(8,128)(2,1)S(1)}, bf16[2,8,32,128]{3,2,0,1:T(8,128)(2,1)S(1)}, u32[]{:S(2)}, u32[]{:S(2)}) collective-permute-start(bf16[2,8,32,128]{3,2,0,1:T(8,128)(2,1)S(1)} %copy.10), channel_id=1, source_target_pairs={{0,1},{1,0},{2,3},{3,2},{4,5},{5,4},{6,7},{7,6},{8,9},{9,8},{10,11... | collective-permute-start | bytes 393224 | tf_op jit(solution)/shard_map/ppermute | solution.py:544
  3.3 11.5 %collective-permute-start.4 = (bf16[4,30,512]{2,1,0:T(8,128)(2,1)S(1)}, bf16[4,30,512]{2,1,0:T(8,128)(2,1)S(1)}, u32[]{:S(2)}, u32[]{:S(2)}) collective-permute-start(bf16[4,30,512]{2,1,0:T(8,128)(2,1)S(1)} %pad_maximum_fusion), channel_id=1, source_target_pairs={{0,14},{2,12},{4,10},{6,8},{8,6},{10,4},{12,2},{14,0},{1,15},{3,13... | collective-permute-start | bytes 368648 | tf_op jit(solution)/shard_map/ppermute | solution.py:549
  9.3 5.7 %collective-permute-start.2 = (bf16[4,32,128]{2,1,0:T(8,128)(2,1)S(1)}, bf16[4,32,128]{2,1,0:T(8,128)(2,1)S(1)}, u32[]{:S(2)}, u32[]{:S(2)}) collective-permute-start(bf16[4,32,128]{2,1,0:T(8,128)(2,1)S(1)} %get-tuple-element.81), channel_id=1, source_target_pairs={{2,4},{4,2},{6,8},{8,6},{10,12},{12,10},{3,5},{5,3},{7,9},{9,7},{1... | collective-permute-start | bytes 98312 | tf_op jit(solution)/shard_map/ppermute | solution.py:557
  10.0 5.1 %collective-permute-start.1 = (bf16[4,32,128]{2,1,0:T(8,128)(2,1)S(1)}, bf16[4,32,128]{2,1,0:T(8,128)(2,1)S(1)}, u32[]{:S(2)}, u32[]{:S(2)}) collective-permute-start(bf16[4,32,128]{2,1,0:T(8,128)(2,1)S(1)} %get-tuple-element.82), channel_id=1, source_target_pairs={{0,2},{2,0},{4,6},{6,4},{8,10},{10,8},{12,14},{14,12},{1,3},{3,1},... | collective-permute-start | bytes 98312 | tf_op jit(solution)/shard_map/ppermute | solution.py:557
  15.6 2.3 %collective-permute-start.5 = (bf16[2,2,8,32,128]{4,3,2,1,0:T(8,128)(2,1)S(1)}, bf16[2,2,8,32,128]{4,3,2,1,0:T(8,128)(2,1)S(1)}, u32[]{:S(2)}, u32[]{:S(2)}) collective-permute-start(bf16[2,2,8,32,128]{4,3,2,1,0:T(8,128)(2,1)S(1)} %get-tuple-element.54.own), channel_id=1, source_target_pairs={{0,1},{1,0},{2,3},{3,2},{4,5},{5,4},{6,7},{7,6},{8,9},{9,8},{10,11... | collective-permute-start | bytes 786440 | tf_op jit(solution)/shard_map/ppermute | solution.py:544
  15.7 5.0 %collective-permute-start.6 = (bf16[2,2,32,128]{3,2,1,0:T(8,128)(2,1)S(1)}, bf16[2,2,32,128]{3,2,1,0:T(8,128)(2,1)S(1)}, u32[]{:S(2)}, u32[]{:S(2)}) collective-permute-start(bf16[2,2,32,128]{3,2,1,0:T(8,128)(2,1)S(1)} %get-tuple-element.58), channel_id=1, source_target_pairs={{0,2},{2,0},{4,6},{6,4},{8,10},{10,8},{12,14},{14,12},{1,3},{3,1},... | collective-permute-start | bytes 98312 | tf_op jit(solution)/shard_map/ppermute | solution.py:557
  17.3 3.4 %collective-permute-start.7 = (bf16[2,2,32,128]{3,2,1,0:T(8,128)(2,1)S(1)}, bf16[2,2,32,128]{3,2,1,0:T(8,128)(2,1)S(1)}, u32[]{:S(2)}, u32[]{:S(2)}) collective-permute-start(bf16[2,2,32,128]{3,2,1,0:T(8,128)(2,1)S(1)} %get-tuple-element.59), channel_id=1, source_target_pairs={{2,4},{4,2},{6,8},{8,6},{10,12},{12,10},{3,5},{5,3},{7,9},{9,7},{1... | collective-permute-start | bytes 98312 | tf_op jit(solution)/shard_map/ppermute | solution.py:557
  20.8 1.3 %collective-permute-start.8 = (bf16[2,2,2,32,128]{4,3,2,1,0:T(8,128)(2,1)S(1)}, bf16[2,2,2,32,128]{4,3,2,1,0:T(8,128)(2,1)S(1)}, u32[]{:S(2)}, u32[]{:S(2)}) collective-permute-start(bf16[2,2,2,32,128]{4,3,2,1,0:T(8,128)(2,1)S(1)} %pad_maximum_fusion.1), channel_id=1, source_target_pairs={{0,1},{1,0},{2,3},{3,2},{4,5},{5,4},{6,7},{7,6},{8,9},{9,8},{10,11... | collective-permute-start | bytes 196616 | tf_op jit(solution)/shard_map/ppermute | solution.py:544
  23.4 1.3 %collective-permute-start.9 = (f32[56,128]{1,0:T(8,128)S(1)}, f32[56,128]{1,0:T(8,128)S(1)}, u32[]{:S(2)}, u32[]{:S(2)}) collective-permute-start(f32[56,128]{1,0:T(8,128)S(1)} %get-tuple-element.74), channel_id=1, source_target_pairs={{0,1},{1,0},{2,3},{3,2},{4,5},{5,4},{6,7},{7,6},{8,9},{9,8},{10,11... | collective-permute-start | bytes 86024 | tf_op jit(solution)/shard_map/ppermute | solution.py:544
  24.7 7.4 %collective-permute-start.13 = (f32[56,128]{1,0:T(8,128)S(1)}, f32[56,128]{1,0:T(8,128)S(1)}, u32[]{:S(2)}, u32[]{:S(2)}) collective-permute-start(f32[56,128]{1,0:T(8,128)S(1)} %add.28), channel_id=1, source_target_pairs={{0,2},{2,0},{4,6},{6,4},{8,10},{10,8},{12,14},{14,12},{1,3},{3,1},... | collective-permute-start | bytes 86024 | tf_op jit(solution)/shard_map/ppermute | solution.py:647
  29.5 8.0 %collective-permute-start.11 = (bf16[64,512]{1,0:T(8,128)(2,1)S(1)}, bf16[64,512]{1,0:T(8,128)(2,1)S(1)}, u32[]{:S(2)}, u32[]{:S(2)}) collective-permute-start(bf16[64,512]{1,0:T(8,128)(2,1)S(1)} %shard_map.93.own), channel_id=1, source_target_pairs={{0,14},{2,12},{4,10},{6,8},{8,6},{10,4},{12,2},{14,0},{1,15},{3,13... | collective-permute-start | bytes 196616 | tf_op jit(solution)/shard_map/ppermute | solution.py:549
  32.0 3.9 %collective-permute-start.14 = (f32[56,128]{1,0:T(8,128)S(1)}, f32[56,128]{1,0:T(8,128)S(1)}, u32[]{:S(2)}, u32[]{:S(2)}) collective-permute-start(f32[56,128]{1,0:T(8,128)S(1)} %add.29), channel_id=1, source_target_pairs={{0,4},{2,6},{4,0},{6,2},{8,12},{10,14},{12,8},{14,10},{1,5},{3,7},... | collective-permute-start | bytes 86024 | tf_op jit(solution)/shard_map/ppermute | solution.py:647
  36.0 4.8 %collective-permute-start.15 = (f32[56,128]{1,0:T(8,128)S(1)}, f32[56,128]{1,0:T(8,128)S(1)}, u32[]{:S(2)}, u32[]{:S(2)}) collective-permute-start(f32[56,128]{1,0:T(8,128)S(1)} %add.30), channel_id=1, source_target_pairs={{0,8},{2,10},{4,12},{6,14},{8,0},{10,2},{12,4},{14,6},{1,9},{3,11}... | collective-permute-start | bytes 86024 | tf_op jit(solution)/shard_map/ppermute | solution.py:647
  37.5 3.9 %collective-permute-start.10 = (bf16[64,512]{1,0:T(8,128)(2,1)S(1)}, bf16[64,512]{1,0:T(8,128)(2,1)S(1)}, u32[]{:S(2)}, u32[]{:S(2)}) collective-permute-start(bf16[64,512]{1,0:T(8,128)(2,1)S(1)} %shard_map.93.own), channel_id=1, source_target_pairs={{0,1},{1,0},{2,3},{3,2},{4,5},{5,4},{6,7},{7,6},{8,9},{9,8},{10,11... | collective-permute-start | bytes 196616 | tf_op jit(solution)/shard_map/ppermute | solution.py:544
  37.5 3.9 %collective-permute-start.12 = (bf16[64,512]{1,0:T(8,128)(2,1)S(1)}, bf16[64,512]{1,0:T(8,128)(2,1)S(1)}, u32[]{:S(2)}, u32[]{:S(2)}) collective-permute-start(bf16[64,512]{1,0:T(8,128)(2,1)S(1)} %collective-permute-done.11.across_x), channel_id=1, source_target_pairs={{0,1},{1,0},{2,3},{3,2},{4,5},{5,4},{6,7},{7,6},{8,9},{9,8},{10,11... | collective-permute-start | bytes 196616 | tf_op jit(solution)/shard_map/ppermute | solution.py:544

commit v10 on v9

--- a/solution.py
+++ b/solution.py
@@ -108,14 +108,6 @@
 
 def is_odd():
     return (lax.axis_index("xp") & 1) == 1
-
-
-def table_row(codes, n, o, last):
-    e = codes[n, o]
-    d = e >> 1
-    dx = lax.div(d, 3)
-    other = jnp.where(d - 3 * dx == 1, 0, 2) + jnp.where(dx == 1, 0, 4)
-    return jnp.where(e >= 18, last, jnp.minimum(other + (e & 1), last))
 
 
 def gathered(pieces_of, masks):
@@ -141,19 +133,18 @@
             columns[o * CH : (o + 1) * CH, at : at + LANES] = moved[p * CH : (p + 1) * CH]
 
 
-def stage_mid(table, own, part):
-    zero = jnp.zeros((CH, LANES), BF)
-    for x in range(8):
-        for s in range(2):
-            table[s, x] = own(s, x)
-            table[2 + s, x] = part(s, x)
-        table[4, x] = zero
-
-
-def mid_columns(codes, masks, table, columns):
-    for n in range(2):
-        planes = gathered(lambda o: [table[table_row(codes, n, 9 + o, 4)].reshape(8 * CH, LANES)], masks)
-        unfold(planes, 8, columns, n * MID)
+def mid_columns(choose, masks, own, part, columns):
+    same_y, other_y = ([planes(s).reshape(16, HALF, LANES) for s in range(2)] for planes in (own, part))
+    for n in range(2):
+        rows = [pick(choose, OTHER_Y + 2 * n + k, same_y, other_y) for k in range(2)]
+        found = (rows[0], same_y, rows[1])
+
+        def pieces(o):
+            first, second = found[o // 3]
+            at = MID_SLOTS + 2 * (9 * n + o)
+            return [(first * choose[at] + second * choose[at + 1]).reshape(8 * CH, LANES)]
+
+        unfold(gathered(pieces, masks), 8, columns, n * MID)
 
 
 def edge_planes_of(own, part, received, far):
@@ -168,19 +159,20 @@
     return [[plane.reshape(2, HALF, LANES) for plane in side] for side in (low, high)]
 
 
-OTHER_X, OTHER_Y, SLOTS, N_CHOICES = 0, 8, 16, 88
+OTHER_X, OTHER_Y, SLOTS, MID_SLOTS, N_CHOICES = 0, 8, 16, 88, 124
+
+
+def pick(choose, row, here, there):
+    return [p * choose[row + 4] + q * choose[row] for p, q in zip(here, there)]
 
 
 def edge_columns(choose, masks, candidates, columns):
-    def pick(row, here, there):
-        return [p * choose[row + 4] + q * choose[row] for p, q in zip(here, there)]
-
     found = []
     for e in range(4):
         own, part, near, far = (candidates[e & 1][2 * k : 2 * k + 2] for k in range(4))
-        same_y = pick(OTHER_X + e, own, near)
-        other_y = pick(OTHER_X + e, part, far)
-        rows = [pick(OTHER_Y + 2 * (e >> 1) + k, same_y, other_y) for k in range(2)]
+        same_y = pick(choose, OTHER_X + e, own, near)
+        other_y = pick(choose, OTHER_X + e, part, far)
+        rows = [pick(choose, OTHER_Y + 2 * (e >> 1) + k, same_y, other_y) for k in range(2)]
         found.append((rows[0], same_y, rows[1]))
 
     def pieces(o):
@@ -222,6 +214,10 @@
             for s in range(2):
                 choose[SLOTS + 2 * (9 * e + o) + s] = one(wide == s)
     for n in range(2):
+        for o in range(9):
+            wide = jnp.broadcast_to(slot[n : n + 1, 9 + o : 10 + o], shape)
+            for s in range(2):
+                choose[MID_SLOTS + 2 * (9 * n + o) + s] = one(wide == s)
         for r in range(3):
             wide = jnp.broadcast_to(mirror[n : n + 1, r : r + 1], shape)
             turn_choice[3 * n + r] = wide.astype(F32).astype(BF)
@@ -270,7 +266,7 @@
             fp[n, x] = planes[first : first + CH, (x & 1) * LANES : (x & 1) * LANES + LANES]
 
 
-def weights_kernel(packed, small, one_out, two_out, turned_out, codes_out, choose, turn_choice, padded, left):
+def weights_kernel(packed, small, one_out, two_out, turned_out, choose, turn_choice, padded, left):
     shape = (CH, LANES)
     i, c = iota(shape, 0), iota(shape, 1)
     double = jnp.where(i >= 20, 2.0, 1.0)
@@ -286,7 +282,6 @@
     padded[...] = jnp.zeros_like(padded)
     for which in range(2):
         padded[which, 0:27, 0:84] = packed[0:27, which * LANES : which * LANES + 84].astype(F32)
-    codes_out[...] = small[:, 0:27]
     write_choices(small[:, 0:LANES], small[:, LANES : 2 * LANES], choose, turn_choice)
     for which, rows, columns, blocks, out, base, flip in (
         (0, rows_out, by_in, True, one_out, 0, False),
@@ -310,11 +305,10 @@
                 out[base + a * CH : base + (a + 1) * CH, g * 128 : g * 128 + width] = tile[:, :width].astype(BF)
 
 
-def first_mid_kernel(codes, own, part, w_first, columns, pre, gate_in, hidden_mid, table):
+def first_mid_kernel(choose, own, part, w_first, columns, pre, gate_in, hidden_mid):
     masks = region_masks()
     inside = masks[4].astype(F32)
-    stage_mid(table, lambda s, x: own[s, x], lambda s, x: part[s, x])
-    mid_columns(codes, masks, table, columns)
+    mid_columns(choose, masks, lambda s: own[s], lambda s: part[s], columns)
     for n in range(2):
         stacked = dot(w_first[...], columns[:, n * MID : (n + 1) * MID])
         a, g = fold_mid(stacked, 0), fold_mid(stacked, 96)
@@ -397,14 +391,13 @@
 
 
 def second_mid_kernel(
-    codes, own, part, pre, gate_in, w_second, w_turned, second, through_edge, columns_h, placed_f, placed_s,
-    table, columns_b,
+    choose, own, part, pre, gate_in, w_second, w_turned, second, through_edge, columns_h, placed_f, placed_s,
+    columns_b,
 ):
     masks = region_masks()
     inside = jnp.concatenate([masks[4].astype(F32)] * 6, axis=1)
     for f, columns in ((0, columns_h), (1, columns_b)):
-        stage_mid(table.at[f], lambda s, x: own[f, s, x], lambda s, x: part[f, s, x])
-        mid_columns(codes, masks, table.at[f], columns)
+        mid_columns(choose, masks, lambda s: own[f, s], lambda s: part[f, s], columns)
     zero = jnp.zeros((CH, LANES), BF)
     rows8 = gate_rows()
     for placed in (placed_f, placed_s):
@@ -585,19 +578,19 @@
     odd = is_odd()
     got = exchange(jnp.where(odd, low, high), jnp.where(odd, high, low))
     w_first, w_second, codes, mirror = after((w_first, w_second, codes, mirror), part)
-    w1, w2, w2t, codes, choose, turn_choice = call(
+    w1, w2, w2t, choose, turn_choice = call(
         weights_kernel, 1, 0,
         [
-            ((192, 288), BF), ((96, 288), BF), ((96, 288), BF), (codes.shape, codes.dtype),
+            ((192, 288), BF), ((96, 288), BF), ((96, 288), BF),
             ((N_CHOICES, HALF, LANES), BF), ((6, HALF, LANES), BF),
         ],
         [((2, CH, LANES), F32), ((288, LANES), BF)],
         side_by_side((w_first, w_second), CH), side_by_side((codes, mirror), 2),
     )
     columns, pre, gate_in, hidden_mid = call(
-        first_mid_kernel, 2, 1,
+        first_mid_kernel, 2, 0,
         [((288, 2 * MID), BF), ((2, CH, MID), F32), ((2, CH, MID), F32), ((2, 6) + plane, BF)],
-        [((5, 8) + plane, BF)], codes, fp, part, w1,
+        [], choose, fp, part, w1,
     )
     (crossed,) = after((crossed,), hidden_mid)
     (back,) = call(
@@ -615,10 +608,10 @@
     got = exchange(face_a, face_b)
     part = swap_y(both)
     second_part, through_e, columns_h, placed_f, placed_s = call(
-        second_mid_kernel, 2.5, 1,
+        second_mid_kernel, 2.5, 0,
         [((2, CH, MID), F32), ((CH, 4 * LANES), F32), ((288, 2 * MID), BF), *[((128, 2 * MID), BF)] * 2],
-        [((2, 5, 8) + plane, BF), ((288, 2 * MID), BF)],
-        codes, both, part, pre, gate_in, w2, w2t,
+        [((288, 2 * MID), BF)],
+        choose, both, part, pre, gate_in, w2, w2t,
     )
     got = after(got, second_part)
     far = swap_y(jnp.stack(got))

time: 42.6 us -> 42.5 us (level)
  Pallas kernels: 9.45 us -> 8.5 us
  starting transfers between devices: 23.1 us -> 24 us
    pallas_call x10, Pallas kernels: 9.45 us -> 8.5 us  [call(): pl.pallas_call(kernel, out_shape=tuple((jax.ShapeDtypeStruct(s, t) for s,...]
    ppermute x4, starting transfers between devices: 5.23 us -> 5.71 us  [pair_swap(): return lax.ppermute(x, 'xp', pairs)]
    ppermute x2, starting transfers between devices: 8.58 us -> 9.01 us  [mirror_x(): return lax.ppermute(x, 'xp', [(i, n - 1 - i) for i in range(n)])]
  transfers between devices with their start and end apart: 16 -> 16, of which waited for: 4 -> 4; matrix products, arithmetic and copies ran while one was open for 4% -> 4% of each run, Pallas kernels for 16% -> 14%
where the time goes in v10:
time: 42.5 us; the launch traced here: 42.3 us
  starting transfers between devices  24 us (56%)
  Pallas kernels  8.5 us (20%)
  waiting for transfers between devices  6.45 us (15%)
  local copies, waits for them, and re-layouts  2.36 us (6%)
  between operations  0.88 us (2%)
    ppermute x2, starting transfers between devices, mirror_x(): return lax.ppermute(x, 'xp', [(i, n - 1 - i) for i in range(n)])  9.01 us
    pallas_call x10, Pallas kernels, call(): pl.pallas_call(kernel, out_shape=tuple((jax.ShapeDtypeStruct(s, t) for s,...  8.5 us
    ppermute x3, starting transfers between devices, on_device(): total = total + lax.ppermute(total, 'xp', [(i, i ^ bit) for i in range(n)])  7.63 us
    ppermute x4, starting transfers between devices, pair_swap(): return lax.ppermute(x, 'xp', pairs)  5.71 us
    ppermute x3, waiting for transfers between devices, on_device(): total = total + lax.ppermute(total, 'xp', [(i, i ^ bit) for i in range(n)])  5.07 us
    unnamed x10, local copies, waits for them, and re-layouts  1.72 us
    ppermute x7, starting transfers between devices, swap_y(): return lax.ppermute(x, 'yp', [(i, n - 1 - i) for i in range(n)])  1.69 us
    ppermute x7, waiting for transfers between devices, swap_y(): return lax.ppermute(x, 'yp', [(i, n - 1 - i) for i in range(n)])  1.36 us
  transfers between devices with their start and end apart: 16, of which 4 were waited for; matrix products, arithmetic and copies ran while one was open for 4% of the time, Pallas kernels for 14%

profile of v10, /device:TPU:0, one launch (start us, length us, event | category | flops | bytes accessed | tf_op | source)
XLA Modules:
  0.0 42.3 jit_solution(14677267564045457463)
XLA Ops:
  0.7 0.9 %copy.16.own = bf16[2,30,512]{2,1,0:T(8,128)(2,1)S(1)} copy(bf16[2,30,512]{2,0,1:T(2,128)(2,1)} %param.7) | data formatting | bytes 122880 | tf_op args[1]
  1.5 0.5 %collective-permute-start.3 = (bf16[2,30,512]{2,1,0:T(8,128)(2,1)S(1)}, bf16[2,30,512]{2,1,0:T(8,128)(2,1)S(1)}, u32[]{:S(2)}, u32[]{:S(2)}) collective-permute-start(bf16[2,30,512]{2,1,0:T(8,128)(2,1)S(1)} %copy.16.own), channel_id=1, source_target_pairs={{0,1},{1,0},{2,3},{3,2},{4,5},{5,4},{6,7},{7,6},{8,9},{9,8},{10,11... | collective-permute-start | bytes 184328 | tf_op jit(solution)/shard_map/ppermute | solution.py:537
  2.1 0.8 %copy.9.features = bf16[2,30,512]{2,1,0:T(8,128)(2,1)S(1)} copy(bf16[2,30,512]{2,0,1:T(2,128)(2,1)} %param.6) | data formatting | bytes 122880 | tf_op args[0]
  2.9 0.2 shard_map.85.own
  3.1 0.1 collective-permute-start
  3.3 6.1 %collective-permute-start.4 = (bf16[4,30,512]{2,1,0:T(8,128)(2,1)S(1)}, bf16[4,30,512]{2,1,0:T(8,128)(2,1)S(1)}, u32[]{:S(2)}, u32[]{:S(2)}) collective-permute-start(bf16[4,30,512]{2,1,0:T(8,128)(2,1)S(1)} %pad_maximum_fusion), channel_id=1, source_target_pairs={{0,14},{2,12},{4,10},{6,8},{8,6},{10,4},{12,2},{14,0},{1,15},{3,13... | collective-permute-start | bytes 368648 | tf_op jit(solution)/shard_map/ppermute | solution.py:542
  9.3 0.7 %collective-permute-start.2 = (bf16[4,32,128]{2,1,0:T(8,128)(2,1)S(1)}, bf16[4,32,128]{2,1,0:T(8,128)(2,1)S(1)}, u32[]{:S(2)}, u32[]{:S(2)}) collective-permute-start(bf16[4,32,128]{2,1,0:T(8,128)(2,1)S(1)} %get-tuple-element.79), channel_id=1, source_target_pairs={{2,4},{4,2},{6,8},{8,6},{10,12},{12,10},{3,5},{5,3},{7,9},{9,7},{1... | collective-permute-start | bytes 98312 | tf_op jit(solution)/shard_map/ppermute | solution.py:550
  10.0 2.3 %collective-permute-start.1 = (bf16[4,32,128]{2,1,0:T(8,128)(2,1)S(1)}, bf16[4,32,128]{2,1,0:T(8,128)(2,1)S(1)}, u32[]{:S(2)}, u32[]{:S(2)}) collective-permute-start(bf16[4,32,128]{2,1,0:T(8,128)(2,1)S(1)} %get-tuple-element.80), channel_id=1, source_target_pairs={{0,2},{2,0},{4,6},{6,4},{8,10},{10,8},{12,14},{14,12},{1,3},{3,1},... | collective-permute-start | bytes 98312 | tf_op jit(solution)/shard_map/ppermute | solution.py:550
  12.4 0.5 %shard_map.86 = (bf16[192,288]{1,0:T(8,128)(2,1)S(1)}, bf16[96,288]{1,0:T(8,128)(2,1)S(1)}, bf16[96,288]{1,0:T(8,128)(2,1)S(1)}, bf16[124,16,128]{2,1,0:T(8,128)(2,1)S(1)}, bf16[6,16,128]{2,1,0:T(8,128)(2,1)S(1)}) custom-call(bf16[32,256]{1,0:T(8,128)(2,1)S(1)} %pad_add_fusion.packed, s32[2,256]{1,0:T(2,128)S(1)} %pad_add_fusion.1.small), custom_call_target="tpu_custom_call" | custom-call | bytes 3000000 | tf_op jit(solution)/shard_map/pallas_call | solution.py:524
  12.9 1.4 %shard_map.87 = (bf16[288,2048]{1,0:T(8,128)(2,1)S(1)}, f32[2,32,1024]{2,1,0:T(8,128)S(1)}, f32[2,32,1024]{2,1,0:T(8,128)S(1)}, bf16[2,6,32,128]{3,2,1,0:T(8,128)(2,1)S(1)}) custom-call(bf16[124,16,128]{2,1,0:T(8,128)(2,1)S(1)} %get-tuple-element.44.choose, bf16[2,8,32,128]{3,2,1,0:T(8,128)(2,1)S(1)} %shard_map.85.own, ...), custom_call_target="tpu_custom_call" | custom-call | bytes 6000000 | tf_op jit(solution)/shard_map/pallas_call | solution.py:524
  14.3 0.3 shard_map.88.back
  14.6 0.5 %shard_map.89 = (bf16[288,512]{1,0:T(8,128)(2,1)S(1)}, f32[32,512]{1,0:T(8,128)S(1)}, f32[32,512]{1,0:T(8,128)S(1)}, bf16[2,2,8,32,128]{4,3,2,1,0:T(8,128)(2,1)S...) custom-call(bf16[124,16,128]{2,1,0:T(8,128)(2,1)S(1)} %get-tuple-element.44.choose, ...), custom_call_target="tpu_custom_call" | custom-call | bytes 3000000 | tf_op jit(solution)/shard_map/pallas_call | solution.py:524
  15.2 0.1 collective-permute-start.5
  15.2 2.1 %collective-permute-start.6 = (bf16[2,2,32,128]{3,2,1,0:T(8,128)(2,1)S(1)}, bf16[2,2,32,128]{3,2,1,0:T(8,128)(2,1)S(1)}, u32[]{:S(2)}, u32[]{:S(2)}) collective-permute-start(bf16[2,2,32,128]{3,2,1,0:T(8,128)(2,1)S(1)} %get-tuple-element.56), channel_id=1, source_target_pairs={{0,2},{2,0},{4,6},{6,4},{8,10},{10,8},{12,14},{14,12},{1,3},{3,1},... | collective-permute-start | bytes 98312 | tf_op jit(solution)/shard_map/ppermute | solution.py:550
  17.3 0.7 %collective-permute-start.7 = (bf16[2,2,32,128]{3,2,1,0:T(8,128)(2,1)S(1)}, bf16[2,2,32,128]{3,2,1,0:T(8,128)(2,1)S(1)}, u32[]{:S(2)}, u32[]{:S(2)}) collective-permute-start(bf16[2,2,32,128]{3,2,1,0:T(8,128)(2,1)S(1)} %get-tuple-element.57), channel_id=1, source_target_pairs={{2,4},{4,2},{6,8},{8,6},{10,12},{12,10},{3,5},{5,3},{7,9},{9,7},{1... | collective-permute-start | bytes 98312 | tf_op jit(solution)/shard_map/ppermute | solution.py:550
  18.0 2.3 %shard_map.90 = (f32[2,32,1024]{2,1,0:T(8,128)S(1)}, f32[32,512]{1,0:T(8,128)S(1)}, bf16[288,2048]{1,0:T(8,128)(2,1)S(1)}, bf16[128,2048]{1,0:T(8,128)(2,1)S(1)}, bf16[128,2048]{1,0:T(8,128)(2,1)S(1)}) custom-call(bf16[124,16,128]{2,1,0:T(8,128)(2,1)S(1)} %get-tuple-element.44.choose, bf16[2,2,8,32,128]{4,3,2,1,0:T(8,128)(2,1)S(1)} %get-tuple-element.52.own, ...), custom_call_target="tpu_custom_call" | custom-call | bytes 7500000 | tf_op jit(solution)/shard_map/pallas_call | solution.py:524
  20.3 0.2 collective-permute-start.8
  20.5 0.8 %shard_map.91.raw = f32[2,288,128]{2,1,0:T(8,128)S(1)} custom-call(bf16[288,2048]{1,0:T(8,128)(2,1)S(1)} %get-tuple-element.63.columns_f, bf16[288,2048]{1,0:T(8,128)(2,1)S(1)} %get-tuple-element.68.columns_h, bf16[128,2048]{1,0:T(8,128)(2,1)S(1)} %get-tuple-element.69.placed_f, bf16[128,2048]{1,0:T(8,128)(2,1)S(1)} %get-tuple-element.70.placed_s), custom_call_target="tpu_custom_call" | custom-call | bytes 3000000 | tf_op jit(solution)/shard_map/pallas_call | solution.py:524
  21.3 0.3 collective-permute-done.8.far
  21.6 1.3 %shard_map.92 = (bf16[288,512]{1,0:T(8,128)(2,1)S(1)}, f32[56,128]{1,0:T(8,128)S(1)}) custom-call(bf16[124,16,128]{2,1,0:T(8,128)(2,1)S(1)} %get-tuple-element.44.choose, bf16[2,2,8,32,128]{4,3,2,1,0:T(8,128)(2,1)S(1)} %get-tuple-element.52.own, bf16[2,2,8,32,128]{4,3,2,1,0:T(8,128)(2,1)S(1)} %collective-permute-done.5.part, ...), custom_call_target="tpu_custom_call" | custom-call | bytes 6000000 | tf_op jit(solution)/shard_map/pallas_call | solution.py:524
  22.9 0.2 collective-permute-start.9
  23.2 1.0 %collective-permute-done.9 = f32[56,128]{1,0:T(8,128)S(1)} collective-permute-done((f32[56,128]{1,0:T(8,128)S(1)}, f32[56,128]{1,0:T(8,128)S(1)}, u32[]{:S(2)}, u32[]{:S(2)}) %collective-permute-start.9) | collective-permute-done | bytes 28704 | tf_op jit(solution)/shard_map/ppermute | solution.py:537
  24.2 4.5 %collective-permute-start.13 = (f32[56,128]{1,0:T(8,128)S(1)}, f32[56,128]{1,0:T(8,128)S(1)}, u32[]{:S(2)}, u32[]{:S(2)}) collective-permute-start(f32[56,128]{1,0:T(8,128)S(1)} %add.28), channel_id=1, source_target_pairs={{0,2},{2,0},{4,6},{6,4},{8,10},{10,8},{12,14},{14,12},{1,3},{3,1},... | collective-permute-start | bytes 86024 | tf_op jit(solution)/shard_map/ppermute | solution.py:640
  28.7 0.3 shard_map.93.own
  29.1 2.9 %collective-permute-start.11 = (bf16[64,512]{1,0:T(8,128)(2,1)S(1)}, bf16[64,512]{1,0:T(8,128)(2,1)S(1)}, u32[]{:S(2)}, u32[]{:S(2)}) collective-permute-start(bf16[64,512]{1,0:T(8,128)(2,1)S(1)} %shard_map.93.own), channel_id=1, source_target_pairs={{0,14},{2,12},{4,10},{6,8},{8,6},{10,4},{12,2},{14,0},{1,15},{3,13... | collective-permute-start | bytes 196616 | tf_op jit(solution)/shard_map/ppermute | solution.py:542
  32.0 1.6 %collective-permute-start.14 = (f32[56,128]{1,0:T(8,128)S(1)}, f32[56,128]{1,0:T(8,128)S(1)}, u32[]{:S(2)}, u32[]{:S(2)}) collective-permute-start(f32[56,128]{1,0:T(8,128)S(1)} %add.29), channel_id=1, source_target_pairs={{0,4},{2,6},{4,0},{6,2},{8,12},{10,14},{12,8},{14,10},{1,5},{3,7},... | collective-permute-start | bytes 86024 | tf_op jit(solution)/shard_map/ppermute | solution.py:640
  33.6 2.4 %collective-permute-done.14 = f32[56,128]{1,0:T(8,128)S(1)} collective-permute-done((f32[56,128]{1,0:T(8,128)S(1)}, f32[56,128]{1,0:T(8,128)S(1)}, u32[]{:S(2)}, u32[]{:S(2)}) %collective-permute-start.14) | collective-permute-done | bytes 28704 | tf_op jit(solution)/shard_map/ppermute | solution.py:640
  35.9 1.5 %collective-permute-start.15 = (f32[56,128]{1,0:T(8,128)S(1)}, f32[56,128]{1,0:T(8,128)S(1)}, u32[]{:S(2)}, u32[]{:S(2)}) collective-permute-start(f32[56,128]{1,0:T(8,128)S(1)} %add.30), channel_id=1, source_target_pairs={{0,8},{2,10},{4,12},{6,14},{8,0},{10,2},{12,4},{14,6},{1,9},{3,11}... | collective-permute-start | bytes 86024 | tf_op jit(solution)/shard_map/ppermute | solution.py:640
  37.5 0.5 %collective-permute-start.12 = (bf16[64,512]{1,0:T(8,128)(2,1)S(1)}, bf16[64,512]{1,0:T(8,128)(2,1)S(1)}, u32[]{:S(2)}, u32[]{:S(2)}) collective-permute-start(bf16[64,512]{1,0:T(8,128)(2,1)S(1)} %collective-permute-done.11.across_x), channel_id=1, source_target_pairs={{0,1},{1,0},{2,3},{3,2},{4,5},{5,4},{6,7},{7,6},{8,9},{9,8},{10,11... | collective-permute-start | bytes 196616 | tf_op jit(solution)/shard_map/ppermute | solution.py:537
  38.0 2.7 %collective-permute-done.15 = f32[56,128]{1,0:T(8,128)S(1)} collective-permute-done((f32[56,128]{1,0:T(8,128)S(1)}, f32[56,128]{1,0:T(8,128)S(1)}, u32[]{:S(2)}, u32[]{:S(2)}) %collective-permute-start.15) | collective-permute-done | bytes 28704 | tf_op jit(solution)/shard_map/ppermute | solution.py:640
  40.7 0.6 %fusion = (f32[27,84]{1,0:T(8,128)}, f32[27,84]{1,0:T(8,128)}) fusion(f32[56,128]{1,0:T(8,128)S(1)} %add.31), kind=kLoop, calls=%fused_computation.12 | loop fusion | bytes 36288 | tf_op jit(solution)/shard_map/slice | solution.py:642
  41.3 0.9 %shard_map.94 = bf16[30,2,512]{2,1,0:T(2,128)(2,1)} custom-call(bf16[6,16,128]{2,1,0:T(8,128)(2,1)S(1)} %get-tuple-element.43.turn_choice, bf16[64,512]{1,0:T(8,128)(2,1)S(1)} %shard_map.93.own, bf16[64,512]{1,0:T(8,128)(2,1)S(1)} %collective-permute-done.10.across_y, bf16[64,512]{1,0:T(8,128)(2,1)S(1)} %collective-permute-done.11.across_x, ...), custom_call_target="tpu_custom_call" | custom-call | bytes 2700000 | tf_op jit(solution)/shard_map/pallas_call | solution.py:524
  (34 shorter events, 0.2 us)
Async XLA Ops:
  0.6 11.7 %copy-start.2 = (s32[2,3]{1,0:T(2,128)S(1)}, s32[2,3]{1,0:T(2,128)}, u32[]{:S(2)}) copy-start(s32[2,3]{1,0:T(2,128)} %param.11) | copy-start | bytes 76
  0.6 11.7 %copy-start.3 = (s32[2,27]{1,0:T(2,128)S(1)}, s32[2,27]{1,0:T(2,128)}, u32[]{:S(2)}) copy-start(s32[2,27]{1,0:T(2,128)} %param.10) | copy-start | bytes 652
  0.7 11.7 %copy-start = (bf16[27,84]{1,0:T(8,128)(2,1)S(1)}, bf16[27,84]{1,0:T(8,128)(2,1)}, u32[]{:S(2)}) copy-start(bf16[27,84]{1,0:T(8,128)(2,1)} %param.9) | copy-start | bytes 13612
  0.7 11.7 %copy-start.1 = (bf16[27,84]{1,0:T(8,128)(2,1)S(1)}, bf16[27,84]{1,0:T(8,128)(2,1)}, u32[]{:S(2)}) copy-start(bf16[27,84]{1,0:T(8,128)(2,1)} %param.8) | copy-start | bytes 13612
  1.5 1.7 %collective-permute-start.3 = (bf16[2,30,512]{2,1,0:T(8,128)(2,1)S(1)}, bf16[2,30,512]{2,1,0:T(8,128)(2,1)S(1)}, u32[]{:S(2)}, u32[]{:S(2)}) collective-permute-start(bf16[2,30,512]{2,1,0:T(8,128)(2,1)S(1)} %copy.16.own), channel_id=1, source_target_pairs={{0,1},{1,0},{2,3},{3,2},{4,5},{5,4},{6,7},{7,6},{8,9},{9,8},{10,11... | collective-permute-start | bytes 184328 | tf_op jit(solution)/shard_map/ppermute | solution.py:537
  3.1 6.2 %collective-permute-start = (bf16[2,8,32,128]{3,2,0,1:T(8,128)(2,1)S(1)}, bf16[2,8,32,128]{3,2,0,1:T(8,128)(2,1)S(1)}, u32[]{:S(2)}, u32[]{:S(2)}) collective-permute-start(bf16[2,8,32,128]{3,2,0,1:T(8,128)(2,1)S(1)} %copy.10), channel_id=1, source_target_pairs={{0,1},{1,0},{2,3},{3,2},{4,5},{5,4},{6,7},{7,6},{8,9},{9,8},{10,11... | collective-permute-start | bytes 393224 | tf_op jit(solution)/shard_map/ppermute | solution.py:537
  3.3 11.0 %collective-permute-start.4 = (bf16[4,30,512]{2,1,0:T(8,128)(2,1)S(1)}, bf16[4,30,512]{2,1,0:T(8,128)(2,1)S(1)}, u32[]{:S(2)}, u32[]{:S(2)}) collective-permute-start(bf16[4,30,512]{2,1,0:T(8,128)(2,1)S(1)} %pad_maximum_fusion), channel_id=1, source_target_pairs={{0,14},{2,12},{4,10},{6,8},{8,6},{10,4},{12,2},{14,0},{1,15},{3,13... | collective-permute-start | bytes 368648 | tf_op jit(solution)/shard_map/ppermute | solution.py:542
  9.3 5.2 %collective-permute-start.2 = (bf16[4,32,128]{2,1,0:T(8,128)(2,1)S(1)}, bf16[4,32,128]{2,1,0:T(8,128)(2,1)S(1)}, u32[]{:S(2)}, u32[]{:S(2)}) collective-permute-start(bf16[4,32,128]{2,1,0:T(8,128)(2,1)S(1)} %get-tuple-element.79), channel_id=1, source_target_pairs={{2,4},{4,2},{6,8},{8,6},{10,12},{12,10},{3,5},{5,3},{7,9},{9,7},{1... | collective-permute-start | bytes 98312 | tf_op jit(solution)/shard_map/ppermute | solution.py:550
  10.0 4.6 %collective-permute-start.1 = (bf16[4,32,128]{2,1,0:T(8,128)(2,1)S(1)}, bf16[4,32,128]{2,1,0:T(8,128)(2,1)S(1)}, u32[]{:S(2)}, u32[]{:S(2)}) collective-permute-start(bf16[4,32,128]{2,1,0:T(8,128)(2,1)S(1)} %get-tuple-element.80), channel_id=1, source_target_pairs={{0,2},{2,0},{4,6},{6,4},{8,10},{10,8},{12,14},{14,12},{1,3},{3,1},... | collective-permute-start | bytes 98312 | tf_op jit(solution)/shard_map/ppermute | solution.py:550
  15.2 2.8 %collective-permute-start.5 = (bf16[2,2,8,32,128]{4,3,2,1,0:T(8,128)(2,1)S(1)}, bf16[2,2,8,32,128]{4,3,2,1,0:T(8,128)(2,1)S(1)}, u32[]{:S(2)}, u32[]{:S(2)}) collective-permute-start(bf16[2,2,8,32,128]{4,3,2,1,0:T(8,128)(2,1)S(1)} %get-tuple-element.52.own), channel_id=1, source_target_pairs={{0,1},{1,0},{2,3},{3,2},{4,5},{5,4},{6,7},{7,6},{8,9},{9,8},{10,11... | collective-permute-start | bytes 786440 | tf_op jit(solution)/shard_map/ppermute | solution.py:537
  15.2 5.0 %collective-permute-start.6 = (bf16[2,2,32,128]{3,2,1,0:T(8,128)(2,1)S(1)}, bf16[2,2,32,128]{3,2,1,0:T(8,128)(2,1)S(1)}, u32[]{:S(2)}, u32[]{:S(2)}) collective-permute-start(bf16[2,2,32,128]{3,2,1,0:T(8,128)(2,1)S(1)} %get-tuple-element.56), channel_id=1, source_target_pairs={{0,2},{2,0},{4,6},{6,4},{8,10},{10,8},{12,14},{14,12},{1,3},{3,1},... | collective-permute-start | bytes 98312 | tf_op jit(solution)/shard_map/ppermute | solution.py:550
  17.3 3.0 %collective-permute-start.7 = (bf16[2,2,32,128]{3,2,1,0:T(8,128)(2,1)S(1)}, bf16[2,2,32,128]{3,2,1,0:T(8,128)(2,1)S(1)}, u32[]{:S(2)}, u32[]{:S(2)}) collective-permute-start(bf16[2,2,32,128]{3,2,1,0:T(8,128)(2,1)S(1)} %get-tuple-element.57), channel_id=1, source_target_pairs={{2,4},{4,2},{6,8},{8,6},{10,12},{12,10},{3,5},{5,3},{7,9},{9,7},{1... | collective-permute-start | bytes 98312 | tf_op jit(solution)/shard_map/ppermute | solution.py:550
  20.3 1.3 %collective-permute-start.8 = (bf16[2,2,2,32,128]{4,3,2,1,0:T(8,128)(2,1)S(1)}, bf16[2,2,2,32,128]{4,3,2,1,0:T(8,128)(2,1)S(1)}, u32[]{:S(2)}, u32[]{:S(2)}) collective-permute-start(bf16[2,2,2,32,128]{4,3,2,1,0:T(8,128)(2,1)S(1)} %pad_maximum_fusion.1), channel_id=1, source_target_pairs={{0,1},{1,0},{2,3},{3,2},{4,5},{5,4},{6,7},{7,6},{8,9},{9,8},{10,11... | collective-permute-start | bytes 196616 | tf_op jit(solution)/shard_map/ppermute | solution.py:537
  22.9 1.3 %collective-permute-start.9 = (f32[56,128]{1,0:T(8,128)S(1)}, f32[56,128]{1,0:T(8,128)S(1)}, u32[]{:S(2)}, u32[]{:S(2)}) collective-permute-start(f32[56,128]{1,0:T(8,128)S(1)} %get-tuple-element.72), channel_id=1, source_target_pairs={{0,1},{1,0},{2,3},{3,2},{4,5},{5,4},{6,7},{7,6},{8,9},{9,8},{10,11... | collective-permute-start | bytes 86024 | tf_op jit(solution)/shard_map/ppermute | solution.py:537
  24.2 7.8 %collective-permute-start.13 = (f32[56,128]{1,0:T(8,128)S(1)}, f32[56,128]{1,0:T(8,128)S(1)}, u32[]{:S(2)}, u32[]{:S(2)}) collective-permute-start(f32[56,128]{1,0:T(8,128)S(1)} %add.28), channel_id=1, source_target_pairs={{0,2},{2,0},{4,6},{6,4},{8,10},{10,8},{12,14},{14,12},{1,3},{3,1},... | collective-permute-start | bytes 86024 | tf_op jit(solution)/shard_map/ppermute | solution.py:640
  29.1 8.4 %collective-permute-start.11 = (bf16[64,512]{1,0:T(8,128)(2,1)S(1)}, bf16[64,512]{1,0:T(8,128)(2,1)S(1)}, u32[]{:S(2)}, u32[]{:S(2)}) collective-permute-start(bf16[64,512]{1,0:T(8,128)(2,1)S(1)} %shard_map.93.own), channel_id=1, source_target_pairs={{0,14},{2,12},{4,10},{6,8},{8,6},{10,4},{12,2},{14,0},{1,15},{3,13... | collective-permute-start | bytes 196616 | tf_op jit(solution)/shard_map/ppermute | solution.py:542
  32.0 3.9 %collective-permute-start.14 = (f32[56,128]{1,0:T(8,128)S(1)}, f32[56,128]{1,0:T(8,128)S(1)}, u32[]{:S(2)}, u32[]{:S(2)}) collective-permute-start(f32[56,128]{1,0:T(8,128)S(1)} %add.29), channel_id=1, source_target_pairs={{0,4},{2,6},{4,0},{6,2},{8,12},{10,14},{12,8},{14,10},{1,5},{3,7},... | collective-permute-start | bytes 86024 | tf_op jit(solution)/shard_map/ppermute | solution.py:640
  35.9 4.8 %collective-permute-start.15 = (f32[56,128]{1,0:T(8,128)S(1)}, f32[56,128]{1,0:T(8,128)S(1)}, u32[]{:S(2)}, u32[]{:S(2)}) collective-permute-start(f32[56,128]{1,0:T(8,128)S(1)} %add.30), channel_id=1, source_target_pairs={{0,8},{2,10},{4,12},{6,14},{8,0},{10,2},{12,4},{14,6},{1,9},{3,11}... | collective-permute-start | bytes 86024 | tf_op jit(solution)/shard_map/ppermute | solution.py:640
  37.5 3.9 %collective-permute-start.10 = (bf16[64,512]{1,0:T(8,128)(2,1)S(1)}, bf16[64,512]{1,0:T(8,128)(2,1)S(1)}, u32[]{:S(2)}, u32[]{:S(2)}) collective-permute-start(bf16[64,512]{1,0:T(8,128)(2,1)S(1)} %shard_map.93.own), channel_id=1, source_target_pairs={{0,1},{1,0},{2,3},{3,2},{4,5},{5,4},{6,7},{7,6},{8,9},{9,8},{10,11... | collective-permute-start | bytes 196616 | tf_op jit(solution)/shard_map/ppermute | solution.py:537
  37.5 3.9 %collective-permute-start.12 = (bf16[64,512]{1,0:T(8,128)(2,1)S(1)}, bf16[64,512]{1,0:T(8,128)(2,1)S(1)}, u32[]{:S(2)}, u32[]{:S(2)}) collective-permute-start(bf16[64,512]{1,0:T(8,128)(2,1)S(1)} %collective-permute-done.11.across_x), channel_id=1, source_target_pairs={{0,1},{1,0},{2,3},{3,2},{4,5},{5,4},{6,7},{7,6},{8,9},{9,8},{10,11... | collective-permute-start | bytes 196616 | tf_op jit(solution)/shard_map/ppermute | solution.py:537

commit v11 on v10

--- a/solution.py
+++ b/solution.py
@@ -625,8 +625,8 @@
         choose, both, part, *got, far, pre_e, gate_e, through_e, columns, columns_e, raw, w2t,
     )
     total = grads + swap_y(grads)
-    second_part, columns_he = after((second_part, columns_he), total)
     (second,) = call(compact_kernel, 0.5, 0, [((64, 512), BF)], [], second_part, columns_he, w2)
+    (second,) = after((second,), total)
     second_y = swap_y(second)
     second_x = mirror_x(second)
     second_xy = swap_y(second_x)

time: 42.5 us -> 42.5 us (level)
  no operation moved by 1% of the time
where the time goes in v11:
time: 42.5 us; the launch traced here: 42.3 us
  starting transfers between devices  24 us (56%)
  Pallas kernels  8.5 us (20%)
  waiting for transfers between devices  6.45 us (15%)
  local copies, waits for them, and re-layouts  2.36 us (6%)
  between operations  0.88 us (2%)
    ppermute x2, starting transfers between devices, mirror_x(): return lax.ppermute(x, 'xp', [(i, n - 1 - i) for i in range(n)])  9.01 us
    pallas_call x10, Pallas kernels, call(): pl.pallas_call(kernel, out_shape=tuple((jax.ShapeDtypeStruct(s, t) for s,...  8.5 us
    ppermute x3, starting transfers between devices, on_device(): total = total + lax.ppermute(total, 'xp', [(i, i ^ bit) for i in range(n)])  7.63 us
    ppermute x4, starting transfers between devices, pair_swap(): return lax.ppermute(x, 'xp', pairs)  5.71 us
    ppermute x3, waiting for transfers between devices, on_device(): total = total + lax.ppermute(total, 'xp', [(i, i ^ bit) for i in range(n)])  5.07 us
    unnamed x10, local copies, waits for them, and re-layouts  1.72 us
    ppermute x7, starting transfers between devices, swap_y(): return lax.ppermute(x, 'yp', [(i, n - 1 - i) for i in range(n)])  1.69 us
    ppermute x7, waiting for transfers between devices, swap_y(): return lax.ppermute(x, 'yp', [(i, n - 1 - i) for i in range(n)])  1.36 us
  transfers between devices with their start and end apart: 16, of which 4 were waited for; matrix products, arithmetic and copies ran while one was open for 4% of the time, Pallas kernels for 14%

profile of v11, /device:TPU:0, one launch (start us, length us, event | category | flops | bytes accessed | tf_op | source)
XLA Modules:
  0.0 42.3 jit_solution(14677267564045457463)
XLA Ops:
  0.7 0.9 %copy.16.own = bf16[2,30,512]{2,1,0:T(8,128)(2,1)S(1)} copy(bf16[2,30,512]{2,0,1:T(2,128)(2,1)} %param.7) | data formatting | bytes 122880 | tf_op args[1]
  1.5 0.5 %collective-permute-start.3 = (bf16[2,30,512]{2,1,0:T(8,128)(2,1)S(1)}, bf16[2,30,512]{2,1,0:T(8,128)(2,1)S(1)}, u32[]{:S(2)}, u32[]{:S(2)}) collective-permute-start(bf16[2,30,512]{2,1,0:T(8,128)(2,1)S(1)} %copy.16.own), channel_id=1, source_target_pairs={{0,1},{1,0},{2,3},{3,2},{4,5},{5,4},{6,7},{7,6},{8,9},{9,8},{10,11... | collective-permute-start | bytes 184328 | tf_op jit(solution)/shard_map/ppermute | solution.py:537
  2.1 0.8 %copy.9.features = bf16[2,30,512]{2,1,0:T(8,128)(2,1)S(1)} copy(bf16[2,30,512]{2,0,1:T(2,128)(2,1)} %param.6) | data formatting | bytes 122880 | tf_op args[0]
  2.9 0.2 shard_map.85.own
  3.1 0.1 collective-permute-start
  3.3 6.1 %collective-permute-start.4 = (bf16[4,30,512]{2,1,0:T(8,128)(2,1)S(1)}, bf16[4,30,512]{2,1,0:T(8,128)(2,1)S(1)}, u32[]{:S(2)}, u32[]{:S(2)}) collective-permute-start(bf16[4,30,512]{2,1,0:T(8,128)(2,1)S(1)} %pad_maximum_fusion), channel_id=1, source_target_pairs={{0,14},{2,12},{4,10},{6,8},{8,6},{10,4},{12,2},{14,0},{1,15},{3,13... | collective-permute-start | bytes 368648 | tf_op jit(solution)/shard_map/ppermute | solution.py:542
  9.3 0.7 %collective-permute-start.2 = (bf16[4,32,128]{2,1,0:T(8,128)(2,1)S(1)}, bf16[4,32,128]{2,1,0:T(8,128)(2,1)S(1)}, u32[]{:S(2)}, u32[]{:S(2)}) collective-permute-start(bf16[4,32,128]{2,1,0:T(8,128)(2,1)S(1)} %get-tuple-element.77), channel_id=1, source_target_pairs={{2,4},{4,2},{6,8},{8,6},{10,12},{12,10},{3,5},{5,3},{7,9},{9,7},{1... | collective-permute-start | bytes 98312 | tf_op jit(solution)/shard_map/ppermute | solution.py:550
  10.0 2.3 %collective-permute-start.1 = (bf16[4,32,128]{2,1,0:T(8,128)(2,1)S(1)}, bf16[4,32,128]{2,1,0:T(8,128)(2,1)S(1)}, u32[]{:S(2)}, u32[]{:S(2)}) collective-permute-start(bf16[4,32,128]{2,1,0:T(8,128)(2,1)S(1)} %get-tuple-element.78), channel_id=1, source_target_pairs={{0,2},{2,0},{4,6},{6,4},{8,10},{10,8},{12,14},{14,12},{1,3},{3,1},... | collective-permute-start | bytes 98312 | tf_op jit(solution)/shard_map/ppermute | solution.py:550
  12.4 0.5 %shard_map.86 = (bf16[192,288]{1,0:T(8,128)(2,1)S(1)}, bf16[96,288]{1,0:T(8,128)(2,1)S(1)}, bf16[96,288]{1,0:T(8,128)(2,1)S(1)}, bf16[124,16,128]{2,1,0:T(8,128)(2,1)S(1)}, bf16[6,16,128]{2,1,0:T(8,128)(2,1)S(1)}) custom-call(bf16[32,256]{1,0:T(8,128)(2,1)S(1)} %pad_add_fusion.packed, s32[2,256]{1,0:T(2,128)S(1)} %pad_add_fusion.1.small), custom_call_target="tpu_custom_call" | custom-call | bytes 3000000 | tf_op jit(solution)/shard_map/pallas_call | solution.py:524
  12.9 1.4 %shard_map.87 = (bf16[288,2048]{1,0:T(8,128)(2,1)S(1)}, f32[2,32,1024]{2,1,0:T(8,128)S(1)}, f32[2,32,1024]{2,1,0:T(8,128)S(1)}, bf16[2,6,32,128]{3,2,1,0:T(8,128)(2,1)S(1)}) custom-call(bf16[124,16,128]{2,1,0:T(8,128)(2,1)S(1)} %get-tuple-element.43.choose, bf16[2,8,32,128]{3,2,1,0:T(8,128)(2,1)S(1)} %shard_map.85.own, ...), custom_call_target="tpu_custom_call" | custom-call | bytes 6000000 | tf_op jit(solution)/shard_map/pallas_call | solution.py:524
  14.3 0.3 shard_map.88.back
  14.6 0.5 %shard_map.89 = (bf16[288,512]{1,0:T(8,128)(2,1)S(1)}, f32[32,512]{1,0:T(8,128)S(1)}, f32[32,512]{1,0:T(8,128)S(1)}, bf16[2,2,8,32,128]{4,3,2,1,0:T(8,128)(2,1)S...) custom-call(bf16[124,16,128]{2,1,0:T(8,128)(2,1)S(1)} %get-tuple-element.43.choose, ...), custom_call_target="tpu_custom_call" | custom-call | bytes 3000000 | tf_op jit(solution)/shard_map/pallas_call | solution.py:524
  15.2 0.1 collective-permute-start.5
  15.2 2.1 %collective-permute-start.6 = (bf16[2,2,32,128]{3,2,1,0:T(8,128)(2,1)S(1)}, bf16[2,2,32,128]{3,2,1,0:T(8,128)(2,1)S(1)}, u32[]{:S(2)}, u32[]{:S(2)}) collective-permute-start(bf16[2,2,32,128]{3,2,1,0:T(8,128)(2,1)S(1)} %get-tuple-element.55), channel_id=1, source_target_pairs={{0,2},{2,0},{4,6},{6,4},{8,10},{10,8},{12,14},{14,12},{1,3},{3,1},... | collective-permute-start | bytes 98312 | tf_op jit(solution)/shard_map/ppermute | solution.py:550
  17.3 0.7 %collective-permute-start.7 = (bf16[2,2,32,128]{3,2,1,0:T(8,128)(2,1)S(1)}, bf16[2,2,32,128]{3,2,1,0:T(8,128)(2,1)S(1)}, u32[]{:S(2)}, u32[]{:S(2)}) collective-permute-start(bf16[2,2,32,128]{3,2,1,0:T(8,128)(2,1)S(1)} %get-tuple-element.56), channel_id=1, source_target_pairs={{2,4},{4,2},{6,8},{8,6},{10,12},{12,10},{3,5},{5,3},{7,9},{9,7},{1... | collective-permute-start | bytes 98312 | tf_op jit(solution)/shard_map/ppermute | solution.py:550
  18.0 2.3 %shard_map.90 = (f32[2,32,1024]{2,1,0:T(8,128)S(1)}, f32[32,512]{1,0:T(8,128)S(1)}, bf16[288,2048]{1,0:T(8,128)(2,1)S(1)}, bf16[128,2048]{1,0:T(8,128)(2,1)S(1)}, bf16[128,2048]{1,0:T(8,128)(2,1)S(1)}) custom-call(bf16[124,16,128]{2,1,0:T(8,128)(2,1)S(1)} %get-tuple-element.43.choose, bf16[2,2,8,32,128]{4,3,2,1,0:T(8,128)(2,1)S(1)} %get-tuple-element.51.own, ...), custom_call_target="tpu_custom_call" | custom-call | bytes 7500000 | tf_op jit(solution)/shard_map/pallas_call | solution.py:524
  20.3 0.2 collective-permute-start.8
  20.5 0.8 %shard_map.91.raw = f32[2,288,128]{2,1,0:T(8,128)S(1)} custom-call(bf16[288,2048]{1,0:T(8,128)(2,1)S(1)} %get-tuple-element.62.columns_f, bf16[288,2048]{1,0:T(8,128)(2,1)S(1)} %get-tuple-element.67.columns_h, bf16[128,2048]{1,0:T(8,128)(2,1)S(1)} %get-tuple-element.68.placed_f, bf16[128,2048]{1,0:T(8,128)(2,1)S(1)} %get-tuple-element.69.placed_s), custom_call_target="tpu_custom_call" | custom-call | bytes 3000000 | tf_op jit(solution)/shard_map/pallas_call | solution.py:524
  21.3 0.3 collective-permute-done.8.far
  21.6 1.3 %shard_map.92 = (bf16[288,512]{1,0:T(8,128)(2,1)S(1)}, f32[56,128]{1,0:T(8,128)S(1)}) custom-call(bf16[124,16,128]{2,1,0:T(8,128)(2,1)S(1)} %get-tuple-element.43.choose, bf16[2,2,8,32,128]{4,3,2,1,0:T(8,128)(2,1)S(1)} %get-tuple-element.51.own, bf16[2,2,8,32,128]{4,3,2,1,0:T(8,128)(2,1)S(1)} %collective-permute-done.5.part, ...), custom_call_target="tpu_custom_call" | custom-call | bytes 6000000 | tf_op jit(solution)/shard_map/pallas_call | solution.py:524
  22.9 0.2 collective-permute-start.9
  23.2 1.0 %collective-permute-done.9 = f32[56,128]{1,0:T(8,128)S(1)} collective-permute-done((f32[56,128]{1,0:T(8,128)S(1)}, f32[56,128]{1,0:T(8,128)S(1)}, u32[]{:S(2)}, u32[]{:S(2)}) %collective-permute-start.9) | collective-permute-done | bytes 28704 | tf_op jit(solution)/shard_map/ppermute | solution.py:537
  24.2 4.5 %collective-permute-start.13 = (f32[56,128]{1,0:T(8,128)S(1)}, f32[56,128]{1,0:T(8,128)S(1)}, u32[]{:S(2)}, u32[]{:S(2)}) collective-permute-start(f32[56,128]{1,0:T(8,128)S(1)} %add.28), channel_id=1, source_target_pairs={{0,2},{2,0},{4,6},{6,4},{8,10},{10,8},{12,14},{14,12},{1,3},{3,1},... | collective-permute-start | bytes 86024 | tf_op jit(solution)/shard_map/ppermute | solution.py:640
  28.7 0.3 shard_map.93.own
  29.1 2.9 %collective-permute-start.11 = (bf16[64,512]{1,0:T(8,128)(2,1)S(1)}, bf16[64,512]{1,0:T(8,128)(2,1)S(1)}, u32[]{:S(2)}, u32[]{:S(2)}) collective-permute-start(bf16[64,512]{1,0:T(8,128)(2,1)S(1)} %shard_map.93.own), channel_id=1, source_target_pairs={{0,14},{2,12},{4,10},{6,8},{8,6},{10,4},{12,2},{14,0},{1,15},{3,13... | collective-permute-start | bytes 196616 | tf_op jit(solution)/shard_map/ppermute | solution.py:542
  32.0 1.6 %collective-permute-start.14 = (f32[56,128]{1,0:T(8,128)S(1)}, f32[56,128]{1,0:T(8,128)S(1)}, u32[]{:S(2)}, u32[]{:S(2)}) collective-permute-start(f32[56,128]{1,0:T(8,128)S(1)} %add.29), channel_id=1, source_target_pairs={{0,4},{2,6},{4,0},{6,2},{8,12},{10,14},{12,8},{14,10},{1,5},{3,7},... | collective-permute-start | bytes 86024 | tf_op jit(solution)/shard_map/ppermute | solution.py:640
  33.6 2.4 %collective-permute-done.14 = f32[56,128]{1,0:T(8,128)S(1)} collective-permute-done((f32[56,128]{1,0:T(8,128)S(1)}, f32[56,128]{1,0:T(8,128)S(1)}, u32[]{:S(2)}, u32[]{:S(2)}) %collective-permute-start.14) | collective-permute-done | bytes 28704 | tf_op jit(solution)/shard_map/ppermute | solution.py:640
  35.9 1.5 %collective-permute-start.15 = (f32[56,128]{1,0:T(8,128)S(1)}, f32[56,128]{1,0:T(8,128)S(1)}, u32[]{:S(2)}, u32[]{:S(2)}) collective-permute-start(f32[56,128]{1,0:T(8,128)S(1)} %add.30), channel_id=1, source_target_pairs={{0,8},{2,10},{4,12},{6,14},{8,0},{10,2},{12,4},{14,6},{1,9},{3,11}... | collective-permute-start | bytes 86024 | tf_op jit(solution)/shard_map/ppermute | solution.py:640
  37.5 0.5 %collective-permute-start.12 = (bf16[64,512]{1,0:T(8,128)(2,1)S(1)}, bf16[64,512]{1,0:T(8,128)(2,1)S(1)}, u32[]{:S(2)}, u32[]{:S(2)}) collective-permute-start(bf16[64,512]{1,0:T(8,128)(2,1)S(1)} %collective-permute-done.11.across_x), channel_id=1, source_target_pairs={{0,1},{1,0},{2,3},{3,2},{4,5},{5,4},{6,7},{7,6},{8,9},{9,8},{10,11... | collective-permute-start | bytes 196616 | tf_op jit(solution)/shard_map/ppermute | solution.py:537
  38.0 2.7 %collective-permute-done.15 = f32[56,128]{1,0:T(8,128)S(1)} collective-permute-done((f32[56,128]{1,0:T(8,128)S(1)}, f32[56,128]{1,0:T(8,128)S(1)}, u32[]{:S(2)}, u32[]{:S(2)}) %collective-permute-start.15) | collective-permute-done | bytes 28704 | tf_op jit(solution)/shard_map/ppermute | solution.py:640
  40.7 0.6 %fusion = (f32[27,84]{1,0:T(8,128)}, f32[27,84]{1,0:T(8,128)}) fusion(f32[56,128]{1,0:T(8,128)S(1)} %add.31), kind=kLoop, calls=%fused_computation.12 | loop fusion | bytes 36288 | tf_op jit(solution)/shard_map/slice | solution.py:642
  41.3 0.9 %shard_map.94 = bf16[30,2,512]{2,1,0:T(2,128)(2,1)} custom-call(bf16[6,16,128]{2,1,0:T(8,128)(2,1)S(1)} %get-tuple-element.42.turn_choice, bf16[64,512]{1,0:T(8,128)(2,1)S(1)} %shard_map.93.own, bf16[64,512]{1,0:T(8,128)(2,1)S(1)} %collective-permute-done.10.across_y, bf16[64,512]{1,0:T(8,128)(2,1)S(1)} %collective-permute-done.11.across_x, ...), custom_call_target="tpu_custom_call" | custom-call | bytes 2700000 | tf_op jit(solution)/shard_map/pallas_call | solution.py:524
  (34 shorter events, 0.2 us)
Async XLA Ops:
  0.6 11.7 %copy-start.2 = (s32[2,3]{1,0:T(2,128)S(1)}, s32[2,3]{1,0:T(2,128)}, u32[]{:S(2)}) copy-start(s32[2,3]{1,0:T(2,128)} %param.11) | copy-start | bytes 76
  0.6 11.7 %copy-start.3 = (s32[2,27]{1,0:T(2,128)S(1)}, s32[2,27]{1,0:T(2,128)}, u32[]{:S(2)}) copy-start(s32[2,27]{1,0:T(2,128)} %param.10) | copy-start | bytes 652
  0.7 11.7 %copy-start = (bf16[27,84]{1,0:T(8,128)(2,1)S(1)}, bf16[27,84]{1,0:T(8,128)(2,1)}, u32[]{:S(2)}) copy-start(bf16[27,84]{1,0:T(8,128)(2,1)} %param.9) | copy-start | bytes 13612
  0.7 11.7 %copy-start.1 = (bf16[27,84]{1,0:T(8,128)(2,1)S(1)}, bf16[27,84]{1,0:T(8,128)(2,1)}, u32[]{:S(2)}) copy-start(bf16[27,84]{1,0:T(8,128)(2,1)} %param.8) | copy-start | bytes 13612
  1.5 1.7 %collective-permute-start.3 = (bf16[2,30,512]{2,1,0:T(8,128)(2,1)S(1)}, bf16[2,30,512]{2,1,0:T(8,128)(2,1)S(1)}, u32[]{:S(2)}, u32[]{:S(2)}) collective-permute-start(bf16[2,30,512]{2,1,0:T(8,128)(2,1)S(1)} %copy.16.own), channel_id=1, source_target_pairs={{0,1},{1,0},{2,3},{3,2},{4,5},{5,4},{6,7},{7,6},{8,9},{9,8},{10,11... | collective-permute-start | bytes 184328 | tf_op jit(solution)/shard_map/ppermute | solution.py:537
  3.1 6.2 %collective-permute-start = (bf16[2,8,32,128]{3,2,0,1:T(8,128)(2,1)S(1)}, bf16[2,8,32,128]{3,2,0,1:T(8,128)(2,1)S(1)}, u32[]{:S(2)}, u32[]{:S(2)}) collective-permute-start(bf16[2,8,32,128]{3,2,0,1:T(8,128)(2,1)S(1)} %copy.10), channel_id=1, source_target_pairs={{0,1},{1,0},{2,3},{3,2},{4,5},{5,4},{6,7},{7,6},{8,9},{9,8},{10,11... | collective-permute-start | bytes 393224 | tf_op jit(solution)/shard_map/ppermute | solution.py:537
  3.3 11.0 %collective-permute-start.4 = (bf16[4,30,512]{2,1,0:T(8,128)(2,1)S(1)}, bf16[4,30,512]{2,1,0:T(8,128)(2,1)S(1)}, u32[]{:S(2)}, u32[]{:S(2)}) collective-permute-start(bf16[4,30,512]{2,1,0:T(8,128)(2,1)S(1)} %pad_maximum_fusion), channel_id=1, source_target_pairs={{0,14},{2,12},{4,10},{6,8},{8,6},{10,4},{12,2},{14,0},{1,15},{3,13... | collective-permute-start | bytes 368648 | tf_op jit(solution)/shard_map/ppermute | solution.py:542
  9.3 5.2 %collective-permute-start.2 = (bf16[4,32,128]{2,1,0:T(8,128)(2,1)S(1)}, bf16[4,32,128]{2,1,0:T(8,128)(2,1)S(1)}, u32[]{:S(2)}, u32[]{:S(2)}) collective-permute-start(bf16[4,32,128]{2,1,0:T(8,128)(2,1)S(1)} %get-tuple-element.77), channel_id=1, source_target_pairs={{2,4},{4,2},{6,8},{8,6},{10,12},{12,10},{3,5},{5,3},{7,9},{9,7},{1... | collective-permute-start | bytes 98312 | tf_op jit(solution)/shard_map/ppermute | solution.py:550
  10.0 4.6 %collective-permute-start.1 = (bf16[4,32,128]{2,1,0:T(8,128)(2,1)S(1)}, bf16[4,32,128]{2,1,0:T(8,128)(2,1)S(1)}, u32[]{:S(2)}, u32[]{:S(2)}) collective-permute-start(bf16[4,32,128]{2,1,0:T(8,128)(2,1)S(1)} %get-tuple-element.78), channel_id=1, source_target_pairs={{0,2},{2,0},{4,6},{6,4},{8,10},{10,8},{12,14},{14,12},{1,3},{3,1},... | collective-permute-start | bytes 98312 | tf_op jit(solution)/shard_map/ppermute | solution.py:550
  15.2 2.8 %collective-permute-start.5 = (bf16[2,2,8,32,128]{4,3,2,1,0:T(8,128)(2,1)S(1)}, bf16[2,2,8,32,128]{4,3,2,1,0:T(8,128)(2,1)S(1)}, u32[]{:S(2)}, u32[]{:S(2)}) collective-permute-start(bf16[2,2,8,32,128]{4,3,2,1,0:T(8,128)(2,1)S(1)} %get-tuple-element.51.own), channel_id=1, source_target_pairs={{0,1},{1,0},{2,3},{3,2},{4,5},{5,4},{6,7},{7,6},{8,9},{9,8},{10,11... | collective-permute-start | bytes 786440 | tf_op jit(solution)/shard_map/ppermute | solution.py:537
  15.2 5.0 %collective-permute-start.6 = (bf16[2,2,32,128]{3,2,1,0:T(8,128)(2,1)S(1)}, bf16[2,2,32,128]{3,2,1,0:T(8,128)(2,1)S(1)}, u32[]{:S(2)}, u32[]{:S(2)}) collective-permute-start(bf16[2,2,32,128]{3,2,1,0:T(8,128)(2,1)S(1)} %get-tuple-element.55), channel_id=1, source_target_pairs={{0,2},{2,0},{4,6},{6,4},{8,10},{10,8},{12,14},{14,12},{1,3},{3,1},... | collective-permute-start | bytes 98312 | tf_op jit(solution)/shard_map/ppermute | solution.py:550
  17.3 3.0 %collective-permute-start.7 = (bf16[2,2,32,128]{3,2,1,0:T(8,128)(2,1)S(1)}, bf16[2,2,32,128]{3,2,1,0:T(8,128)(2,1)S(1)}, u32[]{:S(2)}, u32[]{:S(2)}) collective-permute-start(bf16[2,2,32,128]{3,2,1,0:T(8,128)(2,1)S(1)} %get-tuple-element.56), channel_id=1, source_target_pairs={{2,4},{4,2},{6,8},{8,6},{10,12},{12,10},{3,5},{5,3},{7,9},{9,7},{1... | collective-permute-start | bytes 98312 | tf_op jit(solution)/shard_map/ppermute | solution.py:550
  20.3 1.3 %collective-permute-start.8 = (bf16[2,2,2,32,128]{4,3,2,1,0:T(8,128)(2,1)S(1)}, bf16[2,2,2,32,128]{4,3,2,1,0:T(8,128)(2,1)S(1)}, u32[]{:S(2)}, u32[]{:S(2)}) collective-permute-start(bf16[2,2,2,32,128]{4,3,2,1,0:T(8,128)(2,1)S(1)} %pad_maximum_fusion.1), channel_id=1, source_target_pairs={{0,1},{1,0},{2,3},{3,2},{4,5},{5,4},{6,7},{7,6},{8,9},{9,8},{10,11... | collective-permute-start | bytes 196616 | tf_op jit(solution)/shard_map/ppermute | solution.py:537
  22.9 1.3 %collective-permute-start.9 = (f32[56,128]{1,0:T(8,128)S(1)}, f32[56,128]{1,0:T(8,128)S(1)}, u32[]{:S(2)}, u32[]{:S(2)}) collective-permute-start(f32[56,128]{1,0:T(8,128)S(1)} %get-tuple-element.71), channel_id=1, source_target_pairs={{0,1},{1,0},{2,3},{3,2},{4,5},{5,4},{6,7},{7,6},{8,9},{9,8},{10,11... | collective-permute-start | bytes 86024 | tf_op jit(solution)/shard_map/ppermute | solution.py:537
  24.2 7.8 %collective-permute-start.13 = (f32[56,128]{1,0:T(8,128)S(1)}, f32[56,128]{1,0:T(8,128)S(1)}, u32[]{:S(2)}, u32[]{:S(2)}) collective-permute-start(f32[56,128]{1,0:T(8,128)S(1)} %add.28), channel_id=1, source_target_pairs={{0,2},{2,0},{4,6},{6,4},{8,10},{10,8},{12,14},{14,12},{1,3},{3,1},... | collective-permute-start | bytes 86024 | tf_op jit(solution)/shard_map/ppermute | solution.py:640
  29.1 8.4 %collective-permute-start.11 = (bf16[64,512]{1,0:T(8,128)(2,1)S(1)}, bf16[64,512]{1,0:T(8,128)(2,1)S(1)}, u32[]{:S(2)}, u32[]{:S(2)}) collective-permute-start(bf16[64,512]{1,0:T(8,128)(2,1)S(1)} %shard_map.93.own), channel_id=1, source_target_pairs={{0,14},{2,12},{4,10},{6,8},{8,6},{10,4},{12,2},{14,0},{1,15},{3,13... | collective-permute-start | bytes 196616 | tf_op jit(solution)/shard_map/ppermute | solution.py:542
  32.0 3.9 %collective-permute-start.14 = (f32[56,128]{1,0:T(8,128)S(1)}, f32[56,128]{1,0:T(8,128)S(1)}, u32[]{:S(2)}, u32[]{:S(2)}) collective-permute-start(f32[56,128]{1,0:T(8,128)S(1)} %add.29), channel_id=1, source_target_pairs={{0,4},{2,6},{4,0},{6,2},{8,12},{10,14},{12,8},{14,10},{1,5},{3,7},... | collective-permute-start | bytes 86024 | tf_op jit(solution)/shard_map/ppermute | solution.py:640
  35.9 4.8 %collective-permute-start.15 = (f32[56,128]{1,0:T(8,128)S(1)}, f32[56,128]{1,0:T(8,128)S(1)}, u32[]{:S(2)}, u32[]{:S(2)}) collective-permute-start(f32[56,128]{1,0:T(8,128)S(1)} %add.30), channel_id=1, source_target_pairs={{0,8},{2,10},{4,12},{6,14},{8,0},{10,2},{12,4},{14,6},{1,9},{3,11}... | collective-permute-start | bytes 86024 | tf_op jit(solution)/shard_map/ppermute | solution.py:640
  37.5 3.9 %collective-permute-start.10 = (bf16[64,512]{1,0:T(8,128)(2,1)S(1)}, bf16[64,512]{1,0:T(8,128)(2,1)S(1)}, u32[]{:S(2)}, u32[]{:S(2)}) collective-permute-start(bf16[64,512]{1,0:T(8,128)(2,1)S(1)} %shard_map.93.own), channel_id=1, source_target_pairs={{0,1},{1,0},{2,3},{3,2},{4,5},{5,4},{6,7},{7,6},{8,9},{9,8},{10,11... | collective-permute-start | bytes 196616 | tf_op jit(solution)/shard_map/ppermute | solution.py:537
  37.5 3.9 %collective-permute-start.12 = (bf16[64,512]{1,0:T(8,128)(2,1)S(1)}, bf16[64,512]{1,0:T(8,128)(2,1)S(1)}, u32[]{:S(2)}, u32[]{:S(2)}) collective-permute-start(bf16[64,512]{1,0:T(8,128)(2,1)S(1)} %collective-permute-done.11.across_x), channel_id=1, source_target_pairs={{0,1},{1,0},{2,3},{3,2},{4,5},{5,4},{6,7},{7,6},{8,9},{9,8},{10,11... | collective-permute-start | bytes 196616 | tf_op jit(solution)/shard_map/ppermute | solution.py:537
